TPU v7x, 32 devices: a whole 2x2x4 slice. The times are simulated.
32 devices in a mesh: section: 4 (over y, x), dp: 8 (over z, core).
Axes of the slice: x: 2, y: 2, z: 4, core: 2. Of those that a mesh axis runs over, the one named last changes fastest.
Arguments:
- latents: bfloat16 [2048, 1536], P('dp'), may hold values from -6 to 6
- media: bfloat16 [8192, 1536], P('dp'), may hold values from -6 to 6
- segment_ids: int32 [8, 1024], P('dp'), may hold values from -1 to 3, as said below
- slot_map: int32 [8, 4], P('dp'), may hold values from 0 to 3, each once within a row
- gains: float32 [2, 3, 1536], P(None, None, ('section', 'dp')), may hold values from 0.5 to 1.5
- w_query: bfloat16 [4, 1536, 768], P('section', 'dp'), may hold values from -0.15625 to 0.15625
- w_key: bfloat16 [4, 1536, 768], P('section', 'dp'), may hold values from -0.15625 to 0.15625
- w_value: bfloat16 [4, 1536, 768], P('section', 'dp'), may hold values from -0.15625 to 0.15625
- w_out: bfloat16 [4, 768, 1536], P('section', 'dp'), may hold values from -1.25 to 1.25
- w_up: bfloat16 [4, 1536, 3072], P('section', 'dp'), may hold values from -0.15625 to 0.15625
- w_down: bfloat16 [4, 3072, 1536], P('section', 'dp'), may hold values from -0.078125 to 0.078125
- cotangent: bfloat16 [2048, 1536], P('dp'), may hold values from -6 to 6
Outputs:
- latents_out: float32 [2048, 1536], P('dp', 'section')
- latent_grad: float32 [2048, 1536], P('dp', 'section')
- media_grad: float32 [8192, 1536], P('dp')
- gain_grad: float32 [2, 3, 1536], P(None, None, ('section', 'dp'))
- query_grad: float32 [4, 1536, 768], P('section', 'dp')
- key_grad: float32 [4, 1536, 768], P('section', 'dp')
- value_grad: float32 [4, 1536, 768], P('section', 'dp')
- out_grad: float32 [4, 768, 1536], P('section', 'dp')
- up_grad: float32 [4, 1536, 3072], P('section', 'dp')
- down_grad: float32 [4, 3072, 1536], P('section', 'dp')
Inputs may be any that keep to these rules, and one draw needn't show every extreme that they name: `segment_ids`: in each sequence, images 0 to 3 each hold one run of one or more consecutive rows, in that order, and one or more pad rows (-1) follow them. `slot_map`: each row is a permutation of 0 to 3.
All inputs are finite; a program needn't handle non-finite values.
Results may differ from a plain program's by a relative error of at most 0.024.
Values may be sent and summed in bfloat16 or wider, within the bound.
No kernel may reach another device: no remote copies, remote signals or barrier semaphores. Data moves between devices by JAX's collectives and lax.ppermute only.
A program may use at most 256 MiB of HBM per device.

v0:
```python
import math

import jax
import jax.numpy as jnp
from jax import lax
from jax.sharding import PartitionSpec as P

HEAD_DIM = 96
LATENTS = 64
LAYERS = 2
MICRO = 2


epsilon = 1e-05


def swapped(value, axis, distance):
    mask = 2**distance
    pairs = [(source, source ^ mask) for source in range(lax.axis_size(axis))]
    return lax.ppermute(value, axis, pairs)


def shifted(value, axis, steps):
    count = lax.axis_size(axis)
    first, last = (max(0, -steps), min(count, count - steps))
    return lax.ppermute(value, axis, [(source, source + steps) for source in range(first, last)])


def from_behind(value, axis, steps):
    count = lax.axis_size(axis)
    pairs = [(source, (source + steps) % count) for source in range(count)]
    return lax.ppermute(value, axis, pairs)


def normalize(values, gain_row):
    centered = values - jnp.mean(values, axis=-1, keepdims=True)
    variance = jnp.mean(centered * centered, axis=-1, keepdims=True)
    unit_rows = centered * lax.rsqrt(variance + epsilon)
    return (unit_rows * gain_row, unit_rows)


def norm_back(values, gain_row, grad_rows):

    def apply_norm(inputs):
        return normalize(inputs, gain_row)[0]

    return jax.vjp(apply_norm, values)[1](grad_rows)[0]


def gelu_exact(values):
    return jax.nn.gelu(values, approximate=False)


def matmul(left, right):
    return jnp.dot(left, right, preferred_element_type=jnp.float32)


def matmul_nt(left, right):
    return lax.dot_general(
        left, right, (((1,), (1,)), ((), ())), preferred_element_type=jnp.float32
    )


def matmul_tn(left, right):
    return lax.dot_general(
        left, right, (((0,), (0,)), ((), ())), preferred_element_type=jnp.float32
    )


def joined_product(left_list, right_list):
    return matmul_tn(jnp.concatenate(left_list, axis=0), jnp.concatenate(right_list, axis=0))


def pair_sum(partial_rows):
    return partial_rows + swapped(partial_rows.astype(jnp.bfloat16), "section", 0).astype(
        partial_rows.dtype
    )


def masked_scores(query_heads, key_heads, query_slot, key_slot, score_scale):
    scores = (
        jnp.einsum("sqhd,skhd->shqk", query_heads, key_heads, preferred_element_type=jnp.float32)
        * score_scale
    )
    allowed = query_slot[None, None, :, None] == key_slot[:, None, None, :]
    return jnp.where(allowed, scores, -1e30)


def attend_forward(query_heads, key_heads, value_heads, query_slot, key_slot, score_scale):
    scores = masked_scores(query_heads, key_heads, query_slot, key_slot, score_scale)
    row_max = jnp.max(scores, axis=-1, keepdims=True)
    exponent = jnp.exp(scores - row_max)
    row_total = jnp.sum(exponent, axis=-1, keepdims=True)
    weights_low = (exponent / row_total).astype(jnp.bfloat16)
    attended = jnp.einsum(
        "shqk,skhd->sqhd", weights_low, value_heads, preferred_element_type=jnp.float32
    )
    return (attended, row_max + jnp.log(row_total))


def attend_backward(
    query_heads, key_heads, value_heads, query_slot, key_slot, score_scale, log_total, grad_heads
):
    scores = masked_scores(query_heads, key_heads, query_slot, key_slot, score_scale)
    weights_full = jnp.exp(scores - log_total)
    weights_low = weights_full.astype(jnp.bfloat16)
    grad_value = jnp.einsum(
        "shqk,sqhd->skhd", weights_low, grad_heads, preferred_element_type=jnp.float32
    )
    grad_weights = jnp.einsum(
        "sqhd,skhd->shqk", grad_heads, value_heads, preferred_element_type=jnp.float32
    )
    row_inner = jnp.sum(weights_full * grad_weights, axis=-1, keepdims=True)
    grad_scores = (weights_full * (grad_weights - row_inner)).astype(jnp.bfloat16)
    grad_query = (
        jnp.einsum("shqk,skhd->sqhd", grad_scores, key_heads, preferred_element_type=jnp.float32)
        * score_scale
    )
    grad_key = (
        jnp.einsum("shqk,sqhd->skhd", grad_scores, query_heads, preferred_element_type=jnp.float32)
        * score_scale
    )
    return (grad_query, grad_key, grad_value)


def per_device(
    latents,
    media,
    segment_ids,
    slot_map,
    gains,
    w_query,
    w_key,
    w_value,
    w_out,
    w_up,
    w_down,
    cotangent,
):
    section_index = lax.axis_index("section")
    layer_index = section_index // 2
    section_count = lax.axis_size("section")
    seq_count = segment_ids.shape[0]
    seq_rows = segment_ids.shape[1]
    slot_count = slot_map.shape[1]
    feature_width = latents.shape[1]
    slots_micro = slot_count // MICRO
    micro_rows = slots_micro * LATENTS
    half_inner = w_query.shape[2]
    half_heads = half_inner // HEAD_DIM
    score_scale = 1.0 / math.sqrt(HEAD_DIM)
    tick_count = MICRO + 1
    head_shape = (seq_count, -1, half_heads, HEAD_DIM)
    block_shape = (seq_count * micro_rows, feature_width)
    all_gains = lax.all_gather(gains, ("section", "dp"), axis=2, tiled=True)
    layer_gains = lax.dynamic_index_in_dim(all_gains, layer_index, 0, keepdims=False)
    gain_media = layer_gains[0]
    gain_latent = layer_gains[1]
    gain_ffn = layer_gains[2]
    gathered = (
        lax.all_gather(w_query, "dp", axis=1, tiled=True),
        lax.all_gather(w_key, "dp", axis=1, tiled=True),
        lax.all_gather(w_value, "dp", axis=1, tiled=True),
        lax.all_gather(w_out, "dp", axis=1, tiled=True),
        lax.all_gather(w_up, "dp", axis=1, tiled=True),
        lax.all_gather(w_down, "dp", axis=1, tiled=True),
    )
    query_w, key_w, value_w, out_w, up_w, down_w = [
        gathered_piece[0] for gathered_piece in gathered
    ]
    image_hot = segment_ids[:, :, None] == jnp.arange(slot_count, dtype=jnp.int32)[None, None, :]
    media_slot = jnp.sum(jnp.where(image_hot, slot_map[:, None, :], 0), axis=2) - (
        segment_ids < 0
    ).astype(jnp.int32)
    media_rows = media.astype(jnp.float32)
    media_norm, media_unit = normalize(media_rows, gain_media)
    media_low = media_norm.astype(jnp.bfloat16)
    media_key = matmul(media_low, key_w).astype(jnp.bfloat16)
    media_value = matmul(media_low, value_w).astype(jnp.bfloat16)
    latent_blocks = latents.reshape(seq_count, MICRO, micro_rows, feature_width)
    cotangent_blocks = cotangent.reshape(seq_count, MICRO, micro_rows, feature_width)
    local_slot = jnp.arange(micro_rows, dtype=jnp.int32) // LATENTS

    def slots_for(micro_index):
        query_slot = micro_index * slots_micro + local_slot
        latent_keys = query_slot[None, :]
        return (query_slot, jnp.concatenate([media_slot, latent_keys], axis=1))

    received = jnp.zeros(block_shape, jnp.float32)
    saved_ticks = []
    for tick_index in range(tick_count):
        fresh_rows = (
            latent_blocks[:, min(tick_index, MICRO - 1)].reshape(block_shape).astype(jnp.float32)
        )
        block_input = jnp.where(layer_index == 0, fresh_rows, received)
        query_slot, key_slot = slots_for(jnp.clip(tick_index - layer_index, 0, MICRO - 1))
        latent_norm, latent_unit = normalize(block_input, gain_latent)
        latent_low = latent_norm.astype(jnp.bfloat16)
        query_low = matmul(latent_low, query_w).astype(jnp.bfloat16)
        latent_key = matmul(latent_low, key_w).astype(jnp.bfloat16)
        latent_value = matmul(latent_low, value_w).astype(jnp.bfloat16)
        key_heads = jnp.concatenate(
            [media_key.reshape(head_shape), latent_key.reshape(head_shape)], axis=1
        )
        value_heads = jnp.concatenate(
            [media_value.reshape(head_shape), latent_value.reshape(head_shape)], axis=1
        )
        attended, log_total = attend_forward(
            query_low.reshape(head_shape), key_heads, value_heads, query_slot, key_slot, score_scale
        )
        attended_low = attended.reshape(-1, half_inner).astype(jnp.bfloat16)
        middle = block_input + pair_sum(matmul(attended_low, out_w))
        ffn_norm, ffn_unit = normalize(middle, gain_ffn)
        ffn_low = ffn_norm.astype(jnp.bfloat16)
        hidden_pre = matmul(ffn_low, up_w)
        active_low = gelu_exact(hidden_pre).astype(jnp.bfloat16)
        block_output = middle + pair_sum(matmul(active_low, down_w))
        saved_ticks.append(
            (
                block_input,
                latent_low,
                query_low,
                latent_key,
                latent_value,
                log_total,
                attended_low,
                middle,
                ffn_low,
                hidden_pre,
                active_low,
                block_output,
            )
        )
        if tick_index + 1 < tick_count:
            received = shifted(block_output.astype(jnp.bfloat16), "section", 2).astype(
                block_output.dtype
            )
    stacked = [
        jnp.stack([record[field_index] for record in saved_ticks]) for field_index in range(12)
    ]
    media_key_grad = jnp.zeros((seq_count, seq_rows, half_heads, HEAD_DIM), jnp.float32)
    media_value_grad = jnp.zeros((seq_count, seq_rows, half_heads, HEAD_DIM), jnp.float32)
    gain_latent_grad = jnp.zeros((feature_width,), jnp.float32)
    gain_ffn_grad = jnp.zeros((feature_width,), jnp.float32)
    received = jnp.zeros(block_shape, jnp.float32)
    input_grads = []
    active_list = []
    down_list = []
    ffn_list = []
    hidden_list = []
    attended_list = []
    attended_grad_list = []
    latent_list = []
    query_grad_list = []
    key_grad_list = []
    value_grad_list = []
    for tick_index in range(tick_count):
        if tick_index < MICRO:
            fresh_rows = cotangent_blocks[:, tick_index].reshape(block_shape).astype(jnp.float32)
        else:
            fresh_rows = jnp.zeros(block_shape, jnp.float32)
        grad_output = jnp.where(layer_index == 1, fresh_rows, received)
        forward_tick = jnp.clip(tick_index - 1 + 2 * layer_index, 0, tick_count - 1)
        record = [
            lax.dynamic_index_in_dim(stacked_field, forward_tick, 0, keepdims=False)
            for stacked_field in stacked
        ]
        block_input = record[0]
        latent_low = record[1]
        query_low = record[2]
        latent_key = record[3]
        latent_value = record[4]
        log_total = record[5]
        attended_low = record[6]
        middle = record[7]
        ffn_low = record[8]
        hidden_pre = record[9]
        active_low = record[10]
        query_slot, key_slot = slots_for(jnp.clip(tick_index - 1 + layer_index, 0, MICRO - 1))
        grad_down_in = grad_output.astype(jnp.bfloat16)
        grad_active = matmul_nt(grad_down_in, down_w)
        grad_hidden = jax.vjp(gelu_exact, hidden_pre)[1](grad_active)[0].astype(jnp.bfloat16)
        active_list.append(active_low)
        down_list.append(grad_down_in)
        ffn_list.append(ffn_low)
        hidden_list.append(grad_hidden)
        ffn_part = matmul_nt(grad_hidden, up_w)
        ffn_unit = normalize(middle, gain_ffn)[1]
        gain_ffn_grad = gain_ffn_grad + jnp.sum(ffn_part * ffn_unit, axis=0)
        grad_middle = grad_output + norm_back(middle, gain_ffn, pair_sum(ffn_part))
        grad_attended = grad_middle.astype(jnp.bfloat16)
        attended_list.append(attended_low)
        attended_grad_list.append(grad_attended)
        grad_heads = matmul_nt(grad_attended, out_w).astype(jnp.bfloat16)
        key_heads = jnp.concatenate(
            [media_key.reshape(head_shape), latent_key.reshape(head_shape)], axis=1
        )
        value_heads = jnp.concatenate(
            [media_value.reshape(head_shape), latent_value.reshape(head_shape)], axis=1
        )
        grad_query, grad_key, grad_value = attend_backward(
            query_low.reshape(head_shape),
            key_heads,
            value_heads,
            query_slot,
            key_slot,
            score_scale,
            log_total,
            grad_heads.reshape(head_shape),
        )
        media_key_grad = media_key_grad + grad_key[:, :seq_rows]
        media_value_grad = media_value_grad + grad_value[:, :seq_rows]
        query_grad_low = grad_query.reshape(-1, half_inner).astype(jnp.bfloat16)
        key_grad_low = grad_key[:, seq_rows:].reshape(-1, half_inner).astype(jnp.bfloat16)
        value_grad_low = grad_value[:, seq_rows:].reshape(-1, half_inner).astype(jnp.bfloat16)
        latent_list.append(latent_low)
        query_grad_list.append(query_grad_low)
        key_grad_list.append(key_grad_low)
        value_grad_list.append(value_grad_low)
        latent_part = (
            matmul_nt(query_grad_low, query_w)
            + matmul_nt(key_grad_low, key_w)
            + matmul_nt(value_grad_low, value_w)
        )
        latent_unit = normalize(block_input, gain_latent)[1]
        gain_latent_grad = gain_latent_grad + jnp.sum(latent_part * latent_unit, axis=0)
        grad_input = grad_middle + norm_back(block_input, gain_latent, pair_sum(latent_part))
        input_grads.append(grad_input)
        if tick_index + 1 < tick_count:
            received = shifted(grad_input.astype(jnp.bfloat16), "section", -2).astype(
                grad_input.dtype
            )
    media_key_low = media_key_grad.reshape(-1, half_inner).astype(jnp.bfloat16)
    media_value_low = media_value_grad.reshape(-1, half_inner).astype(jnp.bfloat16)
    grad_query_w = joined_product(latent_list, query_grad_list)
    grad_key_w = joined_product(latent_list + [media_low], key_grad_list + [media_key_low])
    grad_value_w = joined_product(latent_list + [media_low], value_grad_list + [media_value_low])
    grad_out_w = joined_product(attended_list, attended_grad_list)
    media_part = matmul_nt(media_key_low, key_w) + matmul_nt(media_value_low, value_w)
    gain_media_grad = jnp.sum(media_part * media_unit, axis=0)
    media_grad = lax.psum(
        norm_back(media_rows, gain_media, media_part).astype(jnp.bfloat16), "section"
    ).astype(jnp.float32)
    gain_rows = jnp.stack([gain_media_grad, gain_latent_grad, gain_ffn_grad])
    layer_hot = (jnp.arange(LAYERS, dtype=jnp.int32) == layer_index)[:, None, None]
    gain_grad = lax.psum_scatter(
        jnp.where(layer_hot, gain_rows[None], 0.0),
        ("section", "dp"),
        scatter_dimension=2,
        tiled=True,
    )
    grad_up_w = joined_product(ffn_list, hidden_list)
    grad_down_w = joined_product(active_list, down_list)
    weight_grads = (
        lax.psum_scatter(grad_query_w[None], "dp", scatter_dimension=1, tiled=True),
        lax.psum_scatter(grad_key_w[None], "dp", scatter_dimension=1, tiled=True),
        lax.psum_scatter(grad_value_w[None], "dp", scatter_dimension=1, tiled=True),
        lax.psum_scatter(grad_out_w[None], "dp", scatter_dimension=1, tiled=True),
        lax.psum_scatter(grad_up_w[None], "dp", scatter_dimension=1, tiled=True),
        lax.psum_scatter(grad_down_w[None], "dp", scatter_dimension=1, tiled=True),
    )
    result_blocks = []
    for micro_index in range(MICRO):
        forward_rows = saved_ticks[micro_index + 1][11]
        backward_rows = input_grads[micro_index + 1]
        chosen = jnp.where(layer_index == 1, forward_rows, backward_rows)
        result_blocks.append(chosen.reshape(seq_count, micro_rows, feature_width))
    result_rows = jnp.stack(result_blocks, axis=1).reshape(-1, feature_width)
    quarter = feature_width // section_count
    target_section = (section_index + 2) % section_count
    outgoing = lax.dynamic_slice_in_dim(result_rows, target_section * quarter, quarter, 1)
    incoming = from_behind(outgoing.astype(jnp.bfloat16), "section", 2).astype(outgoing.dtype)
    own_block = lax.dynamic_slice_in_dim(result_rows, section_index * quarter, quarter, 1)
    latents_out = jnp.where(layer_index == 1, own_block, incoming)
    latent_grad = jnp.where(layer_index == 0, own_block, incoming)
    return (
        latents_out,
        latent_grad,
        media_grad,
        gain_grad,
        weight_grads[0],
        weight_grads[1],
        weight_grads[2],
        weight_grads[3],
        weight_grads[4],
        weight_grads[5],
    )


def solution(mesh):
    placed = (
        P("dp", None),
        P("dp", None),
        P("dp", None),
        P("dp", None),
        P(None, None, ("section", "dp")),
        P("section", "dp", None),
        P("section", "dp", None),
        P("section", "dp", None),
        P("section", "dp", None),
        P("section", "dp", None),
        P("section", "dp", None),
        P("dp", None),
    )
    return jax.shard_map(
        per_device,
        mesh=mesh,
        in_specs=placed,
        out_specs=(
            P("dp", "section"),
            P("dp", "section"),
            P("dp", None),
            P(None, None, ("section", "dp")),
            P("section", "dp", None),
            P("section", "dp", None),
            P("section", "dp", None),
            P("section", "dp", None),
            P("section", "dp", None),
            P("section", "dp", None),
        ),
        check_vma=False,
    )
```

profile of v0, /device:TPU:0, one launch (start us, length us, event | category | flops | bytes accessed | tf_op | source)
XLA Modules:
  0.0 1453.3 jit_solution(9510114468669472147)
XLA Ops:
  12.2 60.6 %all_gather.21 = f32[2,3,1536]{1,0,2:T(2,128)S(1)} all-gather(f32[2,3,48]{1,0,2:T(2,128)S(1)} %copy.102), channel_id=1, replica_groups=mesh['section'=4,'dp'=8] {'section','dp'}, dimensions={2}, use_global_device_ids=true | all-gather | bytes 38016 | tf_op jit(solution)/shard_map/all_gather | solution.py:155
  76.1 45.4 %dynamic-slice_reduce_fusion = (f32[1536]{0:T(1024)S(1)}, f32[1536]{0:T(1024)S(1)}, f32[1536]{0:T(1024)S(1)}) fusion(f32[2,3,1536]{1,0,2:T(2,128)S(1)} %all_gather.21, s32[]{:T(128)S(6)} %select_n.261, s32[]{:T(128)S(6)} %add.690, s32[]{:T(128)S(6)} %add.689), kind=kLoop, calls=%fused_computation.429 | loop fusion | bytes 36876 | tf_op jit(solution)/shard_map/slice | solution.py:159
  154.8 10.0 collective-permute-done
  167.3 74.4 %all-gather.15.cloned.1.call-done = bf16[1,1536,3072]{2,1,0:T(8,128)(2,1)} async-done(((bf16[1,192,3072]{2,1,0:T(8,128)(2,1)}), bf16[1,1536,3072]{2,1,0:T(8,128)(2,1)}) %all-gather.15.cloned.1.call-update) | async-done | bytes 9437200 | tf_op jit(solution)/shard_map/all_gather | solution.py:165
  241.7 10.2 fusion.153
  251.9 80.5 %all-gather.17.cloned.1.call-done = bf16[1,3072,1536]{2,1,0:T(8,128)(2,1)} async-done(((bf16[1,384,1536]{2,1,0:T(8,128)(2,1)}), bf16[1,3072,1536]{2,1,0:T(8,128)(2,1)}) %all-gather.17.cloned.1.call-update) | async-done | bytes 9437200 | tf_op jit(solution)/shard_map/all_gather | solution.py:166
  341.6 7.6 collective-permute-done.1
  378.4 7.3 collective-permute-done.3
  386.3 7.7 fusion.156
  452.4 11.1 fusion.169
  525.2 8.9 fusion.166
  591.6 8.7 fusion.174
  672.8 8.7 convolution_bitcast_fusion.5
  682.6 8.7 convolution_bitcast_fusion.4
  700.4 9.0 convolution_bitcast_fusion
  726.1 9.2 convolution_bitcast_fusion.1
  736.7 15.1 %reduce-scatter.22.cloned.1.call-done = f32[48,6]{1,0:T(8,128)} async-done(((f32[1536,6]{1,0:T(8,128)}), f32[48,6]{1,0:T(8,128)}) %reduce-scatter.22.cloned.1.call-update) | async-done | bytes 1168
  754.2 87.0 %all-reduce.2.cloned.1.call-done = bf16[1024,1536]{1,0:T(8,128)(2,1)} async-done(((bf16[1024,1536]{1,0:T(8,128)(2,1)}), bf16[1024,1536]{1,0:T(8,128)(2,1)}) %all-reduce.2.cloned.1.call-update) | async-done | bytes 3145744 | tf_op jit(solution)/shard_map/psum | solution.py:341
  846.6 52.5 %reduce-scatter.10.cloned.1.call-done = f32[1,192,768]{2,1,0:T(8,128)} async-done(((f32[1,1536,768]{2,1,0:T(8,128)}), f32[1,192,768]{2,1,0:T(8,128)}) %reduce-scatter.10.cloned.1.call-update) | async-done | bytes 589840 | tf_op jit(solution)/shard_map/reduce_scatter | solution.py:355
  899.1 56.1 %reduce-scatter.12.cloned.1.call-done = f32[1,192,768]{2,1,0:T(8,128)} async-done(((f32[1,1536,768]{2,1,0:T(8,128)}), f32[1,192,768]{2,1,0:T(8,128)}) %reduce-scatter.12.cloned.1.call-update) | async-done | bytes 589840 | tf_op jit(solution)/shard_map/reduce_scatter | solution.py:356
  955.3 56.3 %reduce-scatter.14.cloned.1.call-done = f32[1,192,768]{2,1,0:T(8,128)} async-done(((f32[1,1536,768]{2,1,0:T(8,128)}), f32[1,192,768]{2,1,0:T(8,128)}) %reduce-scatter.14.cloned.1.call-update) | async-done | bytes 589840 | tf_op jit(solution)/shard_map/reduce_scatter | solution.py:357
  1011.6 56.2 %reduce-scatter.16.cloned.1.call-done = f32[1,96,1536]{2,1,0:T(8,128)} async-done(((f32[1,768,1536]{2,1,0:T(8,128)}), f32[1,96,1536]{2,1,0:T(8,128)}) %reduce-scatter.16.cloned.1.call-update) | async-done | bytes 589840 | tf_op jit(solution)/shard_map/reduce_scatter | solution.py:358
  1067.9 189.4 %reduce-scatter.20.cloned.1.call-done = f32[1,384,1536]{2,1,0:T(8,128)} async-done(((f32[1,3072,1536]{2,1,0:T(8,128)}), f32[1,384,1536]{2,1,0:T(8,128)}) %reduce-scatter.20.cloned.1.call-update) | async-done | bytes 2359312 | tf_op jit(solution)/shard_map/reduce_scatter | solution.py:360
  1257.3 189.3 %reduce-scatter.18.cloned.1.call-done = f32[1,192,3072]{2,1,0:T(8,128)} async-done(((f32[1,1536,3072]{2,1,0:T(8,128)}), f32[1,192,3072]{2,1,0:T(8,128)}) %reduce-scatter.18.cloned.1.call-update) | async-done | bytes 2359312 | tf_op jit(solution)/shard_map/reduce_scatter | solution.py:359
  (782 shorter events, 366.0 us)
Async XLA Ops:
  7.2 117.8 %all-gather.9.cloned.1.call-start = ((), (), s32[]{:S(2)}) async-start(), calls=%async_computation.8 | async-start | bytes 2654208 | tf_op jit(solution)/shard_map/all_gather | solution.py:161
  7.9 120.2 %all-gather.11.cloned.1.call-start = ((), (), s32[]{:S(2)}) async-start(), calls=%async_computation.9 | async-start | bytes 2654208 | tf_op jit(solution)/shard_map/all_gather | solution.py:162
  8.7 122.5 %all-gather.7.cloned.1.call-start = ((), (), s32[]{:S(2)}) async-start(), calls=%async_computation.7 | async-start | bytes 2654208 | tf_op jit(solution)/shard_map/all_gather | solution.py:163
  9.4 140.8 %all-gather.13.cloned.1.call-start = ((), (), s32[]{:S(2)}) async-start(), calls=%async_computation.10 | async-start | bytes 2654208 | tf_op jit(solution)/shard_map/all_gather | solution.py:164
  10.0 231.7 %all-gather.15.cloned.1.call-start = ((), (), s32[]{:S(2)}) async-start(), calls=%async_computation.11 | async-start | bytes 10616832 | tf_op jit(solution)/shard_map/all_gather | solution.py:165
  10.6 321.8 %all-gather.17.cloned.1.call-start = ((), (), s32[]{:S(2)}) async-start(), calls=%async_computation.12 | async-start | bytes 10616832 | tf_op jit(solution)/shard_map/all_gather | solution.py:166
  11.2 740.6 %reduce-scatter.22.cloned.1.call-start = ((), (), s32[]{:S(2)}) async-start(), calls=%async_computation.20 | async-start | bytes 811008
  153.4 11.5 collective-permute-start
  337.9 11.3 collective-permute-start.1
  350.2 11.4 collective-permute-start.2
  376.1 9.6 collective-permute-start.3
  404.4 9.7 collective-permute-start.5
  435.0 14.5 collective-permute-start.6
  513.2 10.1 collective-permute-start.9
  580.8 9.9 collective-permute-start.13
  638.1 12.5 collective-permute-start.15
  658.6 182.5 %all-reduce.2.cloned.1.call-start = ((), (), s32[]{:S(2)}) async-start(), calls=%async_computation.13 | async-start | bytes 6291456 | tf_op jit(solution)/shard_map/psum | solution.py:341
  663.6 235.6 %reduce-scatter.10.cloned.1.call-start = ((), (), s32[]{:S(2)}) async-start(), calls=%async_computation.14 | async-start | bytes 5308416 | tf_op jit(solution)/shard_map/reduce_scatter | solution.py:355
  671.7 283.6 %reduce-scatter.12.cloned.1.call-start = ((), (), s32[]{:S(2)}) async-start(), calls=%async_computation.15 | async-start | bytes 5308416 | tf_op jit(solution)/shard_map/reduce_scatter | solution.py:356
  681.5 330.1 %reduce-scatter.14.cloned.1.call-start = ((), (), s32[]{:S(2)}) async-start(), calls=%async_computation.16 | async-start | bytes 5308416 | tf_op jit(solution)/shard_map/reduce_scatter | solution.py:357
  691.4 376.5 %reduce-scatter.16.cloned.1.call-start = ((), (), s32[]{:S(2)}) async-start(), calls=%async_computation.17 | async-start | bytes 5308416 | tf_op jit(solution)/shard_map/reduce_scatter | solution.py:358
  696.4 560.8 %reduce-scatter.20.cloned.1.call-start = ((), (), s32[]{:S(2)}) async-start(), calls=%async_computation.19 | async-start | bytes 21233664 | tf_op jit(solution)/shard_map/reduce_scatter | solution.py:360
  709.5 737.0 %reduce-scatter.18.cloned.1.call-start = ((), (), s32[]{:S(2)}) async-start(), calls=%async_computation.18 | async-start | bytes 21233664 | tf_op jit(solution)/shard_map/reduce_scatter | solution.py:359
  736.6 16.7 %collective-permute-start.16 = (bf16[256,384]{1,0:T(8,128)(2,1)S(1)}, bf16[256,384]{1,0:T(8,128)(2,1)S(1)}, u32[]{:S(2)}, u32[]{:S(2)}) collective-permute-start(bf16[256,384]{1,0:T(8,128)(2,1)S(1)} %dynamic-slice_convert_fusion), channel_id=1, source_target_pairs={{0,16},{8,24},{16,0},{24,8},{1,17},{9,25},{17,1},{25,9},{2,18},{10... | collective-permute-start | bytes 589832 | tf_op jit(solution)/shard_map/ppermute | solution.py:32
  (247 other events, 1634.7 us)
Sparse Core Ops, SparseCore 0:
  9.7 42.9 all-gather.8
  54.3 30.6 all-gather.10
  86.6 31.2 all-gather.6
  119.4 30.7 all-gather.12
  151.7 89.9 all-gather.14
  243.2 89.1 all-gather.16
  658.8 92.9 reduce-scatter.21
  754.8 86.2 all-reduce.1
  844.1 54.9 reduce-scatter.9
  902.0 53.2 reduce-scatter.11
  958.3 53.3 reduce-scatter.13
  1014.5 53.3 reduce-scatter.15
  1070.9 186.3 reduce-scatter.19
  1260.2 186.3 reduce-scatter.17
where the time goes:
time: 1460 us; the launch traced here: 1450 us
  waiting for transfers between devices  958 us (66%)
  matrix products  206 us (14%)
  local copies, waits for them, and re-layouts  116 us (8%)
  other arithmetic  71.5 us (5%)
  blocking collectives  60.6 us (4%)
  starting transfers between devices  24.9 us (2%)
  between operations  17.4 us (1%)
    reduce_scatter x1, waiting for transfers between devices, per_device(): lax.psum_scatter(grad_down_w[None], 'dp', scatter_dimension=1, tiled=True)  189 us
    reduce_scatter x1, waiting for transfers between devices, per_device(): lax.psum_scatter(grad_up_w[None], 'dp', scatter_dimension=1, tiled=True)  189 us
    psum x1, waiting for transfers between devices, per_device(): lax.psum(norm_back(media_rows, gain_media, media_part).astype(jnp.bfloat1...  87 us
    all_gather x1, waiting for transfers between devices, per_device(): lax.all_gather(w_down, 'dp', axis=1, tiled=True)  80.5 us
    all_gather x1, waiting for transfers between devices, per_device(): lax.all_gather(w_up, 'dp', axis=1, tiled=True)  74.4 us
    ppermute x12, waiting for transfers between devices, swapped(): return lax.ppermute(value, axis, pairs)  72.5 us
    dot_general x20, matrix products, matmul(): return jnp.dot(left, right, preferred_element_type=jnp.float32)  72.2 us
    dot_general x20, matrix products, matmul_nt(): lax.dot_general(left, right, (((1,), (1,)), ((), ())), preferred_element_...  60.9 us
  transfers between devices with their start and end apart: 31, of which 25 were waited for; matrix products, arithmetic and copies ran while one was open for 13% of the time, Pallas kernels for 0%

commit v1 on v0

v1 whole, which is shorter than its diff:
```python
import math

import jax
import jax.numpy as jnp
from jax import lax
from jax.sharding import PartitionSpec as P

HEAD_DIM = 96
LATENTS = 64
LAYERS = 2
HALF_HEADS = 8

epsilon = 1e-05
low = jnp.bfloat16
full = jnp.float32


def unit_rows(values):
    centered = values - jnp.mean(values, axis=-1, keepdims=True)
    variance = jnp.mean(centered * centered, axis=-1, keepdims=True)
    inverse = lax.rsqrt(variance + epsilon)
    return centered * inverse, inverse


def norm_back(unit, inverse, scaled):
    first = jnp.mean(scaled, axis=-1, keepdims=True)
    second = jnp.mean(scaled * unit, axis=-1, keepdims=True)
    return (scaled - first - unit * second) * inverse


def gelu_exact(values):
    return jax.nn.gelu(values, approximate=False)


def matmul(left, right):
    return jnp.dot(left, right, preferred_element_type=full)


def matmul_nt(left, right):
    return lax.dot_general(left, right, (((1,), (1,)), ((), ())), preferred_element_type=full)


def matmul_tn(left, right):
    return lax.dot_general(left, right, (((0,), (0,)), ((), ())), preferred_element_type=full)


def attend_forward(query_heads, key_heads, value_heads, allowed, score_scale):
    scores = jnp.einsum("qhd,khd->hqk", query_heads, key_heads, preferred_element_type=full)
    scores = jnp.where(allowed, scores * score_scale, -1e30)
    row_max = jnp.max(scores, axis=-1, keepdims=True)
    exponent = jnp.exp(scores - row_max)
    row_total = jnp.sum(exponent, axis=-1, keepdims=True)
    weights_low = (exponent / row_total).astype(low)
    attended = jnp.einsum("hqk,khd->qhd", weights_low, value_heads, preferred_element_type=full)
    return attended, row_max + jnp.log(row_total)


def attend_backward(
    query_heads, key_heads, value_heads, allowed, score_scale, log_total, grad_heads
):
    scores = jnp.einsum("qhd,khd->hqk", query_heads, key_heads, preferred_element_type=full)
    scores = jnp.where(allowed, scores * score_scale, -1e30)
    weights_full = jnp.exp(scores - log_total)
    weights_low = weights_full.astype(low)
    grad_value = jnp.einsum("hqk,qhd->khd", weights_low, grad_heads, preferred_element_type=full)
    grad_weights = jnp.einsum(
        "qhd,khd->hqk", grad_heads, value_heads, preferred_element_type=full
    )
    row_inner = jnp.sum(weights_full * grad_weights, axis=-1, keepdims=True)
    grad_scores = (weights_full * (grad_weights - row_inner)).astype(low)
    grad_query = (
        jnp.einsum("hqk,khd->qhd", grad_scores, key_heads, preferred_element_type=full)
        * score_scale
    )
    grad_key = (
        jnp.einsum("hqk,qhd->khd", grad_scores, query_heads, preferred_element_type=full)
        * score_scale
    )
    return grad_query, grad_key, grad_value


def per_device(
    latents,
    media,
    segment_ids,
    slot_map,
    gains,
    w_query,
    w_key,
    w_value,
    w_out,
    w_up,
    w_down,
    cotangent,
):
    section = lax.axis_index("section")
    section_count = lax.axis_size("section")
    dp_index = lax.axis_index("dp")
    dp_count = lax.axis_size("dp")
    layer_bit = section // 2
    on_first = layer_bit == 0
    stride = dp_count // HALF_HEADS
    row_bit = (dp_index // stride) % 2
    row_first = row_bit == 0
    seq_rows = segment_ids.shape[1]
    slot_count = slot_map.shape[1]
    feature_width = latents.shape[1]
    latent_rows = latents.shape[0]
    heads = HALF_HEADS // 2
    inner = heads * HEAD_DIM
    score_scale = 1.0 / math.sqrt(HEAD_DIM)

    def pick(first, second):
        return jnp.where(on_first, first, second), jnp.where(on_first, second, first)

    def swap_layer(value):
        pairs = [(source, source ^ 2) for source in range(section_count)]
        return lax.ppermute(value, "section", pairs)

    def with_bit(index, bit):
        high, lowest = index // (2 * stride), index % stride
        return (2 * high + bit) * stride + lowest

    def bit_of(index):
        return (index // stride) % 2

    def turn_pairs(flip, back):
        pairs = []
        for source in range(section_count):
            for index in range(dp_count):
                layer, half = divmod(source, 2)
                target = (bit_of(index) * 2 + half) * dp_count + with_bit(index, layer ^ flip)
                pair = (source * dp_count + index, target)
                pairs.append(pair[::-1] if back else pair)
        return pairs

    def column_parts(weight, block):
        rows, width = weight.shape
        split = weight.reshape(rows, width // (2 * block), 2, block)
        return split[:, :, 0].reshape(rows, -1), split[:, :, 1].reshape(rows, -1)

    def exchange_columns(even, odd):
        own, other = pick(even, odd)
        return pick(own, swap_layer(other))

    def join_columns(first, second, block):
        own, other = pick(first, second)
        even, odd = pick(own, swap_layer(other))
        rows, width = even.shape
        pieces = [part.reshape(rows, width // block, 1, block) for part in (even, odd)]
        return jnp.concatenate(pieces, axis=2).reshape(rows, 2 * width).astype(full)

    def exchange_rows(weight):
        half = weight.shape[0] // 2
        near, far = pick(weight[:half], weight[half:])
        first = lax.ppermute(near, ("section", "dp"), turn_pairs(0, False))
        second = lax.ppermute(far, ("section", "dp"), turn_pairs(1, False))
        return (
            jnp.where(row_first, first, second),
            jnp.where(row_first, second, first),
        )

    def join_rows(first, second):
        near = jnp.where(row_first, first, second)
        far = jnp.where(row_first, second, first)
        near = lax.ppermute(near, ("section", "dp"), turn_pairs(0, True))
        far = lax.ppermute(far, ("section", "dp"), turn_pairs(1, True))
        return jnp.concatenate(pick(near, far), axis=0).astype(full)

    def gather_rows(piece):
        gathered = lax.all_gather(piece, "dp", axis=0, tiled=True)
        if stride > 1:
            width = gathered.shape[1]
            gathered = gathered.reshape(-1, 2, stride, piece.shape[0], width)
            gathered = gathered.transpose(0, 2, 1, 3, 4).reshape(-1, width)
        return gathered

    def scatter_rows(grad):
        if stride > 1:
            width = grad.shape[1]
            piece = grad.shape[0] // dp_count
            grad = grad.reshape(-1, stride, 2, piece, width)
            grad = grad.transpose(0, 2, 1, 3, 4).reshape(-1, width)
        return lax.psum_scatter(grad.astype(low), "dp", scatter_dimension=0, tiled=True)

    def scatter_columns(grad):
        return lax.psum_scatter(grad.astype(low), "dp", scatter_dimension=0, tiled=True)

    def sum_to_slots(partial):
        blocks = partial.astype(low).reshape(section_count, -1, feature_width)
        arrived = lax.all_to_all(blocks, "section", split_axis=0, concat_axis=0)
        return jnp.sum(arrived.astype(full), axis=0)

    def from_slots(rows):
        return lax.all_gather(rows, "section", axis=0, tiled=True)

    def to_columns(rows):
        moved = lax.all_to_all(
            rows.astype(low), "section", split_axis=1, concat_axis=0, tiled=True
        )
        return moved.astype(full)

    query_parts = column_parts(w_query[0], HEAD_DIM)
    key_parts = column_parts(w_key[0], HEAD_DIM)
    value_parts = column_parts(w_value[0], HEAD_DIM)
    joined = [
        jnp.concatenate([query_parts[i], key_parts[i], value_parts[i]], axis=1) for i in range(2)
    ]
    qkv_pieces = exchange_columns(joined[0], joined[1])
    out_pieces = exchange_rows(w_out[0])
    hidden_block = w_up.shape[2] // HALF_HEADS
    up_pieces = exchange_columns(*column_parts(w_up[0], hidden_block))
    down_pieces = exchange_rows(w_down[0])
    qkv_w, out_w, up_w, down_w = [], [], [], []
    for layer in range(LAYERS):
        qkv_w.append(lax.all_gather(qkv_pieces[layer], "dp", axis=0, tiled=True))
        out_w.append(gather_rows(out_pieces[layer]))
        up_w.append(lax.all_gather(up_pieces[layer], "dp", axis=0, tiled=True))
        down_w.append(gather_rows(down_pieces[layer]))
    query_w = [weight[:, :inner] for weight in qkv_w]
    key_w = [weight[:, inner : 2 * inner] for weight in qkv_w]
    value_w = [weight[:, 2 * inner :] for weight in qkv_w]

    all_gains = lax.all_gather(gains, ("section", "dp"), axis=2, tiled=True)
    image_hot = segment_ids[:, :, None] == jnp.arange(slot_count, dtype=jnp.int32)[None, None, :]
    media_slot = jnp.sum(jnp.where(image_hot, slot_map[:, None, :], 0), axis=2) - (
        segment_ids < 0
    ).astype(jnp.int32)
    media_unit, media_inverse = unit_rows(media.astype(full))
    latent_slot = jnp.arange(latent_rows, dtype=jnp.int32) // LATENTS
    key_slot = jnp.concatenate([media_slot[0], latent_slot])
    allowed = latent_slot[None, :, None] == key_slot[None, None, :]

    def split_heads(rows):
        return rows.reshape(rows.shape[0], heads, HEAD_DIM)

    media_low = []
    media_key = []
    media_value = []
    for layer in range(LAYERS):
        media_low.append((media_unit * all_gains[layer, 0]).astype(low))
        media_key.append(matmul(media_low[layer], key_w[layer]).astype(low))
        media_value.append(matmul(media_low[layer], value_w[layer]).astype(low))

    saved = []
    slot_rows = latent_rows // section_count
    current = lax.dynamic_slice_in_dim(latents, section * slot_rows, slot_rows, 0).astype(full)
    for layer in range(LAYERS):
        unit_in, inverse_in = unit_rows(current)
        if layer == 0:
            whole_unit = unit_rows(latents.astype(full))[0]
            latent_low = (whole_unit * all_gains[layer, 1]).astype(low)
        else:
            latent_low = from_slots((unit_in * all_gains[layer, 1]).astype(low))
        projected = matmul(latent_low, qkv_w[layer]).astype(low)
        query_low = projected[:, :inner]
        key_heads = split_heads(
            jnp.concatenate([media_key[layer], projected[:, inner : 2 * inner]], axis=0)
        )
        value_heads = split_heads(
            jnp.concatenate([media_value[layer], projected[:, 2 * inner :]], axis=0)
        )
        query_heads = split_heads(query_low)
        attended, log_total = attend_forward(
            query_heads, key_heads, value_heads, allowed, score_scale
        )
        attended_low = attended.reshape(-1, inner).astype(low)
        middle = current + sum_to_slots(matmul(attended_low, out_w[layer]))
        unit_mid, inverse_mid = unit_rows(middle)
        ffn_low = from_slots((unit_mid * all_gains[layer, 2]).astype(low))
        hidden_pre = matmul(ffn_low, up_w[layer])
        active_low = gelu_exact(hidden_pre).astype(low)
        current = middle + sum_to_slots(matmul(active_low, down_w[layer]))
        saved.append(
            (
                unit_in,
                inverse_in,
                latent_low,
                query_heads,
                key_heads,
                value_heads,
                log_total,
                attended_low,
                unit_mid,
                inverse_mid,
                ffn_low,
                hidden_pre,
                active_low,
            )
        )
    latents_out = to_columns(current)

    gain_rows = [None] * LAYERS
    media_scaled = None
    pieces = [None] * LAYERS
    grad_low = cotangent
    grad_rows = lax.dynamic_slice_in_dim(cotangent, section * slot_rows, slot_rows, 0).astype(full)
    for layer in (1, 0):
        (
            unit_in,
            inverse_in,
            latent_low,
            query_heads,
            key_heads,
            value_heads,
            log_total,
            attended_low,
            unit_mid,
            inverse_mid,
            ffn_low,
            hidden_pre,
            active_low,
        ) = saved[layer]
        grad_active = matmul_nt(grad_low, down_w[layer])
        grad_hidden = jax.vjp(gelu_exact, hidden_pre)[1](grad_active)[0].astype(low)
        down_piece = scatter_rows(matmul_tn(active_low, grad_low))
        up_piece = scatter_columns(matmul_tn(ffn_low, grad_hidden))
        ffn_grad = sum_to_slots(matmul_nt(grad_hidden, up_w[layer]))
        gain_ffn_grad = jnp.sum(ffn_grad * unit_mid, axis=0)
        grad_middle = grad_rows + norm_back(
            unit_mid, inverse_mid, ffn_grad * all_gains[layer, 2]
        )
        middle_low = from_slots(grad_middle.astype(low))
        grad_heads = split_heads(matmul_nt(middle_low, out_w[layer]).astype(low))
        out_piece = scatter_rows(matmul_tn(attended_low, middle_low))
        grad_query, grad_key, grad_value = attend_backward(
            query_heads, key_heads, value_heads, allowed, score_scale, log_total, grad_heads
        )
        grad_query = grad_query.reshape(-1, inner).astype(low)
        grad_key = grad_key.reshape(-1, inner).astype(low)
        grad_value = grad_value.reshape(-1, inner).astype(low)
        latent_part = (
            matmul_nt(grad_query, query_w[layer])
            + matmul_nt(grad_key[seq_rows:], key_w[layer])
            + matmul_nt(grad_value[seq_rows:], value_w[layer])
        )
        latent_grad_rows = sum_to_slots(latent_part)
        gain_latent_grad = jnp.sum(latent_grad_rows * unit_in, axis=0)
        grad_rows = grad_middle + norm_back(
            unit_in, inverse_in, latent_grad_rows * all_gains[layer, 1]
        )
        if layer > 0:
            grad_low = from_slots(grad_rows.astype(low))
        both_low = jnp.concatenate([media_low[layer], latent_low], axis=0)
        query_grad = matmul_tn(latent_low, grad_query)
        key_grad = matmul_tn(both_low, grad_key)
        value_grad = matmul_tn(both_low, grad_value)
        qkv_piece = scatter_columns(
            jnp.concatenate(
                [query_grad.astype(low), key_grad.astype(low), value_grad.astype(low)], axis=1
            )
        )
        media_part = matmul_nt(grad_key[:seq_rows], key_w[layer]) + matmul_nt(
            grad_value[:seq_rows], value_w[layer]
        )
        gain_media_grad = jnp.sum(media_part * media_unit, axis=0)
        scaled = media_part * all_gains[layer, 0]
        media_scaled = scaled if media_scaled is None else media_scaled + scaled
        gain_rows[layer] = jnp.stack([gain_media_grad, gain_latent_grad, gain_ffn_grad])
        pieces[layer] = (qkv_piece, out_piece, up_piece, down_piece)
    latent_grad = to_columns(grad_rows)
    media_grad = lax.psum(
        norm_back(media_unit, media_inverse, media_scaled).astype(low), "section"
    ).astype(full)
    gain_grad = lax.psum_scatter(
        jnp.stack(gain_rows), ("section", "dp"), scatter_dimension=2, tiled=True
    )
    qkv_grads = [
        join_columns(
            pieces[0][0][:, i * inner : (i + 1) * inner],
            pieces[1][0][:, i * inner : (i + 1) * inner],
            HEAD_DIM,
        )
        for i in range(3)
    ]
    out_grad = join_rows(pieces[0][1], pieces[1][1])
    up_grad = join_columns(pieces[0][2], pieces[1][2], hidden_block)
    down_grad = join_rows(pieces[0][3], pieces[1][3])
    return (
        latents_out,
        latent_grad,
        media_grad,
        gain_grad,
        qkv_grads[0][None],
        qkv_grads[1][None],
        qkv_grads[2][None],
        out_grad[None],
        up_grad[None],
        down_grad[None],
    )


def solution(mesh):
    placed = (
        P("dp", None),
        P("dp", None),
        P("dp", None),
        P("dp", None),
        P(None, None, ("section", "dp")),
        P("section", "dp", None),
        P("section", "dp", None),
        P("section", "dp", None),
        P("section", "dp", None),
        P("section", "dp", None),
        P("section", "dp", None),
        P("dp", None),
    )
    return jax.shard_map(
        per_device,
        mesh=mesh,
        in_specs=placed,
        out_specs=(
            P("dp", "section"),
            P("dp", "section"),
            P("dp", None),
            P(None, None, ("section", "dp")),
            P("section", "dp", None),
            P("section", "dp", None),
            P("section", "dp", None),
            P("section", "dp", None),
            P("section", "dp", None),
            P("section", "dp", None),
        ),
        check_vma=False,
    )
```

time: 1460 us -> 1120 us (0.77)
  waiting for transfers between devices: 958 us -> 573 us
  blocking collectives: 60.6 us -> 133 us
  matrix products: 206 us -> 152 us
  starting transfers between devices: 24.9 us -> 61.6 us
    reduce_scatter x6, waiting for transfers between devices: 600 us -> 197 us  [the longest x4 100 us: scatter_rows(): lax.psum_scatter(grad.astype(low), 'dp', scatter_dimension=0, tiled=True)]
    unnamed x15 -> x21, waiting for transfers between devices: 18.9 us -> 130 us
    all_gather x6 -> x8, waiting for transfers between devices: 157 us -> 68.2 us  [the longest x4 44.4 us: gather_rows(): gathered = lax.all_gather(piece, 'dp', axis=0, tiled=True)]
    all_gather x0 -> x6, blocking collectives: none -> 71.2 us  [from_slots(): return lax.all_gather(rows, 'section', axis=0, tiled=True)]
    ppermute x17 -> x14, waiting for transfers between devices: 95.3 us -> 53.4 us  [the longest x6 32.9 us: swap_layer(): return lax.ppermute(value, 'section', pairs)]
    all_to_all x0 -> x10, starting transfers between devices: none -> 39.5 us  [the longest x8 32.1 us: sum_to_slots(): arrived = lax.all_to_all(blocks, 'section', split_axis=0, concat_axis=0)]
    all_to_all x0 -> x10, waiting for transfers between devices: none -> 39.4 us  [the longest x8 37.1 us: sum_to_slots(): arrived = lax.all_to_all(blocks, 'section', split_axis=0, concat_axis=0)]
    dot_general x41 -> x24, matrix products: 102 us -> 71.9 us  [the longest x12 53.1 us: matmul(): return jnp.dot(left, right, preferred_element_type=full)]
  transfers between devices with their start and end apart: 31 -> 42, of which waited for: 25 -> 24; matrix products, arithmetic and copies ran while one was open for 13% -> 24% of each run, Pallas kernels for 0% -> 0%
where the time goes in v1:
time: 1120 us; the launch traced here: 1100 us
  waiting for transfers between devices  573 us (51%)
  matrix products  152 us (14%)
  blocking collectives  133 us (12%)
  local copies, waits for them, and re-layouts  105 us (9%)
  other arithmetic  62.5 us (6%)
  starting transfers between devices  61.6 us (6%)
  between operations  16.5 us (1%)
    unnamed x21, waiting for transfers between devices  130 us
    reduce_scatter x4, waiting for transfers between devices, scatter_rows(): lax.psum_scatter(grad.astype(low), 'dp', scatter_dimension=0, tiled=True)  100 us
    reduce_scatter x2, waiting for transfers between devices, scatter_columns(): lax.psum_scatter(grad.astype(low), 'dp', scatter_dimension=0, tiled=True)  96.5 us
    psum x1, waiting for transfers between devices, per_device(): lax.psum(norm_back(media_unit, media_inverse, media_scaled).astype(low),...  86.1 us
    all_gather x6, blocking collectives, from_slots(): return lax.all_gather(rows, 'section', axis=0, tiled=True)  71.2 us
    all_gather x1, blocking collectives, per_device(): all_gains = lax.all_gather(gains, ('section', 'dp'), axis=2, tiled=True)  62.3 us
    dot_general x12, matrix products, matmul(): return jnp.dot(left, right, preferred_element_type=full)  53.1 us
    dot_general x16, matrix products, matmul_nt(): lax.dot_general(left, right, (((1,), (1,)), ((), ())), preferred_element_...  50 us
  transfers between devices with their start and end apart: 42, of which 24 were waited for; matrix products, arithmetic and copies ran while one was open for 24% of the time, Pallas kernels for 0%

profile of v1, /device:TPU:0, one launch (start us, length us, event | category | flops | bytes accessed | tf_op | source)
XLA Modules:
  0.0 1104.4 jit_solution(2299678862208931435)
XLA Ops:
  21.1 10.2 collective-permute-done
  45.3 13.5 %collective-permute-done.3 = bf16[192,1536]{1,0:T(8,128)(2,1)S(1)} collective-permute-done((bf16[192,1536]{1,0:T(8,128)(2,1)S(1)}, bf16[192,1536]{1,0:T(8,128)(2,1)S(1)}, u32[]{:S(2)}, u32[]{:S(2)}) %collective-permute-start.3) | collective-permute-done | bytes 589856 | tf_op jit(solution)/shard_map/ppermute | solution.py:118
  60.8 9.2 collective-permute-done.5
  72.4 62.3 %all_gather.45 = f32[2,3,1536]{1,0,2:T(2,128)} all-gather(f32[2,3,48]{1,0,2:T(2,128)S(1)} %copy.170), channel_id=1, replica_groups=mesh['section'=4,'dp'=8] {'section','dp'}, dimensions={2}, use_global_device_ids=true | all-gather | bytes 38016 | tf_op jit(solution)/shard_map/all_gather | solution.py:224
  139.6 26.0 %slice_reduce_fusion = (f32[1536]{0:T(1024)S(1)}, f32[1536]{0:T(1024)S(1)}, f32[1536]{0:T(1024)S(1)}, f32[1536]{0:T(1024)S(1)}, f32[1536]{0:T(1024)S(1)}, /*index=5*/f32[1536]{0:T(1024)S(1)}) fusion(f32[2,3,1536]{1,0,2:T(2,128)S(1)} %copy-done.4), kind=kLoop, calls=%fused_computation.166 | loop fusion | bytes 73728 | tf_op jit(solution)/shard_map/slice | solution.py:270
  199.2 10.8 all-to-all-done
  210.7 11.2 %all_gather.48 = bf16[256,1536]{1,0:T(8,128)(2,1)S(1)} all-gather(bf16[64,1536]{1,0:T(8,128)(2,1)S(1)} %multiply_convert_fusion.6), channel_id=1, replica_groups=mesh['section'=4,'dp'=8] {'section'}, dimensions={0}, use_global_device_ids=true | all-gather | bytes 983040 | tf_op jit(solution)/shard_map/all_gather | solution.py:195
  238.7 15.6 %all-gather.17.cloned.1.call-done = bf16[1536,1152]{1,0:T(8,128)(2,1)} async-done(((bf16[192,1152]{1,0:T(8,128)(2,1)}), bf16[1536,1152]{1,0:T(8,128)(2,1)}) %all-gather.17.cloned.1.call-update) | async-done | bytes 3538960 | tf_op jit(solution)/shard_map/all_gather | solution.py:216
  263.9 12.3 %all_gather.52 = bf16[256,1536]{1,0:T(8,128)(2,1)S(1)} all-gather(bf16[64,1536]{1,0:T(8,128)(2,1)S(1)} %multiply_convert_fusion.5), channel_id=1, replica_groups=mesh['section'=4,'dp'=8] {'section'}, dimensions={0}, use_global_device_ids=true | all-gather | bytes 983040 | tf_op jit(solution)/shard_map/all_gather | solution.py:195
  300.0 10.1 all-to-all-done.2
  310.7 12.1 %all_gather.54 = bf16[256,1536]{1,0:T(8,128)(2,1)} all-gather(bf16[64,1536]{1,0:T(8,128)(2,1)S(1)} %multiply_convert_fusion.4), channel_id=1, replica_groups=mesh['section'=4,'dp'=8] {'section'}, dimensions={0}, use_global_device_ids=true | all-gather | bytes 983040 | tf_op jit(solution)/shard_map/all_gather | solution.py:195
  339.4 44.4 %all-gather.23.cloned.1.call-done = bf16[1536,1536]{1,0:T(8,128)(2,1)} async-done(((bf16[192,1536]{1,0:T(8,128)(2,1)}), bf16[1536,1536]{1,0:T(8,128)(2,1)}) %all-gather.23.cloned.1.call-update) | async-done | bytes 4718608 | tf_op jit(solution)/shard_map/all_gather | solution.py:171
  415.5 9.2 all-to-all-done.3
  428.0 12.0 %all_gather.57 = bf16[256,1536]{1,0:T(8,128)(2,1)S(1)} all-gather(bf16[64,1536]{1,0:T(8,128)(2,1)S(1)} %get-tuple-element.103), channel_id=1, replica_groups=mesh['section'=4,'dp'=8] {'section'}, dimensions={0}, use_global_device_ids=true | all-gather | bytes 983040 | tf_op jit(solution)/shard_map/all_gather | solution.py:195
  472.1 12.2 %all_gather.58 = bf16[256,1536]{1,0:T(8,128)(2,1)S(1)} all-gather(bf16[64,1536]{1,0:T(8,128)(2,1)S(1)} %get-tuple-element.101), channel_id=1, replica_groups=mesh['section'=4,'dp'=8] {'section'}, dimensions={0}, use_global_device_ids=true | all-gather | bytes 983040 | tf_op jit(solution)/shard_map/all_gather | solution.py:195
  506.1 11.4 %all_gather.59 = bf16[256,1536]{1,0:T(8,128)(2,1)S(1)} all-gather(bf16[64,1536]{1,0:T(8,128)(2,1)S(1)} %get-tuple-element.99), channel_id=1, replica_groups=mesh['section'=4,'dp'=8] {'section'}, dimensions={0}, use_global_device_ids=true | all-gather | bytes 983040 | tf_op jit(solution)/shard_map/all_gather | solution.py:195
  628.8 44.0 %reduce-scatter.28.cloned.1.call-done = f32[48,6]{1,0:T(8,128)} async-done(((f32[1536,6]{1,0:T(8,128)}), f32[48,6]{1,0:T(8,128)}) %reduce-scatter.28.cloned.1.call-update) | async-done | bytes 1168
  675.9 86.1 %all-reduce.2.cloned.1.call-done = bf16[1024,1536]{1,0:T(8,128)(2,1)} async-done(((bf16[1024,1536]{1,0:T(8,128)(2,1)}), bf16[1024,1536]{1,0:T(8,128)(2,1)}) %all-reduce.2.cloned.1.call-update) | async-done | bytes 3145744 | tf_op jit(solution)/shard_map/psum | solution.py:362
  767.5 40.8 %reduce-scatter.32.cloned.1.call-done = bf16[192,1152]{1,0:T(8,128)(2,1)} async-done(((bf16[1536,1152]{1,0:T(8,128)(2,1)}), bf16[192,1152]{1,0:T(8,128)(2,1)}) %reduce-scatter.32.cloned.1.call-update) | async-done | bytes 442384
  809.8 43.0 %reduce-scatter.30.cloned.1.call-done = bf16[192,1152]{1,0:T(8,128)(2,1)} async-done(((bf16[1536,1152]{1,0:T(8,128)(2,1)}), bf16[192,1152]{1,0:T(8,128)(2,1)}) %reduce-scatter.30.cloned.1.call-update) | async-done | bytes 442384
  867.7 40.9 %reduce-scatter.22.cloned.1.call-done = bf16[192,1536]{1,0:T(8,128)(2,1)} async-done(((bf16[1536,1536]{1,0:T(8,128)(2,1)}), bf16[192,1536]{1,0:T(8,128)(2,1)}) %reduce-scatter.22.cloned.1.call-update) | async-done | bytes 589840 | tf_op jit(solution)/shard_map/reduce_scatter | solution.py:187
  908.6 55.6 %reduce-scatter.20.cloned.1.call-done = bf16[192,1536]{1,0:T(8,128)(2,1)} async-done(((bf16[1536,1536]{1,0:T(8,128)(2,1)}), bf16[192,1536]{1,0:T(8,128)(2,1)}) %reduce-scatter.20.cloned.1.call-update) | async-done | bytes 589840 | tf_op jit(solution)/shard_map/reduce_scatter | solution.py:187
  975.0 44.8 %reduce-scatter.26.cloned.1.call-done = bf16[192,1536]{1,0:T(8,128)(2,1)} async-done(((bf16[1536,1536]{1,0:T(8,128)(2,1)}), bf16[192,1536]{1,0:T(8,128)(2,1)}) %reduce-scatter.26.cloned.1.call-update) | async-done | bytes 589840 | tf_op jit(solution)/shard_map/reduce_scatter | solution.py:184
  1019.8 55.6 %reduce-scatter.24.cloned.1.call-done = bf16[192,1536]{1,0:T(8,128)(2,1)} async-done(((bf16[1536,1536]{1,0:T(8,128)(2,1)}), bf16[192,1536]{1,0:T(8,128)(2,1)}) %reduce-scatter.24.cloned.1.call-update) | async-done | bytes 589840 | tf_op jit(solution)/shard_map/reduce_scatter | solution.py:184
  (499 shorter events, 395.0 us)
Async XLA Ops:
  7.2 163.2 %all-gather.9.cloned.1.call-start = ((), (), s32[]{:S(2)}) async-start(), calls=%async_computation.19 | async-start | bytes 3981312 | tf_op jit(solution)/shard_map/all_gather | solution.py:216
  32.2 159.8 %all-gather.11.cloned.1.call-start = ((), (), s32[]{:S(2)}) async-start(), calls=%async_computation.20 | async-start | bytes 1327104 | tf_op jit(solution)/shard_map/all_gather | solution.py:171
  38.3 183.6 %all-gather.13.cloned.1.call-start = ((), (), s32[]{:S(2)}) async-start(), calls=%async_computation.21 | async-start | bytes 5308416 | tf_op jit(solution)/shard_map/all_gather | solution.py:218
  59.9 170.4 %all-gather.15.cloned.1.call-start = ((), (), s32[]{:S(2)}) async-start(), calls=%async_computation.22 | async-start | bytes 5308416 | tf_op jit(solution)/shard_map/all_gather | solution.py:171
  71.1 183.1 %all-gather.17.cloned.1.call-start = ((), (), s32[]{:S(2)}) async-start(), calls=%async_computation.23 | async-start | bytes 3981312 | tf_op jit(solution)/shard_map/all_gather | solution.py:216
  71.7 222.0 %all-gather.19.cloned.1.call-start = ((), (), s32[]{:S(2)}) async-start(), calls=%async_computation.24 | async-start | bytes 1327104 | tf_op jit(solution)/shard_map/all_gather | solution.py:171
  72.3 258.8 %all-gather.21.cloned.1.call-start = ((), (), s32[]{:S(2)}) async-start(), calls=%async_computation.25 | async-start | bytes 5308416 | tf_op jit(solution)/shard_map/all_gather | solution.py:218
  198.5 185.3 %all-gather.23.cloned.1.call-start = ((), (), s32[]{:S(2)}) async-start(), calls=%async_computation.26 | async-start | bytes 5308416 | tf_op jit(solution)/shard_map/all_gather | solution.py:171
  235.2 28.1 %all-to-all-start.1 = ((bf16[4,64,1536]{2,1,0:T(8,128)(2,1)}), bf16[4,64,1536]{2,1,0:T(8,128)(2,1)S(1)}, u32[]{:S(2)}, u32[]{:S(2)}) async-start(bf16[4,64,1536]{2,1,0:T(8,128)(2,1)} %bitcast.252), calls=%async_computation.1 | async-start | bytes 1572864 | tf_op jit(solution)/shard_map/all_to_all | solution.py:191
  460.7 156.4 %reduce-scatter.18.cloned.1.call-start = ((), (), s32[]{:S(2)}) async-start(), calls=%async_computation.29 | async-start | bytes 1327104 | tf_op jit(solution)/shard_map/reduce_scatter | solution.py:184
  534.4 18.7 %all-to-all-start.8 = ((bf16[4,64,1536]{2,1,0:T(8,128)(2,1)}), bf16[4,64,1536]{2,1,0:T(8,128)(2,1)}, u32[]{:S(2)}, u32[]{:S(2)}) async-start(bf16[4,64,1536]{2,1,0:T(8,128)(2,1)} %bitcast.42), calls=%async_computation.8 | async-start | bytes 1572864 | tf_op jit(solution)/shard_map/all_to_all | solution.py:191
  538.8 78.4 %reduce-scatter.16.cloned.1.call-start = ((), (), s32[]{:S(2)}) async-start(), calls=%async_computation.28 | async-start | bytes 1327104 | tf_op jit(solution)/shard_map/reduce_scatter | solution.py:184
  540.3 132.4 %reduce-scatter.28.cloned.1.call-start = ((), (), s32[]{:S(2)}) async-start(), calls=%async_computation.34 | async-start | bytes 811008
  562.1 199.9 %all-reduce.2.cloned.1.call-start = ((), (), s32[]{:S(2)}) async-start(), calls=%async_computation.27 | async-start | bytes 6291456 | tf_op jit(solution)/shard_map/psum | solution.py:362
  567.3 241.0 %reduce-scatter.32.cloned.1.call-start = ((), (), s32[]{:S(2)}) async-start(), calls=%async_computation.36 | async-start | bytes 3981312
  578.4 274.4 %reduce-scatter.30.cloned.1.call-start = ((), (), s32[]{:S(2)}) async-start(), calls=%async_computation.35 | async-start | bytes 3981312
  589.7 318.9 %reduce-scatter.22.cloned.1.call-start = ((), (), s32[]{:S(2)}) async-start(), calls=%async_computation.31 | async-start | bytes 5308416 | tf_op jit(solution)/shard_map/reduce_scatter | solution.py:187
  594.6 369.5 %reduce-scatter.20.cloned.1.call-start = ((), (), s32[]{:S(2)}) async-start(), calls=%async_computation.30 | async-start | bytes 5308416 | tf_op jit(solution)/shard_map/reduce_scatter | solution.py:187
  599.6 420.2 %reduce-scatter.26.cloned.1.call-start = ((), (), s32[]{:S(2)}) async-start(), calls=%async_computation.33 | async-start | bytes 5308416 | tf_op jit(solution)/shard_map/reduce_scatter | solution.py:184
  604.6 470.7 %reduce-scatter.24.cloned.1.call-start = ((), (), s32[]{:S(2)}) async-start(), calls=%async_computation.32 | async-start | bytes 5308416 | tf_op jit(solution)/shard_map/reduce_scatter | solution.py:184
  620.5 53.8 %all-to-all-start.9 = ((bf16[64,4,384]{2,0,1:T(8,128)(2,1)}), bf16[64,4,384]{2,0,1:T(8,128)(2,1)S(1)}, u32[]{:S(2)}, u32[]{:S(2)}) async-start(bf16[64,4,384]{2,0,1:T(8,128)(2,1)} %bitcast.188), calls=%async_computation.9 | async-start | bytes 393216 | tf_op jit(solution)/shard_map/all_to_all | solution.py:198
  623.9 51.2 %collective-permute-start.9 = (bf16[48,1536]{1,0:T(8,128)(2,1)S(1)}, bf16[48,1536]{1,0:T(8,128)(2,1)S(1)}, u32[]{:S(2)}, u32[]{:S(2)}) collective-permute-start(bf16[48,1536]{1,0:T(8,128)(2,1)S(1)} %get-tuple-element.155), channel_id=1, source_target_pairs={{0,0},{16,1},{2,2},{18,3},{4,4},{20,5},{6,6},{22,7},{8,8},{24,9},{... | collective-permute-start | bytes 442376 | tf_op jit(solution)/shard_map/ppermute | solution.py:166
  624.7 50.3 %collective-permute-start.10 = (bf16[48,1536]{1,0:T(8,128)(2,1)S(1)}, bf16[48,1536]{1,0:T(8,128)(2,1)S(1)}, u32[]{:S(2)}, u32[]{:S(2)}) collective-permute-start(bf16[48,1536]{1,0:T(8,128)(2,1)S(1)} %get-tuple-element.156), channel_id=1, source_target_pairs={{1,0},{17,1},{3,2},{19,3},{5,4},{21,5},{7,6},{23,7},{9,8},{25,9},{... | collective-permute-start | bytes 442376 | tf_op jit(solution)/shard_map/ppermute | solution.py:167
  966.1 115.0 %collective-permute-start.11 = (bf16[192,1536]{1,0:T(8,128)(2,1)}, bf16[192,1536]{1,0:T(8,128)(2,1)}, u32[]{:S(2)}, u32[]{:S(2)}) collective-permute-start(bf16[192,1536]{1,0:T(8,128)(2,1)} %broadcast_select_fusion.8), channel_id=1, source_target_pairs={{0,16},{8,24},{16,0},{24,8},{1,17},{9,25},{17,1},{25,9},{2,18},{10... | collective-permute-start | bytes 1769480 | tf_op jit(solution)/shard_map/ppermute | solution.py:118
  (108 other events, 1289.8 us)
Sparse Core Ops, SparseCore 0:
  32.4 42.9 all-gather.8
  77.6 25.3 all-gather.10
  105.2 53.2 all-gather.12
  160.6 51.7 all-gather.14
  213.9 40.3 all-gather.16
  255.7 21.5 all-gather.18
  279.5 51.4 all-gather.20
  333.2 50.5 all-gather.22
  463.9 32.1 reduce-scatter.17
  542.2 31.5 reduce-scatter.15
  578.9 93.8 reduce-scatter.27
  675.7 86.2 all-reduce.1
  764.4 43.8 reduce-scatter.31
  810.5 42.3 reduce-scatter.29
  855.1 53.4 reduce-scatter.21
  910.8 53.2 reduce-scatter.19
  966.4 53.3 reduce-scatter.25
  1022.0 53.3 reduce-scatter.23

commit v2 on v1

--- a/solution.py
+++ b/solution.py
@@ -3,7 +3,7 @@
 import jax
 import jax.numpy as jnp
 from jax import lax
-from jax.sharding import PartitionSpec as P
+from jax.sharding import Mesh, PartitionSpec as P
 
 HEAD_DIM = 96
 LATENTS = 64
@@ -93,19 +93,19 @@
     w_down,
     cotangent,
 ):
+    dp = ("pair", "core")
     section = lax.axis_index("section")
     section_count = lax.axis_size("section")
-    dp_index = lax.axis_index("dp")
-    dp_count = lax.axis_size("dp")
-    layer_bit = section // 2
-    on_first = layer_bit == 0
+    dp_index = lax.axis_index(dp)
+    dp_count = lax.axis_size("pair") * lax.axis_size("core")
+    on_first = section // 2 == 0
     stride = dp_count // HALF_HEADS
-    row_bit = (dp_index // stride) % 2
-    row_first = row_bit == 0
+    row_first = (dp_index // stride) % 2 == 0
     seq_rows = segment_ids.shape[1]
     slot_count = slot_map.shape[1]
     feature_width = latents.shape[1]
     latent_rows = latents.shape[0]
+    slot_rows = latent_rows // section_count
     heads = HALF_HEADS // 2
     inner = heads * HEAD_DIM
     score_scale = 1.0 / math.sqrt(HEAD_DIM)
@@ -113,48 +113,57 @@
     def pick(first, second):
         return jnp.where(on_first, first, second), jnp.where(on_first, second, first)
 
-    def swap_layer(value):
-        pairs = [(source, source ^ 2) for source in range(section_count)]
+    def swapped(value, mask):
+        pairs = [(source, source ^ mask) for source in range(section_count)]
         return lax.ppermute(value, "section", pairs)
 
-    def with_bit(index, bit):
-        high, lowest = index // (2 * stride), index % stride
-        return (2 * high + bit) * stride + lowest
-
-    def bit_of(index):
-        return (index // stride) % 2
+    def to_second(value):
+        return lax.ppermute(value, "section", [(0, 2), (1, 3)])
+
+    def to_first(value):
+        return lax.ppermute(value, "section", [(2, 0), (3, 1)])
 
     def turn_pairs(flip, back):
         pairs = []
         for source in range(section_count):
             for index in range(dp_count):
                 layer, half = divmod(source, 2)
-                target = (bit_of(index) * 2 + half) * dp_count + with_bit(index, layer ^ flip)
+                high, bit, lowest = (
+                    index // (2 * stride),
+                    (index // stride) % 2,
+                    index % stride,
+                )
+                moved = (2 * high + (layer ^ flip)) * stride + lowest
+                target = (bit * 2 + half) * dp_count + moved
                 pair = (source * dp_count + index, target)
                 pairs.append(pair[::-1] if back else pair)
         return pairs
+
+    everywhere = ("section",) + dp
 
     def column_parts(weight, block):
         rows, width = weight.shape
         split = weight.reshape(rows, width // (2 * block), 2, block)
         return split[:, :, 0].reshape(rows, -1), split[:, :, 1].reshape(rows, -1)
 
+    def interleave(even, odd, block):
+        rows, width = even.shape
+        pieces = [part.reshape(rows, width // block, 1, block) for part in (even, odd)]
+        return jnp.concatenate(pieces, axis=2).reshape(rows, 2 * width)
+
     def exchange_columns(even, odd):
         own, other = pick(even, odd)
-        return pick(own, swap_layer(other))
-
-    def join_columns(first, second, block):
+        return pick(own, swapped(other, 2))
+
+    def join_columns(first, second):
         own, other = pick(first, second)
-        even, odd = pick(own, swap_layer(other))
-        rows, width = even.shape
-        pieces = [part.reshape(rows, width // block, 1, block) for part in (even, odd)]
-        return jnp.concatenate(pieces, axis=2).reshape(rows, 2 * width).astype(full)
+        return pick(own, swapped(other, 2))
 
     def exchange_rows(weight):
         half = weight.shape[0] // 2
         near, far = pick(weight[:half], weight[half:])
-        first = lax.ppermute(near, ("section", "dp"), turn_pairs(0, False))
-        second = lax.ppermute(far, ("section", "dp"), turn_pairs(1, False))
+        first = lax.ppermute(near, everywhere, turn_pairs(0, False))
+        second = lax.ppermute(far, everywhere, turn_pairs(1, False))
         return (
             jnp.where(row_first, first, second),
             jnp.where(row_first, second, first),
@@ -163,28 +172,23 @@
     def join_rows(first, second):
         near = jnp.where(row_first, first, second)
         far = jnp.where(row_first, second, first)
-        near = lax.ppermute(near, ("section", "dp"), turn_pairs(0, True))
-        far = lax.ppermute(far, ("section", "dp"), turn_pairs(1, True))
+        near = lax.ppermute(near, everywhere, turn_pairs(0, True))
+        far = lax.ppermute(far, everywhere, turn_pairs(1, True))
         return jnp.concatenate(pick(near, far), axis=0).astype(full)
 
-    def gather_rows(piece):
-        gathered = lax.all_gather(piece, "dp", axis=0, tiled=True)
+    def rows_in_order(stacked):
+        width = stacked.shape[-1]
         if stride > 1:
-            width = gathered.shape[1]
-            gathered = gathered.reshape(-1, 2, stride, piece.shape[0], width)
-            gathered = gathered.transpose(0, 2, 1, 3, 4).reshape(-1, width)
-        return gathered
-
-    def scatter_rows(grad):
+            piece = stacked.shape[1]
+            stacked = stacked.reshape(-1, 2, stride, piece, width).transpose(0, 2, 1, 3, 4)
+        return stacked.reshape(-1, width)
+
+    def rows_by_device(grad):
+        width = grad.shape[-1]
+        piece = grad.shape[0] // dp_count
         if stride > 1:
-            width = grad.shape[1]
-            piece = grad.shape[0] // dp_count
-            grad = grad.reshape(-1, stride, 2, piece, width)
-            grad = grad.transpose(0, 2, 1, 3, 4).reshape(-1, width)
-        return lax.psum_scatter(grad.astype(low), "dp", scatter_dimension=0, tiled=True)
-
-    def scatter_columns(grad):
-        return lax.psum_scatter(grad.astype(low), "dp", scatter_dimension=0, tiled=True)
+            grad = grad.reshape(-1, stride, 2, piece, width).transpose(0, 2, 1, 3, 4)
+        return grad.reshape(dp_count, piece, width)
 
     def sum_to_slots(partial):
         blocks = partial.astype(low).reshape(section_count, -1, feature_width)
@@ -199,6 +203,56 @@
             rows.astype(low), "section", split_axis=1, concat_axis=0, tiled=True
         )
         return moved.astype(full)
+
+    def from_sequences(rows):
+        pairs = lax.all_gather(rows, "pair", axis=0)
+        both = lax.all_gather(pairs, "core", axis=1)
+        return both.reshape(-1, feature_width)
+
+    def sum_to_sequence(partial):
+        blocks = partial.astype(low).reshape(-1, 2, slot_rows, feature_width)
+        halves = lax.all_to_all(blocks, "core", split_axis=1, concat_axis=1)
+        halves = jnp.sum(halves.astype(full), axis=1).astype(low)
+        arrived = lax.all_to_all(halves, "pair", split_axis=0, concat_axis=0)
+        return jnp.sum(arrived.astype(full), axis=0)
+
+    def spread(shard):
+        own = jnp.where(on_first, to_first(shard), shard)
+        return own, swapped(own, 1)
+
+    def collect(own, other):
+        total = own + swapped(other.astype(low), 1).astype(full)
+        return total + to_second(total.astype(low)).astype(full)
+
+    def block_of(blocks, mask):
+        return lax.dynamic_index_in_dim(blocks, section ^ mask, 0, keepdims=False)
+
+    def sum_over_sections(partial):
+        blocks = partial.reshape(section_count, -1, feature_width)
+        half = blocks.shape[1] // 2
+        own, side, ahead, across = [block_of(blocks, mask) for mask in range(4)]
+        across = across.astype(low)
+        upper = swapped(across[:half], 2).astype(full)
+        lower = swapped(across[half:], 1).astype(full)
+        side = jnp.concatenate([side[:half] + upper, side[half:]], axis=0).astype(low)
+        ahead = jnp.concatenate([ahead[:half], ahead[half:] + lower], axis=0).astype(low)
+        return own + swapped(side, 1).astype(full) + swapped(ahead, 2).astype(full)
+
+    def gather_sections(rows):
+        half = rows.shape[0] // 2
+        side = swapped(rows, 1)
+        ahead = swapped(rows, 2)
+        upper = swapped(side[:half], 2)
+        lower = swapped(ahead[half:], 1)
+        across = jnp.concatenate([upper, lower], axis=0)
+        by_mask = [rows, side, ahead, across]
+        ordered = []
+        for target in range(section_count):
+            chosen = by_mask[0]
+            for mask in range(1, section_count):
+                chosen = jnp.where(section ^ mask == target, by_mask[mask], chosen)
+            ordered.append(chosen)
+        return jnp.concatenate(ordered, axis=0)
 
     query_parts = column_parts(w_query[0], HEAD_DIM)
     key_parts = column_parts(w_key[0], HEAD_DIM)
@@ -208,20 +262,39 @@
     ]
     qkv_pieces = exchange_columns(joined[0], joined[1])
     out_pieces = exchange_rows(w_out[0])
-    hidden_block = w_up.shape[2] // HALF_HEADS
-    up_pieces = exchange_columns(*column_parts(w_up[0], hidden_block))
-    down_pieces = exchange_rows(w_down[0])
-    qkv_w, out_w, up_w, down_w = [], [], [], []
-    for layer in range(LAYERS):
-        qkv_w.append(lax.all_gather(qkv_pieces[layer], "dp", axis=0, tiled=True))
-        out_w.append(gather_rows(out_pieces[layer]))
-        up_w.append(lax.all_gather(up_pieces[layer], "dp", axis=0, tiled=True))
-        down_w.append(gather_rows(down_pieces[layer]))
+    hidden_block = w_down.shape[1] // 2
+    up_even, up_odd = column_parts(w_up[0], hidden_block)
+    up_piece = jnp.where(on_first, up_even, to_second(up_odd))
+    down_piece = jnp.where(
+        on_first, w_down[0, :hidden_block], to_second(w_down[0, hidden_block:])
+    )
+    out_piece_rows = out_pieces[0].shape[0]
+
+    def gather(piece):
+        return lax.all_gather(piece, dp, axis=0)
+
+    qkv_first = gather(qkv_pieces[0]).reshape(-1, 3 * inner)
+    stacked = gather(jnp.concatenate([out_pieces[0], down_piece], axis=0))
+    out_first = rows_in_order(stacked[:, :out_piece_rows])
+    down_first = stacked[:, out_piece_rows:].reshape(-1, feature_width)
+    up_first = gather(up_piece).reshape(feature_width, -1)
+    qkv_piece_rows = qkv_pieces[1].size // feature_width
+    stacked = gather(
+        jnp.concatenate([qkv_pieces[1].reshape(-1, feature_width), out_pieces[1]], axis=0)
+    )
+    qkv_second = stacked[:, :qkv_piece_rows].reshape(-1, 3 * inner)
+    out_second = rows_in_order(stacked[:, qkv_piece_rows:])
+    qkv_w = (qkv_first, qkv_second)
+    out_w = (out_first, out_second)
     query_w = [weight[:, :inner] for weight in qkv_w]
     key_w = [weight[:, inner : 2 * inner] for weight in qkv_w]
     value_w = [weight[:, 2 * inner :] for weight in qkv_w]
-
-    all_gains = lax.all_gather(gains, ("section", "dp"), axis=2, tiled=True)
+    down_second = jnp.concatenate(spread(w_down[0]), axis=0)
+    up_turned = lax.all_to_all(w_up[0], dp, split_axis=1, concat_axis=0, tiled=True)
+    up_second = jnp.concatenate(spread(up_turned), axis=1)
+
+    near_gains = lax.all_gather(gains, dp, axis=2, tiled=True)
+    all_gains = lax.all_gather(near_gains, "section", axis=2, tiled=True)
     image_hot = segment_ids[:, :, None] == jnp.arange(slot_count, dtype=jnp.int32)[None, None, :]
     media_slot = jnp.sum(jnp.where(image_hot, slot_map[:, None, :], 0), axis=2) - (
         segment_ids < 0
@@ -243,8 +316,10 @@
         media_value.append(matmul(media_low[layer], value_w[layer]).astype(low))
 
     saved = []
-    slot_rows = latent_rows // section_count
     current = lax.dynamic_slice_in_dim(latents, section * slot_rows, slot_rows, 0).astype(full)
+    grad_low = lax.dynamic_slice_in_dim(cotangent, section * slot_rows, slot_rows, 0)
+    grad_rows = grad_low.astype(full)
+    grad_low = from_sequences(grad_low)
     for layer in range(LAYERS):
         unit_in, inverse_in = unit_rows(current)
         if layer == 0:
@@ -267,10 +342,14 @@
         attended_low = attended.reshape(-1, inner).astype(low)
         middle = current + sum_to_slots(matmul(attended_low, out_w[layer]))
         unit_mid, inverse_mid = unit_rows(middle)
-        ffn_low = from_slots((unit_mid * all_gains[layer, 2]).astype(low))
-        hidden_pre = matmul(ffn_low, up_w[layer])
+        ffn_low = (unit_mid * all_gains[layer, 2]).astype(low)
+        ffn_low = from_slots(ffn_low) if layer == 0 else from_sequences(ffn_low)
+        hidden_pre = matmul(ffn_low, up_first if layer == 0 else up_second)
         active_low = gelu_exact(hidden_pre).astype(low)
-        current = middle + sum_to_slots(matmul(active_low, down_w[layer]))
+        if layer == 0:
+            current = middle + sum_to_slots(matmul(active_low, down_first))
+        else:
+            current = middle + sum_to_sequence(matmul(active_low, down_second))
         saved.append(
             (
                 unit_in,
@@ -290,11 +369,17 @@
         )
     latents_out = to_columns(current)
 
+    def scatter(blocks):
+        return lax.psum_scatter(blocks, dp, scatter_dimension=0, tiled=False)
+
+    def after(value, earlier):
+        return lax.optimization_barrier((value, earlier))
+
     gain_rows = [None] * LAYERS
     media_scaled = None
-    pieces = [None] * LAYERS
-    grad_low = cotangent
-    grad_rows = lax.dynamic_slice_in_dim(cotangent, section * slot_rows, slot_rows, 0).astype(full)
+    qkv_pieces = [None] * LAYERS
+    out_pieces = [None] * LAYERS
+    last_piece = None
     for layer in (1, 0):
         (
             unit_in,
@@ -311,18 +396,35 @@
             hidden_pre,
             active_low,
         ) = saved[layer]
-        grad_active = matmul_nt(grad_low, down_w[layer])
+        grad_active = matmul_nt(grad_low, down_first if layer == 0 else down_second)
         grad_hidden = jax.vjp(gelu_exact, hidden_pre)[1](grad_active)[0].astype(low)
-        down_piece = scatter_rows(matmul_tn(active_low, grad_low))
-        up_piece = scatter_columns(matmul_tn(ffn_low, grad_hidden))
-        ffn_grad = sum_to_slots(matmul_nt(grad_hidden, up_w[layer]))
+        down_grad = matmul_tn(active_low, grad_low)
+        up_grad = matmul_tn(ffn_low, grad_hidden)
+        if layer == 0:
+            blocks = jnp.concatenate(
+                [
+                    up_grad.astype(low).reshape(dp_count, -1, feature_width),
+                    down_grad.astype(low).reshape(dp_count, -1, feature_width),
+                ],
+                axis=1,
+            )
+            blocks, qkv_pieces[1] = after(blocks, qkv_pieces[1])
+            ffn_piece = scatter(blocks)
+            last_piece = ffn_piece
+            ffn_grad = sum_to_slots(matmul_nt(grad_hidden, up_first))
+        else:
+            middle_of = down_grad.shape[0] // 2
+            down_second_grad = collect(down_grad[:middle_of], down_grad[middle_of:])
+            middle_of = up_grad.shape[1] // 2
+            up_second_grad = collect(up_grad[:, :middle_of], up_grad[:, middle_of:])
+            ffn_grad = sum_to_sequence(matmul_nt(grad_hidden, up_second))
         gain_ffn_grad = jnp.sum(ffn_grad * unit_mid, axis=0)
         grad_middle = grad_rows + norm_back(
             unit_mid, inverse_mid, ffn_grad * all_gains[layer, 2]
         )
         middle_low = from_slots(grad_middle.astype(low))
         grad_heads = split_heads(matmul_nt(middle_low, out_w[layer]).astype(low))
-        out_piece = scatter_rows(matmul_tn(attended_low, middle_low))
+        out_grad = matmul_tn(attended_low, middle_low)
         grad_query, grad_key, grad_value = attend_backward(
             query_heads, key_heads, value_heads, allowed, score_scale, log_total, grad_heads
         )
@@ -345,11 +447,20 @@
         query_grad = matmul_tn(latent_low, grad_query)
         key_grad = matmul_tn(both_low, grad_key)
         value_grad = matmul_tn(both_low, grad_value)
-        qkv_piece = scatter_columns(
-            jnp.concatenate(
-                [query_grad.astype(low), key_grad.astype(low), value_grad.astype(low)], axis=1
-            )
-        )
+        qkv_grad = jnp.concatenate(
+            [query_grad.astype(low), key_grad.astype(low), value_grad.astype(low)], axis=1
+        )
+        blocks = jnp.concatenate(
+            [
+                qkv_grad.reshape(dp_count, -1, feature_width),
+                rows_by_device(out_grad.astype(low)),
+            ],
+            axis=1,
+        )
+        if layer == 0:
+            blocks, ffn_piece = after(blocks, ffn_piece)
+        piece = scatter(blocks)
+        qkv_pieces[layer] = piece
         media_part = matmul_nt(grad_key[:seq_rows], key_w[layer]) + matmul_nt(
             grad_value[:seq_rows], value_w[layer]
         )
@@ -357,25 +468,42 @@
         scaled = media_part * all_gains[layer, 0]
         media_scaled = scaled if media_scaled is None else media_scaled + scaled
         gain_rows[layer] = jnp.stack([gain_media_grad, gain_latent_grad, gain_ffn_grad])
-        pieces[layer] = (qkv_piece, out_piece, up_piece, down_piece)
     latent_grad = to_columns(grad_rows)
-    media_grad = lax.psum(
-        norm_back(media_unit, media_inverse, media_scaled).astype(low), "section"
-    ).astype(full)
-    gain_grad = lax.psum_scatter(
-        jnp.stack(gain_rows), ("section", "dp"), scatter_dimension=2, tiled=True
-    )
+    media_rows = seq_rows // section_count
+    media_sum = sum_over_sections(media_scaled)
+    own_unit = lax.dynamic_slice_in_dim(media_unit, section * media_rows, media_rows, 0)
+    own_inverse = lax.dynamic_slice_in_dim(media_inverse, section * media_rows, media_rows, 0)
+    media_grad = gather_sections(norm_back(own_unit, own_inverse, media_sum).astype(low)).astype(
+        full
+    )
+    gain_parts = jnp.stack(gain_rows).reshape(LAYERS, 3, section_count, -1)
+    gain_parts = jnp.sum(
+        lax.all_to_all(gain_parts, "section", split_axis=2, concat_axis=2), axis=2
+    )
+    gain_parts = gain_parts.reshape(LAYERS, 3, dp_count, -1)
+    gain_grad = jnp.sum(lax.all_to_all(gain_parts, dp, split_axis=2, concat_axis=2), axis=2)
+
+    qkv_parts = []
+    for layer in range(LAYERS):
+        out_pieces[layer] = qkv_pieces[layer][qkv_piece_rows:]
+        qkv_parts.append(qkv_pieces[layer][:qkv_piece_rows].reshape(-1, 3 * inner))
+    even, odd = join_columns(qkv_parts[0], qkv_parts[1])
     qkv_grads = [
-        join_columns(
-            pieces[0][0][:, i * inner : (i + 1) * inner],
-            pieces[1][0][:, i * inner : (i + 1) * inner],
-            HEAD_DIM,
-        )
+        interleave(
+            even[:, i * inner : (i + 1) * inner], odd[:, i * inner : (i + 1) * inner], HEAD_DIM
+        ).astype(full)
         for i in range(3)
     ]
-    out_grad = join_rows(pieces[0][1], pieces[1][1])
-    up_grad = join_columns(pieces[0][2], pieces[1][2], hidden_block)
-    down_grad = join_rows(pieces[0][3], pieces[1][3])
+    out_grad = join_rows(out_pieces[0], out_pieces[1])
+    back = to_first(ffn_piece)
+    up_rows = feature_width * feature_width // dp_count // feature_width
+    up_first_grad = interleave(ffn_piece[:up_rows], back[:up_rows], hidden_block)
+    down_first_grad = jnp.concatenate([ffn_piece[up_rows:], back[up_rows:]], axis=0)
+    up_second_grad = lax.all_to_all(
+        up_second_grad.astype(low), dp, split_axis=0, concat_axis=1, tiled=True
+    )
+    up_grad = jnp.where(on_first, up_first_grad.astype(full), up_second_grad.astype(full))
+    down_grad = jnp.where(on_first, down_first_grad.astype(full), down_second_grad)
     return (
         latents_out,
         latent_grad,
@@ -391,35 +519,40 @@
 
 
 def solution(mesh):
+    section_count, dp_count = mesh.devices.shape
+    fine = Mesh(
+        mesh.devices.reshape(section_count, dp_count // 2, 2), ("section", "pair", "core")
+    )
+    dp = ("pair", "core")
     placed = (
-        P("dp", None),
-        P("dp", None),
-        P("dp", None),
-        P("dp", None),
-        P(None, None, ("section", "dp")),
-        P("section", "dp", None),
-        P("section", "dp", None),
-        P("section", "dp", None),
-        P("section", "dp", None),
-        P("section", "dp", None),
-        P("section", "dp", None),
-        P("dp", None),
+        P(dp, None),
+        P(dp, None),
+        P(dp, None),
+        P(dp, None),
+        P(None, None, ("section",) + dp),
+        P("section", dp, None),
+        P("section", dp, None),
+        P("section", dp, None),
+        P("section", dp, None),
+        P("section", dp, None),
+        P("section", dp, None),
+        P(dp, None),
     )
     return jax.shard_map(
         per_device,
-        mesh=mesh,
+        mesh=fine,
         in_specs=placed,
         out_specs=(
-            P("dp", "section"),
-            P("dp", "section"),
-            P("dp", None),
-            P(None, None, ("section", "dp")),
-            P("section", "dp", None),
-            P("section", "dp", None),
-            P("section", "dp", None),
-            P("section", "dp", None),
-            P("section", "dp", None),
-            P("section", "dp", None),
+            P(dp, "section"),
+            P(dp, "section"),
+            P(dp, None),
+            P(None, None, ("section",) + dp),
+            P("section", dp, None),
+            P("section", dp, None),
+            P("section", dp, None),
+            P("section", dp, None),
+            P("section", dp, None),
+            P("section", dp, None),
         ),
         check_vma=False,
     )

time: 1120 us -> 943 us (0.84)
  waiting for transfers between devices: 573 us -> 273 us
  other arithmetic: 62.5 us -> 116 us
  starting transfers between devices: 61.6 us -> 112 us
  local copies, waits for them, and re-layouts: 105 us -> 153 us
  matrix products: 152 us -> 128 us
    reduce_scatter x6 -> x3, waiting for transfers between devices: 197 us -> 14.3 us  [scatter(): return lax.psum_scatter(blocks, dp, scatter_dimension=0, tiled=False)]
    unnamed x21 -> x9, waiting for transfers between devices: 130 us -> 0.15 us
    psum x1 -> x0, waiting for transfers between devices: 86.1 us -> none  [per_device(): lax.psum(norm_back(media_unit, media_inverse, media_scaled).astype(low),...]
    ppermute x14 -> x25, waiting for transfers between devices: 53.4 us -> 122 us  [the longest x14 81.7 us: swapped(): return lax.ppermute(value, 'section', pairs)]
    all_to_all x0 -> x8, waiting for transfers between devices: none -> 44.8 us  [the longest x2 32.2 us: sum_to_sequence(): arrived = lax.all_to_all(halves, 'pair', split_axis=0, concat_axis=0)]
    all_to_all x0 -> x8, starting transfers between devices: none -> 39.5 us  [the longest x1 10.8 us: per_device(): lax.all_to_all(gain_parts, dp, split_axis=2, concat_axis=2)]
    reshape x4 -> x24, local copies, waits for them, and re-layouts: 0.42 us -> 23.7 us  [the longest x2 11.7 us: per_device(): qkv_grad.reshape(dp_count, -1, feature_width)]
    ppermute x14 -> x25, starting transfers between devices: 20.5 us -> 43.6 us  [the longest x4 19.2 us: to_second(): return lax.ppermute(value, 'section', [(0, 2), (1, 3)])]
  transfers between devices with their start and end apart: 42 -> 49, of which waited for: 24 -> 24; matrix products, arithmetic and copies ran while one was open for 24% -> 31% of each run, Pallas kernels for 0% -> 0%
where the time goes in v2:
time: 943 us; the launch traced here: 930 us
  waiting for transfers between devices  273 us (29%)
  local copies, waits for them, and re-layouts  153 us (16%)
  blocking collectives  132 us (14%)
  matrix products  128 us (14%)
  other arithmetic  116 us (12%)
  starting transfers between devices  112 us (12%)
  between operations  16.7 us (2%)
    ppermute x14, waiting for transfers between devices, swapped(): return lax.ppermute(value, 'section', pairs)  81.7 us
    all_gather x4, waiting for transfers between devices, gather(): return lax.all_gather(piece, dp, axis=0)  67.9 us
    all_gather x5, blocking collectives, from_slots(): return lax.all_gather(rows, 'section', axis=0, tiled=True)  60.1 us
    dot_general x12, matrix products, matmul(): return jnp.dot(left, right, preferred_element_type=full)  46 us
    dot_general x16, matrix products, matmul_nt(): lax.dot_general(left, right, (((1,), (1,)), ((), ())), preferred_element_...  42.7 us
    all_gather x2, blocking collectives, from_sequences(): pairs = lax.all_gather(rows, 'pair', axis=0)  36.6 us
    all_to_all x2, waiting for transfers between devices, sum_to_sequence(): arrived = lax.all_to_all(halves, 'pair', split_axis=0, concat_axis=0)  32.2 us
    ppermute x3, waiting for transfers between devices, to_first(): return lax.ppermute(value, 'section', [(2, 0), (3, 1)])  23.4 us
  transfers between devices with their start and end apart: 49, of which 24 were waited for; matrix products, arithmetic and copies ran while one was open for 31% of the time, Pallas kernels for 0%

profile of v2, /device:TPU:0, one launch (start us, length us, event | category | flops | bytes accessed | tf_op | source)
XLA Modules:
  0.0 930.5 jit_solution(6614316202539049042)
XLA Ops:
  21.0 10.2 %collective-permute-done = bf16[192,1152]{1,0:T(8,128)(2,1)S(1)} collective-permute-done((bf16[192,1152]{1,0:T(8,128)(2,1)S(1)}, bf16[192,1152]{1,0:T(8,128)(2,1)S(1)}, u32[]{:S(2)}, u32[]{:S(2)}) %collective-permute-start) | collective-permute-done | bytes 442400 | tf_op jit(solution)/shard_map/ppermute | solution.py:118
  38.2 12.6 %collective-permute-done.3 = bf16[192,1536]{1,0:T(8,128)(2,1)S(1)} collective-permute-done((bf16[192,1536]{1,0:T(8,128)(2,1)S(1)}, bf16[192,1536]{1,0:T(8,128)(2,1)S(1)}, u32[]{:S(2)}, u32[]{:S(2)}) %collective-permute-start.3) | collective-permute-done | bytes 589856 | tf_op jit(solution)/shard_map/ppermute | solution.py:121
  71.6 15.2 %all_gather.69 = f32[2,3,384]{1,0,2:T(2,128)S(1)} all-gather(f32[2,3,48]{1,0,2:T(2,128)} %copy.257), channel_id=1, replica_groups=mesh['section'=4,'pair'=4,'core'=2] {'pair','core'}, dimensions={2}, use_global_device_ids=true | all-gather | bytes 10368 | tf_op jit(solution)/shard_map/all_gather | solution.py:296
  149.2 41.4 %all-gather.21.cloned.1.call-done = bf16[1536,1536]{1,0:T(8,128)(2,1)} async-done(((bf16[192,1536]{1,0:T(8,128)(2,1)}), bf16[1536,1536]{1,0:T(8,128)(2,1)}) %all-gather.21.cloned.1.call-update) | async-done | bytes 4718608 | tf_op jit(solution)/shard_map/all_gather | solution.py:274
  208.6 13.7 %all_gather.75 = bf16[256,1536]{1,0:T(8,128)(2,1)} all-gather(bf16[64,1536]{1,0:T(8,128)(2,1)S(1)} %multiply_convert_fusion.9), channel_id=1, replica_groups=mesh['section'=4,'pair'=4,'core'=2] {'section'}, dimensions={0}, use_global_device_ids=true | all-gather | bytes 983040 | tf_op jit(solution)/shard_map/all_gather | solution.py:199
  222.2 20.9 %all-gather.19.cloned.1.call-done = bf16[1536,1536]{1,0:T(8,128)(2,1)} async-done(((bf16[192,1536]{1,0:T(8,128)(2,1)}), bf16[1536,1536]{1,0:T(8,128)(2,1)}) %all-gather.19.cloned.1.call-update) | async-done | bytes 4718608 | tf_op jit(solution)/shard_map/all_gather | solution.py:274
  243.1 8.6 multiply_convert_fusion.6
  280.0 12.8 %all_gather.80 = bf16[256,1536]{1,0:T(8,128)(2,1)S(1)} all-gather(bf16[64,1536]{1,0:T(8,128)(2,1)S(1)} %multiply_convert_fusion.8), channel_id=1, replica_groups=mesh['section'=4,'pair'=4,'core'=2] {'section'}, dimensions={0}, use_global_device_ids=true | all-gather | bytes 983040 | tf_op jit(solution)/shard_map/all_gather | solution.py:199
  318.8 10.2 %all-to-all-done.2 = bf16[4,64,1536]{2,1,0:T(8,128)(2,1)} async-done(((bf16[4,64,1536]{2,1,0:T(8,128)(2,1)}), bf16[4,64,1536]{2,1,0:T(8,128)(2,1)}, u32[]{:S(2)}, u32[]{:S(2)}) %all-to-all-start.2) | async-done | bytes 786464 | tf_op jit(solution)/shard_map/all_to_all | solution.py:195
  332.3 18.1 %all-gather.4 = bf16[256,1536]{1,0:T(8,128)(2,1)} all-gather(bf16[64,1536]{1,0:T(8,128)(2,1)S(1)} %multiply_convert_fusion.7), channel_id=6, replica_groups=mesh['section'=4,'pair'=4,'core'=2] {'pair'}, dimensions={0}, use_global_device_ids=true | all-gather | bytes 983040 | tf_op jit(solution)/shard_map/all_gather | solution.py:208
  360.3 18.5 %all-gather.6 = bf16[256,1536]{1,0:T(8,128)(2,1)} all-gather(bf16[64,1536]{1,0:T(8,128)(2,1)S(1)} %constant_dynamic-slice_fusion), channel_id=8, replica_groups=mesh['section'=4,'pair'=4,'core'=2] {'pair'}, dimensions={0}, use_global_device_ids=true | all-gather | bytes 983040 | tf_op jit(solution)/shard_map/all_gather | solution.py:208
  385.1 8.6 multiply_convert_fusion.5
  393.7 14.8 %collective-permute-done.8 = bf16[384,1536]{1,0:T(8,128)(2,1)} collective-permute-done((bf16[384,1536]{1,0:T(8,128)(2,1)}, bf16[384,1536]{1,0:T(8,128)(2,1)}, u32[]{:S(2)}, u32[]{:S(2)}) %collective-permute-start.8) | collective-permute-done | bytes 1179680 | tf_op jit(solution)/shard_map/ppermute | solution.py:118
  441.5 18.3 %all-to-all-done.8 = bf16[4,64,1536]{2,1,0:T(8,128)(2,1)} async-done(((bf16[4,64,1536]{2,1,0:T(8,128)(2,1)}), bf16[4,64,1536]{2,1,0:T(8,128)(2,1)}, u32[]{:S(2)}, u32[]{:S(2)}) %all-to-all-start.8) | async-done | bytes 786464 | tf_op jit(solution)/shard_map/all_to_all | solution.py:216
  470.3 13.9 %all-to-all-done.5 = bf16[4,64,1536]{2,1,0:T(8,128)(2,1)} async-done(((bf16[4,64,1536]{2,1,0:T(8,128)(2,1)}), bf16[4,64,1536]{2,1,0:T(8,128)(2,1)}, u32[]{:S(2)}, u32[]{:S(2)}) %all-to-all-start.5) | async-done | bytes 786464 | tf_op jit(solution)/shard_map/all_to_all | solution.py:216
  487.9 10.5 %all_gather.89 = bf16[256,1536]{1,0:T(8,128)(2,1)S(1)} all-gather(bf16[64,1536]{1,0:T(8,128)(2,1)S(1)} %get-tuple-element.53), channel_id=1, replica_groups=mesh['section'=4,'pair'=4,'core'=2] {'section'}, dimensions={0}, use_global_device_ids=true | all-gather | bytes 983040 | tf_op jit(solution)/shard_map/all_gather | solution.py:199
  541.4 11.8 %all_to_all.118 = bf16[4,64,1536]{2,1,0:T(8,128)(2,1)S(1)} all-to-all(bf16[4,64,1536]{2,1,0:T(8,128)(2,1)S(1)} %bitcast.274), channel_id=1, replica_groups=mesh['section'=4,'pair'=4,'core'=2] {'section'}, dimensions={0} | all-to-all | bytes 1572864 | tf_op jit(solution)/shard_map/all_to_all | solution.py:195
  555.0 11.1 %all_gather.90 = bf16[256,1536]{1,0:T(8,128)(2,1)S(1)} all-gather(bf16[64,1536]{1,0:T(8,128)(2,1)S(1)} %get-tuple-element.51), channel_id=1, replica_groups=mesh['section'=4,'pair'=4,'core'=2] {'section'}, dimensions={0}, use_global_device_ids=true | all-gather | bytes 983040 | tf_op jit(solution)/shard_map/all_gather | solution.py:199
  576.1 14.3 %reduce-scatter.4.cloned.1.call-done = bf16[1,192,1536]{2,1,0:T(8,128)(2,1)} async-done(((bf16[8,192,1536]{2,1,0:T(8,128)(2,1)}), bf16[1,192,1536]{2,1,0:T(8,128)(2,1)}) %reduce-scatter.4.cloned.1.call-update) | async-done | bytes 589840 | tf_op jit(solution)/shard_map/reduce_scatter | solution.py:373
  611.9 14.2 %collective-permute-done.21 = bf16[1536,384]{1,0:T(8,128)(2,1)} collective-permute-done((bf16[1536,384]{1,0:T(8,128)(2,1)}, bf16[1536,384]{1,0:T(8,128)(2,1)}, u32[]{:S(2)}, u32[]{:S(2)}) %collective-permute-start.21) | collective-permute-done | bytes 1179680 | tf_op jit(solution)/shard_map/ppermute | solution.py:118
  664.6 12.1 %all_gather.91 = bf16[256,1536]{1,0:T(8,128)(2,1)S(1)} all-gather(bf16[64,1536]{1,0:T(8,128)(2,1)S(1)} %get-tuple-element.49), channel_id=1, replica_groups=mesh['section'=4,'pair'=4,'core'=2] {'section'}, dimensions={0}, use_global_device_ids=true | all-gather | bytes 983040 | tf_op jit(solution)/shard_map/all_gather | solution.py:199
  763.5 10.8 %all-to-all-start.14 = ((f32[8,1,288]{2,1,0:T(1,128)}), f32[8,1,288]{2,1,0:T(1,128)S(1)}, u32[]{:S(2)}, u32[]{:S(2)}) async-start(f32[8,1,288]{2,1,0:T(1,128)} %reshape.674), calls=%async_computation.14 | async-start | bytes 24576 | tf_op jit(solution)/shard_map/all_to_all | solution.py:484
  825.7 23.9 %collective-permute-done.14 = bf16[128,1536]{1,0:T(8,128)(2,1)} collective-permute-done((bf16[128,1536]{1,0:T(8,128)(2,1)}, bf16[128,1536]{1,0:T(8,128)(2,1)}, u32[]{:S(2)}, u32[]{:S(2)}) %collective-permute-start.14) | collective-permute-done | bytes 393248 | tf_op jit(solution)/shard_map/ppermute | solution.py:118
  859.2 20.9 %collective-permute-done.20 = bf16[384,1536]{1,0:T(8,128)(2,1)} collective-permute-done((bf16[384,1536]{1,0:T(8,128)(2,1)}, bf16[384,1536]{1,0:T(8,128)(2,1)}, u32[]{:S(2)}, u32[]{:S(2)}) %collective-permute-start.20) | collective-permute-done | bytes 1179680 | tf_op jit(solution)/shard_map/ppermute | solution.py:124
  (647 shorter events, 546.5 us)
Async XLA Ops:
  7.2 104.2 %all-gather.15.cloned.1.call-start = ((), (), s32[]{:S(2)}) async-start(), calls=%async_computation.22 | async-start | bytes 3981312 | tf_op jit(solution)/shard_map/all_gather | solution.py:274
  32.1 105.8 %all-gather.17.cloned.1.call-start = ((), (), s32[]{:S(2)}) async-start(), calls=%async_computation.23 | async-start | bytes 6635520 | tf_op jit(solution)/shard_map/all_gather | solution.py:274
  51.8 138.7 %all-gather.21.cloned.1.call-start = ((), (), s32[]{:S(2)}) async-start(), calls=%async_computation.25 | async-start | bytes 5308416 | tf_op jit(solution)/shard_map/all_gather | solution.py:274
  53.1 190.0 %all-gather.19.cloned.1.call-start = ((), (), s32[]{:S(2)}) async-start(), calls=%async_computation.24 | async-start | bytes 5308416 | tf_op jit(solution)/shard_map/all_gather | solution.py:274
  65.7 37.8 %collective-permute-start.4 = (bf16[192,1536]{1,0:T(8,128)(2,1)}, bf16[192,1536]{1,0:T(8,128)(2,1)}, u32[]{:S(2)}, u32[]{:S(2)}) collective-permute-start(bf16[192,1536]{1,0:T(8,128)(2,1)} %reshape_squeeze.47), channel_id=1, source_target_pairs={{0,16},{8,24},{1,17},{9,25},{2,18},{10,26},{3,19},{11,27},{4,20},{... | collective-permute-start | bytes 1769480 | tf_op jit(solution)/shard_map/ppermute | solution.py:121
  141.7 62.9 %all-to-all-start = ((bf16[4,64,1536]{2,1,0:T(8,128)(2,1)}), bf16[4,64,1536]{2,1,0:T(8,128)(2,1)}, u32[]{:S(2)}, u32[]{:S(2)}) async-start(bf16[4,64,1536]{2,1,0:T(8,128)(2,1)} %bitcast.15), calls=%async_computation | async-start | bytes 1572864 | tf_op jit(solution)/shard_map/all_to_all | solution.py:195
  272.4 40.8 %all-to-all-start.3 = ((bf16[192,8,384]{2,0,1:T(8,128)(2,1)}), bf16[192,8,384]{2,0,1:T(8,128)(2,1)}, u32[]{:S(2)}, u32[]{:S(2)}) async-start(bf16[192,8,384]{2,0,1:T(8,128)(2,1)} %copy.273), calls=%async_computation.3 | async-start | bytes 2359296 | tf_op jit(solution)/shard_map/all_to_all | solution.py:293
  317.4 67.7 %all-gather.23.cloned.1.call-start = ((), (), s32[]{:S(2)}) async-start(), calls=%async_computation.26 | async-start | bytes 2359296 | tf_op jit(solution)/shard_map/all_gather | solution.py:209
  317.5 36.8 %collective-permute-start.5 = (bf16[1536,384]{1,0:T(8,128)(2,1)}, bf16[1536,384]{1,0:T(8,128)(2,1)}, u32[]{:S(2)}, u32[]{:S(2)}) collective-permute-start(bf16[1536,384]{1,0:T(8,128)(2,1)} %bitcast.29), channel_id=1, source_target_pairs={{16,0},{24,8},{17,1},{25,9},{18,2},{26,10},{19,3},{27,11},{20,4},{... | collective-permute-start | bytes 3538952 | tf_op jit(solution)/shard_map/ppermute | solution.py:124
  350.4 43.3 %all-gather.25.cloned.1.call-start = ((), (), s32[]{:S(2)}) async-start(), calls=%async_computation.27 | async-start | bytes 2359296 | tf_op jit(solution)/shard_map/all_gather | solution.py:209
  464.0 126.3 %reduce-scatter.4.cloned.1.call-start = ((), (), s32[]{:S(2)}) async-start(), calls=%async_computation.19 | async-start | bytes 5308416 | tf_op jit(solution)/shard_map/reduce_scatter | solution.py:373
  536.6 199.7 %reduce-scatter.6.cloned.1.call-start = ((), (), s32[]{:S(2)}) async-start(), calls=%async_computation.20 | async-start | bytes 10616832 | tf_op jit(solution)/shard_map/reduce_scatter | solution.py:373
  596.8 29.2 %collective-permute-start.21 = (bf16[1536,384]{1,0:T(8,128)(2,1)}, bf16[1536,384]{1,0:T(8,128)(2,1)}, u32[]{:S(2)}, u32[]{:S(2)}) collective-permute-start(bf16[1536,384]{1,0:T(8,128)(2,1)} %slice.471), channel_id=1, source_target_pairs={{0,8},{8,0},{16,24},{24,16},{1,9},{9,1},{17,25},{25,17},{2,10},{10... | collective-permute-start | bytes 3538952 | tf_op jit(solution)/shard_map/ppermute | solution.py:118
  607.3 191.5 %collective-permute-start.23 = (bf16[384,1536]{1,0:T(8,128)(2,1)}, bf16[384,1536]{1,0:T(8,128)(2,1)}, u32[]{:S(2)}, u32[]{:S(2)}) collective-permute-start(bf16[384,1536]{1,0:T(8,128)(2,1)} %slice.470), channel_id=1, source_target_pairs={{0,8},{8,0},{16,24},{24,16},{1,9},{9,1},{17,25},{25,17},{2,10},{10... | collective-permute-start | bytes 3538952 | tf_op jit(solution)/shard_map/ppermute | solution.py:118
  629.6 154.0 %collective-permute-start.22 = (bf16[1536,384]{1,0:T(8,128)(2,1)}, bf16[1536,384]{1,0:T(8,128)(2,1)}, u32[]{:S(2)}, u32[]{:S(2)}) collective-permute-start(bf16[1536,384]{1,0:T(8,128)(2,1)} %fusion.38), channel_id=1, source_target_pairs={{0,16},{8,24},{1,17},{9,25},{2,18},{10,26},{3,19},{11,27},{4,20},{... | collective-permute-start | bytes 3538952 | tf_op jit(solution)/shard_map/ppermute | solution.py:121
  693.7 48.2 %all-to-all-start.11 = ((bf16[4,64,1536]{2,1,0:T(8,128)(2,1)}), bf16[4,64,1536]{2,1,0:T(8,128)(2,1)}, u32[]{:S(2)}, u32[]{:S(2)}) async-start(bf16[4,64,1536]{2,1,0:T(8,128)(2,1)} %bitcast.278), calls=%async_computation.11 | async-start | bytes 1572864 | tf_op jit(solution)/shard_map/all_to_all | solution.py:195
  697.8 198.7 %reduce-scatter.8.cloned.1.call-start = ((), (), s32[]{:S(2)}) async-start(), calls=%async_computation.21 | async-start | bytes 5308416 | tf_op jit(solution)/shard_map/reduce_scatter | solution.py:373
  739.1 53.4 %collective-permute-start.12 = (bf16[256,1536]{1,0:T(8,128)(2,1)}, bf16[256,1536]{1,0:T(8,128)(2,1)S(1)}, u32[]{:S(2)}, u32[]{:S(2)}) collective-permute-start(bf16[256,1536]{1,0:T(8,128)(2,1)} %pad_maximum_fusion.24), channel_id=1, source_target_pairs={{0,16},{8,24},{16,0},{24,8},{1,17},{9,25},{17,1},{25,9},{2,18},{10... | collective-permute-start | bytes 2359304 | tf_op jit(solution)/shard_map/ppermute | solution.py:118
  740.7 51.8 %collective-permute-start.10 = (bf16[256,1536]{1,0:T(8,128)(2,1)}, bf16[256,1536]{1,0:T(8,128)(2,1)S(1)}, u32[]{:S(2)}, u32[]{:S(2)}) collective-permute-start(bf16[256,1536]{1,0:T(8,128)(2,1)} %pad_maximum_fusion.23), channel_id=1, source_target_pairs={{0,8},{8,0},{16,24},{24,16},{1,9},{9,1},{17,25},{25,17},{2,10},{10... | collective-permute-start | bytes 2359304 | tf_op jit(solution)/shard_map/ppermute | solution.py:118
  788.9 33.6 %all-to-all-start.15 = ((bf16[8,192,384]{2,1,0:T(8,128)(2,1)}), bf16[8,192,384]{2,1,0:T(8,128)(2,1)S(1)}, u32[]{:S(2)}, u32[]{:S(2)}) async-start(bf16[8,192,384]{2,1,0:T(8,128)(2,1)} %bitcast.85), calls=%async_computation.18 | async-start | bytes 2359296 | tf_op jit(solution)/shard_map/all_to_all | solution.py:502
  802.2 87.9 %collective-permute-start.24 = (bf16[384,1536]{1,0:T(8,128)(2,1)}, bf16[384,1536]{1,0:T(8,128)(2,1)}, u32[]{:S(2)}, u32[]{:S(2)}) collective-permute-start(bf16[384,1536]{1,0:T(8,128)(2,1)} %fusion.39), channel_id=1, source_target_pairs={{0,16},{8,24},{1,17},{9,25},{2,18},{10,26},{3,19},{11,27},{4,20},{... | collective-permute-start | bytes 3538952 | tf_op jit(solution)/shard_map/ppermute | solution.py:121
  817.5 32.1 %collective-permute-start.14 = (bf16[128,1536]{1,0:T(8,128)(2,1)}, bf16[128,1536]{1,0:T(8,128)(2,1)}, u32[]{:S(2)}, u32[]{:S(2)}) collective-permute-start(bf16[128,1536]{1,0:T(8,128)(2,1)} %slice.385), channel_id=1, source_target_pairs={{0,16},{8,24},{16,0},{24,8},{1,17},{9,25},{17,1},{25,9},{2,18},{10... | collective-permute-start | bytes 1179656 | tf_op jit(solution)/shard_map/ppermute | solution.py:118
  821.7 28.9 %collective-permute-start.16 = (bf16[128,1536]{1,0:T(8,128)(2,1)}, bf16[128,1536]{1,0:T(8,128)(2,1)S(1)}, u32[]{:S(2)}, u32[]{:S(2)}) collective-permute-start(bf16[128,1536]{1,0:T(8,128)(2,1)} %slice.386), channel_id=1, source_target_pairs={{0,8},{8,0},{16,24},{24,16},{1,9},{9,1},{17,25},{25,17},{2,10},{10... | collective-permute-start | bytes 1179656 | tf_op jit(solution)/shard_map/ppermute | solution.py:118
  850.7 29.4 %collective-permute-start.20 = (bf16[384,1536]{1,0:T(8,128)(2,1)}, bf16[384,1536]{1,0:T(8,128)(2,1)}, u32[]{:S(2)}, u32[]{:S(2)}) collective-permute-start(bf16[384,1536]{1,0:T(8,128)(2,1)} %bitcast.298), channel_id=1, source_target_pairs={{16,0},{24,8},{17,1},{25,9},{18,2},{26,10},{19,3},{27,11},{20,4},{... | collective-permute-start | bytes 3538952 | tf_op jit(solution)/shard_map/ppermute | solution.py:124
  (160 other events, 1178.1 us)
Sparse Core Ops, SparseCore 0:
  32.2 42.9 all-gather.14
  77.5 60.3 all-gather.16
  140.1 50.3 all-gather.20
  192.6 50.5 all-gather.18
  350.5 9.6 all-gather.22
  378.9 8.2 all-gather.24
  536.7 53.6 reduce-scatter.3
  592.7 97.8 reduce-scatter.5
  736.4 57.4 reduce-scatter.7

commit v3 on v2

--- a/solution.py
+++ b/solution.py
@@ -8,7 +8,6 @@
 HEAD_DIM = 96
 LATENTS = 64
 LAYERS = 2
-HALF_HEADS = 8
 
 epsilon = 1e-05
 low = jnp.bfloat16
@@ -94,20 +93,21 @@
     cotangent,
 ):
     dp = ("pair", "core")
+    everywhere = ("section",) + dp
     section = lax.axis_index("section")
     section_count = lax.axis_size("section")
     dp_index = lax.axis_index(dp)
     dp_count = lax.axis_size("pair") * lax.axis_size("core")
     on_first = section // 2 == 0
-    stride = dp_count // HALF_HEADS
-    row_first = (dp_index // stride) % 2 == 0
+    stride = dp_count // 2
+    row_first = dp_index // stride == 0
     seq_rows = segment_ids.shape[1]
     slot_count = slot_map.shape[1]
     feature_width = latents.shape[1]
     latent_rows = latents.shape[0]
     slot_rows = latent_rows // section_count
-    heads = HALF_HEADS // 2
-    inner = heads * HEAD_DIM
+    inner = w_query.shape[2] // 2
+    heads = inner // HEAD_DIM
     score_scale = 1.0 / math.sqrt(HEAD_DIM)
 
     def pick(first, second):
@@ -117,47 +117,29 @@
         pairs = [(source, source ^ mask) for source in range(section_count)]
         return lax.ppermute(value, "section", pairs)
 
+    def other_core(value):
+        return lax.ppermute(value, "core", [(0, 1), (1, 0)])
+
     def to_second(value):
         return lax.ppermute(value, "section", [(0, 2), (1, 3)])
 
     def to_first(value):
         return lax.ppermute(value, "section", [(2, 0), (3, 1)])
+
+    def after(value, earlier):
+        return lax.optimization_barrier((value, earlier))[0]
 
     def turn_pairs(flip, back):
         pairs = []
         for source in range(section_count):
             for index in range(dp_count):
                 layer, half = divmod(source, 2)
-                high, bit, lowest = (
-                    index // (2 * stride),
-                    (index // stride) % 2,
-                    index % stride,
-                )
-                moved = (2 * high + (layer ^ flip)) * stride + lowest
+                bit, lowest = divmod(index, stride)
+                moved = (layer ^ flip) * stride + lowest
                 target = (bit * 2 + half) * dp_count + moved
                 pair = (source * dp_count + index, target)
                 pairs.append(pair[::-1] if back else pair)
         return pairs
-
-    everywhere = ("section",) + dp
-
-    def column_parts(weight, block):
-        rows, width = weight.shape
-        split = weight.reshape(rows, width // (2 * block), 2, block)
-        return split[:, :, 0].reshape(rows, -1), split[:, :, 1].reshape(rows, -1)
-
-    def interleave(even, odd, block):
-        rows, width = even.shape
-        pieces = [part.reshape(rows, width // block, 1, block) for part in (even, odd)]
-        return jnp.concatenate(pieces, axis=2).reshape(rows, 2 * width)
-
-    def exchange_columns(even, odd):
-        own, other = pick(even, odd)
-        return pick(own, swapped(other, 2))
-
-    def join_columns(first, second):
-        own, other = pick(first, second)
-        return pick(own, swapped(other, 2))
 
     def exchange_rows(weight):
         half = weight.shape[0] // 2
@@ -178,17 +160,13 @@
 
     def rows_in_order(stacked):
         width = stacked.shape[-1]
-        if stride > 1:
-            piece = stacked.shape[1]
-            stacked = stacked.reshape(-1, 2, stride, piece, width).transpose(0, 2, 1, 3, 4)
+        stacked = stacked.reshape(2, stride, -1, width).transpose(1, 0, 2, 3)
         return stacked.reshape(-1, width)
 
     def rows_by_device(grad):
         width = grad.shape[-1]
-        piece = grad.shape[0] // dp_count
-        if stride > 1:
-            grad = grad.reshape(-1, stride, 2, piece, width).transpose(0, 2, 1, 3, 4)
-        return grad.reshape(dp_count, piece, width)
+        grad = grad.reshape(stride, 2, -1, width).transpose(1, 0, 2, 3)
+        return grad.reshape(dp_count, -1, width)
 
     def sum_to_slots(partial):
         blocks = partial.astype(low).reshape(section_count, -1, feature_width)
@@ -205,24 +183,35 @@
         return moved.astype(full)
 
     def from_sequences(rows):
-        pairs = lax.all_gather(rows, "pair", axis=0)
-        both = lax.all_gather(pairs, "core", axis=1)
-        return both.reshape(-1, feature_width)
-
-    def sum_to_sequence(partial):
-        blocks = partial.astype(low).reshape(-1, 2, slot_rows, feature_width)
-        halves = lax.all_to_all(blocks, "core", split_axis=1, concat_axis=1)
-        halves = jnp.sum(halves.astype(full), axis=1).astype(low)
-        arrived = lax.all_to_all(halves, "pair", split_axis=0, concat_axis=0)
+        near = lax.all_gather(rows, "pair", axis=0, tiled=True)
+        return jnp.concatenate([near, other_core(near)], axis=0)
+
+    def sum_to_sequence(left, right, product):
+        half = left.shape[0] // 2
+        far = product(left[half:], right).astype(low)
+        near = product(left[:half], right) + other_core(far).astype(full)
+        blocks = near.astype(low).reshape(-1, slot_rows, feature_width)
+        arrived = lax.all_to_all(blocks, "pair", split_axis=0, concat_axis=0)
         return jnp.sum(arrived.astype(full), axis=0)
 
-    def spread(shard):
-        own = jnp.where(on_first, to_first(shard), shard)
-        return own, swapped(own, 1)
-
-    def collect(own, other):
+    def by_distance(rows):
+        half = rows.shape[0] // 2
+        side = swapped(rows, 1)
+        ahead = swapped(rows, 2)
+        upper = swapped(side[:half], 2)
+        lower = swapped(ahead[half:], 1)
+        return rows, side, ahead, jnp.concatenate([upper, lower], axis=0)
+
+    def for_layers(rows, axis):
+        own, side, ahead, across = by_distance(rows)
+        near = pick(own, ahead)
+        far = pick(side, across)
+        return [jnp.concatenate([near[i], far[i]], axis=axis) for i in range(LAYERS)]
+
+    def collect(own, other, layer):
         total = own + swapped(other.astype(low), 1).astype(full)
-        return total + to_second(total.astype(low)).astype(full)
+        move = to_second if layer else to_first
+        return total + move(total.astype(low)).astype(full)
 
     def block_of(blocks, mask):
         return lax.dynamic_index_in_dim(blocks, section ^ mask, 0, keepdims=False)
@@ -239,13 +228,7 @@
         return own + swapped(side, 1).astype(full) + swapped(ahead, 2).astype(full)
 
     def gather_sections(rows):
-        half = rows.shape[0] // 2
-        side = swapped(rows, 1)
-        ahead = swapped(rows, 2)
-        upper = swapped(side[:half], 2)
-        lower = swapped(ahead[half:], 1)
-        across = jnp.concatenate([upper, lower], axis=0)
-        by_mask = [rows, side, ahead, across]
+        by_mask = by_distance(rows)
         ordered = []
         for target in range(section_count):
             chosen = by_mask[0]
@@ -254,44 +237,32 @@
             ordered.append(chosen)
         return jnp.concatenate(ordered, axis=0)
 
-    query_parts = column_parts(w_query[0], HEAD_DIM)
-    key_parts = column_parts(w_key[0], HEAD_DIM)
-    value_parts = column_parts(w_value[0], HEAD_DIM)
-    joined = [
-        jnp.concatenate([query_parts[i], key_parts[i], value_parts[i]], axis=1) for i in range(2)
-    ]
-    qkv_pieces = exchange_columns(joined[0], joined[1])
+    halves = [pick(weight[0, :, :inner], weight[0, :, inner:]) for weight in (w_query, w_key, w_value)]
+    own_heads = jnp.concatenate([half[0] for half in halves], axis=1)
+    other_heads = swapped(jnp.concatenate([half[1] for half in halves], axis=1), 2)
+    qkv_pieces = pick(own_heads, other_heads)
     out_pieces = exchange_rows(w_out[0])
-    hidden_block = w_down.shape[1] // 2
-    up_even, up_odd = column_parts(w_up[0], hidden_block)
-    up_piece = jnp.where(on_first, up_even, to_second(up_odd))
-    down_piece = jnp.where(
-        on_first, w_down[0, :hidden_block], to_second(w_down[0, hidden_block:])
-    )
-    out_piece_rows = out_pieces[0].shape[0]
+    out_rows = out_pieces[0].shape[0]
+    qkv_rows = qkv_pieces[1].size // feature_width
 
     def gather(piece):
         return lax.all_gather(piece, dp, axis=0)
 
     qkv_first = gather(qkv_pieces[0]).reshape(-1, 3 * inner)
-    stacked = gather(jnp.concatenate([out_pieces[0], down_piece], axis=0))
-    out_first = rows_in_order(stacked[:, :out_piece_rows])
-    down_first = stacked[:, out_piece_rows:].reshape(-1, feature_width)
-    up_first = gather(up_piece).reshape(feature_width, -1)
-    qkv_piece_rows = qkv_pieces[1].size // feature_width
+    out_first = rows_in_order(gather(out_pieces[0]))
     stacked = gather(
         jnp.concatenate([qkv_pieces[1].reshape(-1, feature_width), out_pieces[1]], axis=0)
     )
-    qkv_second = stacked[:, :qkv_piece_rows].reshape(-1, 3 * inner)
-    out_second = rows_in_order(stacked[:, qkv_piece_rows:])
+    qkv_second = stacked[:, :qkv_rows].reshape(-1, 3 * inner)
+    out_second = rows_in_order(stacked[:, qkv_rows:])
     qkv_w = (qkv_first, qkv_second)
     out_w = (out_first, out_second)
     query_w = [weight[:, :inner] for weight in qkv_w]
     key_w = [weight[:, inner : 2 * inner] for weight in qkv_w]
     value_w = [weight[:, 2 * inner :] for weight in qkv_w]
-    down_second = jnp.concatenate(spread(w_down[0]), axis=0)
+    down_w = for_layers(w_down[0], 0)
     up_turned = lax.all_to_all(w_up[0], dp, split_axis=1, concat_axis=0, tiled=True)
-    up_second = jnp.concatenate(spread(up_turned), axis=1)
+    up_w = for_layers(up_turned, 1)
 
     near_gains = lax.all_gather(gains, dp, axis=2, tiled=True)
     all_gains = lax.all_gather(near_gains, "section", axis=2, tiled=True)
@@ -340,16 +311,14 @@
             query_heads, key_heads, value_heads, allowed, score_scale
         )
         attended_low = attended.reshape(-1, inner).astype(low)
+        if layer == 0:
+            attended_low = after(attended_low, (up_w, down_w, grad_low))
         middle = current + sum_to_slots(matmul(attended_low, out_w[layer]))
         unit_mid, inverse_mid = unit_rows(middle)
-        ffn_low = (unit_mid * all_gains[layer, 2]).astype(low)
-        ffn_low = from_slots(ffn_low) if layer == 0 else from_sequences(ffn_low)
-        hidden_pre = matmul(ffn_low, up_first if layer == 0 else up_second)
+        ffn_low = from_sequences((unit_mid * all_gains[layer, 2]).astype(low))
+        hidden_pre = matmul(ffn_low, up_w[layer])
         active_low = gelu_exact(hidden_pre).astype(low)
-        if layer == 0:
-            current = middle + sum_to_slots(matmul(active_low, down_first))
-        else:
-            current = middle + sum_to_sequence(matmul(active_low, down_second))
+        current = middle + sum_to_sequence(active_low, down_w[layer], matmul)
         saved.append(
             (
                 unit_in,
@@ -367,19 +336,15 @@
                 active_low,
             )
         )
-    latents_out = to_columns(current)
 
     def scatter(blocks):
         return lax.psum_scatter(blocks, dp, scatter_dimension=0, tiled=False)
 
-    def after(value, earlier):
-        return lax.optimization_barrier((value, earlier))
-
     gain_rows = [None] * LAYERS
     media_scaled = None
-    qkv_pieces = [None] * LAYERS
-    out_pieces = [None] * LAYERS
-    last_piece = None
+    pieces = [None] * LAYERS
+    up_grads = [None] * LAYERS
+    down_grads = [None] * LAYERS
     for layer in (1, 0):
         (
             unit_in,
@@ -396,28 +361,14 @@
             hidden_pre,
             active_low,
         ) = saved[layer]
-        grad_active = matmul_nt(grad_low, down_first if layer == 0 else down_second)
+        grad_active = matmul_nt(grad_low, down_w[layer])
         grad_hidden = jax.vjp(gelu_exact, hidden_pre)[1](grad_active)[0].astype(low)
+        ffn_grad = sum_to_sequence(grad_hidden, up_w[layer], matmul_nt)
         down_grad = matmul_tn(active_low, grad_low)
         up_grad = matmul_tn(ffn_low, grad_hidden)
-        if layer == 0:
-            blocks = jnp.concatenate(
-                [
-                    up_grad.astype(low).reshape(dp_count, -1, feature_width),
-                    down_grad.astype(low).reshape(dp_count, -1, feature_width),
-                ],
-                axis=1,
-            )
-            blocks, qkv_pieces[1] = after(blocks, qkv_pieces[1])
-            ffn_piece = scatter(blocks)
-            last_piece = ffn_piece
-            ffn_grad = sum_to_slots(matmul_nt(grad_hidden, up_first))
-        else:
-            middle_of = down_grad.shape[0] // 2
-            down_second_grad = collect(down_grad[:middle_of], down_grad[middle_of:])
-            middle_of = up_grad.shape[1] // 2
-            up_second_grad = collect(up_grad[:, :middle_of], up_grad[:, middle_of:])
-            ffn_grad = sum_to_sequence(matmul_nt(grad_hidden, up_second))
+        middle_of = down_grad.shape[0] // 2
+        down_grads[layer] = collect(down_grad[:middle_of], down_grad[middle_of:], layer)
+        up_grads[layer] = collect(up_grad[:, :middle_of], up_grad[:, middle_of:], layer)
         gain_ffn_grad = jnp.sum(ffn_grad * unit_mid, axis=0)
         grad_middle = grad_rows + norm_back(
             unit_mid, inverse_mid, ffn_grad * all_gains[layer, 2]
@@ -441,8 +392,6 @@
         grad_rows = grad_middle + norm_back(
             unit_in, inverse_in, latent_grad_rows * all_gains[layer, 1]
         )
-        if layer > 0:
-            grad_low = from_slots(grad_rows.astype(low))
         both_low = jnp.concatenate([media_low[layer], latent_low], axis=0)
         query_grad = matmul_tn(latent_low, grad_query)
         key_grad = matmul_tn(both_low, grad_key)
@@ -450,17 +399,18 @@
         qkv_grad = jnp.concatenate(
             [query_grad.astype(low), key_grad.astype(low), value_grad.astype(low)], axis=1
         )
-        blocks = jnp.concatenate(
-            [
-                qkv_grad.reshape(dp_count, -1, feature_width),
-                rows_by_device(out_grad.astype(low)),
-            ],
-            axis=1,
-        )
-        if layer == 0:
-            blocks, ffn_piece = after(blocks, ffn_piece)
-        piece = scatter(blocks)
-        qkv_pieces[layer] = piece
+        pieces[layer] = scatter(
+            jnp.concatenate(
+                [
+                    qkv_grad.reshape(dp_count, -1, feature_width),
+                    rows_by_device(out_grad.astype(low)),
+                ],
+                axis=1,
+            )
+        )
+        if layer > 0:
+            grad_low = from_sequences(grad_rows.astype(low))
+            grad_low = after(grad_low, (up_grads[layer], down_grads[layer]))
         media_part = matmul_nt(grad_key[:seq_rows], key_w[layer]) + matmul_nt(
             grad_value[:seq_rows], value_w[layer]
         )
@@ -468,6 +418,7 @@
         scaled = media_part * all_gains[layer, 0]
         media_scaled = scaled if media_scaled is None else media_scaled + scaled
         gain_rows[layer] = jnp.stack([gain_media_grad, gain_latent_grad, gain_ffn_grad])
+    latents_out = to_columns(current)
     latent_grad = to_columns(grad_rows)
     media_rows = seq_rows // section_count
     media_sum = sum_over_sections(media_scaled)
@@ -483,27 +434,19 @@
     gain_parts = gain_parts.reshape(LAYERS, 3, dp_count, -1)
     gain_grad = jnp.sum(lax.all_to_all(gain_parts, dp, split_axis=2, concat_axis=2), axis=2)
 
-    qkv_parts = []
-    for layer in range(LAYERS):
-        out_pieces[layer] = qkv_pieces[layer][qkv_piece_rows:]
-        qkv_parts.append(qkv_pieces[layer][:qkv_piece_rows].reshape(-1, 3 * inner))
-    even, odd = join_columns(qkv_parts[0], qkv_parts[1])
+    qkv_parts = [piece[:qkv_rows].reshape(-1, 3 * inner) for piece in pieces]
+    own, other = pick(qkv_parts[0], qkv_parts[1])
+    lower, upper = pick(own, swapped(other, 2))
     qkv_grads = [
-        interleave(
-            even[:, i * inner : (i + 1) * inner], odd[:, i * inner : (i + 1) * inner], HEAD_DIM
+        jnp.concatenate(
+            [lower[:, i * inner : (i + 1) * inner], upper[:, i * inner : (i + 1) * inner]], axis=1
         ).astype(full)
         for i in range(3)
     ]
-    out_grad = join_rows(out_pieces[0], out_pieces[1])
-    back = to_first(ffn_piece)
-    up_rows = feature_width * feature_width // dp_count // feature_width
-    up_first_grad = interleave(ffn_piece[:up_rows], back[:up_rows], hidden_block)
-    down_first_grad = jnp.concatenate([ffn_piece[up_rows:], back[up_rows:]], axis=0)
-    up_second_grad = lax.all_to_all(
-        up_second_grad.astype(low), dp, split_axis=0, concat_axis=1, tiled=True
-    )
-    up_grad = jnp.where(on_first, up_first_grad.astype(full), up_second_grad.astype(full))
-    down_grad = jnp.where(on_first, down_first_grad.astype(full), down_second_grad)
+    out_grad = join_rows(pieces[0][qkv_rows:], pieces[1][qkv_rows:])
+    up_grad = jnp.where(on_first, up_grads[0], up_grads[1]).astype(low)
+    up_grad = lax.all_to_all(up_grad, dp, split_axis=0, concat_axis=1, tiled=True).astype(full)
+    down_grad = jnp.where(on_first, down_grads[0], down_grads[1])
     return (
         latents_out,
         latent_grad,

time: 943 us -> 884 us (0.937)
  waiting for transfers between devices: 273 us -> 148 us
  blocking collectives: 132 us -> 240 us
  local copies, waits for them, and re-layouts: 153 us -> 121 us
    all_gather x4 -> x3, waiting for transfers between devices: 67.9 us -> 0.02 us  [gather(): return lax.all_gather(piece, dp, axis=0)]
    all_gather x2 -> x4, blocking collectives: 36.6 us -> 86.3 us  [from_sequences(): near = lax.all_gather(rows, 'pair', axis=0, tiled=True)]
    all_gather x1, blocking collectives: 15.2 us -> 56.6 us  [per_device(): near_gains = lax.all_gather(gains, dp, axis=2, tiled=True)]
    ppermute x3 -> x2, waiting for transfers between devices: 23.4 us -> 0.01 us  [to_first(): return lax.ppermute(value, 'section', [(2, 0), (3, 1)])]
    ppermute x14 -> x22, waiting for transfers between devices: 81.7 us -> 101 us  [swapped(): return lax.ppermute(value, 'section', pairs)]
    all_to_all x5, waiting for transfers between devices: 32.2 us -> 14.6 us  [the longest x1 14.6 us: per_device(): lax.all_to_all(up_grad, dp, split_axis=0, concat_axis=1, tiled=True)]
    all_gather x5 -> x3, blocking collectives: 60.1 us -> 75.4 us  [from_slots(): return lax.all_gather(rows, 'section', axis=0, tiled=True)]
    slice x19 -> x13, local copies, waits for them, and re-layouts: 37 us -> 22.7 us  [the longest x3 5.7 us: by_distance(): lower = swapped(ahead[half:], 1)]
  transfers between devices with their start and end apart: 49 -> 56, of which waited for: 24 -> 19; matrix products, arithmetic and copies ran while one was open for 31% -> 36% of each run, Pallas kernels for 0% -> 0%
where the time goes in v3:
time: 884 us; the launch traced here: 876 us
  blocking collectives  240 us (27%)
  waiting for transfers between devices  148 us (17%)
  other arithmetic  124 us (14%)
  local copies, waits for them, and re-layouts  121 us (14%)
  matrix products  121 us (14%)
  starting transfers between devices  105 us (12%)
  between operations  16.5 us (2%)
    ppermute x22, waiting for transfers between devices, swapped(): return lax.ppermute(value, 'section', pairs)  101 us
    all_gather x4, blocking collectives, from_sequences(): near = lax.all_gather(rows, 'pair', axis=0, tiled=True)  86.3 us
    all_gather x3, blocking collectives, from_slots(): return lax.all_gather(rows, 'section', axis=0, tiled=True)  75.4 us
    all_gather x1, blocking collectives, per_device(): near_gains = lax.all_gather(gains, dp, axis=2, tiled=True)  56.6 us
    dot_general x18, matrix products, matmul_nt(): lax.dot_general(left, right, (((1,), (1,)), ((), ())), preferred_element_...  40.3 us
    dot_general x14, matrix products, matmul(): return jnp.dot(left, right, preferred_element_type=full)  38.5 us
    ppermute x22, starting transfers between devices, swapped(): return lax.ppermute(value, 'section', pairs)  30.3 us
    unnamed x308, local copies, waits for them, and re-layouts  21.9 us
  transfers between devices with their start and end apart: 56, of which 19 were waited for; matrix products, arithmetic and copies ran while one was open for 36% of the time, Pallas kernels for 0%

profile of v3, /device:TPU:0, one launch (start us, length us, event | category | flops | bytes accessed | tf_op | source)
XLA Modules:
  0.0 875.8 jit_solution(982911247323412740)
XLA Ops:
  16.6 8.5 collective-permute-start
  25.1 9.3 %collective-permute-done = bf16[192,1152]{1,0:T(8,128)(2,1)S(1)} collective-permute-done((bf16[192,1152]{1,0:T(8,128)(2,1)S(1)}, bf16[192,1152]{1,0:T(8,128)(2,1)S(1)}, u32[]{:S(2)}, u32[]{:S(2)}) %collective-permute-start) | collective-permute-done | bytes 442400 | tf_op jit(solution)/shard_map/ppermute | solution.py:118
  39.7 21.0 %all_gather.49 = bf16[256,1536]{1,0:T(8,128)(2,1)} all-gather(bf16[64,1536]{1,0:T(8,128)(2,1)S(1)} %constant_dynamic-slice_fusion), channel_id=1, replica_groups=mesh['section'=4,'pair'=4,'core'=2] {'pair'}, dimensions={0}, use_global_device_ids=true | all-gather | bytes 983040 | tf_op jit(solution)/shard_map/all_gather | solution.py:186
  67.5 56.6 %all_gather.45 = f32[2,3,384]{1,0,2:T(2,128)S(1)} all-gather(f32[2,3,48]{1,0,2:T(2,128)} %copy.141), channel_id=1, replica_groups=mesh['section'=4,'pair'=4,'core'=2] {'pair','core'}, dimensions={2}, use_global_device_ids=true | all-gather | bytes 10368 | tf_op jit(solution)/shard_map/all_gather | solution.py:267
  125.3 8.4 all_gather.46
  161.3 7.3 collective-permute-done.7
  178.5 15.7 %collective-permute-done.2 = bf16[1536,384]{1,0:T(8,128)(2,1)S(1)} collective-permute-done((bf16[1536,384]{1,0:T(8,128)(2,1)}, bf16[1536,384]{1,0:T(8,128)(2,1)S(1)}, u32[]{:S(2)}, u32[]{:S(2)}) %collective-permute-start.2) | collective-permute-done | bytes 1179680 | tf_op jit(solution)/shard_map/ppermute | solution.py:118
  241.9 17.4 %all_gather.52 = bf16[256,1536]{1,0:T(8,128)(2,1)S(1)} all-gather(bf16[64,1536]{1,0:T(8,128)(2,1)S(1)} %multiply_convert_fusion.9), channel_id=1, replica_groups=mesh['section'=4,'pair'=4,'core'=2] {'pair'}, dimensions={0}, use_global_device_ids=true | all-gather | bytes 983040 | tf_op jit(solution)/shard_map/all_gather | solution.py:186
  301.9 12.6 %all_gather.55 = bf16[256,1536]{1,0:T(8,128)(2,1)S(1)} all-gather(bf16[64,1536]{1,0:T(8,128)(2,1)S(1)} %multiply_convert_fusion.8), channel_id=1, replica_groups=mesh['section'=4,'pair'=4,'core'=2] {'section'}, dimensions={0}, use_global_device_ids=true | all-gather | bytes 983040 | tf_op jit(solution)/shard_map/all_gather | solution.py:177
  333.4 13.3 %all_to_all.108 = bf16[4,64,1536]{2,1,0:T(8,128)(2,1)S(1)} all-to-all(bf16[4,64,1536]{2,1,0:T(8,128)(2,1)S(1)} %bitcast.284), channel_id=1, replica_groups=mesh['section'=4,'pair'=4,'core'=2] {'section'}, dimensions={0} | all-to-all | bytes 1572864 | tf_op jit(solution)/shard_map/all_to_all | solution.py:173
  347.8 18.5 %all_gather.56 = bf16[256,1536]{1,0:T(8,128)(2,1)} all-gather(bf16[64,1536]{1,0:T(8,128)(2,1)S(1)} %multiply_convert_fusion.7), channel_id=1, replica_groups=mesh['section'=4,'pair'=4,'core'=2] {'pair'}, dimensions={0}, use_global_device_ids=true | all-gather | bytes 983040 | tf_op jit(solution)/shard_map/all_gather | solution.py:186
  400.6 12.2 %collective-permute-done.18 = bf16[1536,384]{1,0:T(8,128)(2,1)} collective-permute-done((bf16[1536,384]{1,0:T(8,128)(2,1)}, bf16[1536,384]{1,0:T(8,128)(2,1)}, u32[]{:S(2)}, u32[]{:S(2)}) %collective-permute-start.18) | collective-permute-done | bytes 1179680 | tf_op jit(solution)/shard_map/ppermute | solution.py:118
  424.1 13.5 %collective-permute-done.20 = bf16[384,1536]{1,0:T(8,128)(2,1)} collective-permute-done((bf16[384,1536]{1,0:T(8,128)(2,1)}, bf16[384,1536]{1,0:T(8,128)(2,1)}, u32[]{:S(2)}, u32[]{:S(2)}) %collective-permute-start.20) | collective-permute-done | bytes 1179680 | tf_op jit(solution)/shard_map/ppermute | solution.py:118
  451.9 27.0 %all_gather.57 = bf16[256,1536]{1,0:T(8,128)(2,1)S(1)} all-gather(bf16[64,1536]{1,0:T(8,128)(2,1)S(1)} %get-tuple-element.41), channel_id=1, replica_groups=mesh['section'=4,'pair'=4,'core'=2] {'section'}, dimensions={0}, use_global_device_ids=true | all-gather | bytes 983040 | tf_op jit(solution)/shard_map/all_gather | solution.py:177
  518.1 6.5 reshape.643
  547.4 29.3 %all_gather.58 = bf16[256,1536]{1,0:T(8,128)(2,1)S(1)} all-gather(bf16[64,1536]{1,0:T(8,128)(2,1)S(1)} %get-tuple-element.39), channel_id=1, replica_groups=mesh['section'=4,'pair'=4,'core'=2] {'pair'}, dimensions={0}, use_global_device_ids=true | all-gather | bytes 983040 | tf_op jit(solution)/shard_map/all_gather | solution.py:186
  614.5 7.8 collective-permute-done.34
  627.0 19.8 %collective-permute-done.36 = bf16[384,1536]{1,0:T(8,128)(2,1)} collective-permute-done((bf16[384,1536]{1,0:T(8,128)(2,1)}, bf16[384,1536]{1,0:T(8,128)(2,1)}, u32[]{:S(2)}, u32[]{:S(2)}) %collective-permute-start.36) | collective-permute-done | bytes 1179680 | tf_op jit(solution)/shard_map/ppermute | solution.py:118
  653.1 35.8 %all_gather.59 = bf16[256,1536]{1,0:T(8,128)(2,1)S(1)} all-gather(bf16[64,1536]{1,0:T(8,128)(2,1)S(1)} %get-tuple-element.37), channel_id=1, replica_groups=mesh['section'=4,'pair'=4,'core'=2] {'section'}, dimensions={0}, use_global_device_ids=true | all-gather | bytes 983040 | tf_op jit(solution)/shard_map/all_gather | solution.py:177
  725.8 8.3 multiply_reduce_fusion.1
  762.4 10.2 %all-to-all-done.11 = f32[2,3,4,384]{3,0,1,2:T(2,128)S(1)} async-done(((f32[2,3,4,384]{3,0,1,2:T(2,128)}), f32[2,3,4,384]{3,0,1,2:T(2,128)S(1)}, u32[]{:S(2)}, u32[]{:S(2)}) %all-to-all-start.11) | async-done | bytes 36896 | tf_op jit(solution)/shard_map/all_to_all | solution.py:432
  792.6 10.5 %collective-permute-done.27 = bf16[256,1536]{1,0:T(8,128)(2,1)} collective-permute-done((bf16[256,1536]{1,0:T(8,128)(2,1)S(1)}, bf16[256,1536]{1,0:T(8,128)(2,1)}, u32[]{:S(2)}, u32[]{:S(2)}) %collective-permute-start.27) | collective-permute-done | bytes 786464 | tf_op jit(solution)/shard_map/ppermute | solution.py:118
  828.9 14.6 %all-to-all-done.13 = bf16[8,192,384]{2,1,0:T(8,128)(2,1)S(1)} async-done(((bf16[8,192,384]{2,1,0:T(8,128)(2,1)}), bf16[8,192,384]{2,1,0:T(8,128)(2,1)S(1)}, u32[]{:S(2)}, u32[]{:S(2)}) %all-to-all-start.13) | async-done | bytes 1179680 | tf_op jit(solution)/shard_map/all_to_all | solution.py:448
  852.8 11.7 %collective-permute-done.33 = bf16[48,1536]{1,0:T(8,128)(2,1)S(1)} collective-permute-done((bf16[48,1536]{1,0:T(8,128)(2,1)S(1)}, bf16[48,1536]{1,0:T(8,128)(2,1)S(1)}, u32[]{:S(2)}, u32[]{:S(2)}) %collective-permute-start.33) | collective-permute-done | bytes 147488 | tf_op jit(solution)/shard_map/ppermute | solution.py:158
  (656 shorter events, 463.5 us)
Async XLA Ops:
  7.2 168.9 %all-gather.9.cloned.1.call-start = ((), (), s32[]{:S(2)}) async-start(), calls=%async_computation.19 | async-start | bytes 1327104 | tf_op jit(solution)/shard_map/all_gather | solution.py:249
  16.3 182.9 %all-gather.7.cloned.1.call-start = ((), (), s32[]{:S(2)}) async-start(), calls=%async_computation.18 | async-start | bytes 3981312 | tf_op jit(solution)/shard_map/all_gather | solution.py:249
  35.5 114.3 %collective-permute-start.6 = (bf16[384,1536]{1,0:T(8,128)(2,1)}, bf16[384,1536]{1,0:T(8,128)(2,1)}, u32[]{:S(2)}, u32[]{:S(2)}) collective-permute-start(bf16[384,1536]{1,0:T(8,128)(2,1)} %bitcast.18), channel_id=1, source_target_pairs={{0,8},{8,0},{16,24},{24,16},{1,9},{9,1},{17,25},{25,17},{2,10},{10... | collective-permute-start | bytes 3538952 | tf_op jit(solution)/shard_map/ppermute | solution.py:118
  37.0 116.6 %collective-permute-start.5 = (bf16[384,1536]{1,0:T(8,128)(2,1)}, bf16[384,1536]{1,0:T(8,128)(2,1)}, u32[]{:S(2)}, u32[]{:S(2)}) collective-permute-start(bf16[384,1536]{1,0:T(8,128)(2,1)} %bitcast.18), channel_id=1, source_target_pairs={{0,16},{8,24},{16,0},{24,8},{1,17},{9,25},{17,1},{25,9},{2,18},{10... | collective-permute-start | bytes 3538952 | tf_op jit(solution)/shard_map/ppermute | solution.py:118
  60.7 87.6 %collective-permute-start.9 = (bf16[256,1536]{1,0:T(8,128)(2,1)}, bf16[256,1536]{1,0:T(8,128)(2,1)}, u32[]{:S(2)}, u32[]{:S(2)}) collective-permute-start(bf16[256,1536]{1,0:T(8,128)(2,1)} %all_gather.49), channel_id=1, source_target_pairs={{0,1},{1,0},{2,3},{3,2},{4,5},{5,4},{6,7},{7,6},{8,9},{9,8},{10,11... | collective-permute-start | bytes 2359304 | tf_op jit(solution)/shard_map/ppermute | solution.py:121
  62.2 93.9 %all-to-all-start = ((bf16[192,8,384]{2,0,1:T(8,128)(2,1)}), bf16[192,8,384]{2,0,1:T(8,128)(2,1)}, u32[]{:S(2)}, u32[]{:S(2)}) async-start(bf16[192,8,384]{2,0,1:T(8,128)(2,1)} %copy.146), calls=%async_computation | async-start | bytes 2359296 | tf_op jit(solution)/shard_map/all_to_all | solution.py:264
  66.7 210.5 %all-gather.11.cloned.1.call-start = ((), (), s32[]{:S(2)}) async-start(), calls=%async_computation.20 | async-start | bytes 5308416 | tf_op jit(solution)/shard_map/all_gather | solution.py:249
  156.1 38.2 %collective-permute-start.2 = (bf16[1536,384]{1,0:T(8,128)(2,1)}, bf16[1536,384]{1,0:T(8,128)(2,1)S(1)}, u32[]{:S(2)}, u32[]{:S(2)}) collective-permute-start(bf16[1536,384]{1,0:T(8,128)(2,1)} %bitcast.16), channel_id=1, source_target_pairs={{0,8},{8,0},{16,24},{24,16},{1,9},{9,1},{17,25},{25,17},{2,10},{10... | collective-permute-start | bytes 3538952 | tf_op jit(solution)/shard_map/ppermute | solution.py:118
  157.6 38.3 %collective-permute-start.1 = (bf16[1536,384]{1,0:T(8,128)(2,1)}, bf16[1536,384]{1,0:T(8,128)(2,1)}, u32[]{:S(2)}, u32[]{:S(2)}) collective-permute-start(bf16[1536,384]{1,0:T(8,128)(2,1)} %bitcast.16), channel_id=1, source_target_pairs={{0,16},{8,24},{16,0},{24,8},{1,17},{9,25},{17,1},{25,9},{2,18},{10... | collective-permute-start | bytes 3538952 | tf_op jit(solution)/shard_map/ppermute | solution.py:118
  195.2 38.8 %collective-permute-start.3 = (bf16[768,384]{1,0:T(8,128)(2,1)}, bf16[768,384]{1,0:T(8,128)(2,1)}, u32[]{:S(2)}, u32[]{:S(2)}) collective-permute-start(bf16[768,384]{1,0:T(8,128)(2,1)} %slice.377), channel_id=1, source_target_pairs={{0,16},{8,24},{16,0},{24,8},{1,17},{9,25},{17,1},{25,9},{2,18},{10... | collective-permute-start | bytes 1769480 | tf_op jit(solution)/shard_map/ppermute | solution.py:118
  197.8 37.8 %collective-permute-start.4 = (bf16[768,384]{1,0:T(8,128)(2,1)}, bf16[768,384]{1,0:T(8,128)(2,1)}, u32[]{:S(2)}, u32[]{:S(2)}) collective-permute-start(bf16[768,384]{1,0:T(8,128)(2,1)} %slice.378), channel_id=1, source_target_pairs={{0,8},{8,0},{16,24},{24,16},{1,9},{9,1},{17,25},{25,17},{2,10},{10... | collective-permute-start | bytes 1769480 | tf_op jit(solution)/shard_map/ppermute | solution.py:118
  387.7 49.9 %collective-permute-start.20 = (bf16[384,1536]{1,0:T(8,128)(2,1)}, bf16[384,1536]{1,0:T(8,128)(2,1)}, u32[]{:S(2)}, u32[]{:S(2)}) collective-permute-start(bf16[384,1536]{1,0:T(8,128)(2,1)} %slice.540), channel_id=1, source_target_pairs={{0,8},{8,0},{16,24},{24,16},{1,9},{9,1},{17,25},{25,17},{2,10},{10... | collective-permute-start | bytes 3538952 | tf_op jit(solution)/shard_map/ppermute | solution.py:118
  390.1 29.3 %all-to-all-start.6 = ((bf16[4,64,1536]{2,1,0:T(8,128)(2,1)}), bf16[4,64,1536]{2,1,0:T(8,128)(2,1)}, u32[]{:S(2)}, u32[]{:S(2)}) async-start(bf16[4,64,1536]{2,1,0:T(8,128)(2,1)} %bitcast.310), calls=%async_computation.6 | async-start | bytes 1572864 | tf_op jit(solution)/shard_map/all_to_all | solution.py:194
  415.4 161.3 %collective-permute-start.19 = (bf16[1536,384]{1,0:T(8,128)(2,1)}, bf16[1536,384]{1,0:T(8,128)(2,1)}, u32[]{:S(2)}, u32[]{:S(2)}) collective-permute-start(bf16[1536,384]{1,0:T(8,128)(2,1)} %fusion.40), channel_id=1, source_target_pairs={{0,16},{8,24},{1,17},{9,25},{2,18},{10,26},{3,19},{11,27},{4,20},{... | collective-permute-start | bytes 3538952 | tf_op jit(solution)/shard_map/ppermute | solution.py:124
  441.0 139.6 %collective-permute-start.21 = (bf16[384,1536]{1,0:T(8,128)(2,1)}, bf16[384,1536]{1,0:T(8,128)(2,1)}, u32[]{:S(2)}, u32[]{:S(2)}) collective-permute-start(bf16[384,1536]{1,0:T(8,128)(2,1)} %fusion.41), channel_id=1, source_target_pairs={{0,16},{8,24},{1,17},{9,25},{2,18},{10,26},{3,19},{11,27},{4,20},{... | collective-permute-start | bytes 3538952 | tf_op jit(solution)/shard_map/ppermute | solution.py:124
  498.0 41.2 %all-to-all-start.7 = ((bf16[4,64,1536]{2,1,0:T(8,128)(2,1)}), bf16[4,64,1536]{2,1,0:T(8,128)(2,1)}, u32[]{:S(2)}, u32[]{:S(2)}) async-start(bf16[4,64,1536]{2,1,0:T(8,128)(2,1)} %bitcast.283), calls=%async_computation.7 | async-start | bytes 1572864 | tf_op jit(solution)/shard_map/all_to_all | solution.py:173
  502.2 344.5 %reduce-scatter.5.cloned.1.call-start = ((), (), s32[]{:S(2)}) async-start(), calls=%async_computation.17 | async-start | bytes 5308416 | tf_op jit(solution)/shard_map/reduce_scatter | solution.py:341
  539.2 64.4 %all-to-all-start.5 = ((bf16[64,4,384]{2,0,1:T(8,128)(2,1)}), bf16[64,4,384]{2,0,1:T(8,128)(2,1)}, u32[]{:S(2)}, u32[]{:S(2)}) async-start(bf16[64,4,384]{2,0,1:T(8,128)(2,1)} %bitcast.311), calls=%async_computation.5 | async-start | bytes 393216 | tf_op jit(solution)/shard_map/all_to_all | solution.py:180
  597.8 49.1 %collective-permute-start.36 = (bf16[384,1536]{1,0:T(8,128)(2,1)}, bf16[384,1536]{1,0:T(8,128)(2,1)}, u32[]{:S(2)}, u32[]{:S(2)}) collective-permute-start(bf16[384,1536]{1,0:T(8,128)(2,1)} %slice.538), channel_id=1, source_target_pairs={{0,8},{8,0},{16,24},{24,16},{1,9},{9,1},{17,25},{25,17},{2,10},{10... | collective-permute-start | bytes 3538952 | tf_op jit(solution)/shard_map/ppermute | solution.py:118
  610.2 41.5 %all-to-all-start.8 = ((bf16[4,64,1536]{2,1,0:T(8,128)(2,1)}), bf16[4,64,1536]{2,1,0:T(8,128)(2,1)S(1)}, u32[]{:S(2)}, u32[]{:S(2)}) async-start(bf16[4,64,1536]{2,1,0:T(8,128)(2,1)} %bitcast.48), calls=%async_computation.8 | async-start | bytes 1572864 | tf_op jit(solution)/shard_map/all_to_all | solution.py:194
  614.5 232.1 %reduce-scatter.3.cloned.1.call-start = ((), (), s32[]{:S(2)}) async-start(), calls=%async_computation.16 | async-start | bytes 5308416 | tf_op jit(solution)/shard_map/reduce_scatter | solution.py:341
  625.6 163.0 %collective-permute-start.35 = (bf16[1536,384]{1,0:T(8,128)(2,1)}, bf16[1536,384]{1,0:T(8,128)(2,1)}, u32[]{:S(2)}, u32[]{:S(2)}) collective-permute-start(bf16[1536,384]{1,0:T(8,128)(2,1)} %fusion.42), channel_id=1, source_target_pairs={{16,0},{24,8},{17,1},{25,9},{18,2},{26,10},{19,3},{27,11},{20,4},{... | collective-permute-start | bytes 3538952 | tf_op jit(solution)/shard_map/ppermute | solution.py:127
  650.3 163.9 %collective-permute-start.37 = (bf16[384,1536]{1,0:T(8,128)(2,1)}, bf16[384,1536]{1,0:T(8,128)(2,1)}, u32[]{:S(2)}, u32[]{:S(2)}) collective-permute-start(bf16[384,1536]{1,0:T(8,128)(2,1)} %fusion.43), channel_id=1, source_target_pairs={{16,0},{24,8},{17,1},{25,9},{18,2},{26,10},{19,3},{27,11},{20,4},{... | collective-permute-start | bytes 3538952 | tf_op jit(solution)/shard_map/ppermute | solution.py:127
  809.0 34.5 %all-to-all-start.13 = ((bf16[8,192,384]{2,1,0:T(8,128)(2,1)}), bf16[8,192,384]{2,1,0:T(8,128)(2,1)S(1)}, u32[]{:S(2)}, u32[]{:S(2)}) async-start(bf16[8,192,384]{2,1,0:T(8,128)(2,1)} %bitcast.94), calls=%async_computation.15 | async-start | bytes 2359296 | tf_op jit(solution)/shard_map/all_to_all | solution.py:448
  (181 other events, 1614.6 us)
Sparse Core Ops, SparseCore 0:
  16.5 33.9 all-gather.8
  52.7 64.2 all-gather.6
  148.4 51.2 all-gather.10
  533.6 67.8 reduce-scatter.4
  720.7 54.7 reduce-scatter.2

commit v4 on v3

--- a/solution.py
+++ b/solution.py
@@ -158,15 +158,25 @@
         far = lax.ppermute(far, everywhere, turn_pairs(1, True))
         return jnp.concatenate(pick(near, far), axis=0).astype(full)
 
-    def rows_in_order(stacked):
-        width = stacked.shape[-1]
-        stacked = stacked.reshape(2, stride, -1, width).transpose(1, 0, 2, 3)
-        return stacked.reshape(-1, width)
-
-    def rows_by_device(grad):
-        width = grad.shape[-1]
-        grad = grad.reshape(stride, 2, -1, width).transpose(1, 0, 2, 3)
-        return grad.reshape(dp_count, -1, width)
+    def fold(piece):
+        blocks = [piece[:, i * inner : (i + 1) * inner] for i in range(feature_width // inner)]
+        return jnp.concatenate(blocks, axis=0)
+
+    def unfold(stacked):
+        count = feature_width // inner
+        blocks = stacked.reshape(2, stride, count, -1, inner).transpose(1, 0, 3, 2, 4)
+        return blocks.reshape(-1, feature_width)
+
+    def fold_grad(grad):
+        count = feature_width // inner
+        blocks = grad.reshape(stride, 2, -1, count, inner).transpose(1, 0, 3, 2, 4)
+        return blocks.reshape(-1, inner)
+
+    def unfold_piece(piece):
+        count = feature_width // inner
+        rows = piece.shape[0] // count
+        blocks = [piece[i * rows : (i + 1) * rows] for i in range(count)]
+        return jnp.concatenate(blocks, axis=1)
 
     def sum_to_slots(partial):
         blocks = partial.astype(low).reshape(section_count, -1, feature_width)
@@ -208,8 +218,10 @@
         far = pick(side, across)
         return [jnp.concatenate([near[i], far[i]], axis=axis) for i in range(LAYERS)]
 
-    def collect(own, other, layer):
-        total = own + swapped(other.astype(low), 1).astype(full)
+    def collect_side(own, other):
+        return own + swapped(other.astype(low), 1).astype(full)
+
+    def collect_ahead(total, layer):
         move = to_second if layer else to_first
         return total + move(total.astype(low)).astype(full)
 
@@ -237,35 +249,35 @@
             ordered.append(chosen)
         return jnp.concatenate(ordered, axis=0)
 
+    near_gains = lax.all_gather(gains, dp, axis=2, tiled=True)
+    all_gains = lax.all_gather(near_gains, "section", axis=2, tiled=True)
     halves = [pick(weight[0, :, :inner], weight[0, :, inner:]) for weight in (w_query, w_key, w_value)]
     own_heads = jnp.concatenate([half[0] for half in halves], axis=1)
     other_heads = swapped(jnp.concatenate([half[1] for half in halves], axis=1), 2)
     qkv_pieces = pick(own_heads, other_heads)
-    out_pieces = exchange_rows(w_out[0])
-    out_rows = out_pieces[0].shape[0]
-    qkv_rows = qkv_pieces[1].size // feature_width
+    down_in, up_in = after((w_down[0], w_up[0]), all_gains)
+    out_pieces = exchange_rows(after(w_out[0], all_gains))
 
     def gather(piece):
-        return lax.all_gather(piece, dp, axis=0)
-
-    qkv_first = gather(qkv_pieces[0]).reshape(-1, 3 * inner)
-    out_first = rows_in_order(gather(out_pieces[0]))
+        return lax.all_gather(piece, dp, axis=0, tiled=True)
+
+    qkv_first = gather(after(qkv_pieces[0], all_gains))
+    out_first = gather(after(fold(out_pieces[0]), qkv_first))
     stacked = gather(
-        jnp.concatenate([qkv_pieces[1].reshape(-1, feature_width), out_pieces[1]], axis=0)
-    )
-    qkv_second = stacked[:, :qkv_rows].reshape(-1, 3 * inner)
-    out_second = rows_in_order(stacked[:, qkv_rows:])
+        after(jnp.concatenate([qkv_pieces[1], fold(out_pieces[1])], axis=1), out_first)
+    )
+    out_first = unfold(out_first)
+    qkv_second = stacked[:, : 3 * inner]
+    out_second = unfold(stacked[:, 3 * inner :])
     qkv_w = (qkv_first, qkv_second)
     out_w = (out_first, out_second)
     query_w = [weight[:, :inner] for weight in qkv_w]
     key_w = [weight[:, inner : 2 * inner] for weight in qkv_w]
     value_w = [weight[:, 2 * inner :] for weight in qkv_w]
-    down_w = for_layers(w_down[0], 0)
-    up_turned = lax.all_to_all(w_up[0], dp, split_axis=1, concat_axis=0, tiled=True)
+    down_w = for_layers(down_in, 0)
+    up_turned = lax.all_to_all(up_in, dp, split_axis=1, concat_axis=0, tiled=True)
     up_w = for_layers(up_turned, 1)
 
-    near_gains = lax.all_gather(gains, dp, axis=2, tiled=True)
-    all_gains = lax.all_gather(near_gains, "section", axis=2, tiled=True)
     image_hot = segment_ids[:, :, None] == jnp.arange(slot_count, dtype=jnp.int32)[None, None, :]
     media_slot = jnp.sum(jnp.where(image_hot, slot_map[:, None, :], 0), axis=2) - (
         segment_ids < 0
@@ -338,7 +350,7 @@
         )
 
     def scatter(blocks):
-        return lax.psum_scatter(blocks, dp, scatter_dimension=0, tiled=False)
+        return lax.psum_scatter(blocks, dp, scatter_dimension=0, tiled=True)
 
     gain_rows = [None] * LAYERS
     media_scaled = None
@@ -367,13 +379,13 @@
         down_grad = matmul_tn(active_low, grad_low)
         up_grad = matmul_tn(ffn_low, grad_hidden)
         middle_of = down_grad.shape[0] // 2
-        down_grads[layer] = collect(down_grad[:middle_of], down_grad[middle_of:], layer)
-        up_grads[layer] = collect(up_grad[:, :middle_of], up_grad[:, middle_of:], layer)
+        down_side = collect_side(down_grad[:middle_of], down_grad[middle_of:])
+        up_side = collect_side(up_grad[:, :middle_of], up_grad[:, middle_of:])
         gain_ffn_grad = jnp.sum(ffn_grad * unit_mid, axis=0)
         grad_middle = grad_rows + norm_back(
             unit_mid, inverse_mid, ffn_grad * all_gains[layer, 2]
         )
-        middle_low = from_slots(grad_middle.astype(low))
+        middle_low = from_slots(after(grad_middle.astype(low), down_side))
         grad_heads = split_heads(matmul_nt(middle_low, out_w[layer]).astype(low))
         out_grad = matmul_tn(attended_low, middle_low)
         grad_query, grad_key, grad_value = attend_backward(
@@ -387,6 +399,10 @@
             + matmul_nt(grad_key[seq_rows:], key_w[layer])
             + matmul_nt(grad_value[seq_rows:], value_w[layer])
         )
+        down_grads[layer] = collect_ahead(down_side, layer)
+        up_grads[layer] = collect_ahead(up_side, layer)
+        if layer > 0:
+            latent_part = after(latent_part, (up_side, down_grads[layer]))
         latent_grad_rows = sum_to_slots(latent_part)
         gain_latent_grad = jnp.sum(latent_grad_rows * unit_in, axis=0)
         grad_rows = grad_middle + norm_back(
@@ -400,17 +416,11 @@
             [query_grad.astype(low), key_grad.astype(low), value_grad.astype(low)], axis=1
         )
         pieces[layer] = scatter(
-            jnp.concatenate(
-                [
-                    qkv_grad.reshape(dp_count, -1, feature_width),
-                    rows_by_device(out_grad.astype(low)),
-                ],
-                axis=1,
-            )
+            jnp.concatenate([qkv_grad, fold_grad(out_grad.astype(low))], axis=1)
         )
         if layer > 0:
             grad_low = from_sequences(grad_rows.astype(low))
-            grad_low = after(grad_low, (up_grads[layer], down_grads[layer]))
+            grad_low = after(grad_low, up_grads[layer])
         media_part = matmul_nt(grad_key[:seq_rows], key_w[layer]) + matmul_nt(
             grad_value[:seq_rows], value_w[layer]
         )
@@ -434,7 +444,7 @@
     gain_parts = gain_parts.reshape(LAYERS, 3, dp_count, -1)
     gain_grad = jnp.sum(lax.all_to_all(gain_parts, dp, split_axis=2, concat_axis=2), axis=2)
 
-    qkv_parts = [piece[:qkv_rows].reshape(-1, 3 * inner) for piece in pieces]
+    qkv_parts = [piece[:, : 3 * inner] for piece in pieces]
     own, other = pick(qkv_parts[0], qkv_parts[1])
     lower, upper = pick(own, swapped(other, 2))
     qkv_grads = [
@@ -443,7 +453,7 @@
         ).astype(full)
         for i in range(3)
     ]
-    out_grad = join_rows(pieces[0][qkv_rows:], pieces[1][qkv_rows:])
+    out_grad = join_rows(*[unfold_piece(piece[:, 3 * inner :]) for piece in pieces])
     up_grad = jnp.where(on_first, up_grads[0], up_grads[1]).astype(low)
     up_grad = lax.all_to_all(up_grad, dp, split_axis=0, concat_axis=1, tiled=True).astype(full)
     down_grad = jnp.where(on_first, down_grads[0], down_grads[1])

time: 884 us -> 892 us (level)
  starting transfers between devices: 105 us -> 129 us
  other arithmetic: 124 us -> 113 us
  waiting for transfers between devices: 148 us -> 157 us
    all_gather x1, blocking collectives: 56.6 us -> 16.2 us  [per_device(): near_gains = lax.all_gather(gains, dp, axis=2, tiled=True)]
    ppermute x22, starting transfers between devices: 30.3 us -> 59.6 us  [swapped(): return lax.ppermute(value, 'section', pairs)]
    all_to_all x0 -> x1, blocking collectives: none -> 29.2 us  [sum_to_sequence(): arrived = lax.all_to_all(blocks, 'pair', split_axis=0, concat_axis=0)]
    unnamed x308 -> x317, local copies, waits for them, and re-layouts: 21.9 us -> 41.6 us
    all_gather x3, waiting for transfers between devices: 0.02 us -> 13 us  [gather(): return lax.all_gather(piece, dp, axis=0, tiled=True)]
    concatenate x2 -> x0, local copies, waits for them, and re-layouts: 9.6 us -> none  [per_device(): jnp.concatenate([query_grad.astype(low), key_grad.astype(low), value_grad...]
  transfers between devices with their start and end apart: 56 -> 55, of which waited for: 19 -> 17; matrix products, arithmetic and copies ran while one was open for 36% -> 34% of each run, Pallas kernels for 0% -> 0%
where the time goes in v4:
time: 892 us; the launch traced here: 885 us
  blocking collectives  233 us (26%)
  waiting for transfers between devices  157 us (18%)
  starting transfers between devices  129 us (14%)
  matrix products  123 us (14%)
  local copies, waits for them, and re-layouts  113 us (13%)
  other arithmetic  113 us (13%)
  between operations  16.5 us (2%)
    ppermute x22, waiting for transfers between devices, swapped(): return lax.ppermute(value, 'section', pairs)  98.3 us
    all_gather x4, blocking collectives, from_sequences(): near = lax.all_gather(rows, 'pair', axis=0, tiled=True)  92.3 us
    all_gather x3, blocking collectives, from_slots(): return lax.all_gather(rows, 'section', axis=0, tiled=True)  75 us
    ppermute x22, starting transfers between devices, swapped(): return lax.ppermute(value, 'section', pairs)  59.6 us
    dot_general x18, matrix products, matmul_nt(): lax.dot_general(left, right, (((1,), (1,)), ((), ())), preferred_element_...  43.5 us
    unnamed x317, local copies, waits for them, and re-layouts  41.6 us
    dot_general x14, matrix products, matmul(): return jnp.dot(left, right, preferred_element_type=full)  39.2 us
    all_to_all x1, blocking collectives, sum_to_sequence(): arrived = lax.all_to_all(blocks, 'pair', split_axis=0, concat_axis=0)  29.2 us
  transfers between devices with their start and end apart: 55, of which 17 were waited for; matrix products, arithmetic and copies ran while one was open for 34% of the time, Pallas kernels for 0%

profile of v4, /device:TPU:0, one launch (start us, length us, event | category | flops | bytes accessed | tf_op | source)
XLA Modules:
  0.0 884.7 jit_solution(2734033130281240062)
XLA Ops:
  8.0 16.2 %all_gather.36 = f32[2,3,384]{1,0,2:T(2,128)S(1)} all-gather(f32[2,3,48]{1,0,2:T(2,128)S(1)} %copy.179), channel_id=1, replica_groups=mesh['section'=4,'pair'=4,'core'=2] {'pair','core'}, dimensions={2}, use_global_device_ids=true | all-gather | bytes 10368 | tf_op jit(solution)/shard_map/all_gather | solution.py:252
  24.4 8.3 all_gather.37
  39.7 17.7 %all_gather.39 = bf16[256,1536]{1,0:T(8,128)(2,1)} all-gather(bf16[64,1536]{1,0:T(8,128)(2,1)S(1)} %constant_dynamic-slice_fusion), channel_id=1, replica_groups=mesh['section'=4,'pair'=4,'core'=2] {'pair'}, dimensions={0}, use_global_device_ids=true | all-gather | bytes 983040 | tf_op jit(solution)/shard_map/all_gather | solution.py:196
  92.7 38.7 %collective-permute-start.7 = (bf16[192,1536]{1,0:T(8,128)(2,1)}, bf16[192,1536]{1,0:T(8,128)(2,1)S(1)}, u32[]{:S(2)}, u32[]{:S(2)}) collective-permute-start(bf16[192,1536]{1,0:T(8,128)(2,1)} %slice.442), channel_id=1, source_target_pairs={{0,16},{8,24},{16,0},{24,8},{1,17},{9,25},{17,1},{25,9},{2,18},{10... | collective-permute-start | bytes 1769480 | tf_op jit(solution)/shard_map/ppermute | solution.py:118
  138.3 7.6 collective-permute-done.7
  153.9 18.6 %collective-permute-done.2 = bf16[1536,384]{1,0:T(8,128)(2,1)S(1)} collective-permute-done((bf16[1536,384]{1,0:T(8,128)(2,1)}, bf16[1536,384]{1,0:T(8,128)(2,1)S(1)}, u32[]{:S(2)}, u32[]{:S(2)}) %collective-permute-start.2) | collective-permute-done | bytes 1179680 | tf_op jit(solution)/shard_map/ppermute | solution.py:118
  200.6 13.0 %all-gather.6.cloned.1.call-done = bf16[1536,384]{1,0:T(8,128)(2,1)} async-done(((bf16[192,384]{1,0:T(8,128)(2,1)}), bf16[1536,384]{1,0:T(8,128)(2,1)}) %all-gather.6.cloned.1.call-update) | async-done | bytes 1179664 | tf_op jit(solution)/shard_map/all_gather | solution.py:262
  234.8 28.7 %all_gather.41 = bf16[256,1536]{1,0:T(8,128)(2,1)S(1)} all-gather(bf16[64,1536]{1,0:T(8,128)(2,1)S(1)} %multiply_convert_fusion.9), channel_id=1, replica_groups=mesh['section'=4,'pair'=4,'core'=2] {'pair'}, dimensions={0}, use_global_device_ids=true | all-gather | bytes 983040 | tf_op jit(solution)/shard_map/all_gather | solution.py:196
  276.7 29.2 %all_to_all.108 = bf16[4,64,1536]{2,1,0:T(8,128)(2,1)S(1)} all-to-all(bf16[4,64,1536]{2,1,0:T(8,128)(2,1)S(1)} %bitcast.308), channel_id=1, replica_groups=mesh['section'=4,'pair'=4,'core'=2] {'pair'}, dimensions={0} | all-to-all | bytes 1572864 | tf_op jit(solution)/shard_map/all_to_all | solution.py:204
  306.5 11.1 %all_gather.43 = bf16[256,1536]{1,0:T(8,128)(2,1)S(1)} all-gather(bf16[64,1536]{1,0:T(8,128)(2,1)S(1)} %multiply_convert_fusion.8), channel_id=1, replica_groups=mesh['section'=4,'pair'=4,'core'=2] {'section'}, dimensions={0}, use_global_device_ids=true | all-gather | bytes 983040 | tf_op jit(solution)/shard_map/all_gather | solution.py:187
  338.4 12.2 %all_to_all.109 = bf16[4,64,1536]{2,1,0:T(8,128)(2,1)S(1)} all-to-all(bf16[4,64,1536]{2,1,0:T(8,128)(2,1)S(1)} %bitcast.280), channel_id=1, replica_groups=mesh['section'=4,'pair'=4,'core'=2] {'section'}, dimensions={0} | all-to-all | bytes 1572864 | tf_op jit(solution)/shard_map/all_to_all | solution.py:183
  351.4 17.5 %all_gather.44 = bf16[256,1536]{1,0:T(8,128)(2,1)S(1)} all-gather(bf16[64,1536]{1,0:T(8,128)(2,1)S(1)} %multiply_convert_fusion.7), channel_id=1, replica_groups=mesh['section'=4,'pair'=4,'core'=2] {'pair'}, dimensions={0}, use_global_device_ids=true | all-gather | bytes 983040 | tf_op jit(solution)/shard_map/all_gather | solution.py:196
  402.1 13.2 %collective-permute-done.17 = bf16[384,1536]{1,0:T(8,128)(2,1)} collective-permute-done((bf16[384,1536]{1,0:T(8,128)(2,1)}, bf16[384,1536]{1,0:T(8,128)(2,1)}, u32[]{:S(2)}, u32[]{:S(2)}) %collective-permute-start.17) | collective-permute-done | bytes 1179680 | tf_op jit(solution)/shard_map/ppermute | solution.py:118
  428.4 11.8 %collective-permute-done.18 = bf16[1536,384]{1,0:T(8,128)(2,1)} collective-permute-done((bf16[1536,384]{1,0:T(8,128)(2,1)}, bf16[1536,384]{1,0:T(8,128)(2,1)}, u32[]{:S(2)}, u32[]{:S(2)}) %collective-permute-start.18) | collective-permute-done | bytes 1179680 | tf_op jit(solution)/shard_map/ppermute | solution.py:118
  454.0 28.0 %all_gather.45 = bf16[256,1536]{1,0:T(8,128)(2,1)S(1)} all-gather(bf16[64,1536]{1,0:T(8,128)(2,1)S(1)} %get-tuple-element.28), channel_id=1, replica_groups=mesh['section'=4,'pair'=4,'core'=2] {'section'}, dimensions={0}, use_global_device_ids=true | all-gather | bytes 983040 | tf_op jit(solution)/shard_map/all_gather | solution.py:187
  542.5 28.3 %all_gather.46 = bf16[256,1536]{1,0:T(8,128)(2,1)S(1)} all-gather(bf16[64,1536]{1,0:T(8,128)(2,1)S(1)} %get-tuple-element.81), channel_id=1, replica_groups=mesh['section'=4,'pair'=4,'core'=2] {'pair'}, dimensions={0}, use_global_device_ids=true | all-gather | bytes 983040 | tf_op jit(solution)/shard_map/all_gather | solution.py:196
  614.2 8.6 collective-permute-done.35
  627.6 19.8 %collective-permute-done.23 = bf16[384,1536]{1,0:T(8,128)(2,1)} collective-permute-done((bf16[384,1536]{1,0:T(8,128)(2,1)}, bf16[384,1536]{1,0:T(8,128)(2,1)}, u32[]{:S(2)}, u32[]{:S(2)}) %collective-permute-start.23) | collective-permute-done | bytes 1179680 | tf_op jit(solution)/shard_map/ppermute | solution.py:118
  654.5 35.8 %all_gather.47 = bf16[256,1536]{1,0:T(8,128)(2,1)S(1)} all-gather(bf16[64,1536]{1,0:T(8,128)(2,1)S(1)} %get-tuple-element.31), channel_id=1, replica_groups=mesh['section'=4,'pair'=4,'core'=2] {'section'}, dimensions={0}, use_global_device_ids=true | all-gather | bytes 983040 | tf_op jit(solution)/shard_map/all_gather | solution.py:187
  733.2 8.2 multiply_reduce_fusion.1
  770.0 9.9 %all-to-all-done.11 = f32[2,3,4,384]{3,0,1,2:T(2,128)S(1)} async-done(((f32[2,3,4,384]{3,0,1,2:T(2,128)}), f32[2,3,4,384]{3,0,1,2:T(2,128)S(1)}, u32[]{:S(2)}, u32[]{:S(2)}) %all-to-all-start.11) | async-done | bytes 36896 | tf_op jit(solution)/shard_map/all_to_all | solution.py:442
  800.2 10.7 %collective-permute-done.28 = bf16[256,1536]{1,0:T(8,128)(2,1)} collective-permute-done((bf16[256,1536]{1,0:T(8,128)(2,1)}, bf16[256,1536]{1,0:T(8,128)(2,1)}, u32[]{:S(2)}, u32[]{:S(2)}) %collective-permute-start.28) | collective-permute-done | bytes 786464 | tf_op jit(solution)/shard_map/ppermute | solution.py:118
  836.7 14.8 %all-to-all-done.13 = bf16[8,192,384]{2,1,0:T(8,128)(2,1)S(1)} async-done(((bf16[8,192,384]{2,1,0:T(8,128)(2,1)}), bf16[8,192,384]{2,1,0:T(8,128)(2,1)S(1)}, u32[]{:S(2)}, u32[]{:S(2)}) %all-to-all-start.13) | async-done | bytes 1179680 | tf_op jit(solution)/shard_map/all_to_all | solution.py:458
  861.0 12.4 %collective-permute-done.34 = bf16[48,1536]{1,0:T(8,128)(2,1)S(1)} collective-permute-done((bf16[48,1536]{1,0:T(8,128)(2,1)S(1)}, bf16[48,1536]{1,0:T(8,128)(2,1)S(1)}, u32[]{:S(2)}, u32[]{:S(2)}) %collective-permute-start.34) | collective-permute-done | bytes 147488 | tf_op jit(solution)/shard_map/ppermute | solution.py:158
  (664 shorter events, 447.7 us)
Async XLA Ops:
  32.7 57.6 %collective-permute-start.6 = (bf16[384,1536]{1,0:T(8,128)(2,1)}, bf16[384,1536]{1,0:T(8,128)(2,1)}, u32[]{:S(2)}, u32[]{:S(2)}) collective-permute-start(bf16[384,1536]{1,0:T(8,128)(2,1)} %bitcast.294), channel_id=1, source_target_pairs={{0,8},{8,0},{16,24},{24,16},{1,9},{9,1},{17,25},{25,17},{2,10},{10... | collective-permute-start | bytes 3538952 | tf_op jit(solution)/shard_map/ppermute | solution.py:118
  34.2 97.3 %collective-permute-start.5 = (bf16[384,1536]{1,0:T(8,128)(2,1)}, bf16[384,1536]{1,0:T(8,128)(2,1)}, u32[]{:S(2)}, u32[]{:S(2)}) collective-permute-start(bf16[384,1536]{1,0:T(8,128)(2,1)} %bitcast.295), channel_id=1, source_target_pairs={{0,16},{8,24},{16,0},{24,8},{1,17},{9,25},{17,1},{25,9},{2,18},{10... | collective-permute-start | bytes 3538952 | tf_op jit(solution)/shard_map/ppermute | solution.py:118
  37.3 34.2 %collective-permute-start = (bf16[192,1152]{1,0:T(8,128)(2,1)}, bf16[192,1152]{1,0:T(8,128)(2,1)}, u32[]{:S(2)}, u32[]{:S(2)}) collective-permute-start(bf16[192,1152]{1,0:T(8,128)(2,1)} %pad_maximum_fusion.20), channel_id=1, source_target_pairs={{0,16},{8,24},{16,0},{24,8},{1,17},{9,25},{17,1},{25,9},{2,18},{10... | collective-permute-start | bytes 1327112 | tf_op jit(solution)/shard_map/ppermute | solution.py:118
  57.5 31.6 %collective-permute-start.9 = (bf16[256,1536]{1,0:T(8,128)(2,1)}, bf16[256,1536]{1,0:T(8,128)(2,1)}, u32[]{:S(2)}, u32[]{:S(2)}) collective-permute-start(bf16[256,1536]{1,0:T(8,128)(2,1)} %all_gather.39), channel_id=1, source_target_pairs={{0,1},{1,0},{2,3},{3,2},{4,5},{5,4},{6,7},{7,6},{8,9},{9,8},{10,11... | collective-permute-start | bytes 2359304 | tf_op jit(solution)/shard_map/ppermute | solution.py:121
  60.2 74.4 %all-to-all-start = ((bf16[192,8,384]{2,0,1:T(8,128)(2,1)}), bf16[192,8,384]{2,0,1:T(8,128)(2,1)}, u32[]{:S(2)}, u32[]{:S(2)}) async-start(bf16[192,8,384]{2,0,1:T(8,128)(2,1)} %bitcast.254), calls=%async_computation | async-start | bytes 2359296 | tf_op jit(solution)/shard_map/all_to_all | solution.py:278
  64.7 113.1 %all-gather.4.cloned.1.call-start = ((), (), s32[]{:S(2)}) async-start(), calls=%async_computation.16 | async-start | bytes 3981312 | tf_op jit(solution)/shard_map/all_gather | solution.py:262
  76.4 137.2 %all-gather.6.cloned.1.call-start = ((), (), s32[]{:S(2)}) async-start(), calls=%async_computation.17 | async-start | bytes 1327104 | tf_op jit(solution)/shard_map/all_gather | solution.py:262
  92.7 53.2 %collective-permute-start.7 = (bf16[192,1536]{1,0:T(8,128)(2,1)}, bf16[192,1536]{1,0:T(8,128)(2,1)S(1)}, u32[]{:S(2)}, u32[]{:S(2)}) collective-permute-start(bf16[192,1536]{1,0:T(8,128)(2,1)} %slice.442), channel_id=1, source_target_pairs={{0,16},{8,24},{16,0},{24,8},{1,17},{9,25},{17,1},{25,9},{2,18},{10... | collective-permute-start | bytes 1769480 | tf_op jit(solution)/shard_map/ppermute | solution.py:118
  134.6 37.9 %collective-permute-start.2 = (bf16[1536,384]{1,0:T(8,128)(2,1)}, bf16[1536,384]{1,0:T(8,128)(2,1)S(1)}, u32[]{:S(2)}, u32[]{:S(2)}) collective-permute-start(bf16[1536,384]{1,0:T(8,128)(2,1)} %bitcast.18), channel_id=1, source_target_pairs={{0,8},{8,0},{16,24},{24,16},{1,9},{9,1},{17,25},{25,17},{2,10},{10... | collective-permute-start | bytes 3538952 | tf_op jit(solution)/shard_map/ppermute | solution.py:118
  135.4 39.3 %collective-permute-start.1 = (bf16[1536,384]{1,0:T(8,128)(2,1)}, bf16[1536,384]{1,0:T(8,128)(2,1)S(1)}, u32[]{:S(2)}, u32[]{:S(2)}) collective-permute-start(bf16[1536,384]{1,0:T(8,128)(2,1)} %bitcast.18), channel_id=1, source_target_pairs={{0,16},{8,24},{16,0},{24,8},{1,17},{9,25},{17,1},{25,9},{2,18},{10... | collective-permute-start | bytes 3538952 | tf_op jit(solution)/shard_map/ppermute | solution.py:118
  174.4 50.6 %collective-permute-start.3 = (bf16[768,384]{1,0:T(8,128)(2,1)}, bf16[768,384]{1,0:T(8,128)(2,1)}, u32[]{:S(2)}, u32[]{:S(2)}) collective-permute-start(bf16[768,384]{1,0:T(8,128)(2,1)} %slice.440), channel_id=1, source_target_pairs={{0,16},{8,24},{16,0},{24,8},{1,17},{9,25},{17,1},{25,9},{2,18},{10... | collective-permute-start | bytes 1769480 | tf_op jit(solution)/shard_map/ppermute | solution.py:118
  176.6 49.6 %collective-permute-start.4 = (bf16[768,384]{1,0:T(8,128)(2,1)}, bf16[768,384]{1,0:T(8,128)(2,1)}, u32[]{:S(2)}, u32[]{:S(2)}) collective-permute-start(bf16[768,384]{1,0:T(8,128)(2,1)} %slice.441), channel_id=1, source_target_pairs={{0,8},{8,0},{16,24},{24,16},{1,9},{9,1},{17,25},{25,17},{2,10},{10... | collective-permute-start | bytes 1769480 | tf_op jit(solution)/shard_map/ppermute | solution.py:118
  221.7 96.0 %all-gather.8.cloned.1.call-start = ((), (), s32[]{:S(2)}) async-start(), calls=%async_computation.18 | async-start | bytes 5308416 | tf_op jit(solution)/shard_map/all_gather | solution.py:262
  386.2 29.1 %collective-permute-start.17 = (bf16[384,1536]{1,0:T(8,128)(2,1)}, bf16[384,1536]{1,0:T(8,128)(2,1)}, u32[]{:S(2)}, u32[]{:S(2)}) collective-permute-start(bf16[384,1536]{1,0:T(8,128)(2,1)} %slice.614), channel_id=1, source_target_pairs={{0,8},{8,0},{16,24},{24,16},{1,9},{9,1},{17,25},{25,17},{2,10},{10... | collective-permute-start | bytes 3538952 | tf_op jit(solution)/shard_map/ppermute | solution.py:118
  392.2 48.0 %collective-permute-start.18 = (bf16[1536,384]{1,0:T(8,128)(2,1)}, bf16[1536,384]{1,0:T(8,128)(2,1)}, u32[]{:S(2)}, u32[]{:S(2)}) collective-permute-start(bf16[1536,384]{1,0:T(8,128)(2,1)} %slice.613), channel_id=1, source_target_pairs={{0,8},{8,0},{16,24},{24,16},{1,9},{9,1},{17,25},{25,17},{2,10},{10... | collective-permute-start | bytes 3538952 | tf_op jit(solution)/shard_map/ppermute | solution.py:118
  419.6 99.9 %collective-permute-start.19 = (bf16[384,1536]{1,0:T(8,128)(2,1)}, bf16[384,1536]{1,0:T(8,128)(2,1)}, u32[]{:S(2)}, u32[]{:S(2)}) collective-permute-start(bf16[384,1536]{1,0:T(8,128)(2,1)} %get-tuple-element.83), channel_id=1, source_target_pairs={{0,16},{8,24},{1,17},{9,25},{2,18},{10,26},{3,19},{11,27},{4,20},{... | collective-permute-start | bytes 3538952 | tf_op jit(solution)/shard_map/ppermute | solution.py:124
  443.6 138.9 %collective-permute-start.21 = (bf16[1536,384]{1,0:T(8,128)(2,1)}, bf16[1536,384]{1,0:T(8,128)(2,1)}, u32[]{:S(2)}, u32[]{:S(2)}) collective-permute-start(bf16[1536,384]{1,0:T(8,128)(2,1)} %get-tuple-element.79), channel_id=1, source_target_pairs={{0,16},{8,24},{1,17},{9,25},{2,18},{10,26},{3,19},{11,27},{4,20},{... | collective-permute-start | bytes 3538952 | tf_op jit(solution)/shard_map/ppermute | solution.py:124
  526.7 328.0 %reduce-scatter.9.cloned.1.call-start = ((), (), s32[]{:S(2)}) async-start(), calls=%async_computation.20 | async-start | bytes 5308416 | tf_op jit(solution)/shard_map/reduce_scatter | solution.py:353
  598.1 49.4 %collective-permute-start.23 = (bf16[384,1536]{1,0:T(8,128)(2,1)}, bf16[384,1536]{1,0:T(8,128)(2,1)}, u32[]{:S(2)}, u32[]{:S(2)}) collective-permute-start(bf16[384,1536]{1,0:T(8,128)(2,1)} %slice.612), channel_id=1, source_target_pairs={{0,8},{8,0},{16,24},{24,16},{1,9},{9,1},{17,25},{25,17},{2,10},{10... | collective-permute-start | bytes 3538952 | tf_op jit(solution)/shard_map/ppermute | solution.py:118
  610.1 43.0 %all-to-all-start.8 = ((bf16[4,64,1536]{2,1,0:T(8,128)(2,1)}), bf16[4,64,1536]{2,1,0:T(8,128)(2,1)S(1)}, u32[]{:S(2)}, u32[]{:S(2)}) async-start(bf16[4,64,1536]{2,1,0:T(8,128)(2,1)} %bitcast.45), calls=%async_computation.8 | async-start | bytes 1572864 | tf_op jit(solution)/shard_map/all_to_all | solution.py:204
  614.2 241.4 %reduce-scatter.7.cloned.1.call-start = ((), (), s32[]{:S(2)}) async-start(), calls=%async_computation.19 | async-start | bytes 5308416 | tf_op jit(solution)/shard_map/reduce_scatter | solution.py:353
  626.2 170.4 %collective-permute-start.36 = (bf16[1536,384]{1,0:T(8,128)(2,1)}, bf16[1536,384]{1,0:T(8,128)(2,1)}, u32[]{:S(2)}, u32[]{:S(2)}) collective-permute-start(bf16[1536,384]{1,0:T(8,128)(2,1)} %fusion.43), channel_id=1, source_target_pairs={{16,0},{24,8},{17,1},{25,9},{18,2},{26,10},{19,3},{27,11},{20,4},{... | collective-permute-start | bytes 3538952 | tf_op jit(solution)/shard_map/ppermute | solution.py:127
  651.7 170.5 %collective-permute-start.37 = (bf16[384,1536]{1,0:T(8,128)(2,1)}, bf16[384,1536]{1,0:T(8,128)(2,1)}, u32[]{:S(2)}, u32[]{:S(2)}) collective-permute-start(bf16[384,1536]{1,0:T(8,128)(2,1)} %get-tuple-element.74), channel_id=1, source_target_pairs={{16,0},{24,8},{17,1},{25,9},{18,2},{26,10},{19,3},{27,11},{20,4},{... | collective-permute-start | bytes 3538952 | tf_op jit(solution)/shard_map/ppermute | solution.py:127
  817.2 34.4 %all-to-all-start.13 = ((bf16[8,192,384]{2,1,0:T(8,128)(2,1)}), bf16[8,192,384]{2,1,0:T(8,128)(2,1)S(1)}, u32[]{:S(2)}, u32[]{:S(2)}) async-start(bf16[8,192,384]{2,1,0:T(8,128)(2,1)} %bitcast.87), calls=%async_computation.13 | async-start | bytes 2359296 | tf_op jit(solution)/shard_map/all_to_all | solution.py:458
  (184 other events, 1681.2 us)
Sparse Core Ops, SparseCore 0:
  76.5 54.0 all-gather.3
  191.1 22.3 all-gather.5
  227.5 66.4 all-gather.7
  538.8 65.4 reduce-scatter.8
  728.1 54.3 reduce-scatter.6

commit v5 on v4

--- a/solution.py
+++ b/solution.py
@@ -212,32 +212,26 @@
         lower = swapped(ahead[half:], 1)
         return rows, side, ahead, jnp.concatenate([upper, lower], axis=0)
 
-    def for_layers(rows, axis):
-        own, side, ahead, across = by_distance(rows)
-        near = pick(own, ahead)
-        far = pick(side, across)
-        return [jnp.concatenate([near[i], far[i]], axis=axis) for i in range(LAYERS)]
-
-    def collect_side(own, other):
-        return own + swapped(other.astype(low), 1).astype(full)
-
-    def collect_ahead(total, layer):
-        move = to_second if layer else to_first
-        return total + move(total.astype(low)).astype(full)
-
-    def block_of(blocks, mask):
-        return lax.dynamic_index_in_dim(blocks, section ^ mask, 0, keepdims=False)
-
-    def sum_over_sections(partial):
-        blocks = partial.reshape(section_count, -1, feature_width)
-        half = blocks.shape[1] // 2
-        own, side, ahead, across = [block_of(blocks, mask) for mask in range(4)]
+    def sum_by_distance(own, side, ahead, across):
+        half = own.shape[0] // 2
         across = across.astype(low)
         upper = swapped(across[:half], 2).astype(full)
         lower = swapped(across[half:], 1).astype(full)
         side = jnp.concatenate([side[:half] + upper, side[half:]], axis=0).astype(low)
         ahead = jnp.concatenate([ahead[:half], ahead[half:] + lower], axis=0).astype(low)
         return own + swapped(side, 1).astype(full) + swapped(ahead, 2).astype(full)
+
+    def share_first(lower, upper):
+        return jnp.where(on_first, lower, to_second(upper))
+
+    def sum_over_sections(partial):
+        blocks = partial.reshape(section_count, -1, feature_width)
+        return sum_by_distance(
+            *[
+                lax.dynamic_index_in_dim(blocks, section ^ mask, 0, keepdims=False)
+                for mask in range(4)
+            ]
+        )
 
     def gather_sections(rows):
         by_mask = by_distance(rows)
@@ -249,34 +243,79 @@
             ordered.append(chosen)
         return jnp.concatenate(ordered, axis=0)
 
-    near_gains = lax.all_gather(gains, dp, axis=2, tiled=True)
-    all_gains = lax.all_gather(near_gains, "section", axis=2, tiled=True)
+    def column_parts(weight, block):
+        rows, width = weight.shape
+        split = weight.reshape(rows, width // (2 * block), 2, block)
+        return split[:, :, 0].reshape(rows, -1), split[:, :, 1].reshape(rows, -1)
+
+    def interleave(even, odd, block):
+        rows, width = even.shape
+        parts = [part.reshape(rows, width // block, 1, block) for part in (even, odd)]
+        return jnp.concatenate(parts, axis=2).reshape(rows, 2 * width)
+
     halves = [pick(weight[0, :, :inner], weight[0, :, inner:]) for weight in (w_query, w_key, w_value)]
     own_heads = jnp.concatenate([half[0] for half in halves], axis=1)
     other_heads = swapped(jnp.concatenate([half[1] for half in halves], axis=1), 2)
     qkv_pieces = pick(own_heads, other_heads)
-    down_in, up_in = after((w_down[0], w_up[0]), all_gains)
-    out_pieces = exchange_rows(after(w_out[0], all_gains))
+    near_gains = lax.all_gather(after(gains, other_heads), dp, axis=2, tiled=True)
+    all_gains = lax.all_gather(near_gains, "section", axis=2, tiled=True)
+    out_pieces = exchange_rows(after(w_out[0], other_heads))
 
     def gather(piece):
         return lax.all_gather(piece, dp, axis=0, tiled=True)
 
-    qkv_first = gather(after(qkv_pieces[0], all_gains))
-    out_first = gather(after(fold(out_pieces[0]), qkv_first))
+    half_hidden = w_down.shape[1] // 2
+    half_depth = w_up.shape[1] // 2
+    down_shared = by_distance(
+        share_first(*[after(half, other_heads) for half in (w_down[0, :half_hidden], w_down[0, half_hidden:])])
+    )
+    up_turned = lax.all_to_all(
+        after(share_first(w_up[0, :half_depth], w_up[0, half_depth:]), (all_gains, down_shared[3])),
+        dp,
+        split_axis=1,
+        concat_axis=0,
+        tiled=True,
+    )
+    up_shared = by_distance(up_turned)
+
+    def in_depth(near, far):
+        parts = [part.reshape(dp_count, 1, half_depth, -1) for part in pick(near, far)]
+        return jnp.concatenate(parts, axis=1).reshape(feature_width, -1)
+
+    down_first = jnp.concatenate(
+        pick(down_shared[0], down_shared[2]) + pick(down_shared[1], down_shared[3]), axis=0
+    )
+    up_first = jnp.concatenate(
+        [in_depth(up_shared[0], up_shared[2]), in_depth(up_shared[1], up_shared[3])], axis=1
+    )
+
+    qkv_first = gather(qkv_pieces[0])
+    out_first = unfold(gather(after(fold(out_pieces[0]), qkv_pieces[0])))
     stacked = gather(
-        after(jnp.concatenate([qkv_pieces[1], fold(out_pieces[1])], axis=1), out_first)
-    )
-    out_first = unfold(out_first)
+        jnp.concatenate([qkv_pieces[1], fold(out_pieces[1])], axis=1)
+    )
+    up_even, up_odd = column_parts(w_up[0], half_hidden)
+    up_piece, down_piece = after(
+        (up_even, w_down[0, :half_hidden]), (up_turned, down_shared[3])
+    )
+    ffn_piece = jnp.concatenate(
+        [
+            jnp.where(on_first, to_first(up_piece), up_odd),
+            jnp.where(on_first, to_first(down_piece), w_down[0, half_hidden:]),
+        ],
+        axis=1,
+    )
+    ffn_second = gather(ffn_piece)
+    hidden_width = up_even.shape[1]
     qkv_second = stacked[:, : 3 * inner]
     out_second = unfold(stacked[:, 3 * inner :])
+    up_w = (up_first, ffn_second[:, :hidden_width])
+    down_w = (down_first, ffn_second[:, hidden_width:])
     qkv_w = (qkv_first, qkv_second)
     out_w = (out_first, out_second)
     query_w = [weight[:, :inner] for weight in qkv_w]
     key_w = [weight[:, inner : 2 * inner] for weight in qkv_w]
     value_w = [weight[:, 2 * inner :] for weight in qkv_w]
-    down_w = for_layers(down_in, 0)
-    up_turned = lax.all_to_all(up_in, dp, split_axis=1, concat_axis=0, tiled=True)
-    up_w = for_layers(up_turned, 1)
 
     image_hot = segment_ids[:, :, None] == jnp.arange(slot_count, dtype=jnp.int32)[None, None, :]
     media_slot = jnp.sum(jnp.where(image_hot, slot_map[:, None, :], 0), axis=2) - (
@@ -300,9 +339,8 @@
 
     saved = []
     current = lax.dynamic_slice_in_dim(latents, section * slot_rows, slot_rows, 0).astype(full)
-    grad_low = lax.dynamic_slice_in_dim(cotangent, section * slot_rows, slot_rows, 0)
-    grad_rows = grad_low.astype(full)
-    grad_low = from_sequences(grad_low)
+    grad_rows = lax.dynamic_slice_in_dim(cotangent, section * slot_rows, slot_rows, 0).astype(full)
+    grad_low = cotangent
     for layer in range(LAYERS):
         unit_in, inverse_in = unit_rows(current)
         if layer == 0:
@@ -324,13 +362,17 @@
         )
         attended_low = attended.reshape(-1, inner).astype(low)
         if layer == 0:
-            attended_low = after(attended_low, (up_w, down_w, grad_low))
+            attended_low = after(attended_low, up_turned)
         middle = current + sum_to_slots(matmul(attended_low, out_w[layer]))
         unit_mid, inverse_mid = unit_rows(middle)
-        ffn_low = from_sequences((unit_mid * all_gains[layer, 2]).astype(low))
+        ffn_low = (unit_mid * all_gains[layer, 2]).astype(low)
+        ffn_low = from_slots(ffn_low) if layer else from_sequences(ffn_low)
         hidden_pre = matmul(ffn_low, up_w[layer])
         active_low = gelu_exact(hidden_pre).astype(low)
-        current = middle + sum_to_sequence(active_low, down_w[layer], matmul)
+        if layer:
+            current = middle + sum_to_slots(matmul(active_low, down_w[layer]))
+        else:
+            current = middle + sum_to_sequence(active_low, down_w[layer], matmul)
         saved.append(
             (
                 unit_in,
@@ -355,8 +397,6 @@
     gain_rows = [None] * LAYERS
     media_scaled = None
     pieces = [None] * LAYERS
-    up_grads = [None] * LAYERS
-    down_grads = [None] * LAYERS
     for layer in (1, 0):
         (
             unit_in,
@@ -375,17 +415,34 @@
         ) = saved[layer]
         grad_active = matmul_nt(grad_low, down_w[layer])
         grad_hidden = jax.vjp(gelu_exact, hidden_pre)[1](grad_active)[0].astype(low)
-        ffn_grad = sum_to_sequence(grad_hidden, up_w[layer], matmul_nt)
         down_grad = matmul_tn(active_low, grad_low)
         up_grad = matmul_tn(ffn_low, grad_hidden)
-        middle_of = down_grad.shape[0] // 2
-        down_side = collect_side(down_grad[:middle_of], down_grad[middle_of:])
-        up_side = collect_side(up_grad[:, :middle_of], up_grad[:, middle_of:])
+        if layer:
+            ffn_piece = scatter(
+                jnp.concatenate([up_grad.astype(low), down_grad.astype(low)], axis=1)
+            )
+            ffn_grad = sum_to_slots(matmul_nt(grad_hidden, up_w[layer]))
+        else:
+            ffn_grad = sum_to_sequence(grad_hidden, up_w[layer], matmul_nt)
+            blocks = down_grad.reshape(2, 2, half_hidden, feature_width)
+            own, ahead = pick(blocks[0, 0], blocks[0, 1])
+            side, across = pick(blocks[1, 0], blocks[1, 1])
+            down_half = sum_by_distance(own, side, ahead, across).astype(low)
+            width = up_grad.shape[1] // 2
+            blocks = up_grad.reshape(dp_count, 2, half_depth, 2 * width)
+            blocks = [blocks[:, i].reshape(-1, 2 * width) for i in range(2)]
+            own, ahead = pick(blocks[0][:, :width], blocks[1][:, :width])
+            side, across = pick(blocks[0][:, width:], blocks[1][:, width:])
+            up_half = sum_by_distance(own, side, ahead, across).astype(low)
+            up_half = lax.all_to_all(up_half, dp, split_axis=0, concat_axis=1, tiled=True)
         gain_ffn_grad = jnp.sum(ffn_grad * unit_mid, axis=0)
         grad_middle = grad_rows + norm_back(
             unit_mid, inverse_mid, ffn_grad * all_gains[layer, 2]
         )
-        middle_low = from_slots(after(grad_middle.astype(low), down_side))
+        middle_low = grad_middle.astype(low)
+        if layer == 0:
+            middle_low = after(middle_low, ffn_piece)
+        middle_low = from_slots(middle_low)
         grad_heads = split_heads(matmul_nt(middle_low, out_w[layer]).astype(low))
         out_grad = matmul_tn(attended_low, middle_low)
         grad_query, grad_key, grad_value = attend_backward(
@@ -399,10 +456,6 @@
             + matmul_nt(grad_key[seq_rows:], key_w[layer])
             + matmul_nt(grad_value[seq_rows:], value_w[layer])
         )
-        down_grads[layer] = collect_ahead(down_side, layer)
-        up_grads[layer] = collect_ahead(up_side, layer)
-        if layer > 0:
-            latent_part = after(latent_part, (up_side, down_grads[layer]))
         latent_grad_rows = sum_to_slots(latent_part)
         gain_latent_grad = jnp.sum(latent_grad_rows * unit_in, axis=0)
         grad_rows = grad_middle + norm_back(
@@ -420,7 +473,6 @@
         )
         if layer > 0:
             grad_low = from_sequences(grad_rows.astype(low))
-            grad_low = after(grad_low, up_grads[layer])
         media_part = matmul_nt(grad_key[:seq_rows], key_w[layer]) + matmul_nt(
             grad_value[:seq_rows], value_w[layer]
         )
@@ -454,9 +506,13 @@
         for i in range(3)
     ]
     out_grad = join_rows(*[unfold_piece(piece[:, 3 * inner :]) for piece in pieces])
-    up_grad = jnp.where(on_first, up_grads[0], up_grads[1]).astype(low)
-    up_grad = lax.all_to_all(up_grad, dp, split_axis=0, concat_axis=1, tiled=True).astype(full)
-    down_grad = jnp.where(on_first, down_grads[0], down_grads[1])
+    back = to_second(ffn_piece)
+    up_second_grad = interleave(back[:, :hidden_width], ffn_piece[:, :hidden_width], half_hidden)
+    down_second_grad = jnp.concatenate([back[:, hidden_width:], ffn_piece[:, hidden_width:]], axis=0)
+    up_first_grad = jnp.concatenate([up_half, to_first(up_half)], axis=0)
+    down_first_grad = jnp.concatenate([down_half, to_first(down_half)], axis=0)
+    up_grad = jnp.where(on_first, up_first_grad, up_second_grad).astype(full)
+    down_grad = jnp.where(on_first, down_first_grad, down_second_grad).astype(full)
     return (
         latents_out,
         latent_grad,

time: 892 us -> 887 us (level)
  blocking collectives: 233 us -> 150 us
  waiting for transfers between devices: 157 us -> 186 us
  local copies, waits for them, and re-layouts: 113 us -> 140 us
  matrix products: 123 us -> 140 us
    ppermute x22 -> x26, waiting for transfers between devices: 98.3 us -> 44.2 us  [swapped(): return lax.ppermute(value, 'section', pairs)]
    all_gather x4 -> x2, blocking collectives: 92.3 us -> 51.2 us  [from_sequences(): near = lax.all_gather(rows, 'pair', axis=0, tiled=True)]
    all_to_all x2, waiting for transfers between devices: 14.8 us -> 45.9 us  [the longest x1 27.9 us: per_device(): lax.all_to_all(after(share_first(w_up[0, :half_depth], w_up[0, half_depth...]
    all_to_all x1 -> x0, blocking collectives: 29.2 us -> none  [sum_to_sequence(): arrived = lax.all_to_all(blocks, 'pair', split_axis=0, concat_axis=0)]
    concatenate x3 -> x11, other arithmetic: 3.3 us -> 25.2 us  [the longest x1 12.1 us: per_device(): jnp.concatenate([up_grad.astype(low), down_grad.astype(low)], axis=1)]
    ppermute x22 -> x26, starting transfers between devices: 59.6 us -> 38.4 us  [swapped(): return lax.ppermute(value, 'section', pairs)]
    ppermute x2 -> x4, waiting for transfers between devices: 0.01 us -> 17.1 us  [to_first(): return lax.ppermute(value, 'section', [(2, 0), (3, 1)])]
    all_to_all x1, waiting for transfers between devices: 9.9 us -> 25.3 us  [per_device(): lax.all_to_all(gain_parts, 'section', split_axis=2, concat_axis=2)]
  transfers between devices with their start and end apart: 55 -> 61, of which waited for: 17 -> 26; matrix products, arithmetic and copies ran while one was open for 34% -> 37% of each run, Pallas kernels for 0% -> 0%
where the time goes in v5:
time: 887 us; the launch traced here: 875 us
  waiting for transfers between devices  186 us (21%)
  blocking collectives  150 us (17%)
  local copies, waits for them, and re-layouts  140 us (16%)
  matrix products  140 us (16%)
  starting transfers between devices  124 us (14%)
  other arithmetic  118 us (13%)
  between operations  17 us (2%)
    all_gather x4, blocking collectives, from_slots(): return lax.all_gather(rows, 'section', axis=0, tiled=True)  62.4 us
    dot_general x17, matrix products, matmul_nt(): lax.dot_general(left, right, (((1,), (1,)), ((), ())), preferred_element_...  51.3 us
    all_gather x2, blocking collectives, from_sequences(): near = lax.all_gather(rows, 'pair', axis=0, tiled=True)  51.2 us
    unnamed x311, local copies, waits for them, and re-layouts  50.7 us
    ppermute x26, waiting for transfers between devices, swapped(): return lax.ppermute(value, 'section', pairs)  44.2 us
    dot_general x13, matrix products, matmul(): return jnp.dot(left, right, preferred_element_type=full)  43.2 us
    ppermute x26, starting transfers between devices, swapped(): return lax.ppermute(value, 'section', pairs)  38.4 us
    all_to_all x1, waiting for transfers between devices, per_device(): lax.all_to_all(after(share_first(w_up[0, :half_depth], w_up[0, half_depth...  27.9 us
  transfers between devices with their start and end apart: 61, of which 26 were waited for; matrix products, arithmetic and copies ran while one was open for 37% of the time, Pallas kernels for 0%

profile of v5, /device:TPU:0, one launch (start us, length us, event | category | flops | bytes accessed | tf_op | source)
XLA Modules:
  0.0 874.6 jit_solution(13845872239109076214)
XLA Ops:
  12.6 10.2 %collective-permute-done = bf16[192,1152]{1,0:T(8,128)(2,1)S(1)} collective-permute-done((bf16[192,1152]{1,0:T(8,128)(2,1)S(1)}, bf16[192,1152]{1,0:T(8,128)(2,1)S(1)}, u32[]{:S(2)}, u32[]{:S(2)}) %collective-permute-start) | collective-permute-done | bytes 442400 | tf_op jit(solution)/shard_map/ppermute | solution.py:118
  31.9 10.8 %collective-permute-start.1 = (bf16[96,3072]{1,0:T(8,128)(2,1)}, bf16[96,3072]{1,0:T(8,128)(2,1)}, u32[]{:S(2)}, u32[]{:S(2)}) collective-permute-start(bf16[96,3072]{1,0:T(8,128)(2,1)} %slice_bitcast_fusion.6), channel_id=1, source_target_pairs={{0,16},{8,24},{1,17},{9,25},{2,18},{10,26},{3,19},{11,27},{4,20},{... | collective-permute-start | bytes 1769480 | tf_op jit(solution)/shard_map/ppermute | solution.py:124
  57.1 7.5 slice_reduce_fusion
  86.7 16.4 %all_gather.36 = f32[2,3,384]{1,0,2:T(2,128)S(1)} all-gather(f32[2,3,48]{1,0,2:T(2,128)} %copy.274), channel_id=1, replica_groups=mesh['section'=4,'pair'=4,'core'=2] {'pair','core'}, dimensions={2}, use_global_device_ids=true | all-gather | bytes 10368 | tf_op jit(solution)/shard_map/all_gather | solution.py:260
  103.2 7.5 all_gather.37
  132.0 27.9 %all-to-all-done = bf16[96,8,384]{2,0,1:T(8,128)(2,1)} async-done(((bf16[96,8,384]{2,0,1:T(8,128)(2,1)}), bf16[96,8,384]{2,0,1:T(8,128)(2,1)}, u32[]{:S(2)}, u32[]{:S(2)}) %all-to-all-start) | async-done | bytes 589856 | tf_op jit(solution)/shard_map/all_to_all | solution.py:272
  178.3 12.6 %collective-permute-done.15 = bf16[192,1536]{1,0:T(8,128)(2,1)S(1)} collective-permute-done((bf16[192,1536]{1,0:T(8,128)(2,1)S(1)}, bf16[192,1536]{1,0:T(8,128)(2,1)S(1)}, u32[]{:S(2)}, u32[]{:S(2)}) %collective-permute-start.15) | collective-permute-done | bytes 589856 | tf_op jit(solution)/shard_map/ppermute | solution.py:127
  235.5 30.3 %all_gather.40 = bf16[256,1536]{1,0:T(8,128)(2,1)S(1)} all-gather(bf16[64,1536]{1,0:T(8,128)(2,1)S(1)} %multiply_convert_fusion.9), channel_id=1, replica_groups=mesh['section'=4,'pair'=4,'core'=2] {'pair'}, dimensions={0}, use_global_device_ids=true | all-gather | bytes 983040 | tf_op jit(solution)/shard_map/all_gather | solution.py:196
  295.0 12.9 %all-to-all-done.2 = bf16[4,64,1536]{2,1,0:T(8,128)(2,1)} async-done(((bf16[4,64,1536]{2,1,0:T(8,128)(2,1)}), bf16[4,64,1536]{2,1,0:T(8,128)(2,1)}, u32[]{:S(2)}, u32[]{:S(2)}) %all-to-all-start.2) | async-done | bytes 786464 | tf_op jit(solution)/shard_map/all_to_all | solution.py:204
  309.7 11.9 %all_gather.42 = bf16[256,1536]{1,0:T(8,128)(2,1)S(1)} all-gather(bf16[64,1536]{1,0:T(8,128)(2,1)S(1)} %multiply_convert_fusion.8), channel_id=1, replica_groups=mesh['section'=4,'pair'=4,'core'=2] {'section'}, dimensions={0}, use_global_device_ids=true | all-gather | bytes 983040 | tf_op jit(solution)/shard_map/all_gather | solution.py:187
  337.0 13.0 %all_to_all.114 = bf16[4,64,1536]{2,1,0:T(8,128)(2,1)S(1)} all-to-all(bf16[4,64,1536]{2,1,0:T(8,128)(2,1)S(1)} %bitcast.353), channel_id=1, replica_groups=mesh['section'=4,'pair'=4,'core'=2] {'section'}, dimensions={0} | all-to-all | bytes 1572864 | tf_op jit(solution)/shard_map/all_to_all | solution.py:183
  350.8 11.5 %all_gather.43 = bf16[256,1536]{1,0:T(8,128)(2,1)S(1)} all-gather(bf16[64,1536]{1,0:T(8,128)(2,1)S(1)} %multiply_convert_fusion.7), channel_id=1, replica_groups=mesh['section'=4,'pair'=4,'core'=2] {'section'}, dimensions={0}, use_global_device_ids=true | all-gather | bytes 983040 | tf_op jit(solution)/shard_map/all_gather | solution.py:187
  362.4 7.8 multiply_convert_fusion.5
  405.9 11.4 %all_gather.45 = bf16[256,1536]{1,0:T(8,128)(2,1)S(1)} all-gather(bf16[64,1536]{1,0:T(8,128)(2,1)S(1)} %get-tuple-element.89), channel_id=1, replica_groups=mesh['section'=4,'pair'=4,'core'=2] {'section'}, dimensions={0}, use_global_device_ids=true | all-gather | bytes 983040 | tf_op jit(solution)/shard_map/all_gather | solution.py:187
  455.3 12.1 %pad_maximum_fusion = bf16[1536,3072]{0,1:T(8,128)(2,1)} fusion(bf16[1536,1536]{0,1:T(8,128)(2,1)S(1)} %convolution_convert_fusion, bf16[1536,1536]{0,1:T(8,128)(2,1)S(1)} %convolution_convert_fusion.1), kind=kLoop, calls=%fused_computation | loop fusion | flops 18874368 | bytes 18874368 | tf_op jit(solution)/shard_map/concatenate | solution.py:422
  467.4 12.7 %copy.322 = bf16[1536,3072]{1,0:T(8,128)(2,1)} copy(bf16[1536,3072]{0,1:T(8,128)(2,1)} %pad_maximum_fusion) | data formatting | bytes 18874368
  503.9 20.9 %all_gather.46 = bf16[256,1536]{1,0:T(8,128)(2,1)} all-gather(bf16[64,1536]{1,0:T(8,128)(2,1)S(1)} %get-tuple-element.87), channel_id=1, replica_groups=mesh['section'=4,'pair'=4,'core'=2] {'pair'}, dimensions={0}, use_global_device_ids=true | all-gather | bytes 983040 | tf_op jit(solution)/shard_map/all_gather | solution.py:196
  565.0 9.4 %collective-permute-done.33 = bf16[768,384]{1,0:T(8,128)(2,1)S(1)} collective-permute-done((bf16[768,384]{1,0:T(8,128)(2,1)S(1)}, bf16[768,384]{1,0:T(8,128)(2,1)S(1)}, u32[]{:S(2)}, u32[]{:S(2)}) %collective-permute-start.33) | collective-permute-done | bytes 589856 | tf_op jit(solution)/shard_map/ppermute | solution.py:118
  590.9 18.0 %all-to-all-done.13 = bf16[8,96,384]{2,1,0:T(8,128)(2,1)S(1)} async-done(((bf16[8,96,384]{2,1,0:T(8,128)(2,1)}), bf16[8,96,384]{2,1,0:T(8,128)(2,1)S(1)}, u32[]{:S(2)}, u32[]{:S(2)}) %all-to-all-start.13) | async-done | bytes 589856 | tf_op jit(solution)/shard_map/all_to_all | solution.py:437
  616.1 7.8 convolution_add_fusion.1
  643.7 27.7 %all_gather.47 = bf16[256,1536]{1,0:T(8,128)(2,1)S(1)} all-gather(bf16[64,1536]{1,0:T(8,128)(2,1)S(1)} %get-tuple-element.29), channel_id=1, replica_groups=mesh['section'=4,'pair'=4,'core'=2] {'section'}, dimensions={0}, use_global_device_ids=true | all-gather | bytes 983040 | tf_op jit(solution)/shard_map/all_gather | solution.py:187
  723.1 8.1 multiply_reduce_fusion.1
  759.4 25.3 %all-to-all-done.11 = f32[2,3,4,384]{3,0,1,2:T(2,128)S(1)} async-done(((f32[2,3,4,384]{3,0,1,2:T(2,128)}), f32[2,3,4,384]{3,0,1,2:T(2,128)S(1)}, u32[]{:S(2)}, u32[]{:S(2)}) %all-to-all-start.11) | async-done | bytes 36896 | tf_op jit(solution)/shard_map/all_to_all | solution.py:494
  852.5 11.1 %collective-permute-done.29 = bf16[48,1536]{1,0:T(8,128)(2,1)S(1)} collective-permute-done((bf16[48,1536]{1,0:T(8,128)(2,1)S(1)}, bf16[48,1536]{1,0:T(8,128)(2,1)S(1)}, u32[]{:S(2)}, u32[]{:S(2)}) %collective-permute-start.29) | collective-permute-done | bytes 147488 | tf_op jit(solution)/shard_map/ppermute | solution.py:158
  (697 shorter events, 512.8 us)
Async XLA Ops:
  7.2 160.0 %all-gather.7.cloned.1.call-start = ((), (), s32[]{:S(2)}) async-start(), calls=%async_computation.18 | async-start | bytes 1327104 | tf_op jit(solution)/shard_map/all_gather | solution.py:265
  29.1 163.1 %all-gather.5.cloned.1.call-start = ((), (), s32[]{:S(2)}) async-start(), calls=%async_computation.17 | async-start | bytes 3981312 | tf_op jit(solution)/shard_map/all_gather | solution.py:265
  29.8 253.6 %all-gather.9.cloned.1.call-start = ((), (), s32[]{:S(2)}) async-start(), calls=%async_computation.19 | async-start | bytes 5308416 | tf_op jit(solution)/shard_map/all_gather | solution.py:265
  31.9 83.0 %collective-permute-start.1 = (bf16[96,3072]{1,0:T(8,128)(2,1)}, bf16[96,3072]{1,0:T(8,128)(2,1)}, u32[]{:S(2)}, u32[]{:S(2)}) collective-permute-start(bf16[96,3072]{1,0:T(8,128)(2,1)} %slice_bitcast_fusion.6), channel_id=1, source_target_pairs={{0,16},{8,24},{1,17},{9,25},{2,18},{10,26},{3,19},{11,27},{4,20},{... | collective-permute-start | bytes 1769480 | tf_op jit(solution)/shard_map/ppermute | solution.py:124
  80.1 30.7 %collective-permute-start.3 = (bf16[192,1536]{1,0:T(8,128)(2,1)}, bf16[192,1536]{1,0:T(8,128)(2,1)}, u32[]{:S(2)}, u32[]{:S(2)}) collective-permute-start(bf16[192,1536]{1,0:T(8,128)(2,1)} %broadcast_select_fusion.10), channel_id=1, source_target_pairs={{0,8},{8,0},{16,24},{24,16},{1,9},{9,1},{17,25},{25,17},{2,10},{10... | collective-permute-start | bytes 1769480 | tf_op jit(solution)/shard_map/ppermute | solution.py:118
  81.5 31.8 %collective-permute-start.5 = (bf16[192,1536]{1,0:T(8,128)(2,1)}, bf16[192,1536]{1,0:T(8,128)(2,1)}, u32[]{:S(2)}, u32[]{:S(2)}) collective-permute-start(bf16[192,1536]{1,0:T(8,128)(2,1)} %broadcast_select_fusion.10), channel_id=1, source_target_pairs={{0,16},{8,24},{16,0},{24,8},{1,17},{9,25},{17,1},{25,9},{2,18},{10... | collective-permute-start | bytes 1769480 | tf_op jit(solution)/shard_map/ppermute | solution.py:118
  122.8 37.1 %all-to-all-start = ((bf16[96,8,384]{2,0,1:T(8,128)(2,1)}), bf16[96,8,384]{2,0,1:T(8,128)(2,1)}, u32[]{:S(2)}, u32[]{:S(2)}) async-start(bf16[96,8,384]{2,0,1:T(8,128)(2,1)} %bitcast.356), calls=%async_computation | async-start | bytes 1179648 | tf_op jit(solution)/shard_map/all_to_all | solution.py:272
  127.0 235.3 %all-gather.11.cloned.1.call-start = ((), (), s32[]{:S(2)}) async-start(), calls=%async_computation.20 | async-start | bytes 10616832 | tf_op jit(solution)/shard_map/all_gather | solution.py:265
  170.2 50.2 %collective-permute-start.11 = (bf16[768,384]{1,0:T(8,128)(2,1)}, bf16[768,384]{1,0:T(8,128)(2,1)}, u32[]{:S(2)}, u32[]{:S(2)}) collective-permute-start(bf16[768,384]{1,0:T(8,128)(2,1)} %bitcast.20), channel_id=1, source_target_pairs={{0,8},{8,0},{16,24},{24,16},{1,9},{9,1},{17,25},{25,17},{2,10},{10... | collective-permute-start | bytes 1769480 | tf_op jit(solution)/shard_map/ppermute | solution.py:118
  170.9 52.7 %collective-permute-start.10 = (bf16[768,384]{1,0:T(8,128)(2,1)}, bf16[768,384]{1,0:T(8,128)(2,1)}, u32[]{:S(2)}, u32[]{:S(2)}) collective-permute-start(bf16[768,384]{1,0:T(8,128)(2,1)} %bitcast.20), channel_id=1, source_target_pairs={{0,16},{8,24},{16,0},{24,8},{1,17},{9,25},{17,1},{25,9},{2,18},{10... | collective-permute-start | bytes 1769480 | tf_op jit(solution)/shard_map/ppermute | solution.py:118
  225.3 40.5 %collective-permute-start.13 = (bf16[384,384]{1,0:T(8,128)(2,1)}, bf16[384,384]{1,0:T(8,128)(2,1)S(1)}, u32[]{:S(2)}, u32[]{:S(2)}) collective-permute-start(bf16[384,384]{1,0:T(8,128)(2,1)} %slice.562), channel_id=1, source_target_pairs={{0,8},{8,0},{16,24},{24,16},{1,9},{9,1},{17,25},{25,17},{2,10},{10... | collective-permute-start | bytes 884744 | tf_op jit(solution)/shard_map/ppermute | solution.py:118
  394.4 245.2 %reduce-scatter.14.cloned.1.call-start = ((), (), s32[]{:S(2)}) async-start(), calls=%async_computation.23 | async-start | bytes 5308416 | tf_op jit(solution)/shard_map/reduce_scatter | solution.py:395
  450.1 191.0 %reduce-scatter.10.cloned.1.call-start = ((), (), s32[]{:S(2)}) async-start(), calls=%async_computation.21 | async-start | bytes 10616832 | tf_op jit(solution)/shard_map/reduce_scatter | solution.py:395
  527.0 50.3 %all-to-all-start.5 = ((bf16[64,4,384]{2,0,1:T(8,128)(2,1)}), bf16[64,4,384]{2,0,1:T(8,128)(2,1)S(1)}, u32[]{:S(2)}, u32[]{:S(2)}) async-start(bf16[64,4,384]{2,0,1:T(8,128)(2,1)} %bitcast.297), calls=%async_computation.5 | async-start | bytes 393216 | tf_op jit(solution)/shard_map/all_to_all | solution.py:190
  545.5 42.4 %collective-permute-start.18 = (bf16[256,1536]{1,0:T(8,128)(2,1)}, bf16[256,1536]{1,0:T(8,128)(2,1)}, u32[]{:S(2)}, u32[]{:S(2)}) collective-permute-start(bf16[256,1536]{1,0:T(8,128)(2,1)} %convolution_convert_fusion.12), channel_id=1, source_target_pairs={{0,1},{1,0},{2,3},{3,2},{4,5},{5,4},{6,7},{7,6},{8,9},{9,8},{10,11... | collective-permute-start | bytes 2359304 | tf_op jit(solution)/shard_map/ppermute | solution.py:121
  577.3 31.6 %all-to-all-start.13 = ((bf16[8,96,384]{2,1,0:T(8,128)(2,1)}), bf16[8,96,384]{2,1,0:T(8,128)(2,1)S(1)}, u32[]{:S(2)}, u32[]{:S(2)}) async-start(bf16[8,96,384]{2,1,0:T(8,128)(2,1)} %bitcast.103), calls=%async_computation.13 | async-start | bytes 1179648 | tf_op jit(solution)/shard_map/all_to_all | solution.py:437
  584.4 40.9 %collective-permute-start.39 = (bf16[192,1536]{1,0:T(8,128)(2,1)}, bf16[192,1536]{1,0:T(8,128)(2,1)}, u32[]{:S(2)}, u32[]{:S(2)}) collective-permute-start(bf16[192,1536]{1,0:T(8,128)(2,1)} %pad_maximum_fusion.29), channel_id=1, source_target_pairs={{0,16},{8,24},{16,0},{24,8},{1,17},{9,25},{17,1},{25,9},{2,18},{10... | collective-permute-start | bytes 1769480 | tf_op jit(solution)/shard_map/ppermute | solution.py:118
  632.9 201.0 %collective-permute-start.40 = (bf16[192,1536]{1,0:T(8,128)(2,1)}, bf16[192,1536]{1,0:T(8,128)(2,1)}, u32[]{:S(2)}, u32[]{:S(2)}) collective-permute-start(bf16[192,1536]{1,0:T(8,128)(2,1)} %fusion.67), channel_id=1, source_target_pairs={{16,0},{24,8},{17,1},{25,9},{18,2},{26,10},{19,3},{27,11},{20,4},{... | collective-permute-start | bytes 1769480 | tf_op jit(solution)/shard_map/ppermute | solution.py:127
  635.1 193.4 %collective-permute-start.34 = (bf16[96,3072]{1,0:T(8,128)(2,1)}, bf16[96,3072]{1,0:T(8,128)(2,1)}, u32[]{:S(2)}, u32[]{:S(2)}) collective-permute-start(bf16[96,3072]{1,0:T(8,128)(2,1)} %bitcast.144), channel_id=1, source_target_pairs={{16,0},{24,8},{17,1},{25,9},{18,2},{26,10},{19,3},{27,11},{20,4},{... | collective-permute-start | bytes 1769480 | tf_op jit(solution)/shard_map/ppermute | solution.py:127
  692.2 61.6 %all-to-all-start.9 = ((bf16[4,64,1536]{2,1,0:T(8,128)(2,1)}), bf16[4,64,1536]{2,1,0:T(8,128)(2,1)}, u32[]{:S(2)}, u32[]{:S(2)}) async-start(bf16[4,64,1536]{2,1,0:T(8,128)(2,1)} %bitcast.354), calls=%async_computation.9 | async-start | bytes 1572864 | tf_op jit(solution)/shard_map/all_to_all | solution.py:183
  696.4 150.0 %reduce-scatter.12.cloned.1.call-start = ((), (), s32[]{:S(2)}) async-start(), calls=%async_computation.22 | async-start | bytes 5308416 | tf_op jit(solution)/shard_map/reduce_scatter | solution.py:395
  741.9 69.6 %collective-permute-start.35 = (bf16[192,3072]{1,0:T(8,128)(2,1)}, bf16[192,3072]{1,0:T(8,128)(2,1)}, u32[]{:S(2)}, u32[]{:S(2)}) collective-permute-start(bf16[192,3072]{1,0:T(8,128)(2,1)} %reduce-scatter.10.cloned.1.call-done), channel_id=1, source_target_pairs={{0,16},{8,24},{1,17},{9,25},{2,18},{10,26},{3,19},{11,27},{4,20},{... | collective-permute-start | bytes 3538952 | tf_op jit(solution)/shard_map/ppermute | solution.py:124
  751.3 50.4 %collective-permute-start.22 = (bf16[256,1536]{1,0:T(8,128)(2,1)}, bf16[256,1536]{1,0:T(8,128)(2,1)}, u32[]{:S(2)}, u32[]{:S(2)}) collective-permute-start(bf16[256,1536]{1,0:T(8,128)(2,1)} %pad_maximum_fusion.20), channel_id=1, source_target_pairs={{0,16},{8,24},{16,0},{24,8},{1,17},{9,25},{17,1},{25,9},{2,18},{10... | collective-permute-start | bytes 2359304 | tf_op jit(solution)/shard_map/ppermute | solution.py:118
  752.4 49.4 %collective-permute-start.20 = (bf16[256,1536]{1,0:T(8,128)(2,1)}, bf16[256,1536]{1,0:T(8,128)(2,1)}, u32[]{:S(2)}, u32[]{:S(2)}) collective-permute-start(bf16[256,1536]{1,0:T(8,128)(2,1)} %pad_maximum_fusion.19), channel_id=1, source_target_pairs={{0,8},{8,0},{16,24},{24,16},{1,9},{9,1},{17,25},{25,17},{2,10},{10... | collective-permute-start | bytes 2359304 | tf_op jit(solution)/shard_map/ppermute | solution.py:118
  (188 other events, 1757.0 us)
Sparse Core Ops, SparseCore 0:
  29.2 30.3 all-gather.6
  61.2 44.2 all-gather.4
  107.2 62.9 all-gather.8
  192.2 107.5 all-gather.10
  450.2 53.0 reduce-scatter.13
  505.5 111.3 reduce-scatter.9
  720.0 56.2 reduce-scatter.11

commit v6 on v5

--- a/solution.py
+++ b/solution.py
@@ -167,16 +167,9 @@
         blocks = stacked.reshape(2, stride, count, -1, inner).transpose(1, 0, 3, 2, 4)
         return blocks.reshape(-1, feature_width)
 
-    def fold_grad(grad):
-        count = feature_width // inner
-        blocks = grad.reshape(stride, 2, -1, count, inner).transpose(1, 0, 3, 2, 4)
-        return blocks.reshape(-1, inner)
-
-    def unfold_piece(piece):
-        count = feature_width // inner
-        rows = piece.shape[0] // count
-        blocks = [piece[i * rows : (i + 1) * rows] for i in range(count)]
-        return jnp.concatenate(blocks, axis=1)
+    def by_device(grad):
+        blocks = grad.reshape(stride, 2, -1, feature_width).transpose(1, 0, 2, 3)
+        return blocks.reshape(-1, feature_width)
 
     def sum_to_slots(partial):
         blocks = partial.astype(low).reshape(section_count, -1, feature_width)
@@ -264,18 +257,25 @@
     def gather(piece):
         return lax.all_gather(piece, dp, axis=0, tiled=True)
 
+    stacked = [
+        gather(jnp.concatenate([qkv_pieces[layer], fold(out_pieces[layer])], axis=1))
+        for layer in range(LAYERS)
+    ]
+    qkv_w = [weight[:, : 3 * inner] for weight in stacked]
+    out_w = [unfold(weight[:, 3 * inner :]) for weight in stacked]
+
     half_hidden = w_down.shape[1] // 2
     half_depth = w_up.shape[1] // 2
-    down_shared = by_distance(
-        share_first(*[after(half, other_heads) for half in (w_down[0, :half_hidden], w_down[0, half_hidden:])])
-    )
     up_turned = lax.all_to_all(
-        after(share_first(w_up[0, :half_depth], w_up[0, half_depth:]), (all_gains, down_shared[3])),
+        share_first(*after((w_up[0, :half_depth], w_up[0, half_depth:]), other_heads)),
         dp,
         split_axis=1,
         concat_axis=0,
         tiled=True,
     )
+    down_shared = by_distance(
+        share_first(*after((w_down[0, :half_hidden], w_down[0, half_hidden:]), other_heads))
+    )
     up_shared = by_distance(up_turned)
 
     def in_depth(near, far):
@@ -289,30 +289,14 @@
         [in_depth(up_shared[0], up_shared[2]), in_depth(up_shared[1], up_shared[3])], axis=1
     )
 
-    qkv_first = gather(qkv_pieces[0])
-    out_first = unfold(gather(after(fold(out_pieces[0]), qkv_pieces[0])))
-    stacked = gather(
-        jnp.concatenate([qkv_pieces[1], fold(out_pieces[1])], axis=1)
-    )
     up_even, up_odd = column_parts(w_up[0], half_hidden)
-    up_piece, down_piece = after(
-        (up_even, w_down[0, :half_hidden]), (up_turned, down_shared[3])
-    )
-    ffn_piece = jnp.concatenate(
-        [
-            jnp.where(on_first, to_first(up_piece), up_odd),
-            jnp.where(on_first, to_first(down_piece), w_down[0, half_hidden:]),
-        ],
-        axis=1,
-    )
-    ffn_second = gather(ffn_piece)
-    hidden_width = up_even.shape[1]
-    qkv_second = stacked[:, : 3 * inner]
-    out_second = unfold(stacked[:, 3 * inner :])
-    up_w = (up_first, ffn_second[:, :hidden_width])
-    down_w = (down_first, ffn_second[:, hidden_width:])
-    qkv_w = (qkv_first, qkv_second)
-    out_w = (out_first, out_second)
+    up_piece, down_piece = after((up_even, w_down[0, :half_hidden]), other_heads)
+    down_second = gather(
+        jnp.where(on_first, to_first(down_piece), w_down[0, half_hidden:])
+    )
+    up_second = gather(jnp.where(on_first, to_first(up_piece), up_odd))
+    up_w = (up_first, up_second)
+    down_w = (down_first, down_second)
     query_w = [weight[:, :inner] for weight in qkv_w]
     key_w = [weight[:, inner : 2 * inner] for weight in qkv_w]
     value_w = [weight[:, 2 * inner :] for weight in qkv_w]
@@ -361,8 +345,6 @@
             query_heads, key_heads, value_heads, allowed, score_scale
         )
         attended_low = attended.reshape(-1, inner).astype(low)
-        if layer == 0:
-            attended_low = after(attended_low, up_turned)
         middle = current + sum_to_slots(matmul(attended_low, out_w[layer]))
         unit_mid, inverse_mid = unit_rows(middle)
         ffn_low = (unit_mid * all_gains[layer, 2]).astype(low)
@@ -416,11 +398,12 @@
         grad_active = matmul_nt(grad_low, down_w[layer])
         grad_hidden = jax.vjp(gelu_exact, hidden_pre)[1](grad_active)[0].astype(low)
         down_grad = matmul_tn(active_low, grad_low)
+        if layer:
+            down_grad = down_grad.astype(low)
+            grad_hidden = after(grad_hidden, down_grad)
         up_grad = matmul_tn(ffn_low, grad_hidden)
         if layer:
-            ffn_piece = scatter(
-                jnp.concatenate([up_grad.astype(low), down_grad.astype(low)], axis=1)
-            )
+            ffn_pieces = (scatter(down_grad), scatter(up_grad.astype(low)))
             ffn_grad = sum_to_slots(matmul_nt(grad_hidden, up_w[layer]))
         else:
             ffn_grad = sum_to_sequence(grad_hidden, up_w[layer], matmul_nt)
@@ -439,12 +422,9 @@
         grad_middle = grad_rows + norm_back(
             unit_mid, inverse_mid, ffn_grad * all_gains[layer, 2]
         )
-        middle_low = grad_middle.astype(low)
-        if layer == 0:
-            middle_low = after(middle_low, ffn_piece)
-        middle_low = from_slots(middle_low)
+        middle_low = from_slots(grad_middle.astype(low))
         grad_heads = split_heads(matmul_nt(middle_low, out_w[layer]).astype(low))
-        out_grad = matmul_tn(attended_low, middle_low)
+        out_piece = scatter(by_device(matmul_tn(attended_low, middle_low)).astype(low))
         grad_query, grad_key, grad_value = attend_backward(
             query_heads, key_heads, value_heads, allowed, score_scale, log_total, grad_heads
         )
@@ -462,17 +442,14 @@
             unit_in, inverse_in, latent_grad_rows * all_gains[layer, 1]
         )
         both_low = jnp.concatenate([media_low[layer], latent_low], axis=0)
-        query_grad = matmul_tn(latent_low, grad_query)
-        key_grad = matmul_tn(both_low, grad_key)
-        value_grad = matmul_tn(both_low, grad_value)
-        qkv_grad = jnp.concatenate(
-            [query_grad.astype(low), key_grad.astype(low), value_grad.astype(low)], axis=1
-        )
-        pieces[layer] = scatter(
-            jnp.concatenate([qkv_grad, fold_grad(out_grad.astype(low))], axis=1)
-        )
+        all_grads = jnp.concatenate(
+            [jnp.pad(grad_query, ((seq_rows, 0), (0, 0))), grad_key, grad_value], axis=1
+        )
+        qkv_grad = matmul_tn(both_low, all_grads).astype(low)
+        pieces[layer] = (scatter(qkv_grad), out_piece)
         if layer > 0:
             grad_low = from_sequences(grad_rows.astype(low))
+            grad_low = after(grad_low, ffn_pieces)
         media_part = matmul_nt(grad_key[:seq_rows], key_w[layer]) + matmul_nt(
             grad_value[:seq_rows], value_w[layer]
         )
@@ -481,7 +458,7 @@
         media_scaled = scaled if media_scaled is None else media_scaled + scaled
         gain_rows[layer] = jnp.stack([gain_media_grad, gain_latent_grad, gain_ffn_grad])
     latents_out = to_columns(current)
-    latent_grad = to_columns(grad_rows)
+    latent_grad = to_columns(after(grad_rows, pieces[1]))
     media_rows = seq_rows // section_count
     media_sum = sum_over_sections(media_scaled)
     own_unit = lax.dynamic_slice_in_dim(media_unit, section * media_rows, media_rows, 0)
@@ -496,7 +473,7 @@
     gain_parts = gain_parts.reshape(LAYERS, 3, dp_count, -1)
     gain_grad = jnp.sum(lax.all_to_all(gain_parts, dp, split_axis=2, concat_axis=2), axis=2)
 
-    qkv_parts = [piece[:, : 3 * inner] for piece in pieces]
+    qkv_parts = [piece[0] for piece in pieces]
     own, other = pick(qkv_parts[0], qkv_parts[1])
     lower, upper = pick(own, swapped(other, 2))
     qkv_grads = [
@@ -505,10 +482,10 @@
         ).astype(full)
         for i in range(3)
     ]
-    out_grad = join_rows(*[unfold_piece(piece[:, 3 * inner :]) for piece in pieces])
-    back = to_second(ffn_piece)
-    up_second_grad = interleave(back[:, :hidden_width], ffn_piece[:, :hidden_width], half_hidden)
-    down_second_grad = jnp.concatenate([back[:, hidden_width:], ffn_piece[:, hidden_width:]], axis=0)
+    out_grad = join_rows(*[piece[1] for piece in pieces])
+    down_piece, up_piece = ffn_pieces
+    up_second_grad = interleave(to_second(up_piece), up_piece, half_hidden)
+    down_second_grad = jnp.concatenate([to_second(down_piece), down_piece], axis=0)
     up_first_grad = jnp.concatenate([up_half, to_first(up_half)], axis=0)
     down_first_grad = jnp.concatenate([down_half, to_first(down_half)], axis=0)
     up_grad = jnp.where(on_first, up_first_grad, up_second_grad).astype(full)

time: 887 us -> 755 us (0.85)
  waiting for transfers between devices: 186 us -> 124 us
  local copies, waits for them, and re-layouts: 140 us -> 82.2 us
  other arithmetic: 118 us -> 87.3 us
  blocking collectives: 150 us -> 166 us
  matrix products: 140 us -> 152 us
  starting transfers between devices: 124 us -> 113 us
    unnamed x311 -> x292, local copies, waits for them, and re-layouts: 50.7 us -> 21.8 us
    all_gather x1, blocking collectives: 7.49 us -> 26.1 us  [per_device(): all_gains = lax.all_gather(near_gains, 'section', axis=2, tiled=True)]
    concatenate x6 -> x3, other arithmetic: 19.6 us -> 3.26 us  [the longest x2 1.73 us: per_device(): jnp.concatenate([qkv_pieces[layer], fold(out_pieces[layer])], axis=1)]
    all_to_all x1, waiting for transfers between devices: 25.3 us -> 10.5 us  [per_device(): lax.all_to_all(gain_parts, 'section', split_axis=2, concat_axis=2)]
    all_to_all x1, waiting for transfers between devices: 27.9 us -> 13.8 us  [per_device(): lax.all_to_all(share_first(*after((w_up[0, :half_depth], w_up[0, half_dep...]
    all_to_all x2, waiting for transfers between devices: 0.01 us -> 13.3 us  [to_columns(): lax.all_to_all(rows.astype(low), 'section', split_axis=1, concat_axis=0,...]
    all_to_all x2, waiting for transfers between devices: 12.9 us -> 0.01 us  [sum_to_sequence(): arrived = lax.all_to_all(blocks, 'pair', split_axis=0, concat_axis=0)]
    reshape x6 -> x2, local copies, waits for them, and re-layouts: 13.3 us -> 0.97 us  [unfold(): stacked.reshape(2, stride, count, -1, inner).transpose(1, 0, 3, 2, 4)]
  transfers between devices with their start and end apart: 61 -> 65, of which waited for: 26 -> 23; matrix products, arithmetic and copies ran while one was open for 37% -> 40% of each run, Pallas kernels for 0% -> 0%
where the time goes in v6:
time: 755 us; the launch traced here: 742 us
  blocking collectives  166 us (22%)
  matrix products  152 us (20%)
  waiting for transfers between devices  124 us (16%)
  starting transfers between devices  113 us (15%)
  other arithmetic  87.3 us (12%)
  local copies, waits for them, and re-layouts  82.2 us (11%)
  between operations  17 us (2%)
    all_gather x4, blocking collectives, from_slots(): return lax.all_gather(rows, 'section', axis=0, tiled=True)  60.1 us
    dot_general x17, matrix products, matmul_nt(): lax.dot_general(left, right, (((1,), (1,)), ((), ())), preferred_element_...  57 us
    ppermute x26, waiting for transfers between devices, swapped(): return lax.ppermute(value, 'section', pairs)  50.7 us
    dot_general x13, matrix products, matmul(): return jnp.dot(left, right, preferred_element_type=full)  45.5 us
    all_gather x2, blocking collectives, from_sequences(): near = lax.all_gather(rows, 'pair', axis=0, tiled=True)  44.9 us
    ppermute x26, starting transfers between devices, swapped(): return lax.ppermute(value, 'section', pairs)  36.3 us
    dot_general x8, matrix products, matmul_tn(): lax.dot_general(left, right, (((0,), (0,)), ((), ())), preferred_element_...  27.5 us
    all_gather x1, blocking collectives, per_device(): all_gains = lax.all_gather(near_gains, 'section', axis=2, tiled=True)  26.1 us
  transfers between devices with their start and end apart: 65, of which 23 were waited for; matrix products, arithmetic and copies ran while one was open for 40% of the time, Pallas kernels for 0%

profile of v6, /device:TPU:0, one launch (start us, length us, event | category | flops | bytes accessed | tf_op | source)
XLA Modules:
  0.0 742.0 jit_solution(18096882168583924178)
XLA Ops:
  12.6 10.2 %collective-permute-done = bf16[192,1152]{1,0:T(8,128)(2,1)S(1)} collective-permute-done((bf16[192,1152]{1,0:T(8,128)(2,1)S(1)}, bf16[192,1152]{1,0:T(8,128)(2,1)S(1)}, u32[]{:S(2)}, u32[]{:S(2)}) %collective-permute-start) | collective-permute-done | bytes 442400 | tf_op jit(solution)/shard_map/ppermute | solution.py:118
  32.6 7.4 slice_reduce_fusion
  53.1 24.2 %all_gather.36 = f32[2,3,384]{1,0,2:T(2,128)} all-gather(f32[2,3,48]{1,0,2:T(2,128)S(1)} %copy.177), channel_id=1, replica_groups=mesh['section'=4,'pair'=4,'core'=2] {'pair','core'}, dimensions={2}, use_global_device_ids=true | all-gather | bytes 10368 | tf_op jit(solution)/shard_map/all_gather | solution.py:253
  83.7 26.1 %all_gather.37 = f32[2,3,1536]{2,0,1:T(2,128)S(1)} all-gather(f32[2,3,384]{2,0,1:T(2,128)S(1)} %copy.178), channel_id=1, replica_groups=mesh['section'=4,'pair'=4,'core'=2] {'section'}, dimensions={2}, use_global_device_ids=true | all-gather | bytes 46080 | tf_op jit(solution)/shard_map/all_gather | solution.py:254
  140.3 13.8 %all-to-all-done.1 = bf16[96,8,384]{2,0,1:T(8,128)(2,1)} async-done(((bf16[96,8,384]{2,0,1:T(8,128)(2,1)}), bf16[96,8,384]{2,0,1:T(8,128)(2,1)}, u32[]{:S(2)}, u32[]{:S(2)}) %all-to-all-start.1) | async-done | bytes 589856 | tf_op jit(solution)/shard_map/all_to_all | solution.py:269
  206.3 17.9 %all_gather.39 = bf16[256,1536]{1,0:T(8,128)(2,1)S(1)} all-gather(bf16[64,1536]{1,0:T(8,128)(2,1)S(1)} %multiply_convert_fusion.9), channel_id=1, replica_groups=mesh['section'=4,'pair'=4,'core'=2] {'pair'}, dimensions={0}, use_global_device_ids=true | all-gather | bytes 983040 | tf_op jit(solution)/shard_map/all_gather | solution.py:189
  243.0 9.6 %collective-permute-done.16 = bf16[192,1536]{1,0:T(8,128)(2,1)S(1)} collective-permute-done((bf16[192,1536]{1,0:T(8,128)(2,1)S(1)}, bf16[192,1536]{1,0:T(8,128)(2,1)S(1)}, u32[]{:S(2)}, u32[]{:S(2)}) %collective-permute-start.16) | collective-permute-done | bytes 589856 | tf_op jit(solution)/shard_map/ppermute | solution.py:127
  267.0 14.2 %all_gather.41 = bf16[256,1536]{1,0:T(8,128)(2,1)S(1)} all-gather(bf16[64,1536]{1,0:T(8,128)(2,1)S(1)} %multiply_convert_fusion.8), channel_id=1, replica_groups=mesh['section'=4,'pair'=4,'core'=2] {'section'}, dimensions={0}, use_global_device_ids=true | all-gather | bytes 983040 | tf_op jit(solution)/shard_map/all_gather | solution.py:180
  299.3 11.1 %all_to_all.114 = bf16[4,64,1536]{2,1,0:T(8,128)(2,1)S(1)} all-to-all(bf16[4,64,1536]{2,1,0:T(8,128)(2,1)S(1)} %bitcast.358), channel_id=1, replica_groups=mesh['section'=4,'pair'=4,'core'=2] {'section'}, dimensions={0} | all-to-all | bytes 1572864 | tf_op jit(solution)/shard_map/all_to_all | solution.py:176
  311.1 10.6 %all_gather.42 = bf16[256,1536]{1,0:T(8,128)(2,1)S(1)} all-gather(bf16[64,1536]{1,0:T(8,128)(2,1)S(1)} %multiply_convert_fusion.7), channel_id=1, replica_groups=mesh['section'=4,'pair'=4,'core'=2] {'section'}, dimensions={0}, use_global_device_ids=true | all-gather | bytes 983040 | tf_op jit(solution)/shard_map/all_gather | solution.py:180
  321.7 7.9 %multiply_convert_fusion.5 = (bf16[256,1536]{1,0:T(8,128)(2,1)S(1)}, f32[256,1536]{1,0:T(8,128)}) fusion(bf16[256,1536]{1,0:T(8,128)(2,1)S(1)} %all_gather.42, bf16[1536,1536]{1,0:T(8,128)(2,1)} %all-gather.9.cloned.1.call-done), kind=kOutput, calls=%fused_computation.119 | convolution fusion | flops 1233518592 | bytes 7864320 | tf_op jit(solution)/shard_map/dot_general | solution.py:35
  334.6 7.7 %add_convert_fusion.2 = bf16[256,1536]{1,0:T(8,128)(2,1)S(1)} fusion(bf16[1536,1536]{1,0:T(8,128)(2,1)} %all-gather.11.cloned.1.call-done, bf16[256,1536]{1,0:T(8,128)(2,1)} %param.23, f32[256,1536]{1,0:T(8,128)} %get-tuple-element.153), kind=kOutput, calls=%fused_computation.117 | convolution fusion | flops 1236271104 | bytes 7864320 | tf_op jit(solution)/shard_map/dot_general | solution.py:39
  381.6 11.2 %all_gather.45 = bf16[256,1536]{1,0:T(8,128)(2,1)S(1)} all-gather(bf16[64,1536]{1,0:T(8,128)(2,1)S(1)} %get-tuple-element.61), channel_id=1, replica_groups=mesh['section'=4,'pair'=4,'core'=2] {'section'}, dimensions={0}, use_global_device_ids=true | all-gather | bytes 983040 | tf_op jit(solution)/shard_map/all_gather | solution.py:180
  428.9 27.0 %all_gather.46 = bf16[256,1536]{1,0:T(8,128)(2,1)S(1)} all-gather(bf16[64,1536]{1,0:T(8,128)(2,1)S(1)} %get-tuple-element.59), channel_id=1, replica_groups=mesh['section'=4,'pair'=4,'core'=2] {'pair'}, dimensions={0}, use_global_device_ids=true | all-gather | bytes 983040 | tf_op jit(solution)/shard_map/all_gather | solution.py:189
  455.9 9.3 %convolution_convert_fusion.1 = bf16[1536,1152]{1,0:T(8,128)(2,1)} fusion(bf16[256,1536]{1,0:T(8,128)(2,1)S(1)} %copy-done.75, bf16[1024,1536]{1,0:T(8,128)(2,1)} %get-tuple-element.83, bf16[256,384]{0,1:T(8,128)(2,1)S(1)} %bitcast.393, bf16[1280,384]{0,1:T(8,128)(2,1)S(1)} %bitcast.342, bf16[1280,384]{0,1:T(8,128)(2,1)S(1)} %bitcast.352), kind=kOutput, calls=%fused_computation.3 | convolution fusion | flops 4551278592 | bytes 9633792 | tf_op jit(solution)/shard_map/dot_general | solution.py:43
  484.1 6.4 collective-permute-done.32
  498.3 9.6 %collective-permute-done.33 = bf16[768,384]{1,0:T(8,128)(2,1)S(1)} collective-permute-done((bf16[768,384]{1,0:T(8,128)(2,1)S(1)}, bf16[768,384]{1,0:T(8,128)(2,1)S(1)}, u32[]{:S(2)}, u32[]{:S(2)}) %collective-permute-start.33) | collective-permute-done | bytes 589856 | tf_op jit(solution)/shard_map/ppermute | solution.py:118
  531.2 8.5 %all-to-all-done.13 = bf16[8,96,384]{2,1,0:T(8,128)(2,1)S(1)} async-done(((bf16[8,96,384]{2,1,0:T(8,128)(2,1)}), bf16[8,96,384]{2,1,0:T(8,128)(2,1)S(1)}, u32[]{:S(2)}, u32[]{:S(2)}) %all-to-all-start.13) | async-done | bytes 589856 | tf_op jit(solution)/shard_map/all_to_all | solution.py:420
  547.8 7.7 %convolution_add_fusion.1 = f32[1024,1536]{1,0:T(8,128)} fusion(f32[1024,1536]{1,0:T(8,128)} %fusion.84, bf16[1024,384]{0,1:T(8,128)(2,1)S(1)} %bitcast.356, bf16[1536,1536]{1,0:T(8,128)(2,1)} %all-gather.7.cloned.1.call-done), kind=kOutput, calls=%fused_computation.32 | convolution fusion | flops 1209532416 | bytes 14548992 | tf_op jit(solution)/shard_map/dot_general | solution.py:39
  572.7 24.2 %all_gather.47 = bf16[256,1536]{1,0:T(8,128)(2,1)S(1)} all-gather(bf16[64,1536]{1,0:T(8,128)(2,1)S(1)} %get-tuple-element.57), channel_id=1, replica_groups=mesh['section'=4,'pair'=4,'core'=2] {'section'}, dimensions={0}, use_global_device_ids=true | all-gather | bytes 983040 | tf_op jit(solution)/shard_map/all_gather | solution.py:180
  612.2 8.0 %multiply_reduce_fusion.1 = (f32[1536]{0:T(1024)S(1)}, f32[1536]{0:T(1024)S(1)}, f32[1024,1536]{1,0:T(8,128)S(1)}, f32[1024,1536]{1,0:T(8,128)}) fusion(bf16[1024,1536]{1,0:T(8,128)(2,1)S(1)} %copy-done.3, f32[1024]{0:T(1024)S(1)} %copy-done.104, f32[1024]{0:T(1024)S(1)} %copy-done.102, f32[1024,1536]{1,0:T(8,128)} %convolution_add_fusion.1, ...), kind=kOutput, calls=%fused_computation.10 | convolution fusion | flops 1225257984 | bytes 30310400 | tf_op jit(solution)/shard_map/dot_general | solution.py:39
  626.1 7.2 convolution_convert_fusion
  660.7 10.5 %all-to-all-done.11 = f32[2,3,4,384]{3,0,1,2:T(2,128)S(1)} async-done(((f32[2,3,4,384]{3,0,1,2:T(2,128)}), f32[2,3,4,384]{3,0,1,2:T(2,128)S(1)}, u32[]{:S(2)}, u32[]{:S(2)}) %all-to-all-start.11) | async-done | bytes 36896 | tf_op jit(solution)/shard_map/all_to_all | solution.py:471
  690.7 13.3 %all-to-all-done.10 = bf16[64,4,384]{2,0,1:T(8,128)(2,1)S(1)} async-done(((bf16[64,4,384]{2,0,1:T(8,128)(2,1)}), bf16[64,4,384]{2,0,1:T(8,128)(2,1)S(1)}, u32[]{:S(2)}, u32[]{:S(2)}) %all-to-all-start.10) | async-done | bytes 196640 | tf_op jit(solution)/shard_map/all_to_all | solution.py:183
  (675 shorter events, 421.6 us)
Async XLA Ops:
  7.2 149.3 %all-gather.5.cloned.1.call-start = ((), (), s32[]{:S(2)}) async-start(), calls=%async_computation.20 | async-start | bytes 5308416 | tf_op jit(solution)/shard_map/all_gather | solution.py:258
  29.3 224.3 %all-gather.7.cloned.1.call-start = ((), (), s32[]{:S(2)}) async-start(), calls=%async_computation.21 | async-start | bytes 5308416 | tf_op jit(solution)/shard_map/all_gather | solution.py:258
  78.4 40.2 %collective-permute-start.4 = (bf16[96,3072]{1,0:T(8,128)(2,1)}, bf16[96,3072]{1,0:T(8,128)(2,1)S(1)}, u32[]{:S(2)}, u32[]{:S(2)}) collective-permute-start(bf16[96,3072]{1,0:T(8,128)(2,1)} %get-tuple-element.24), channel_id=1, source_target_pairs={{0,16},{8,24},{1,17},{9,25},{2,18},{10,26},{3,19},{11,27},{4,20},{... | collective-permute-start | bytes 1769480 | tf_op jit(solution)/shard_map/ppermute | solution.py:124
  81.1 33.7 %collective-permute-start.9 = (bf16[192,1536]{1,0:T(8,128)(2,1)}, bf16[192,1536]{1,0:T(8,128)(2,1)S(1)}, u32[]{:S(2)}, u32[]{:S(2)}) collective-permute-start(bf16[192,1536]{1,0:T(8,128)(2,1)} %get-tuple-element.26), channel_id=1, source_target_pairs={{0,16},{8,24},{1,17},{9,25},{2,18},{10,26},{3,19},{11,27},{4,20},{... | collective-permute-start | bytes 1769480 | tf_op jit(solution)/shard_map/ppermute | solution.py:124
  82.4 41.7 %collective-permute-start.15 = (bf16[192,1536]{1,0:T(8,128)(2,1)}, bf16[192,1536]{1,0:T(8,128)(2,1)}, u32[]{:S(2)}, u32[]{:S(2)}) collective-permute-start(bf16[192,1536]{1,0:T(8,128)(2,1)} %reshape_squeeze.16), channel_id=1, source_target_pairs={{16,0},{24,8},{17,1},{25,9},{18,2},{26,10},{19,3},{27,11},{20,4},{... | collective-permute-start | bytes 1769480 | tf_op jit(solution)/shard_map/ppermute | solution.py:127
  119.5 34.6 %all-to-all-start.1 = ((bf16[96,8,384]{2,0,1:T(8,128)(2,1)}), bf16[96,8,384]{2,0,1:T(8,128)(2,1)}, u32[]{:S(2)}, u32[]{:S(2)}) async-start(bf16[96,8,384]{2,0,1:T(8,128)(2,1)} %bitcast.298), calls=%async_computation.1 | async-start | bytes 1179648 | tf_op jit(solution)/shard_map/all_to_all | solution.py:269
  123.7 197.9 %all-gather.9.cloned.1.call-start = ((), (), s32[]{:S(2)}) async-start(), calls=%async_computation.22 | async-start | bytes 5308416 | tf_op jit(solution)/shard_map/all_gather | solution.py:258
  154.1 35.6 %collective-permute-start.6 = (bf16[768,384]{1,0:T(8,128)(2,1)}, bf16[768,384]{1,0:T(8,128)(2,1)}, u32[]{:S(2)}, u32[]{:S(2)}) collective-permute-start(bf16[768,384]{1,0:T(8,128)(2,1)} %bitcast.22), channel_id=1, source_target_pairs={{0,8},{8,0},{16,24},{24,16},{1,9},{9,1},{17,25},{25,17},{2,10},{10... | collective-permute-start | bytes 1769480 | tf_op jit(solution)/shard_map/ppermute | solution.py:118
  155.6 37.3 %collective-permute-start.5 = (bf16[768,384]{1,0:T(8,128)(2,1)}, bf16[768,384]{1,0:T(8,128)(2,1)}, u32[]{:S(2)}, u32[]{:S(2)}) collective-permute-start(bf16[768,384]{1,0:T(8,128)(2,1)} %bitcast.22), channel_id=1, source_target_pairs={{0,16},{8,24},{16,0},{24,8},{1,17},{9,25},{17,1},{25,9},{2,18},{10... | collective-permute-start | bytes 1769480 | tf_op jit(solution)/shard_map/ppermute | solution.py:118
  242.9 91.7 %all-gather.11.cloned.1.call-start = ((), (), s32[]{:S(2)}) async-start(), calls=%async_computation.23 | async-start | bytes 5308416 | tf_op jit(solution)/shard_map/all_gather | solution.py:258
  253.5 213.3 %reduce-scatter.7.cloned.1.call-start = ((), (), s32[]{:S(2)}) async-start(), calls=%async_computation.24 | async-start | bytes 5308416 | tf_op jit(solution)/shard_map/reduce_scatter | solution.py:377
  334.1 132.7 %reduce-scatter.9.cloned.1.call-start = ((), (), s32[]{:S(2)}) async-start(), calls=%async_computation.25 | async-start | bytes 5308416 | tf_op jit(solution)/shard_map/reduce_scatter | solution.py:377
  412.8 247.1 %reduce-scatter.13.cloned.1.call-start = ((), (), s32[]{:S(2)}) async-start(), calls=%async_computation.27 | async-start | bytes 1327104 | tf_op jit(solution)/shard_map/reduce_scatter | solution.py:377
  421.7 88.0 %all-to-all-start.5 = ((bf16[64,4,384]{2,0,1:T(8,128)(2,1)}), bf16[64,4,384]{2,0,1:T(8,128)(2,1)S(1)}, u32[]{:S(2)}, u32[]{:S(2)}) async-start(bf16[64,4,384]{2,0,1:T(8,128)(2,1)} %bitcast.300), calls=%async_computation.5 | async-start | bytes 393216 | tf_op jit(solution)/shard_map/all_to_all | solution.py:183
  425.1 234.9 %reduce-scatter.11.cloned.1.call-start = ((), (), s32[]{:S(2)}) async-start(), calls=%async_computation.26 | async-start | bytes 3981312 | tf_op jit(solution)/shard_map/reduce_scatter | solution.py:377
  478.7 49.6 %collective-permute-start.18 = (bf16[256,1536]{1,0:T(8,128)(2,1)}, bf16[256,1536]{1,0:T(8,128)(2,1)}, u32[]{:S(2)}, u32[]{:S(2)}) collective-permute-start(bf16[256,1536]{1,0:T(8,128)(2,1)} %convolution_convert_fusion.8), channel_id=1, source_target_pairs={{0,1},{1,0},{2,3},{3,2},{4,5},{5,4},{6,7},{7,6},{8,9},{9,8},{10,11... | collective-permute-start | bytes 2359304 | tf_op jit(solution)/shard_map/ppermute | solution.py:121
  482.9 30.3 %collective-permute-start.36 = (bf16[96,1536]{1,0:T(8,128)(2,1)}, bf16[96,1536]{1,0:T(8,128)(2,1)}, u32[]{:S(2)}, u32[]{:S(2)}) collective-permute-start(bf16[96,1536]{1,0:T(8,128)(2,1)} %get-tuple-element.108), channel_id=1, source_target_pairs={{0,16},{8,24},{16,0},{24,8},{1,17},{9,25},{17,1},{25,9},{2,18},{10... | collective-permute-start | bytes 884744 | tf_op jit(solution)/shard_map/ppermute | solution.py:118
  497.8 45.5 %collective-permute-start.39 = (bf16[192,1536]{1,0:T(8,128)(2,1)}, bf16[192,1536]{1,0:T(8,128)(2,1)}, u32[]{:S(2)}, u32[]{:S(2)}) collective-permute-start(bf16[192,1536]{1,0:T(8,128)(2,1)} %pad_maximum_fusion.20), channel_id=1, source_target_pairs={{0,16},{8,24},{16,0},{24,8},{1,17},{9,25},{17,1},{25,9},{2,18},{10... | collective-permute-start | bytes 1769480 | tf_op jit(solution)/shard_map/ppermute | solution.py:118
  522.6 42.5 %collective-permute-start.41 = (bf16[192,1536]{1,0:T(8,128)(2,1)}, bf16[192,1536]{1,0:T(8,128)(2,1)}, u32[]{:S(2)}, u32[]{:S(2)}) collective-permute-start(bf16[192,1536]{1,0:T(8,128)(2,1)} %reduce-scatter.7.cloned.1.call-done), channel_id=1, source_target_pairs={{0,16},{8,24},{1,17},{9,25},{2,18},{10,26},{3,19},{11,27},{4,20},{... | collective-permute-start | bytes 1769480 | tf_op jit(solution)/shard_map/ppermute | solution.py:124
  526.2 31.9 %collective-permute-start.35 = (bf16[192,1536]{1,0:T(8,128)(2,1)}, bf16[192,1536]{1,0:T(8,128)(2,1)}, u32[]{:S(2)}, u32[]{:S(2)}) collective-permute-start(bf16[192,1536]{1,0:T(8,128)(2,1)} %reduce-scatter.9.cloned.1.call-done), channel_id=1, source_target_pairs={{0,16},{8,24},{1,17},{9,25},{2,18},{10,26},{3,19},{11,27},{4,20},{... | collective-permute-start | bytes 1769480 | tf_op jit(solution)/shard_map/ppermute | solution.py:124
  539.7 32.3 %all-to-all-start.8 = ((bf16[4,64,1536]{2,1,0:T(8,128)(2,1)}), bf16[4,64,1536]{2,1,0:T(8,128)(2,1)S(1)}, u32[]{:S(2)}, u32[]{:S(2)}) async-start(bf16[4,64,1536]{2,1,0:T(8,128)(2,1)} %bitcast.388), calls=%async_computation.10 | async-start | bytes 1572864 | tf_op jit(solution)/shard_map/all_to_all | solution.py:197
  543.2 164.3 %reduce-scatter.17.cloned.1.call-start = ((), (), s32[]{:S(2)}) async-start(), calls=%async_computation.29 | async-start | bytes 1327104 | tf_op jit(solution)/shard_map/reduce_scatter | solution.py:377
  570.6 115.4 %collective-permute-start.34 = (bf16[96,3072]{1,0:T(8,128)(2,1)}, bf16[96,3072]{1,0:T(8,128)(2,1)}, u32[]{:S(2)}, u32[]{:S(2)}) collective-permute-start(bf16[96,3072]{1,0:T(8,128)(2,1)} %bitcast.150), channel_id=1, source_target_pairs={{16,0},{24,8},{17,1},{25,9},{18,2},{26,10},{19,3},{27,11},{20,4},{... | collective-permute-start | bytes 1769480 | tf_op jit(solution)/shard_map/ppermute | solution.py:127
  608.7 113.2 %reduce-scatter.15.cloned.1.call-start = ((), (), s32[]{:S(2)}) async-start(), calls=%async_computation.28 | async-start | bytes 3981312 | tf_op jit(solution)/shard_map/reduce_scatter | solution.py:377
  (185 other events, 2178.6 us)
Sparse Core Ops, SparseCore 0:
  29.4 62.3 all-gather.4
  93.4 63.0 all-gather.6
  158.2 50.3 all-gather.8
  253.6 50.1 all-gather.10
  334.2 54.6 reduce-scatter.6
  391.1 65.3 reduce-scatter.8
  458.8 31.5 reduce-scatter.12
  492.7 51.7 reduce-scatter.10
  608.8 33.1 reduce-scatter.16
  644.3 42.1 reduce-scatter.14

commit v7 on v6

--- a/solution.py
+++ b/solution.py
@@ -205,11 +205,13 @@
         lower = swapped(ahead[half:], 1)
         return rows, side, ahead, jnp.concatenate([upper, lower], axis=0)
 
-    def sum_by_distance(own, side, ahead, across):
+    def sum_by_distance(own, side, ahead, across, gate=None):
         half = own.shape[0] // 2
         across = across.astype(low)
         upper = swapped(across[:half], 2).astype(full)
         lower = swapped(across[half:], 1).astype(full)
+        if gate is not None:
+            upper, lower = after((upper, lower), gate)
         side = jnp.concatenate([side[:half] + upper, side[half:]], axis=0).astype(low)
         ahead = jnp.concatenate([ahead[:half], ahead[half:] + lower], axis=0).astype(low)
         return own + swapped(side, 1).astype(full) + swapped(ahead, 2).astype(full)
@@ -250,8 +252,9 @@
     own_heads = jnp.concatenate([half[0] for half in halves], axis=1)
     other_heads = swapped(jnp.concatenate([half[1] for half in halves], axis=1), 2)
     qkv_pieces = pick(own_heads, other_heads)
-    near_gains = lax.all_gather(after(gains, other_heads), dp, axis=2, tiled=True)
-    all_gains = lax.all_gather(near_gains, "section", axis=2, tiled=True)
+    all_gains = after(gains, other_heads)
+    for axis in ("core", "pair", "section"):
+        all_gains = lax.all_gather(all_gains, axis, axis=2, tiled=True)
     out_pieces = exchange_rows(after(w_out[0], other_heads))
 
     def gather(piece):
@@ -267,14 +270,14 @@
     half_hidden = w_down.shape[1] // 2
     half_depth = w_up.shape[1] // 2
     up_turned = lax.all_to_all(
-        share_first(*after((w_up[0, :half_depth], w_up[0, half_depth:]), other_heads)),
+        share_first(*after((w_up[0, :half_depth], w_up[0, half_depth:]), all_gains)),
         dp,
         split_axis=1,
         concat_axis=0,
         tiled=True,
     )
     down_shared = by_distance(
-        share_first(*after((w_down[0, :half_hidden], w_down[0, half_hidden:]), other_heads))
+        share_first(*after((w_down[0, :half_hidden], w_down[0, half_hidden:]), all_gains))
     )
     up_shared = by_distance(up_turned)
 
@@ -290,7 +293,7 @@
     )
 
     up_even, up_odd = column_parts(w_up[0], half_hidden)
-    up_piece, down_piece = after((up_even, w_down[0, :half_hidden]), other_heads)
+    up_piece, down_piece = after((up_even, w_down[0, :half_hidden]), all_gains)
     down_second = gather(
         jnp.where(on_first, to_first(down_piece), w_down[0, half_hidden:])
     )
@@ -351,9 +354,7 @@
         ffn_low = from_slots(ffn_low) if layer else from_sequences(ffn_low)
         hidden_pre = matmul(ffn_low, up_w[layer])
         active_low = gelu_exact(hidden_pre).astype(low)
-        if layer:
-            current = middle + sum_to_slots(matmul(active_low, down_w[layer]))
-        else:
+        if layer == 0:
             current = middle + sum_to_sequence(active_low, down_w[layer], matmul)
         saved.append(
             (
@@ -410,19 +411,22 @@
             blocks = down_grad.reshape(2, 2, half_hidden, feature_width)
             own, ahead = pick(blocks[0, 0], blocks[0, 1])
             side, across = pick(blocks[1, 0], blocks[1, 1])
-            down_half = sum_by_distance(own, side, ahead, across).astype(low)
+            down_blocks = (own, side, ahead, across)
             width = up_grad.shape[1] // 2
             blocks = up_grad.reshape(dp_count, 2, half_depth, 2 * width)
             blocks = [blocks[:, i].reshape(-1, 2 * width) for i in range(2)]
             own, ahead = pick(blocks[0][:, :width], blocks[1][:, :width])
             side, across = pick(blocks[0][:, width:], blocks[1][:, width:])
-            up_half = sum_by_distance(own, side, ahead, across).astype(low)
-            up_half = lax.all_to_all(up_half, dp, split_axis=0, concat_axis=1, tiled=True)
+            up_blocks = (own, side, ahead, across)
         gain_ffn_grad = jnp.sum(ffn_grad * unit_mid, axis=0)
         grad_middle = grad_rows + norm_back(
             unit_mid, inverse_mid, ffn_grad * all_gains[layer, 2]
         )
         middle_low = from_slots(grad_middle.astype(low))
+        if layer == 0:
+            up_half = sum_by_distance(*up_blocks, middle_low).astype(low)
+            up_half = lax.all_to_all(up_half, dp, split_axis=0, concat_axis=1, tiled=True)
+            down_half = sum_by_distance(*down_blocks, middle_low).astype(low)
         grad_heads = split_heads(matmul_nt(middle_low, out_w[layer]).astype(low))
         out_piece = scatter(by_device(matmul_tn(attended_low, middle_low)).astype(low))
         grad_query, grad_key, grad_value = attend_backward(
@@ -457,6 +461,7 @@
         scaled = media_part * all_gains[layer, 0]
         media_scaled = scaled if media_scaled is None else media_scaled + scaled
         gain_rows[layer] = jnp.stack([gain_media_grad, gain_latent_grad, gain_ffn_grad])
+    current = middle + sum_to_slots(matmul(after(saved[1][12], latent_part), down_w[1]))
     latents_out = to_columns(current)
     latent_grad = to_columns(after(grad_rows, pieces[1]))
     media_rows = seq_rows // section_count

time: 755 us -> 777 us (1.029)
  waiting for transfers between devices: 124 us -> 149 us
  blocking collectives: 166 us -> 142 us
  other arithmetic: 87.3 us -> 102 us
    ppermute x26, waiting for transfers between devices: 50.7 us -> 26.3 us  [swapped(): return lax.ppermute(value, 'section', pairs)]
    all_gather x4, blocking collectives: 60.1 us -> 44.6 us  [from_slots(): return lax.all_gather(rows, 'section', axis=0, tiled=True)]
    ppermute x4, waiting for transfers between devices: 0.01 us -> 15.2 us  [to_second(): return lax.ppermute(value, 'section', [(0, 2), (1, 3)])]
    all_to_all x5, waiting for transfers between devices: 13.4 us -> 27.9 us  [sum_to_slots(): arrived = lax.all_to_all(blocks, 'section', split_axis=0, concat_axis=0)]
    all_gather x2 -> x3, blocking collectives: 50.3 us -> 37.8 us  [per_device(): all_gains = lax.all_gather(all_gains, axis, axis=2, tiled=True)]
    all_to_all x2, waiting for transfers between devices: 13.3 us -> 25 us  [to_columns(): lax.all_to_all(rows.astype(low), 'section', split_axis=1, concat_axis=0,...]
    convert_element_type x2 -> x7, other arithmetic: 4.32 us -> 12.4 us  [the longest x2 3.65 us: sum_by_distance(): upper = swapped(across[:half], 2).astype(full)]
    unnamed x292 -> x258, local copies, waits for them, and re-layouts: 21.8 us -> 21.1 us
  transfers between devices with their start and end apart: 65 -> 65, of which waited for: 23 -> 18; matrix products, arithmetic and copies ran while one was open for 40% -> 41% of each run, Pallas kernels for 0% -> 0%
where the time goes in v7:
time: 777 us; the launch traced here: 765 us
  matrix products  150 us (19%)
  waiting for transfers between devices  149 us (19%)
  blocking collectives  142 us (18%)
  starting transfers between devices  117 us (15%)
  other arithmetic  102 us (13%)
  local copies, waits for them, and re-layouts  88.7 us (11%)
  between operations  16.8 us (2%)
    dot_general x17, matrix products, matmul_nt(): lax.dot_general(left, right, (((1,), (1,)), ((), ())), preferred_element_...  53.3 us
    all_gather x2, blocking collectives, from_sequences(): near = lax.all_gather(rows, 'pair', axis=0, tiled=True)  46.3 us
    dot_general x13, matrix products, matmul(): return jnp.dot(left, right, preferred_element_type=full)  45.5 us
    all_gather x4, blocking collectives, from_slots(): return lax.all_gather(rows, 'section', axis=0, tiled=True)  44.6 us
    all_gather x3, blocking collectives, per_device(): all_gains = lax.all_gather(all_gains, axis, axis=2, tiled=True)  37.8 us
    ppermute x26, starting transfers between devices, swapped(): return lax.ppermute(value, 'section', pairs)  37 us
    dot_general x8, matrix products, matmul_tn(): lax.dot_general(left, right, (((0,), (0,)), ((), ())), preferred_element_...  29.9 us
    all_to_all x5, waiting for transfers between devices, sum_to_slots(): arrived = lax.all_to_all(blocks, 'section', split_axis=0, concat_axis=0)  27.9 us
  transfers between devices with their start and end apart: 65, of which 18 were waited for; matrix products, arithmetic and copies ran while one was open for 41% of the time, Pallas kernels for 0%

profile of v7, /device:TPU:0, one launch (start us, length us, event | category | flops | bytes accessed | tf_op | source)
XLA Modules:
  0.0 765.4 jit_solution(11136856361576528967)
XLA Ops:
  12.6 10.2 %collective-permute-done = bf16[192,1152]{1,0:T(8,128)(2,1)S(1)} collective-permute-done((bf16[192,1152]{1,0:T(8,128)(2,1)S(1)}, bf16[192,1152]{1,0:T(8,128)(2,1)S(1)}, u32[]{:S(2)}, u32[]{:S(2)}) %collective-permute-start) | collective-permute-done | bytes 442400 | tf_op jit(solution)/shard_map/ppermute | solution.py:118
  32.6 7.4 slice_reduce_fusion
  54.2 27.6 %all_gather.40 = f32[2,3,384]{1,0,2:T(2,128)} all-gather(f32[2,3,96]{1,0,2:T(2,128)S(1)} %all_gather.39), channel_id=1, replica_groups=mesh['section'=4,'pair'=4,'core'=2] {'pair'}, dimensions={2}, use_global_device_ids=true | all-gather | bytes 11520 | tf_op jit(solution)/shard_map/all_gather | solution.py:257
  83.0 8.2 %all_gather.41 = f32[2,3,1536]{2,0,1:T(2,128)S(1)} all-gather(f32[2,3,384]{2,0,1:T(2,128)S(1)} %copy.178), channel_id=1, replica_groups=mesh['section'=4,'pair'=4,'core'=2] {'section'}, dimensions={2}, use_global_device_ids=true | all-gather | bytes 46080 | tf_op jit(solution)/shard_map/all_gather | solution.py:257
  101.2 15.2 %collective-permute-done.9 = bf16[192,1536]{1,0:T(8,128)(2,1)S(1)} collective-permute-done((bf16[192,1536]{1,0:T(8,128)(2,1)}, bf16[192,1536]{1,0:T(8,128)(2,1)S(1)}, u32[]{:S(2)}, u32[]{:S(2)}) %collective-permute-start.9) | collective-permute-done | bytes 589856 | tf_op jit(solution)/shard_map/ppermute | solution.py:124
  139.5 17.8 %all-to-all-done.1 = bf16[96,8,384]{2,0,1:T(8,128)(2,1)} async-done(((bf16[96,8,384]{2,0,1:T(8,128)(2,1)}), bf16[96,8,384]{2,0,1:T(8,128)(2,1)}, u32[]{:S(2)}, u32[]{:S(2)}) %all-to-all-start.1) | async-done | bytes 589856 | tf_op jit(solution)/shard_map/all_to_all | solution.py:272
  199.7 6.8 collective-permute-done.7
  208.3 17.8 %all_gather.43 = bf16[256,1536]{1,0:T(8,128)(2,1)S(1)} all-gather(bf16[64,1536]{1,0:T(8,128)(2,1)S(1)} %multiply_convert_fusion.9), channel_id=1, replica_groups=mesh['section'=4,'pair'=4,'core'=2] {'pair'}, dimensions={0}, use_global_device_ids=true | all-gather | bytes 983040 | tf_op jit(solution)/shard_map/all_gather | solution.py:189
  244.2 10.4 %collective-permute-done.16 = bf16[192,1536]{1,0:T(8,128)(2,1)} collective-permute-done((bf16[192,1536]{1,0:T(8,128)(2,1)S(1)}, bf16[192,1536]{1,0:T(8,128)(2,1)}, u32[]{:S(2)}, u32[]{:S(2)}) %collective-permute-start.16) | collective-permute-done | bytes 589856 | tf_op jit(solution)/shard_map/ppermute | solution.py:127
  268.4 11.2 %all_gather.45 = bf16[256,1536]{1,0:T(8,128)(2,1)S(1)} all-gather(bf16[64,1536]{1,0:T(8,128)(2,1)S(1)} %multiply_convert_fusion.8), channel_id=1, replica_groups=mesh['section'=4,'pair'=4,'core'=2] {'section'}, dimensions={0}, use_global_device_ids=true | all-gather | bytes 983040 | tf_op jit(solution)/shard_map/all_gather | solution.py:180
  297.3 13.1 %all_to_all.114 = bf16[4,64,1536]{2,1,0:T(8,128)(2,1)S(1)} all-to-all(bf16[4,64,1536]{2,1,0:T(8,128)(2,1)S(1)} %bitcast.362), channel_id=1, replica_groups=mesh['section'=4,'pair'=4,'core'=2] {'section'}, dimensions={0} | all-to-all | bytes 1572864 | tf_op jit(solution)/shard_map/all_to_all | solution.py:176
  311.0 11.4 %all_gather.46 = bf16[256,1536]{1,0:T(8,128)(2,1)S(1)} all-gather(bf16[64,1536]{1,0:T(8,128)(2,1)S(1)} %multiply_convert_fusion.7), channel_id=1, replica_groups=mesh['section'=4,'pair'=4,'core'=2] {'section'}, dimensions={0}, use_global_device_ids=true | all-gather | bytes 983040 | tf_op jit(solution)/shard_map/all_gather | solution.py:180
  322.4 7.9 %multiply_convert_fusion.5 = (bf16[256,1536]{1,0:T(8,128)(2,1)S(1)}, f32[256,1536]{1,0:T(8,128)}) fusion(bf16[256,1536]{1,0:T(8,128)(2,1)S(1)} %all_gather.46, bf16[1536,1536]{1,0:T(8,128)(2,1)} %all-gather.9.cloned.1.call-done), kind=kOutput, calls=%fused_computation.118 | convolution fusion | flops 1233518592 | bytes 7864320 | tf_op jit(solution)/shard_map/dot_general | solution.py:35
  335.0 7.7 %add_convert_fusion.2 = bf16[256,1536]{1,0:T(8,128)(2,1)S(1)} fusion(bf16[1536,1536]{1,0:T(8,128)(2,1)} %all-gather.11.cloned.1.call-done, bf16[256,1536]{1,0:T(8,128)(2,1)} %param.23, f32[256,1536]{1,0:T(8,128)} %get-tuple-element.162), kind=kOutput, calls=%fused_computation.117 | convolution fusion | flops 1236271104 | bytes 7864320 | tf_op jit(solution)/shard_map/dot_general | solution.py:39
  357.4 8.0 %all-to-all-done.4 = bf16[4,64,1536]{2,1,0:T(8,128)(2,1)} async-done(((bf16[4,64,1536]{2,1,0:T(8,128)(2,1)}), bf16[4,64,1536]{2,1,0:T(8,128)(2,1)}, u32[]{:S(2)}, u32[]{:S(2)}) %all-to-all-start.4) | async-done | bytes 786464 | tf_op jit(solution)/shard_map/all_to_all | solution.py:176
  368.8 11.2 %all_gather.49 = bf16[256,1536]{1,0:T(8,128)(2,1)S(1)} all-gather(bf16[64,1536]{1,0:T(8,128)(2,1)S(1)} %get-tuple-element.71), channel_id=1, replica_groups=mesh['section'=4,'pair'=4,'core'=2] {'section'}, dimensions={0}, use_global_device_ids=true | all-gather | bytes 983040 | tf_op jit(solution)/shard_map/all_gather | solution.py:180
  404.8 9.3 %convolution_convert_fusion.1 = bf16[1536,1152]{1,0:T(8,128)(2,1)} fusion(bf16[256,1536]{1,0:T(8,128)(2,1)S(1)} %copy-done.88, bf16[1024,1536]{1,0:T(8,128)(2,1)} %get-tuple-element.93, bf16[256,384]{0,1:T(8,128)(2,1)S(1)} %bitcast.402, bf16[1280,384]{0,1:T(8,128)(2,1)S(1)} %bitcast.348, bf16[1280,384]{0,1:T(8,128)(2,1)} %bitcast.358), kind=kOutput, calls=%fused_computation.3 | convolution fusion | flops 4551278592 | bytes 9633792 | tf_op jit(solution)/shard_map/dot_general | solution.py:43
  417.9 28.5 %all_gather.50 = bf16[256,1536]{1,0:T(8,128)(2,1)S(1)} all-gather(bf16[64,1536]{1,0:T(8,128)(2,1)S(1)} %get-tuple-element.69), channel_id=1, replica_groups=mesh['section'=4,'pair'=4,'core'=2] {'pair'}, dimensions={0}, use_global_device_ids=true | all-gather | bytes 983040 | tf_op jit(solution)/shard_map/all_gather | solution.py:189
  513.5 10.8 %all_gather.51 = bf16[256,1536]{1,0:T(8,128)(2,1)S(1)} all-gather(bf16[64,1536]{1,0:T(8,128)(2,1)S(1)} %get-tuple-element.67), channel_id=1, replica_groups=mesh['section'=4,'pair'=4,'core'=2] {'section'}, dimensions={0}, use_global_device_ids=true | all-gather | bytes 983040 | tf_op jit(solution)/shard_map/all_gather | solution.py:180
  561.9 8.9 %multiply_reduce_fusion.1 = (f32[1536]{0:T(1024)S(1)}, f32[1536]{0:T(1024)S(1)}, f32[1024,1536]{1,0:T(8,128)}, f32[1024,1536]{1,0:T(8,128)}) fusion(bf16[1024,1536]{1,0:T(8,128)(2,1)S(1)} %copy-done.3, f32[1024]{0:T(1024)S(1)} %add_rsqrt_fusion, f32[1024]{0:T(1024)S(1)} %copy-done.109, f32[1024,1536]{1,0:T(8,128)} %convolution_add_fusion.1, ...), kind=kOutput, calls=%fused_computation.10 | convolution fusion | flops 1225257984 | bytes 30310400 | tf_op jit(solution)/shard_map/dot_general | solution.py:39
  580.9 8.4 %convolution_convert_fusion = bf16[1536,1152]{1,0:T(8,128)(2,1)} fusion(bf16[256,1536]{1,0:T(8,128)(2,1)} %fusion.55, bf16[1024,1536]{1,0:T(8,128)(2,1)S(1)} %copy-done.44, bf16[256,384]{0,1:T(8,128)(2,1)S(1)} %bitcast.400, bf16[1280,384]{0,1:T(8,128)(2,1)S(1)} %bitcast.346, bf16[1280,384]{0,1:T(8,128)(2,1)S(1)} %bitcast.356), kind=kOutput, calls=%fused_computation.2 | convolution fusion | flops 4551278592 | bytes 9633792 | tf_op jit(solution)/shard_map/dot_general | solution.py:43
  617.4 19.9 %all-to-all-done.7 = bf16[4,64,1536]{2,1,0:T(8,128)(2,1)} async-done(((bf16[4,64,1536]{2,1,0:T(8,128)(2,1)}), bf16[4,64,1536]{2,1,0:T(8,128)(2,1)}, u32[]{:S(2)}, u32[]{:S(2)}) %all-to-all-start.7) | async-done | bytes 786464 | tf_op jit(solution)/shard_map/all_to_all | solution.py:176
  657.0 9.7 %all-to-all-done.13 = bf16[8,96,384]{2,1,0:T(8,128)(2,1)S(1)} async-done(((bf16[8,96,384]{2,1,0:T(8,128)(2,1)}), bf16[8,96,384]{2,1,0:T(8,128)(2,1)S(1)}, u32[]{:S(2)}, u32[]{:S(2)}) %all-to-all-start.13) | async-done | bytes 589856 | tf_op jit(solution)/shard_map/all_to_all | solution.py:428
  682.5 25.0 %all-to-all-done.10 = bf16[64,4,384]{2,0,1:T(8,128)(2,1)S(1)} async-done(((bf16[64,4,384]{2,0,1:T(8,128)(2,1)}), bf16[64,4,384]{2,0,1:T(8,128)(2,1)S(1)}, u32[]{:S(2)}, u32[]{:S(2)}) %all-to-all-start.10) | async-done | bytes 196640 | tf_op jit(solution)/shard_map/all_to_all | solution.py:183
  (649 shorter events, 436.1 us)
Async XLA Ops:
  7.2 151.4 %all-gather.5.cloned.1.call-start = ((), (), s32[]{:S(2)}) async-start(), calls=%async_computation.20 | async-start | bytes 5308416 | tf_op jit(solution)/shard_map/all_gather | solution.py:261
  29.3 227.4 %all-gather.7.cloned.1.call-start = ((), (), s32[]{:S(2)}) async-start(), calls=%async_computation.21 | async-start | bytes 5308416 | tf_op jit(solution)/shard_map/all_gather | solution.py:261
  95.0 31.5 %collective-permute-start.15 = (bf16[192,1536]{1,0:T(8,128)(2,1)}, bf16[192,1536]{1,0:T(8,128)(2,1)}, u32[]{:S(2)}, u32[]{:S(2)}) collective-permute-start(bf16[192,1536]{1,0:T(8,128)(2,1)} %reshape_squeeze.16), channel_id=1, source_target_pairs={{16,0},{24,8},{17,1},{25,9},{18,2},{26,10},{19,3},{27,11},{20,4},{... | collective-permute-start | bytes 1769480 | tf_op jit(solution)/shard_map/ppermute | solution.py:127
  122.1 35.1 %all-to-all-start.1 = ((bf16[96,8,384]{2,0,1:T(8,128)(2,1)}), bf16[96,8,384]{2,0,1:T(8,128)(2,1)}, u32[]{:S(2)}, u32[]{:S(2)}) async-start(bf16[96,8,384]{2,0,1:T(8,128)(2,1)} %bitcast.298), calls=%async_computation.1 | async-start | bytes 1179648 | tf_op jit(solution)/shard_map/all_to_all | solution.py:272
  126.4 196.1 %all-gather.9.cloned.1.call-start = ((), (), s32[]{:S(2)}) async-start(), calls=%async_computation.22 | async-start | bytes 5308416 | tf_op jit(solution)/shard_map/all_gather | solution.py:261
  157.2 34.4 %collective-permute-start.6 = (bf16[768,384]{1,0:T(8,128)(2,1)}, bf16[768,384]{1,0:T(8,128)(2,1)}, u32[]{:S(2)}, u32[]{:S(2)}) collective-permute-start(bf16[768,384]{1,0:T(8,128)(2,1)} %bitcast.22), channel_id=1, source_target_pairs={{0,8},{8,0},{16,24},{24,16},{1,9},{9,1},{17,25},{25,17},{2,10},{10... | collective-permute-start | bytes 1769480 | tf_op jit(solution)/shard_map/ppermute | solution.py:118
  157.7 36.9 %collective-permute-start.5 = (bf16[768,384]{1,0:T(8,128)(2,1)}, bf16[768,384]{1,0:T(8,128)(2,1)}, u32[]{:S(2)}, u32[]{:S(2)}) collective-permute-start(bf16[768,384]{1,0:T(8,128)(2,1)} %bitcast.22), channel_id=1, source_target_pairs={{0,16},{8,24},{16,0},{24,8},{1,17},{9,25},{17,1},{25,9},{2,18},{10... | collective-permute-start | bytes 1769480 | tf_op jit(solution)/shard_map/ppermute | solution.py:118
  244.2 90.7 %all-gather.11.cloned.1.call-start = ((), (), s32[]{:S(2)}) async-start(), calls=%async_computation.23 | async-start | bytes 5308416 | tf_op jit(solution)/shard_map/all_gather | solution.py:261
  256.6 197.8 %reduce-scatter.7.cloned.1.call-start = ((), (), s32[]{:S(2)}) async-start(), calls=%async_computation.24 | async-start | bytes 5308416 | tf_op jit(solution)/shard_map/reduce_scatter | solution.py:378
  334.9 122.3 %reduce-scatter.9.cloned.1.call-start = ((), (), s32[]{:S(2)}) async-start(), calls=%async_computation.25 | async-start | bytes 5308416 | tf_op jit(solution)/shard_map/reduce_scatter | solution.py:378
  357.3 294.0 %reduce-scatter.13.cloned.1.call-start = ((), (), s32[]{:S(2)}) async-start(), calls=%async_computation.27 | async-start | bytes 1327104 | tf_op jit(solution)/shard_map/reduce_scatter | solution.py:378
  404.7 246.6 %reduce-scatter.11.cloned.1.call-start = ((), (), s32[]{:S(2)}) async-start(), calls=%async_computation.26 | async-start | bytes 3981312 | tf_op jit(solution)/shard_map/reduce_scatter | solution.py:378
  494.7 225.7 %collective-permute-start.41 = (bf16[192,1536]{1,0:T(8,128)(2,1)}, bf16[192,1536]{1,0:T(8,128)(2,1)}, u32[]{:S(2)}, u32[]{:S(2)}) collective-permute-start(bf16[192,1536]{1,0:T(8,128)(2,1)} %reduce-scatter.7.cloned.1.call-done), channel_id=1, source_target_pairs={{0,16},{8,24},{1,17},{9,25},{2,18},{10,26},{3,19},{11,27},{4,20},{... | collective-permute-start | bytes 1769480 | tf_op jit(solution)/shard_map/ppermute | solution.py:124
  544.7 55.5 %collective-permute-start.39 = (bf16[192,1536]{1,0:T(8,128)(2,1)}, bf16[192,1536]{1,0:T(8,128)(2,1)}, u32[]{:S(2)}, u32[]{:S(2)}) collective-permute-start(bf16[192,1536]{1,0:T(8,128)(2,1)} %pad_maximum_fusion.20), channel_id=1, source_target_pairs={{0,16},{8,24},{16,0},{24,8},{1,17},{9,25},{17,1},{25,9},{2,18},{10... | collective-permute-start | bytes 1769480 | tf_op jit(solution)/shard_map/ppermute | solution.py:118
  547.1 54.9 %collective-permute-start.38 = (bf16[192,1536]{1,0:T(8,128)(2,1)}, bf16[192,1536]{1,0:T(8,128)(2,1)}, u32[]{:S(2)}, u32[]{:S(2)}) collective-permute-start(bf16[192,1536]{1,0:T(8,128)(2,1)} %pad_maximum_fusion.19), channel_id=1, source_target_pairs={{0,8},{8,0},{16,24},{24,16},{1,9},{9,1},{17,25},{25,17},{2,10},{10... | collective-permute-start | bytes 1769480 | tf_op jit(solution)/shard_map/ppermute | solution.py:118
  554.1 51.9 %all-to-all-start.9 = ((bf16[4,64,1536]{2,1,0:T(8,128)(2,1)}), bf16[4,64,1536]{2,1,0:T(8,128)(2,1)}, u32[]{:S(2)}, u32[]{:S(2)}) async-start(bf16[4,64,1536]{2,1,0:T(8,128)(2,1)} %bitcast.361), calls=%async_computation.11 | async-start | bytes 1572864 | tf_op jit(solution)/shard_map/all_to_all | solution.py:176
  558.4 174.0 %reduce-scatter.17.cloned.1.call-start = ((), (), s32[]{:S(2)}) async-start(), calls=%async_computation.29 | async-start | bytes 1327104 | tf_op jit(solution)/shard_map/reduce_scatter | solution.py:378
  570.8 173.6 %reduce-scatter.15.cloned.1.call-start = ((), (), s32[]{:S(2)}) async-start(), calls=%async_computation.28 | async-start | bytes 3981312 | tf_op jit(solution)/shard_map/reduce_scatter | solution.py:378
  600.2 54.0 %collective-permute-start.22 = (bf16[256,1536]{1,0:T(8,128)(2,1)}, bf16[256,1536]{1,0:T(8,128)(2,1)}, u32[]{:S(2)}, u32[]{:S(2)}) collective-permute-start(bf16[256,1536]{1,0:T(8,128)(2,1)} %pad_maximum_fusion.11), channel_id=1, source_target_pairs={{0,16},{8,24},{16,0},{24,8},{1,17},{9,25},{17,1},{25,9},{2,18},{10... | collective-permute-start | bytes 2359304 | tf_op jit(solution)/shard_map/ppermute | solution.py:118
  602.0 52.1 %collective-permute-start.20 = (bf16[256,1536]{1,0:T(8,128)(2,1)}, bf16[256,1536]{1,0:T(8,128)(2,1)}, u32[]{:S(2)}, u32[]{:S(2)}) collective-permute-start(bf16[256,1536]{1,0:T(8,128)(2,1)} %pad_maximum_fusion.10), channel_id=1, source_target_pairs={{0,8},{8,0},{16,24},{24,16},{1,9},{9,1},{17,25},{25,17},{2,10},{10... | collective-permute-start | bytes 2359304 | tf_op jit(solution)/shard_map/ppermute | solution.py:118
  613.4 107.1 %collective-permute-start.40 = (bf16[192,1536]{1,0:T(8,128)(2,1)}, bf16[192,1536]{1,0:T(8,128)(2,1)}, u32[]{:S(2)}, u32[]{:S(2)}) collective-permute-start(bf16[192,1536]{1,0:T(8,128)(2,1)} %fusion.78), channel_id=1, source_target_pairs={{16,0},{24,8},{17,1},{25,9},{18,2},{26,10},{19,3},{27,11},{20,4},{... | collective-permute-start | bytes 1769480 | tf_op jit(solution)/shard_map/ppermute | solution.py:127
  672.7 51.3 %collective-permute-start.25 = (bf16[256,1536]{1,0:T(8,128)(2,1)}, bf16[256,1536]{1,0:T(8,128)(2,1)}, u32[]{:S(2)}, u32[]{:S(2)}) collective-permute-start(bf16[256,1536]{1,0:T(8,128)(2,1)} %multiply_convert_fusion.4), channel_id=1, source_target_pairs={{0,16},{8,24},{16,0},{24,8},{1,17},{9,25},{17,1},{25,9},{2,18},{10... | collective-permute-start | bytes 2359304 | tf_op jit(solution)/shard_map/ppermute | solution.py:118
  673.3 53.7 %collective-permute-start.23 = (bf16[256,1536]{1,0:T(8,128)(2,1)}, bf16[256,1536]{1,0:T(8,128)(2,1)}, u32[]{:S(2)}, u32[]{:S(2)}) collective-permute-start(bf16[256,1536]{1,0:T(8,128)(2,1)} %multiply_convert_fusion.4), channel_id=1, source_target_pairs={{0,8},{8,0},{16,24},{24,16},{1,9},{9,1},{17,25},{25,17},{2,10},{10... | collective-permute-start | bytes 2359304 | tf_op jit(solution)/shard_map/ppermute | solution.py:118
  674.7 54.9 %collective-permute-start.34 = (bf16[96,3072]{1,0:T(8,128)(2,1)}, bf16[96,3072]{1,0:T(8,128)(2,1)}, u32[]{:S(2)}, u32[]{:S(2)}) collective-permute-start(bf16[96,3072]{1,0:T(8,128)(2,1)} %bitcast.150), channel_id=1, source_target_pairs={{16,0},{24,8},{17,1},{25,9},{18,2},{26,10},{19,3},{27,11},{20,4},{... | collective-permute-start | bytes 1769480 | tf_op jit(solution)/shard_map/ppermute | solution.py:127
  (168 other events, 1722.3 us)
Sparse Core Ops, SparseCore 0:
  29.4 65.5 all-gather.4
  96.6 63.0 all-gather.6
  161.3 50.4 all-gather.8
  256.7 50.6 all-gather.10
  335.0 54.0 reduce-scatter.6
  391.3 65.9 reduce-scatter.8
  459.5 31.9 reduce-scatter.12
  493.9 43.1 reduce-scatter.10
  571.0 33.8 reduce-scatter.16
  607.1 41.7 reduce-scatter.14

commit v8 on v7

--- a/solution.py
+++ b/solution.py
@@ -252,7 +252,10 @@
     own_heads = jnp.concatenate([half[0] for half in halves], axis=1)
     other_heads = swapped(jnp.concatenate([half[1] for half in halves], axis=1), 2)
     qkv_pieces = pick(own_heads, other_heads)
-    all_gains = after(gains, other_heads)
+    half_hidden = w_down.shape[1] // 2
+    half_depth = w_up.shape[1] // 2
+    up_share = share_first(w_up[0, :half_depth], w_up[0, half_depth:])
+    all_gains = after(gains, (other_heads, up_share))
     for axis in ("core", "pair", "section"):
         all_gains = lax.all_gather(all_gains, axis, axis=2, tiled=True)
     out_pieces = exchange_rows(after(w_out[0], other_heads))
@@ -267,15 +270,7 @@
     qkv_w = [weight[:, : 3 * inner] for weight in stacked]
     out_w = [unfold(weight[:, 3 * inner :]) for weight in stacked]
 
-    half_hidden = w_down.shape[1] // 2
-    half_depth = w_up.shape[1] // 2
-    up_turned = lax.all_to_all(
-        share_first(*after((w_up[0, :half_depth], w_up[0, half_depth:]), all_gains)),
-        dp,
-        split_axis=1,
-        concat_axis=0,
-        tiled=True,
-    )
+    up_turned = lax.all_to_all(up_share, dp, split_axis=1, concat_axis=0, tiled=True)
     down_shared = by_distance(
         share_first(*after((w_down[0, :half_hidden], w_down[0, half_hidden:]), all_gains))
     )
@@ -425,7 +420,6 @@
         middle_low = from_slots(grad_middle.astype(low))
         if layer == 0:
             up_half = sum_by_distance(*up_blocks, middle_low).astype(low)
-            up_half = lax.all_to_all(up_half, dp, split_axis=0, concat_axis=1, tiled=True)
             down_half = sum_by_distance(*down_blocks, middle_low).astype(low)
         grad_heads = split_heads(matmul_nt(middle_low, out_w[layer]).astype(low))
         out_piece = scatter(by_device(matmul_tn(attended_low, middle_low)).astype(low))
@@ -440,6 +434,8 @@
             + matmul_nt(grad_key[seq_rows:], key_w[layer])
             + matmul_nt(grad_value[seq_rows:], value_w[layer])
         )
+        if layer == 0:
+            latent_part = after(latent_part, up_half)
         latent_grad_rows = sum_to_slots(latent_part)
         gain_latent_grad = jnp.sum(latent_grad_rows * unit_in, axis=0)
         grad_rows = grad_middle + norm_back(
@@ -450,6 +446,9 @@
             [jnp.pad(grad_query, ((seq_rows, 0), (0, 0))), grad_key, grad_value], axis=1
         )
         qkv_grad = matmul_tn(both_low, all_grads).astype(low)
+        if layer == 0:
+            up_half, qkv_grad = lax.optimization_barrier((up_half, qkv_grad))
+            up_half = lax.all_to_all(up_half, dp, split_axis=0, concat_axis=1, tiled=True)
         pieces[layer] = (scatter(qkv_grad), out_piece)
         if layer > 0:
             grad_low = from_sequences(grad_rows.astype(low))
@@ -461,9 +460,14 @@
         scaled = media_part * all_gains[layer, 0]
         media_scaled = scaled if media_scaled is None else media_scaled + scaled
         gain_rows[layer] = jnp.stack([gain_media_grad, gain_latent_grad, gain_ffn_grad])
-    current = middle + sum_to_slots(matmul(after(saved[1][12], latent_part), down_w[1]))
-    latents_out = to_columns(current)
-    latent_grad = to_columns(after(grad_rows, pieces[1]))
+    last = matmul(after(saved[1][12], latent_part), down_w[1])
+    start = section * slot_rows
+    rows = lax.dynamic_slice_in_dim(last, start, slot_rows, 0) + middle
+    last = lax.dynamic_update_slice_in_dim(last, rows, start, 0).astype(low)
+    last = last.reshape(latent_rows, section_count, -1)
+    last = lax.all_to_all(last, "section", split_axis=1, concat_axis=0)
+    latents_out = jnp.sum(last.astype(full), axis=0)
+    latent_grad = to_columns(after(grad_rows, (pieces[1], up_half)))
     media_rows = seq_rows // section_count
     media_sum = sum_over_sections(media_scaled)
     own_unit = lax.dynamic_slice_in_dim(media_unit, section * media_rows, media_rows, 0)

time: 777 us -> 770 us (level)
  waiting for transfers between devices: 149 us -> 135 us
  local copies, waits for them, and re-layouts: 88.7 us -> 97.5 us
    ppermute x26, waiting for transfers between devices: 26.3 us -> 51.9 us  [swapped(): return lax.ppermute(value, 'section', pairs)]
    all_to_all x1 -> x2, waiting for transfers between devices: 17.8 us -> 2.88 us  [the longest x1 2.88 us: per_device(): last = lax.all_to_all(last, 'section', split_axis=1, concat_axis=0)]
    all_to_all x2 -> x1, waiting for transfers between devices: 25 us -> 13.9 us  [to_columns(): lax.all_to_all(rows.astype(low), 'section', split_axis=1, concat_axis=0,...]
    all_to_all x1, waiting for transfers between devices: 9.72 us -> 20.2 us  [per_device(): lax.all_to_all(up_half, dp, split_axis=0, concat_axis=1, tiled=True)]
    ppermute x4, starting transfers between devices: 10.5 us -> 20.3 us  [to_second(): return lax.ppermute(value, 'section', [(0, 2), (1, 3)])]
    ppermute x4, waiting for transfers between devices: 15.2 us -> 6.07 us  [to_second(): return lax.ppermute(value, 'section', [(0, 2), (1, 3)])]
    all_gather x3, blocking collectives: 37.8 us -> 29 us  [per_device(): all_gains = lax.all_gather(all_gains, axis, axis=2, tiled=True)]
    all_to_all x5 -> x4, waiting for transfers between devices: 27.9 us -> 20.9 us  [sum_to_slots(): arrived = lax.all_to_all(blocks, 'section', split_axis=0, concat_axis=0)]
  transfers between devices with their start and end apart: 65 -> 64, of which waited for: 18 -> 21; matrix products, arithmetic and copies ran while one was open for 41% -> 43% of each run, Pallas kernels for 0% -> 0%
where the time goes in v8:
time: 770 us; the launch traced here: 758 us
  matrix products  152 us (20%)
  blocking collectives  137 us (18%)
  waiting for transfers between devices  135 us (18%)
  starting transfers between devices  118 us (15%)
  other arithmetic  102 us (13%)
  local copies, waits for them, and re-layouts  97.5 us (13%)
  between operations  16.8 us (2%)
    dot_general x17, matrix products, matmul_nt(): lax.dot_general(left, right, (((1,), (1,)), ((), ())), preferred_element_...  53.1 us
    ppermute x26, waiting for transfers between devices, swapped(): return lax.ppermute(value, 'section', pairs)  51.9 us
    all_gather x2, blocking collectives, from_sequences(): near = lax.all_gather(rows, 'pair', axis=0, tiled=True)  48.4 us
    all_gather x4, blocking collectives, from_slots(): return lax.all_gather(rows, 'section', axis=0, tiled=True)  48 us
    dot_general x13, matrix products, matmul(): return jnp.dot(left, right, preferred_element_type=full)  46 us
    ppermute x26, starting transfers between devices, swapped(): return lax.ppermute(value, 'section', pairs)  36.2 us
    dot_general x8, matrix products, matmul_tn(): lax.dot_general(left, right, (((0,), (0,)), ((), ())), preferred_element_...  30.7 us
    all_gather x3, blocking collectives, per_device(): all_gains = lax.all_gather(all_gains, axis, axis=2, tiled=True)  29 us
  transfers between devices with their start and end apart: 64, of which 21 were waited for; matrix products, arithmetic and copies ran while one was open for 43% of the time, Pallas kernels for 0%

profile of v8, /device:TPU:0, one launch (start us, length us, event | category | flops | bytes accessed | tf_op | source)
XLA Modules:
  0.0 757.9 jit_solution(11638463895416369890)
XLA Ops:
  12.6 10.2 %collective-permute-done = bf16[192,1152]{1,0:T(8,128)(2,1)S(1)} collective-permute-done((bf16[192,1152]{1,0:T(8,128)(2,1)S(1)}, bf16[192,1152]{1,0:T(8,128)(2,1)S(1)}, u32[]{:S(2)}, u32[]{:S(2)}) %collective-permute-start) | collective-permute-done | bytes 442400 | tf_op jit(solution)/shard_map/ppermute | solution.py:118
  31.6 11.0 %collective-permute-start.1 = (bf16[96,3072]{1,0:T(8,128)(2,1)}, bf16[96,3072]{1,0:T(8,128)(2,1)}, u32[]{:S(2)}, u32[]{:S(2)}) collective-permute-start(bf16[96,3072]{1,0:T(8,128)(2,1)} %slice_bitcast_fusion.4), channel_id=1, source_target_pairs={{0,16},{8,24},{1,17},{9,25},{2,18},{10,26},{3,19},{11,27},{4,20},{... | collective-permute-start | bytes 1769480 | tf_op jit(solution)/shard_map/ppermute | solution.py:124
  54.1 7.5 slice_reduce_fusion
  72.4 19.0 %all_gather.40 = f32[2,3,384]{1,0,2:T(2,128)} all-gather(f32[2,3,96]{1,0,2:T(2,128)S(1)} %all_gather.39), channel_id=1, replica_groups=mesh['section'=4,'pair'=4,'core'=2] {'pair'}, dimensions={2}, use_global_device_ids=true | all-gather | bytes 11520 | tf_op jit(solution)/shard_map/all_gather | solution.py:260
  98.7 8.2 %all_gather.41 = f32[2,3,1536]{2,0,1:T(2,128)S(1)} all-gather(f32[2,3,384]{2,0,1:T(2,128)S(1)} %copy.175), channel_id=1, replica_groups=mesh['section'=4,'pair'=4,'core'=2] {'section'}, dimensions={2}, use_global_device_ids=true | all-gather | bytes 46080 | tf_op jit(solution)/shard_map/all_gather | solution.py:260
  130.0 7.5 collective-permute-done.11
  142.8 14.0 %collective-permute-done.12 = bf16[96,1536]{1,0:T(8,128)(2,1)S(1)} collective-permute-done((bf16[96,1536]{1,0:T(8,128)(2,1)S(1)}, bf16[96,1536]{1,0:T(8,128)(2,1)S(1)}, u32[]{:S(2)}, u32[]{:S(2)}) %collective-permute-start.12) | collective-permute-done | bytes 294944 | tf_op jit(solution)/shard_map/ppermute | solution.py:118
  206.8 20.8 %all_gather.43 = bf16[256,1536]{1,0:T(8,128)(2,1)S(1)} all-gather(bf16[64,1536]{1,0:T(8,128)(2,1)S(1)} %multiply_convert_fusion.9), channel_id=1, replica_groups=mesh['section'=4,'pair'=4,'core'=2] {'pair'}, dimensions={0}, use_global_device_ids=true | all-gather | bytes 983040 | tf_op jit(solution)/shard_map/all_gather | solution.py:189
  247.4 9.7 %collective-permute-done.16 = bf16[192,1536]{1,0:T(8,128)(2,1)} collective-permute-done((bf16[192,1536]{1,0:T(8,128)(2,1)S(1)}, bf16[192,1536]{1,0:T(8,128)(2,1)}, u32[]{:S(2)}, u32[]{:S(2)}) %collective-permute-start.16) | collective-permute-done | bytes 589856 | tf_op jit(solution)/shard_map/ppermute | solution.py:127
  272.2 14.1 %all_gather.45 = bf16[256,1536]{1,0:T(8,128)(2,1)S(1)} all-gather(bf16[64,1536]{1,0:T(8,128)(2,1)S(1)} %multiply_convert_fusion.8), channel_id=1, replica_groups=mesh['section'=4,'pair'=4,'core'=2] {'section'}, dimensions={0}, use_global_device_ids=true | all-gather | bytes 983040 | tf_op jit(solution)/shard_map/all_gather | solution.py:180
  305.6 11.2 %all_to_all.105 = bf16[4,64,1536]{2,1,0:T(8,128)(2,1)S(1)} all-to-all(bf16[4,64,1536]{2,1,0:T(8,128)(2,1)S(1)} %bitcast.353), channel_id=1, replica_groups=mesh['section'=4,'pair'=4,'core'=2] {'section'}, dimensions={0} | all-to-all | bytes 1572864 | tf_op jit(solution)/shard_map/all_to_all | solution.py:176
  317.6 10.9 %all_gather.46 = bf16[256,1536]{1,0:T(8,128)(2,1)S(1)} all-gather(bf16[64,1536]{1,0:T(8,128)(2,1)S(1)} %multiply_convert_fusion.7), channel_id=1, replica_groups=mesh['section'=4,'pair'=4,'core'=2] {'section'}, dimensions={0}, use_global_device_ids=true | all-gather | bytes 983040 | tf_op jit(solution)/shard_map/all_gather | solution.py:180
  328.5 7.9 %multiply_convert_fusion.5 = (bf16[256,1536]{1,0:T(8,128)(2,1)S(1)}, f32[256,1536]{1,0:T(8,128)}) fusion(bf16[256,1536]{1,0:T(8,128)(2,1)S(1)} %all_gather.46, bf16[1536,1536]{1,0:T(8,128)(2,1)} %all-gather.9.cloned.1.call-done), kind=kOutput, calls=%fused_computation.117 | convolution fusion | flops 1233518592 | bytes 7864320 | tf_op jit(solution)/shard_map/dot_general | solution.py:35
  341.2 7.7 %add_convert_fusion.2 = bf16[256,1536]{1,0:T(8,128)(2,1)S(1)} fusion(bf16[1536,1536]{1,0:T(8,128)(2,1)} %all-gather.11.cloned.1.call-done, bf16[256,1536]{1,0:T(8,128)(2,1)} %param.23, f32[256,1536]{1,0:T(8,128)} %get-tuple-element.162), kind=kOutput, calls=%fused_computation.116 | convolution fusion | flops 1236271104 | bytes 7864320 | tf_op jit(solution)/shard_map/dot_general | solution.py:39
  363.7 8.4 %all-to-all-done.4 = bf16[4,64,1536]{2,1,0:T(8,128)(2,1)S(1)} async-done(((bf16[4,64,1536]{2,1,0:T(8,128)(2,1)}), bf16[4,64,1536]{2,1,0:T(8,128)(2,1)S(1)}, u32[]{:S(2)}, u32[]{:S(2)}) %all-to-all-start.4) | async-done | bytes 786464 | tf_op jit(solution)/shard_map/all_to_all | solution.py:176
  374.4 11.6 %all_gather.49 = bf16[256,1536]{1,0:T(8,128)(2,1)S(1)} all-gather(bf16[64,1536]{1,0:T(8,128)(2,1)S(1)} %get-tuple-element.73), channel_id=1, replica_groups=mesh['section'=4,'pair'=4,'core'=2] {'section'}, dimensions={0}, use_global_device_ids=true | all-gather | bytes 983040 | tf_op jit(solution)/shard_map/all_gather | solution.py:180
  411.9 9.3 %convolution_convert_fusion.1 = bf16[1536,1152]{1,0:T(8,128)(2,1)} fusion(bf16[256,1536]{1,0:T(8,128)(2,1)} %copy-done.91, bf16[1024,1536]{1,0:T(8,128)(2,1)} %get-tuple-element.95, bf16[256,384]{0,1:T(8,128)(2,1)S(1)} %bitcast.389, bf16[1280,384]{0,1:T(8,128)(2,1)S(1)} %bitcast.338, bf16[1280,384]{0,1:T(8,128)(2,1)S(1)} %bitcast.349), kind=kOutput, calls=%fused_computation.3 | convolution fusion | flops 4551278592 | bytes 9633792 | tf_op jit(solution)/shard_map/dot_general | solution.py:43
  425.1 27.6 %all_gather.50 = bf16[256,1536]{1,0:T(8,128)(2,1)} all-gather(bf16[64,1536]{1,0:T(8,128)(2,1)S(1)} %get-tuple-element.71), channel_id=1, replica_groups=mesh['section'=4,'pair'=4,'core'=2] {'pair'}, dimensions={0}, use_global_device_ids=true | all-gather | bytes 983040 | tf_op jit(solution)/shard_map/all_gather | solution.py:189
  518.9 11.4 %all_gather.51 = bf16[256,1536]{1,0:T(8,128)(2,1)S(1)} all-gather(bf16[64,1536]{1,0:T(8,128)(2,1)S(1)} %get-tuple-element.69), channel_id=1, replica_groups=mesh['section'=4,'pair'=4,'core'=2] {'section'}, dimensions={0}, use_global_device_ids=true | all-gather | bytes 983040 | tf_op jit(solution)/shard_map/all_gather | solution.py:180
  554.5 8.1 %multiply_reduce_fusion.1 = (f32[1536]{0:T(1024)S(1)}, f32[1536]{0:T(1024)S(1)}, f32[1024,1536]{1,0:T(8,128)}, f32[1024,1536]{1,0:T(8,128)}) fusion(bf16[1024,1536]{1,0:T(8,128)(2,1)S(1)} %copy-done.3, f32[1024]{0:T(1024)S(1)} %copy-done.117, f32[1024]{0:T(1024)S(1)} %copy-done.115, f32[1024,1536]{1,0:T(8,128)S(1)} %bitcast.302, f32[1536]{0:T(1024)S(1)} %copy-done.113, ...), kind=kOutput, calls=%fused_computation.10 | convolution fusion | flops 1225257984 | bytes 30310400 | tf_op jit(solution)/shard_map/dot_general | solution.py:39
  573.0 9.2 %convolution_convert_fusion = bf16[1536,1152]{1,0:T(8,128)(2,1)} fusion(bf16[256,1536]{1,0:T(8,128)(2,1)} %fusion.55, bf16[1024,1536]{1,0:T(8,128)(2,1)} %get-tuple-element.96, bf16[256,384]{0,1:T(8,128)(2,1)} %bitcast.390, bf16[1280,384]{0,1:T(8,128)(2,1)S(1)} %bitcast.336, bf16[1280,384]{0,1:T(8,128)(2,1)S(1)} %bitcast.346), kind=kOutput, calls=%fused_computation.2 | convolution fusion | flops 4551278592 | bytes 9633792 | tf_op jit(solution)/shard_map/dot_general | solution.py:43
  620.4 12.5 %all-to-all-done.8 = bf16[4,64,1536]{2,1,0:T(8,128)(2,1)S(1)} async-done(((bf16[4,64,1536]{2,1,0:T(8,128)(2,1)}), bf16[4,64,1536]{2,1,0:T(8,128)(2,1)S(1)}, u32[]{:S(2)}, u32[]{:S(2)}) %all-to-all-start.8) | async-done | bytes 786464 | tf_op jit(solution)/shard_map/all_to_all | solution.py:176
  650.6 20.2 %all-to-all-done.9 = bf16[8,96,384]{2,1,0:T(8,128)(2,1)S(1)} async-done(((bf16[8,96,384]{2,1,0:T(8,128)(2,1)}), bf16[8,96,384]{2,1,0:T(8,128)(2,1)S(1)}, u32[]{:S(2)}, u32[]{:S(2)}) %all-to-all-start.9) | async-done | bytes 589856 | tf_op jit(solution)/shard_map/all_to_all | solution.py:451
  704.2 13.9 %all-to-all-done.10 = bf16[64,4,384]{2,0,1:T(8,128)(2,1)S(1)} async-done(((bf16[64,4,384]{2,0,1:T(8,128)(2,1)}), bf16[64,4,384]{2,0,1:T(8,128)(2,1)S(1)}, u32[]{:S(2)}, u32[]{:S(2)}) %all-to-all-start.10) | async-done | bytes 196640 | tf_op jit(solution)/shard_map/all_to_all | solution.py:183
  (671 shorter events, 449.2 us)
Async XLA Ops:
  7.2 149.7 %all-gather.5.cloned.1.call-start = ((), (), s32[]{:S(2)}) async-start(), calls=%async_computation.19 | async-start | bytes 5308416 | tf_op jit(solution)/shard_map/all_gather | solution.py:264
  29.3 229.9 %all-gather.7.cloned.1.call-start = ((), (), s32[]{:S(2)}) async-start(), calls=%async_computation.20 | async-start | bytes 5308416 | tf_op jit(solution)/shard_map/all_gather | solution.py:264
  31.6 38.0 %collective-permute-start.1 = (bf16[96,3072]{1,0:T(8,128)(2,1)}, bf16[96,3072]{1,0:T(8,128)(2,1)}, u32[]{:S(2)}, u32[]{:S(2)}) collective-permute-start(bf16[96,3072]{1,0:T(8,128)(2,1)} %slice_bitcast_fusion.4), channel_id=1, source_target_pairs={{0,16},{8,24},{1,17},{9,25},{2,18},{10,26},{3,19},{11,27},{4,20},{... | collective-permute-start | bytes 1769480 | tf_op jit(solution)/shard_map/ppermute | solution.py:124
  94.5 33.3 %all-to-all-start.1 = ((bf16[96,8,384]{2,0,1:T(8,128)(2,1)}), bf16[96,8,384]{2,0,1:T(8,128)(2,1)}, u32[]{:S(2)}, u32[]{:S(2)}) async-start(bf16[96,8,384]{2,0,1:T(8,128)(2,1)} %bitcast.356), calls=%async_computation.1 | async-start | bytes 1179648 | tf_op jit(solution)/shard_map/all_to_all | solution.py:273
  98.7 229.8 %all-gather.9.cloned.1.call-start = ((), (), s32[]{:S(2)}) async-start(), calls=%async_computation.21 | async-start | bytes 5308416 | tf_op jit(solution)/shard_map/all_gather | solution.py:264
  127.8 63.2 %collective-permute-start.6 = (bf16[768,384]{1,0:T(8,128)(2,1)}, bf16[768,384]{1,0:T(8,128)(2,1)}, u32[]{:S(2)}, u32[]{:S(2)}) collective-permute-start(bf16[768,384]{1,0:T(8,128)(2,1)} %bitcast.22), channel_id=1, source_target_pairs={{0,8},{8,0},{16,24},{24,16},{1,9},{9,1},{17,25},{25,17},{2,10},{10... | collective-permute-start | bytes 1769480 | tf_op jit(solution)/shard_map/ppermute | solution.py:118
  130.0 64.0 %collective-permute-start.5 = (bf16[768,384]{1,0:T(8,128)(2,1)}, bf16[768,384]{1,0:T(8,128)(2,1)}, u32[]{:S(2)}, u32[]{:S(2)}) collective-permute-start(bf16[768,384]{1,0:T(8,128)(2,1)} %bitcast.22), channel_id=1, source_target_pairs={{0,16},{8,24},{16,0},{24,8},{1,17},{9,25},{17,1},{25,9},{2,18},{10... | collective-permute-start | bytes 1769480 | tf_op jit(solution)/shard_map/ppermute | solution.py:118
  247.4 93.9 %all-gather.11.cloned.1.call-start = ((), (), s32[]{:S(2)}) async-start(), calls=%async_computation.22 | async-start | bytes 5308416 | tf_op jit(solution)/shard_map/all_gather | solution.py:264
  259.1 203.1 %reduce-scatter.7.cloned.1.call-start = ((), (), s32[]{:S(2)}) async-start(), calls=%async_computation.23 | async-start | bytes 5308416 | tf_op jit(solution)/shard_map/reduce_scatter | solution.py:373
  341.0 122.3 %reduce-scatter.9.cloned.1.call-start = ((), (), s32[]{:S(2)}) async-start(), calls=%async_computation.24 | async-start | bytes 5308416 | tf_op jit(solution)/shard_map/reduce_scatter | solution.py:373
  363.1 331.2 %reduce-scatter.13.cloned.1.call-start = ((), (), s32[]{:S(2)}) async-start(), calls=%async_computation.26 | async-start | bytes 1327104 | tf_op jit(solution)/shard_map/reduce_scatter | solution.py:373
  411.9 282.4 %reduce-scatter.11.cloned.1.call-start = ((), (), s32[]{:S(2)}) async-start(), calls=%async_computation.25 | async-start | bytes 3981312 | tf_op jit(solution)/shard_map/reduce_scatter | solution.py:373
  482.5 33.8 %all-to-all-start.6 = ((bf16[4,64,1536]{2,1,0:T(8,128)(2,1)}), bf16[4,64,1536]{2,1,0:T(8,128)(2,1)}, u32[]{:S(2)}, u32[]{:S(2)}) async-start(bf16[4,64,1536]{2,1,0:T(8,128)(2,1)} %bitcast.384), calls=%async_computation.8 | async-start | bytes 1572864 | tf_op jit(solution)/shard_map/all_to_all | solution.py:197
  486.7 238.7 %reduce-scatter.17.cloned.1.call-start = ((), (), s32[]{:S(2)}) async-start(), calls=%async_computation.28 | async-start | bytes 1327104 | tf_op jit(solution)/shard_map/reduce_scatter | solution.py:373
  499.6 191.3 %collective-permute-start.41 = (bf16[192,1536]{1,0:T(8,128)(2,1)}, bf16[192,1536]{1,0:T(8,128)(2,1)}, u32[]{:S(2)}, u32[]{:S(2)}) collective-permute-start(bf16[192,1536]{1,0:T(8,128)(2,1)} %reduce-scatter.7.cloned.1.call-done), channel_id=1, source_target_pairs={{0,16},{8,24},{1,17},{9,25},{2,18},{10,26},{3,19},{11,27},{4,20},{... | collective-permute-start | bytes 1769480 | tf_op jit(solution)/shard_map/ppermute | solution.py:124
  548.2 62.7 %collective-permute-start.39 = (bf16[192,1536]{1,0:T(8,128)(2,1)}, bf16[192,1536]{1,0:T(8,128)(2,1)}, u32[]{:S(2)}, u32[]{:S(2)}) collective-permute-start(bf16[192,1536]{1,0:T(8,128)(2,1)} %pad_maximum_fusion.20), channel_id=1, source_target_pairs={{0,16},{8,24},{16,0},{24,8},{1,17},{9,25},{17,1},{25,9},{2,18},{10... | collective-permute-start | bytes 1769480 | tf_op jit(solution)/shard_map/ppermute | solution.py:118
  549.8 61.1 %collective-permute-start.38 = (bf16[192,1536]{1,0:T(8,128)(2,1)}, bf16[192,1536]{1,0:T(8,128)(2,1)}, u32[]{:S(2)}, u32[]{:S(2)}) collective-permute-start(bf16[192,1536]{1,0:T(8,128)(2,1)} %pad_maximum_fusion.19), channel_id=1, source_target_pairs={{0,8},{8,0},{16,24},{24,16},{1,9},{9,1},{17,25},{25,17},{2,10},{10... | collective-permute-start | bytes 1769480 | tf_op jit(solution)/shard_map/ppermute | solution.py:118
  603.7 44.0 %collective-permute-start.26 = (bf16[256,1536]{1,0:T(8,128)(2,1)}, bf16[256,1536]{1,0:T(8,128)(2,1)}, u32[]{:S(2)}, u32[]{:S(2)}) collective-permute-start(bf16[256,1536]{1,0:T(8,128)(2,1)} %pad_maximum_fusion.11), channel_id=1, source_target_pairs={{0,16},{8,24},{16,0},{24,8},{1,17},{9,25},{17,1},{25,9},{2,18},{10... | collective-permute-start | bytes 2359304 | tf_op jit(solution)/shard_map/ppermute | solution.py:118
  604.4 43.2 %collective-permute-start.24 = (bf16[256,1536]{1,0:T(8,128)(2,1)}, bf16[256,1536]{1,0:T(8,128)(2,1)}, u32[]{:S(2)}, u32[]{:S(2)}) collective-permute-start(bf16[256,1536]{1,0:T(8,128)(2,1)} %pad_maximum_fusion.10), channel_id=1, source_target_pairs={{0,8},{8,0},{16,24},{24,16},{1,9},{9,1},{17,25},{25,17},{2,10},{10... | collective-permute-start | bytes 2359304 | tf_op jit(solution)/shard_map/ppermute | solution.py:118
  610.3 127.3 %reduce-scatter.15.cloned.1.call-start = ((), (), s32[]{:S(2)}) async-start(), calls=%async_computation.27 | async-start | bytes 3981312 | tf_op jit(solution)/shard_map/reduce_scatter | solution.py:373
  614.1 76.8 %collective-permute-start.40 = (bf16[192,1536]{1,0:T(8,128)(2,1)}, bf16[192,1536]{1,0:T(8,128)(2,1)}, u32[]{:S(2)}, u32[]{:S(2)}) collective-permute-start(bf16[192,1536]{1,0:T(8,128)(2,1)} %fusion.78), channel_id=1, source_target_pairs={{16,0},{24,8},{17,1},{25,9},{18,2},{26,10},{19,3},{27,11},{20,4},{... | collective-permute-start | bytes 1769480 | tf_op jit(solution)/shard_map/ppermute | solution.py:127
  677.9 40.9 %collective-permute-start.29 = (bf16[256,1536]{1,0:T(8,128)(2,1)}, bf16[256,1536]{1,0:T(8,128)(2,1)}, u32[]{:S(2)}, u32[]{:S(2)}) collective-permute-start(bf16[256,1536]{1,0:T(8,128)(2,1)} %multiply_convert_fusion.4), channel_id=1, source_target_pairs={{0,16},{8,24},{16,0},{24,8},{1,17},{9,25},{17,1},{25,9},{2,18},{10... | collective-permute-start | bytes 2359304 | tf_op jit(solution)/shard_map/ppermute | solution.py:118
  679.9 41.5 %collective-permute-start.27 = (bf16[256,1536]{1,0:T(8,128)(2,1)}, bf16[256,1536]{1,0:T(8,128)(2,1)}, u32[]{:S(2)}, u32[]{:S(2)}) collective-permute-start(bf16[256,1536]{1,0:T(8,128)(2,1)} %multiply_convert_fusion.4), channel_id=1, source_target_pairs={{0,8},{8,0},{16,24},{24,16},{1,9},{9,1},{17,25},{25,17},{2,10},{10... | collective-permute-start | bytes 2359304 | tf_op jit(solution)/shard_map/ppermute | solution.py:118
  682.3 40.2 %collective-permute-start.34 = (bf16[96,3072]{1,0:T(8,128)(2,1)}, bf16[96,3072]{1,0:T(8,128)(2,1)}, u32[]{:S(2)}, u32[]{:S(2)}) collective-permute-start(bf16[96,3072]{1,0:T(8,128)(2,1)} %bitcast.144), channel_id=1, source_target_pairs={{16,0},{24,8},{17,1},{25,9},{18,2},{26,10},{19,3},{27,11},{20,4},{... | collective-permute-start | bytes 1769480 | tf_op jit(solution)/shard_map/ppermute | solution.py:127
  (179 other events, 1738.8 us)
Sparse Core Ops, SparseCore 0:
  29.4 65.6 all-gather.4
  96.7 58.4 all-gather.6
  156.8 49.5 all-gather.8
  259.2 49.5 all-gather.10
  341.1 53.9 reduce-scatter.6
  397.2 65.9 reduce-scatter.8
  465.5 33.0 reduce-scatter.12
  500.9 42.0 reduce-scatter.10
  571.4 33.7 reduce-scatter.16
  613.2 51.7 reduce-scatter.14

commit v9 on v8

--- a/solution.py
+++ b/solution.py
@@ -271,21 +271,21 @@
     out_w = [unfold(weight[:, 3 * inner :]) for weight in stacked]
 
     up_turned = lax.all_to_all(up_share, dp, split_axis=1, concat_axis=0, tiled=True)
-    down_shared = by_distance(
-        share_first(*after((w_down[0, :half_hidden], w_down[0, half_hidden:]), all_gains))
-    )
-    up_shared = by_distance(up_turned)
+    down_share = share_first(
+        *after((w_down[0, :half_hidden], w_down[0, half_hidden:]), other_heads)
+    )
 
     def in_depth(near, far):
         parts = [part.reshape(dp_count, 1, half_depth, -1) for part in pick(near, far)]
         return jnp.concatenate(parts, axis=1).reshape(feature_width, -1)
 
-    down_first = jnp.concatenate(
-        pick(down_shared[0], down_shared[2]) + pick(down_shared[1], down_shared[3]), axis=0
-    )
-    up_first = jnp.concatenate(
-        [in_depth(up_shared[0], up_shared[2]), in_depth(up_shared[1], up_shared[3])], axis=1
-    )
+    def first_ffn(gate):
+        down, up = after((down_share, up_turned), gate)
+        down, up = by_distance(down), by_distance(up)
+        return (
+            jnp.concatenate([in_depth(up[0], up[2]), in_depth(up[1], up[3])], axis=1),
+            jnp.concatenate(pick(down[0], down[2]) + pick(down[1], down[3]), axis=0),
+        )
 
     up_even, up_odd = column_parts(w_up[0], half_hidden)
     up_piece, down_piece = after((up_even, w_down[0, :half_hidden]), all_gains)
@@ -293,8 +293,8 @@
         jnp.where(on_first, to_first(down_piece), w_down[0, half_hidden:])
     )
     up_second = gather(jnp.where(on_first, to_first(up_piece), up_odd))
-    up_w = (up_first, up_second)
-    down_w = (down_first, down_second)
+    up_w = [None, up_second]
+    down_w = [None, down_second]
     query_w = [weight[:, :inner] for weight in qkv_w]
     key_w = [weight[:, inner : 2 * inner] for weight in qkv_w]
     value_w = [weight[:, 2 * inner :] for weight in qkv_w]
@@ -331,6 +331,8 @@
         else:
             latent_low = from_slots((unit_in * all_gains[layer, 1]).astype(low))
         projected = matmul(latent_low, qkv_w[layer]).astype(low)
+        if layer == 0:
+            up_w[0], down_w[0] = first_ffn(projected)
         query_low = projected[:, :inner]
         key_heads = split_heads(
             jnp.concatenate([media_key[layer], projected[:, inner : 2 * inner]], axis=0)
@@ -422,7 +424,9 @@
             up_half = sum_by_distance(*up_blocks, middle_low).astype(low)
             down_half = sum_by_distance(*down_blocks, middle_low).astype(low)
         grad_heads = split_heads(matmul_nt(middle_low, out_w[layer]).astype(low))
-        out_piece = scatter(by_device(matmul_tn(attended_low, middle_low)).astype(low))
+        out_grad = by_device(matmul_tn(attended_low, middle_low)).astype(low)
+        out_piece = scatter(out_grad)
+        grad_heads = after(grad_heads, out_grad)
         grad_query, grad_key, grad_value = attend_backward(
             query_heads, key_heads, value_heads, allowed, score_scale, log_total, grad_heads
         )
@@ -434,8 +438,6 @@
             + matmul_nt(grad_key[seq_rows:], key_w[layer])
             + matmul_nt(grad_value[seq_rows:], value_w[layer])
         )
-        if layer == 0:
-            latent_part = after(latent_part, up_half)
         latent_grad_rows = sum_to_slots(latent_part)
         gain_latent_grad = jnp.sum(latent_grad_rows * unit_in, axis=0)
         grad_rows = grad_middle + norm_back(
@@ -452,6 +454,14 @@
         pieces[layer] = (scatter(qkv_grad), out_piece)
         if layer > 0:
             grad_low = from_sequences(grad_rows.astype(low))
+            last = matmul(after(active_low, latent_part), down_w[layer])
+            start = section * slot_rows
+            rows = lax.dynamic_slice_in_dim(last, start, slot_rows, 0) + middle
+            last = lax.dynamic_update_slice_in_dim(last, rows, start, 0).astype(low)
+            last = last.reshape(latent_rows, section_count, -1)
+            last = lax.all_to_all(last, "section", split_axis=1, concat_axis=0)
+            latents_out = jnp.sum(last.astype(full), axis=0)
+            grad_low = after(grad_low, latents_out)
             grad_low = after(grad_low, ffn_pieces)
         media_part = matmul_nt(grad_key[:seq_rows], key_w[layer]) + matmul_nt(
             grad_value[:seq_rows], value_w[layer]
@@ -460,13 +470,6 @@
         scaled = media_part * all_gains[layer, 0]
         media_scaled = scaled if media_scaled is None else media_scaled + scaled
         gain_rows[layer] = jnp.stack([gain_media_grad, gain_latent_grad, gain_ffn_grad])
-    last = matmul(after(saved[1][12], latent_part), down_w[1])
-    start = section * slot_rows
-    rows = lax.dynamic_slice_in_dim(last, start, slot_rows, 0) + middle
-    last = lax.dynamic_update_slice_in_dim(last, rows, start, 0).astype(low)
-    last = last.reshape(latent_rows, section_count, -1)
-    last = lax.all_to_all(last, "section", split_axis=1, concat_axis=0)
-    latents_out = jnp.sum(last.astype(full), axis=0)
     latent_grad = to_columns(after(grad_rows, (pieces[1], up_half)))
     media_rows = seq_rows // section_count
     media_sum = sum_over_sections(media_scaled)

time: 770 us -> 738 us (0.958)
  waiting for transfers between devices: 135 us -> 81.4 us
  other arithmetic: 102 us -> 113 us
  local copies, waits for them, and re-layouts: 97.5 us -> 108 us
    ppermute x26, waiting for transfers between devices: 51.9 us -> 21.6 us  [swapped(): return lax.ppermute(value, 'section', pairs)]
    all_to_all x4, waiting for transfers between devices: 20.9 us -> 7.33 us  [sum_to_slots(): arrived = lax.all_to_all(blocks, 'section', split_axis=0, concat_axis=0)]
    all_to_all x1, waiting for transfers between devices: 0.26 us -> 12.3 us  [per_device(): lax.all_to_all(gain_parts, 'section', split_axis=2, concat_axis=2)]
    all_to_all x1, waiting for transfers between devices: 13.9 us -> 3.8 us  [to_columns(): lax.all_to_all(rows.astype(low), 'section', split_axis=1, concat_axis=0,...]
    all_to_all x1, waiting for transfers between devices: 20.2 us -> 10.6 us  [per_device(): lax.all_to_all(up_half, dp, split_axis=0, concat_axis=1, tiled=True)]
    all_to_all x1, waiting for transfers between devices: 0.01 us -> 9.22 us  [per_device(): lax.all_to_all(up_share, dp, split_axis=1, concat_axis=0, tiled=True)]
    ppermute x26, starting transfers between devices: 36.2 us -> 27.6 us  [swapped(): return lax.ppermute(value, 'section', pairs)]
    unnamed x282 -> x244, local copies, waits for them, and re-layouts: 21.4 us -> 22.6 us
  transfers between devices with their start and end apart: 64 -> 64, of which waited for: 21 -> 15; matrix products, arithmetic and copies ran while one was open for 43% -> 47% of each run, Pallas kernels for 0% -> 0%
where the time goes in v9:
time: 738 us; the launch traced here: 726 us
  matrix products  145 us (20%)
  blocking collectives  144 us (20%)
  starting transfers between devices  117 us (16%)
  other arithmetic  113 us (15%)
  local copies, waits for them, and re-layouts  108 us (15%)
  waiting for transfers between devices  81.4 us (11%)
  between operations  16.6 us (2%)
    all_gather x2, blocking collectives, from_sequences(): near = lax.all_gather(rows, 'pair', axis=0, tiled=True)  55.9 us
    dot_general x17, matrix products, matmul_nt(): lax.dot_general(left, right, (((1,), (1,)), ((), ())), preferred_element_...  49.4 us
    all_gather x4, blocking collectives, from_slots(): return lax.all_gather(rows, 'section', axis=0, tiled=True)  46.8 us
    dot_general x13, matrix products, matmul(): return jnp.dot(left, right, preferred_element_type=full)  45.2 us
    dot_general x8, matrix products, matmul_tn(): lax.dot_general(left, right, (((0,), (0,)), ((), ())), preferred_element_...  30.7 us
    all_gather x3, blocking collectives, per_device(): all_gains = lax.all_gather(all_gains, axis, axis=2, tiled=True)  29.1 us
    ppermute x26, starting transfers between devices, swapped(): return lax.ppermute(value, 'section', pairs)  27.6 us
    unnamed x244, local copies, waits for them, and re-layouts  22.6 us
  transfers between devices with their start and end apart: 64, of which 15 were waited for; matrix products, arithmetic and copies ran while one was open for 47% of the time, Pallas kernels for 0%

profile of v9, /device:TPU:0, one launch (start us, length us, event | category | flops | bytes accessed | tf_op | source)
XLA Modules:
  0.0 726.0 jit_solution(7770815472133652601)
XLA Ops:
  12.6 10.2 %collective-permute-done = bf16[192,1152]{1,0:T(8,128)(2,1)S(1)} collective-permute-done((bf16[192,1152]{1,0:T(8,128)(2,1)S(1)}, bf16[192,1152]{1,0:T(8,128)(2,1)S(1)}, u32[]{:S(2)}, u32[]{:S(2)}) %collective-permute-start) | collective-permute-done | bytes 442400 | tf_op jit(solution)/shard_map/ppermute | solution.py:118
  30.2 11.1 %collective-permute-start.1 = (bf16[96,3072]{1,0:T(8,128)(2,1)}, bf16[96,3072]{1,0:T(8,128)(2,1)}, u32[]{:S(2)}, u32[]{:S(2)}) collective-permute-start(bf16[96,3072]{1,0:T(8,128)(2,1)} %slice_bitcast_fusion.4), channel_id=1, source_target_pairs={{0,16},{8,24},{1,17},{9,25},{2,18},{10,26},{3,19},{11,27},{4,20},{... | collective-permute-start | bytes 1769480 | tf_op jit(solution)/shard_map/ppermute | solution.py:124
  51.5 7.5 %slice_reduce_fusion = (bf16[192,8,192]{2,1,0:T(8,128)(2,1)}, bf16[192,8,192]{2,1,0:T(8,128)(2,1)}) fusion(bf16[192,8,2,192]{3,2,1,0:T(2,128)(2,1)S(1)} %copy-done.7), kind=kLoop, calls=%fused_computation.100 | loop fusion | bytes 2359296 | tf_op jit(solution)/shard_map/slice | solution.py:244
  73.7 19.0 %all_gather.40 = f32[2,3,384]{1,0,2:T(2,128)} all-gather(f32[2,3,96]{1,0,2:T(2,128)S(1)} %all_gather.39), channel_id=1, replica_groups=mesh['section'=4,'pair'=4,'core'=2] {'pair'}, dimensions={2}, use_global_device_ids=true | all-gather | bytes 11520 | tf_op jit(solution)/shard_map/all_gather | solution.py:260
  100.0 8.3 %all_gather.41 = f32[2,3,1536]{2,0,1:T(2,128)S(1)} all-gather(f32[2,3,384]{2,0,1:T(2,128)S(1)} %copy.173), channel_id=1, replica_groups=mesh['section'=4,'pair'=4,'core'=2] {'section'}, dimensions={2}, use_global_device_ids=true | all-gather | bytes 46080 | tf_op jit(solution)/shard_map/all_gather | solution.py:260
  120.0 9.2 %all-to-all-done.1 = bf16[96,8,384]{2,0,1:T(8,128)(2,1)} async-done(((bf16[96,8,384]{2,0,1:T(8,128)(2,1)}), bf16[96,8,384]{2,0,1:T(8,128)(2,1)}, u32[]{:S(2)}, u32[]{:S(2)}) %all-to-all-start.1) | async-done | bytes 589856 | tf_op jit(solution)/shard_map/all_to_all | solution.py:273
  173.0 30.4 %all_gather.43 = bf16[256,1536]{1,0:T(8,128)(2,1)S(1)} all-gather(bf16[64,1536]{1,0:T(8,128)(2,1)S(1)} %multiply_convert_fusion.9), channel_id=1, replica_groups=mesh['section'=4,'pair'=4,'core'=2] {'pair'}, dimensions={0}, use_global_device_ids=true | all-gather | bytes 983040 | tf_op jit(solution)/shard_map/all_gather | solution.py:189
  224.8 6.6 all-to-all-start.2
  231.4 7.4 %collective-permute-done.16 = bf16[192,1536]{1,0:T(8,128)(2,1)} collective-permute-done((bf16[192,1536]{1,0:T(8,128)(2,1)S(1)}, bf16[192,1536]{1,0:T(8,128)(2,1)}, u32[]{:S(2)}, u32[]{:S(2)}) %collective-permute-start.16) | collective-permute-done | bytes 589856 | tf_op jit(solution)/shard_map/ppermute | solution.py:127
  253.9 12.8 %all_gather.45 = bf16[256,1536]{1,0:T(8,128)(2,1)S(1)} all-gather(bf16[64,1536]{1,0:T(8,128)(2,1)S(1)} %multiply_convert_fusion.8), channel_id=1, replica_groups=mesh['section'=4,'pair'=4,'core'=2] {'section'}, dimensions={0}, use_global_device_ids=true | all-gather | bytes 983040 | tf_op jit(solution)/shard_map/all_gather | solution.py:180
  281.0 12.6 %all_to_all.105 = bf16[4,64,1536]{2,1,0:T(8,128)(2,1)S(1)} all-to-all(bf16[4,64,1536]{2,1,0:T(8,128)(2,1)S(1)} %bitcast.351), channel_id=1, replica_groups=mesh['section'=4,'pair'=4,'core'=2] {'section'}, dimensions={0} | all-to-all | bytes 1572864 | tf_op jit(solution)/shard_map/all_to_all | solution.py:176
  294.3 11.0 %all_gather.46 = bf16[256,1536]{1,0:T(8,128)(2,1)S(1)} all-gather(bf16[64,1536]{1,0:T(8,128)(2,1)S(1)} %multiply_convert_fusion.7), channel_id=1, replica_groups=mesh['section'=4,'pair'=4,'core'=2] {'section'}, dimensions={0}, use_global_device_ids=true | all-gather | bytes 983040 | tf_op jit(solution)/shard_map/all_gather | solution.py:180
  305.3 8.0 %multiply_convert_fusion.5 = (bf16[256,1536]{1,0:T(8,128)(2,1)S(1)}, f32[256,1536]{1,0:T(8,128)}) fusion(bf16[256,1536]{1,0:T(8,128)(2,1)S(1)} %all_gather.46, bf16[1536,1536]{1,0:T(8,128)(2,1)} %all-gather.9.cloned.1.call-done), kind=kOutput, calls=%fused_computation.117 | convolution fusion | flops 1233518592 | bytes 7864320 | tf_op jit(solution)/shard_map/dot_general | solution.py:35
  318.0 7.7 %add_convert_fusion.2 = bf16[256,1536]{1,0:T(8,128)(2,1)S(1)} fusion(bf16[1536,1536]{1,0:T(8,128)(2,1)} %all-gather.11.cloned.1.call-done, bf16[256,1536]{1,0:T(8,128)(2,1)} %param.23, f32[256,1536]{1,0:T(8,128)} %get-tuple-element.170), kind=kOutput, calls=%fused_computation.116 | convolution fusion | flops 1236271104 | bytes 7864320 | tf_op jit(solution)/shard_map/dot_general | solution.py:39
  340.3 7.3 %all-to-all-done.4 = bf16[4,64,1536]{2,1,0:T(8,128)(2,1)S(1)} async-done(((bf16[4,64,1536]{2,1,0:T(8,128)(2,1)}), bf16[4,64,1536]{2,1,0:T(8,128)(2,1)S(1)}, u32[]{:S(2)}, u32[]{:S(2)}) %all-to-all-start.4) | async-done | bytes 786464 | tf_op jit(solution)/shard_map/all_to_all | solution.py:176
  350.0 11.3 %all_gather.49 = bf16[256,1536]{1,0:T(8,128)(2,1)S(1)} all-gather(bf16[64,1536]{1,0:T(8,128)(2,1)S(1)} %get-tuple-element.81), channel_id=1, replica_groups=mesh['section'=4,'pair'=4,'core'=2] {'section'}, dimensions={0}, use_global_device_ids=true | all-gather | bytes 983040 | tf_op jit(solution)/shard_map/all_gather | solution.py:180
  385.3 9.3 %convolution_convert_fusion.1 = bf16[1536,1152]{1,0:T(8,128)(2,1)} fusion(bf16[256,1536]{1,0:T(8,128)(2,1)} %copy-done.73, bf16[1024,1536]{1,0:T(8,128)(2,1)} %get-tuple-element.103, bf16[256,384]{0,1:T(8,128)(2,1)S(1)} %bitcast.388, bf16[1280,384]{0,1:T(8,128)(2,1)S(1)} %bitcast.336, bf16[1280,384]{0,1:T(8,128)(2,1)S(1)} %bitcast.346), kind=kOutput, calls=%fused_computation.3 | convolution fusion | flops 4551278592 | bytes 9633792 | tf_op jit(solution)/shard_map/dot_general | solution.py:43
  415.6 25.5 %all_gather.50 = bf16[256,1536]{1,0:T(8,128)(2,1)S(1)} all-gather(bf16[64,1536]{1,0:T(8,128)(2,1)S(1)} %get-tuple-element.79), channel_id=1, replica_groups=mesh['section'=4,'pair'=4,'core'=2] {'pair'}, dimensions={0}, use_global_device_ids=true | all-gather | bytes 983040 | tf_op jit(solution)/shard_map/all_gather | solution.py:189
  515.6 11.8 %all_gather.51 = bf16[256,1536]{1,0:T(8,128)(2,1)S(1)} all-gather(bf16[64,1536]{1,0:T(8,128)(2,1)S(1)} %get-tuple-element.77), channel_id=1, replica_groups=mesh['section'=4,'pair'=4,'core'=2] {'section'}, dimensions={0}, use_global_device_ids=true | all-gather | bytes 983040 | tf_op jit(solution)/shard_map/all_gather | solution.py:180
  568.8 7.9 %multiply_reduce_fusion.1 = (f32[1536]{0:T(1024)S(1)}, f32[1536]{0:T(1024)S(1)}, f32[1024,1536]{1,0:T(8,128)S(1)}, f32[1024,1536]{1,0:T(8,128)}) fusion(bf16[1024,1536]{1,0:T(8,128)(2,1)S(1)} %copy-done.3, f32[1024]{0:T(1024)S(1)} %add_rsqrt_fusion, f32[1024]{0:T(1024)S(1)} %copy-done.95, f32[1024,1536]{1,0:T(8,128)} %convolution_add_fusion.1, ...), kind=kOutput, calls=%fused_computation.10 | convolution fusion | flops 1225257984 | bytes 30310400 | tf_op jit(solution)/shard_map/dot_general | solution.py:39
  583.7 9.2 %convolution_convert_fusion = bf16[1536,1152]{1,0:T(8,128)(2,1)} fusion(bf16[256,1536]{1,0:T(8,128)(2,1)S(1)} %copy-done.72, bf16[1024,1536]{1,0:T(8,128)(2,1)} %get-tuple-element.104, bf16[256,384]{0,1:T(8,128)(2,1)S(1)} %bitcast.386, bf16[1280,384]{0,1:T(8,128)(2,1)S(1)} %bitcast.334, bf16[1280,384]{0,1:T(8,128)(2,1)S(1)} %bitcast.344), kind=kOutput, calls=%fused_computation.2 | convolution fusion | flops 4551278592 | bytes 9633792 | tf_op jit(solution)/shard_map/dot_general | solution.py:43
  607.8 6.1 collective-permute-done.39
  625.5 12.3 %all-to-all-done.11 = f32[2,3,4,384]{3,0,1,2:T(2,128)S(1)} async-done(((f32[2,3,4,384]{3,0,1,2:T(2,128)}), f32[2,3,4,384]{3,0,1,2:T(2,128)S(1)}, u32[]{:S(2)}, u32[]{:S(2)}) %all-to-all-start.11) | async-done | bytes 36896 | tf_op jit(solution)/shard_map/all_to_all | solution.py:483
  649.1 10.6 %all-to-all-done.9 = bf16[8,96,384]{2,1,0:T(8,128)(2,1)S(1)} async-done(((bf16[8,96,384]{2,1,0:T(8,128)(2,1)}), bf16[8,96,384]{2,1,0:T(8,128)(2,1)S(1)}, u32[]{:S(2)}, u32[]{:S(2)}) %all-to-all-start.9) | async-done | bytes 589856 | tf_op jit(solution)/shard_map/all_to_all | solution.py:453
  (633 shorter events, 436.5 us)
Async XLA Ops:
  7.2 108.4 %all-gather.5.cloned.1.call-start = ((), (), s32[]{:S(2)}) async-start(), calls=%async_computation.19 | async-start | bytes 5308416 | tf_op jit(solution)/shard_map/all_gather | solution.py:264
  29.3 211.5 %all-gather.7.cloned.1.call-start = ((), (), s32[]{:S(2)}) async-start(), calls=%async_computation.20 | async-start | bytes 5308416 | tf_op jit(solution)/shard_map/all_gather | solution.py:264
  30.2 40.6 %collective-permute-start.1 = (bf16[96,3072]{1,0:T(8,128)(2,1)}, bf16[96,3072]{1,0:T(8,128)(2,1)}, u32[]{:S(2)}, u32[]{:S(2)}) collective-permute-start(bf16[96,3072]{1,0:T(8,128)(2,1)} %slice_bitcast_fusion.4), channel_id=1, source_target_pairs={{0,16},{8,24},{1,17},{9,25},{2,18},{10,26},{3,19},{11,27},{4,20},{... | collective-permute-start | bytes 1769480 | tf_op jit(solution)/shard_map/ppermute | solution.py:124
  68.7 46.0 %collective-permute-start.5 = (bf16[192,1536]{1,0:T(8,128)(2,1)}, bf16[192,1536]{1,0:T(8,128)(2,1)}, u32[]{:S(2)}, u32[]{:S(2)}) collective-permute-start(bf16[192,1536]{1,0:T(8,128)(2,1)} %get-tuple-element.34), channel_id=1, source_target_pairs={{0,16},{8,24},{1,17},{9,25},{2,18},{10,26},{3,19},{11,27},{4,20},{... | collective-permute-start | bytes 1769480 | tf_op jit(solution)/shard_map/ppermute | solution.py:124
  108.3 50.8 %collective-permute-start.15 = (bf16[192,1536]{1,0:T(8,128)(2,1)}, bf16[192,1536]{1,0:T(8,128)(2,1)}, u32[]{:S(2)}, u32[]{:S(2)}) collective-permute-start(bf16[192,1536]{1,0:T(8,128)(2,1)} %reshape_squeeze.16), channel_id=1, source_target_pairs={{16,0},{24,8},{17,1},{25,9},{18,2},{26,10},{19,3},{27,11},{20,4},{... | collective-permute-start | bytes 1769480 | tf_op jit(solution)/shard_map/ppermute | solution.py:127
  159.0 146.2 %all-gather.9.cloned.1.call-start = ((), (), s32[]{:S(2)}) async-start(), calls=%async_computation.21 | async-start | bytes 5308416 | tf_op jit(solution)/shard_map/all_gather | solution.py:264
  162.1 44.5 %collective-permute-start.8 = (bf16[384,384]{1,0:T(8,128)(2,1)S(1)}, bf16[384,384]{1,0:T(8,128)(2,1)}, u32[]{:S(2)}, u32[]{:S(2)}) collective-permute-start(bf16[384,384]{1,0:T(8,128)(2,1)S(1)} %slice.498), channel_id=1, source_target_pairs={{0,16},{8,24},{16,0},{24,8},{1,17},{9,25},{17,1},{25,9},{2,18},{10... | collective-permute-start | bytes 884744 | tf_op jit(solution)/shard_map/ppermute | solution.py:118
  164.7 43.1 %collective-permute-start.9 = (bf16[384,384]{1,0:T(8,128)(2,1)}, bf16[384,384]{1,0:T(8,128)(2,1)}, u32[]{:S(2)}, u32[]{:S(2)}) collective-permute-start(bf16[384,384]{1,0:T(8,128)(2,1)} %slice.499), channel_id=1, source_target_pairs={{0,8},{8,0},{16,24},{24,16},{1,9},{9,1},{17,25},{25,17},{2,10},{10... | collective-permute-start | bytes 884744 | tf_op jit(solution)/shard_map/ppermute | solution.py:118
  167.9 42.2 %collective-permute-start.12 = (bf16[96,1536]{1,0:T(8,128)(2,1)}, bf16[96,1536]{1,0:T(8,128)(2,1)}, u32[]{:S(2)}, u32[]{:S(2)}) collective-permute-start(bf16[96,1536]{1,0:T(8,128)(2,1)} %slice.501), channel_id=1, source_target_pairs={{0,16},{8,24},{16,0},{24,8},{1,17},{9,25},{17,1},{25,9},{2,18},{10... | collective-permute-start | bytes 884744 | tf_op jit(solution)/shard_map/ppermute | solution.py:118
  231.4 86.6 %all-gather.11.cloned.1.call-start = ((), (), s32[]{:S(2)}) async-start(), calls=%async_computation.22 | async-start | bytes 5308416 | tf_op jit(solution)/shard_map/all_gather | solution.py:264
  240.7 212.5 %reduce-scatter.7.cloned.1.call-start = ((), (), s32[]{:S(2)}) async-start(), calls=%async_computation.23 | async-start | bytes 5308416 | tf_op jit(solution)/shard_map/reduce_scatter | solution.py:375
  317.7 135.5 %reduce-scatter.9.cloned.1.call-start = ((), (), s32[]{:S(2)}) async-start(), calls=%async_computation.24 | async-start | bytes 5308416 | tf_op jit(solution)/shard_map/reduce_scatter | solution.py:375
  339.6 332.2 %reduce-scatter.13.cloned.1.call-start = ((), (), s32[]{:S(2)}) async-start(), calls=%async_computation.26 | async-start | bytes 1327104 | tf_op jit(solution)/shard_map/reduce_scatter | solution.py:375
  384.8 287.1 %reduce-scatter.11.cloned.1.call-start = ((), (), s32[]{:S(2)}) async-start(), calls=%async_computation.25 | async-start | bytes 3981312 | tf_op jit(solution)/shard_map/reduce_scatter | solution.py:375
  408.7 41.1 %all-to-all-start.5 = ((bf16[1,256,4,384]{3,1,0,2:T(8,128)(2,1)}), bf16[1,256,4,384]{3,1,0,2:T(8,128)(2,1)}, u32[]{:S(2)}, u32[]{:S(2)}) async-start(bf16[1,256,4,384]{3,1,0,2:T(8,128)(2,1)} %copy.192), calls=%async_computation.5 | async-start | bytes 1572864 | tf_op jit(solution)/shard_map/all_to_all | solution.py:462
  472.5 40.5 %all-to-all-start.7 = ((bf16[4,64,1536]{2,1,0:T(8,128)(2,1)}), bf16[4,64,1536]{2,1,0:T(8,128)(2,1)}, u32[]{:S(2)}, u32[]{:S(2)}) async-start(bf16[4,64,1536]{2,1,0:T(8,128)(2,1)} %bitcast.61), calls=%async_computation.9 | async-start | bytes 1572864 | tf_op jit(solution)/shard_map/all_to_all | solution.py:197
  476.9 214.5 %reduce-scatter.17.cloned.1.call-start = ((), (), s32[]{:S(2)}) async-start(), calls=%async_computation.28 | async-start | bytes 1327104 | tf_op jit(solution)/shard_map/reduce_scatter | solution.py:375
  491.2 185.6 %collective-permute-start.41 = (bf16[192,1536]{1,0:T(8,128)(2,1)}, bf16[192,1536]{1,0:T(8,128)(2,1)}, u32[]{:S(2)}, u32[]{:S(2)}) collective-permute-start(bf16[192,1536]{1,0:T(8,128)(2,1)} %reduce-scatter.7.cloned.1.call-done), channel_id=1, source_target_pairs={{0,16},{8,24},{1,17},{9,25},{2,18},{10,26},{3,19},{11,27},{4,20},{... | collective-permute-start | bytes 1769480 | tf_op jit(solution)/shard_map/ppermute | solution.py:124
  554.6 42.6 %collective-permute-start.22 = (bf16[768,384]{1,0:T(8,128)(2,1)}, bf16[768,384]{1,0:T(8,128)(2,1)}, u32[]{:S(2)}, u32[]{:S(2)}) collective-permute-start(bf16[768,384]{1,0:T(8,128)(2,1)} %pad_maximum_fusion.18), channel_id=1, source_target_pairs={{0,16},{8,24},{16,0},{24,8},{1,17},{9,25},{17,1},{25,9},{2,18},{10... | collective-permute-start | bytes 1769480 | tf_op jit(solution)/shard_map/ppermute | solution.py:118
  555.5 42.3 %collective-permute-start.21 = (bf16[768,384]{1,0:T(8,128)(2,1)}, bf16[768,384]{1,0:T(8,128)(2,1)}, u32[]{:S(2)}, u32[]{:S(2)}) collective-permute-start(bf16[768,384]{1,0:T(8,128)(2,1)} %pad_maximum_fusion.17), channel_id=1, source_target_pairs={{0,8},{8,0},{16,24},{24,16},{1,9},{9,1},{17,25},{25,17},{2,10},{10... | collective-permute-start | bytes 1769480 | tf_op jit(solution)/shard_map/ppermute | solution.py:118
  560.6 56.9 %all-to-all-start.8 = ((bf16[4,64,1536]{2,1,0:T(8,128)(2,1)}), bf16[4,64,1536]{2,1,0:T(8,128)(2,1)}, u32[]{:S(2)}, u32[]{:S(2)}) async-start(bf16[4,64,1536]{2,1,0:T(8,128)(2,1)} %bitcast.349), calls=%async_computation.10 | async-start | bytes 1572864 | tf_op jit(solution)/shard_map/all_to_all | solution.py:176
  564.9 140.2 %reduce-scatter.15.cloned.1.call-start = ((), (), s32[]{:S(2)}) async-start(), calls=%async_computation.27 | async-start | bytes 3981312 | tf_op jit(solution)/shard_map/reduce_scatter | solution.py:375
  603.7 40.1 %collective-permute-start.26 = (bf16[256,1536]{1,0:T(8,128)(2,1)}, bf16[256,1536]{1,0:T(8,128)(2,1)S(1)}, u32[]{:S(2)}, u32[]{:S(2)}) collective-permute-start(bf16[256,1536]{1,0:T(8,128)(2,1)} %pad_maximum_fusion.11), channel_id=1, source_target_pairs={{0,16},{8,24},{16,0},{24,8},{1,17},{9,25},{17,1},{25,9},{2,18},{10... | collective-permute-start | bytes 2359304 | tf_op jit(solution)/shard_map/ppermute | solution.py:118
  616.2 60.7 %collective-permute-start.40 = (bf16[192,1536]{1,0:T(8,128)(2,1)S(1)}, bf16[192,1536]{1,0:T(8,128)(2,1)}, u32[]{:S(2)}, u32[]{:S(2)}) collective-permute-start(bf16[192,1536]{1,0:T(8,128)(2,1)S(1)} %fusion.78), channel_id=1, source_target_pairs={{16,0},{24,8},{17,1},{25,9},{18,2},{26,10},{19,3},{27,11},{20,4},{... | collective-permute-start | bytes 1769480 | tf_op jit(solution)/shard_map/ppermute | solution.py:127
  (160 other events, 1825.3 us)
Sparse Core Ops, SparseCore 0:
  29.4 65.6 all-gather.4
  96.7 59.7 all-gather.6
  162.0 66.0 all-gather.8
  240.8 54.0 all-gather.10
  317.8 55.9 reduce-scatter.6
  375.9 63.5 reduce-scatter.8
  441.8 32.3 reduce-scatter.12
  476.5 49.7 reduce-scatter.10
  546.9 33.4 reduce-scatter.16
  601.1 45.6 reduce-scatter.14

commit v10 on v9

--- a/solution.py
+++ b/solution.py
@@ -208,12 +208,13 @@
     def sum_by_distance(own, side, ahead, across, gate=None):
         half = own.shape[0] // 2
         across = across.astype(low)
-        upper = swapped(across[:half], 2).astype(full)
-        lower = swapped(across[half:], 1).astype(full)
+        upper = swapped(across[:half], 2)
+        lower = swapped(across[half:], 1)
         if gate is not None:
             upper, lower = after((upper, lower), gate)
-        side = jnp.concatenate([side[:half] + upper, side[half:]], axis=0).astype(low)
-        ahead = jnp.concatenate([ahead[:half], ahead[half:] + lower], axis=0).astype(low)
+        side = jnp.concatenate([side[:half] + upper.astype(full), side[half:]], axis=0)
+        ahead = jnp.concatenate([ahead[:half], ahead[half:] + lower.astype(full)], axis=0)
+        side, ahead = side.astype(low), ahead.astype(low)
         return own + swapped(side, 1).astype(full) + swapped(ahead, 2).astype(full)
 
     def share_first(lower, upper):
@@ -275,24 +276,32 @@
         *after((w_down[0, :half_hidden], w_down[0, half_hidden:]), other_heads)
     )
 
-    def in_depth(near, far):
-        parts = [part.reshape(dp_count, 1, half_depth, -1) for part in pick(near, far)]
-        return jnp.concatenate(parts, axis=1).reshape(feature_width, -1)
+    def by_depth(rows):
+        return rows.reshape(-1, dp_count, 2, half_depth).swapaxes(1, 2).reshape(rows.shape)
+
+    def in_depth(rows):
+        return rows.reshape(-1, 2, dp_count, half_depth).swapaxes(1, 2).reshape(rows.shape)
 
     def first_ffn(gate):
         down, up = after((down_share, up_turned), gate)
         down, up = by_distance(down), by_distance(up)
         return (
-            jnp.concatenate([in_depth(up[0], up[2]), in_depth(up[1], up[3])], axis=1),
+            jnp.concatenate(
+                [
+                    jnp.concatenate(pick(up[0], up[2]), axis=0),
+                    jnp.concatenate(pick(up[1], up[3]), axis=0),
+                ],
+                axis=1,
+            ),
             jnp.concatenate(pick(down[0], down[2]) + pick(down[1], down[3]), axis=0),
         )
 
-    up_even, up_odd = column_parts(w_up[0], half_hidden)
-    up_piece, down_piece = after((up_even, w_down[0, :half_hidden]), all_gains)
+    up_late, down_late = after((w_up[0], w_down[0]), all_gains)
     down_second = gather(
-        jnp.where(on_first, to_first(down_piece), w_down[0, half_hidden:])
-    )
-    up_second = gather(jnp.where(on_first, to_first(up_piece), up_odd))
+        jnp.where(on_first, to_first(down_late[:half_hidden]), down_late[half_hidden:])
+    )
+    up_even, up_odd = column_parts(up_late, half_hidden)
+    up_second = gather(jnp.where(on_first, to_first(up_even), up_odd))
     up_w = [None, up_second]
     down_w = [None, down_second]
     query_w = [weight[:, :inner] for weight in qkv_w]
@@ -348,7 +357,7 @@
         middle = current + sum_to_slots(matmul(attended_low, out_w[layer]))
         unit_mid, inverse_mid = unit_rows(middle)
         ffn_low = (unit_mid * all_gains[layer, 2]).astype(low)
-        ffn_low = from_slots(ffn_low) if layer else from_sequences(ffn_low)
+        ffn_low = from_slots(ffn_low) if layer else from_sequences(by_depth(ffn_low))
         hidden_pre = matmul(ffn_low, up_w[layer])
         active_low = gelu_exact(hidden_pre).astype(low)
         if layer == 0:
@@ -375,7 +384,15 @@
         return lax.psum_scatter(blocks, dp, scatter_dimension=0, tiled=True)
 
     gain_rows = [None] * LAYERS
-    media_scaled = None
+    media_parts = []
+    media_gains = []
+
+    def add_media(layer, grad_key, grad_value, gate):
+        grad_key, grad_value = after((grad_key[:seq_rows], grad_value[:seq_rows]), gate)
+        part = matmul_nt(grad_key, key_w[layer]) + matmul_nt(grad_value, value_w[layer])
+        media_gains.append(jnp.sum(part * media_unit, axis=0))
+        media_parts.append(part * all_gains[layer, 0])
+
     pieces = [None] * LAYERS
     for layer in (1, 0):
         (
@@ -395,6 +412,8 @@
         ) = saved[layer]
         grad_active = matmul_nt(grad_low, down_w[layer])
         grad_hidden = jax.vjp(gelu_exact, hidden_pre)[1](grad_active)[0].astype(low)
+        if layer == 0:
+            add_media(1, *media_grads, grad_hidden)
         down_grad = matmul_tn(active_low, grad_low)
         if layer:
             down_grad = down_grad.astype(low)
@@ -404,14 +423,13 @@
             ffn_pieces = (scatter(down_grad), scatter(up_grad.astype(low)))
             ffn_grad = sum_to_slots(matmul_nt(grad_hidden, up_w[layer]))
         else:
-            ffn_grad = sum_to_sequence(grad_hidden, up_w[layer], matmul_nt)
+            ffn_grad = in_depth(sum_to_sequence(grad_hidden, up_w[layer], matmul_nt))
             blocks = down_grad.reshape(2, 2, half_hidden, feature_width)
             own, ahead = pick(blocks[0, 0], blocks[0, 1])
             side, across = pick(blocks[1, 0], blocks[1, 1])
             down_blocks = (own, side, ahead, across)
             width = up_grad.shape[1] // 2
-            blocks = up_grad.reshape(dp_count, 2, half_depth, 2 * width)
-            blocks = [blocks[:, i].reshape(-1, 2 * width) for i in range(2)]
+            blocks = up_grad.reshape(2, -1, 2 * width)
             own, ahead = pick(blocks[0][:, :width], blocks[1][:, :width])
             side, across = pick(blocks[0][:, width:], blocks[1][:, width:])
             up_blocks = (own, side, ahead, across)
@@ -454,30 +472,34 @@
         pieces[layer] = (scatter(qkv_grad), out_piece)
         if layer > 0:
             grad_low = from_sequences(grad_rows.astype(low))
-            last = matmul(after(active_low, latent_part), down_w[layer])
-            start = section * slot_rows
-            rows = lax.dynamic_slice_in_dim(last, start, slot_rows, 0) + middle
-            last = lax.dynamic_update_slice_in_dim(last, rows, start, 0).astype(low)
-            last = last.reshape(latent_rows, section_count, -1)
-            last = lax.all_to_all(last, "section", split_axis=1, concat_axis=0)
+            late = after(active_low, latent_part)
+            here = (latent_slot == section)[:, None]
+            kept = jnp.where(here, jnp.tile(middle, (section_count, 1)), 0.0)
+            width = feature_width // section_count
+            last = []
+            for i in range(section_count):
+                cut = slice(i * width, (i + 1) * width)
+                last.append((matmul(late, down_w[layer][:, cut]) + kept[:, cut]).astype(low))
+            last = lax.all_to_all(jnp.stack(last), "section", split_axis=0, concat_axis=0)
             latents_out = jnp.sum(last.astype(full), axis=0)
             grad_low = after(grad_low, latents_out)
             grad_low = after(grad_low, ffn_pieces)
-        media_part = matmul_nt(grad_key[:seq_rows], key_w[layer]) + matmul_nt(
-            grad_value[:seq_rows], value_w[layer]
-        )
-        gain_media_grad = jnp.sum(media_part * media_unit, axis=0)
-        scaled = media_part * all_gains[layer, 0]
-        media_scaled = scaled if media_scaled is None else media_scaled + scaled
-        gain_rows[layer] = jnp.stack([gain_media_grad, gain_latent_grad, gain_ffn_grad])
+        if layer == 0:
+            add_media(0, grad_key, grad_value, qkv_grad)
+        else:
+            media_grads = (grad_key, grad_value)
+        gain_rows[layer] = (gain_latent_grad, gain_ffn_grad)
     latent_grad = to_columns(after(grad_rows, (pieces[1], up_half)))
     media_rows = seq_rows // section_count
-    media_sum = sum_over_sections(media_scaled)
+    media_sum = sum_over_sections(media_parts[0] + media_parts[1])
     own_unit = lax.dynamic_slice_in_dim(media_unit, section * media_rows, media_rows, 0)
     own_inverse = lax.dynamic_slice_in_dim(media_inverse, section * media_rows, media_rows, 0)
     media_grad = gather_sections(norm_back(own_unit, own_inverse, media_sum).astype(low)).astype(
         full
     )
+    gain_rows = [
+        jnp.stack([media_gains[1 - layer], *gain_rows[layer]]) for layer in range(LAYERS)
+    ]
     gain_parts = jnp.stack(gain_rows).reshape(LAYERS, 3, section_count, -1)
     gain_parts = jnp.sum(
         lax.all_to_all(gain_parts, "section", split_axis=2, concat_axis=2), axis=2

time: 738 us -> 730 us (0.989)
  waiting for transfers between devices: 81.4 us -> 65.6 us
  matrix products: 145 us -> 157 us
  other arithmetic: 113 us -> 101 us
  local copies, waits for them, and re-layouts: 108 us -> 99.1 us
  blocking collectives: 144 us -> 152 us
  starting transfers between devices: 117 us -> 125 us
    all_to_all x1, waiting for transfers between devices: 12.3 us -> 0.01 us  [per_device(): lax.all_to_all(gain_parts, 'section', split_axis=2, concat_axis=2)]
    dot_general x13 -> x16, matrix products: 45.2 us -> 57.1 us  [matmul(): return jnp.dot(left, right, preferred_element_type=full)]
    another operation x10 -> x7, local copies, waits for them, and re-layouts: 11.2 us -> 0.74 us  [the longest x1 5.35 us: column_parts(): split = weight.reshape(rows, width // (2 * block), 2, block)]
    convert_element_type x5 -> x0, other arithmetic: 9.7 us -> none  [the longest x2 3.65 us: sum_by_distance(): lower = swapped(across[half:], 1).astype(full)]
    all_to_all x1, waiting for transfers between devices: 9.22 us -> 0.01 us  [per_device(): lax.all_to_all(up_share, dp, split_axis=1, concat_axis=0, tiled=True)]
    unnamed x244 -> x250, local copies, waits for them, and re-layouts: 22.6 us -> 20.8 us
  transfers between devices with their start and end apart: 64 -> 64, of which waited for: 15 -> 14; matrix products, arithmetic and copies ran while one was open for 47% -> 46% of each run, Pallas kernels for 0% -> 0%
where the time goes in v10:
time: 730 us; the launch traced here: 716 us
  matrix products  157 us (22%)
  blocking collectives  152 us (21%)
  starting transfers between devices  125 us (17%)
  other arithmetic  101 us (14%)
  local copies, waits for them, and re-layouts  99.1 us (14%)
  waiting for transfers between devices  65.6 us (9%)
  between operations  16.9 us (2%)
    all_gather x2, blocking collectives, from_sequences(): near = lax.all_gather(rows, 'pair', axis=0, tiled=True)  59.6 us
    dot_general x16, matrix products, matmul(): return jnp.dot(left, right, preferred_element_type=full)  57.1 us
    dot_general x17, matrix products, matmul_nt(): lax.dot_general(left, right, (((1,), (1,)), ((), ())), preferred_element_...  51.6 us
    all_gather x4, blocking collectives, from_slots(): return lax.all_gather(rows, 'section', axis=0, tiled=True)  47.7 us
    ppermute x26, starting transfers between devices, swapped(): return lax.ppermute(value, 'section', pairs)  33.6 us
    all_gather x3, blocking collectives, per_device(): all_gains = lax.all_gather(all_gains, axis, axis=2, tiled=True)  31.7 us
    dot_general x8, matrix products, matmul_tn(): lax.dot_general(left, right, (((0,), (0,)), ((), ())), preferred_element_...  27.5 us
    ppermute x26, waiting for transfers between devices, swapped(): return lax.ppermute(value, 'section', pairs)  24.6 us
  transfers between devices with their start and end apart: 64, of which 14 were waited for; matrix products, arithmetic and copies ran while one was open for 46% of the time, Pallas kernels for 0%

profile of v10, /device:TPU:0, one launch (start us, length us, event | category | flops | bytes accessed | tf_op | source)
XLA Modules:
  0.0 716.2 jit_solution(4094244898999170386)
XLA Ops:
  12.6 10.2 %collective-permute-done = bf16[192,1152]{1,0:T(8,128)(2,1)S(1)} collective-permute-done((bf16[192,1152]{1,0:T(8,128)(2,1)S(1)}, bf16[192,1152]{1,0:T(8,128)(2,1)S(1)}, u32[]{:S(2)}, u32[]{:S(2)}) %collective-permute-start) | collective-permute-done | bytes 442400 | tf_op jit(solution)/shard_map/ppermute | solution.py:118
  32.0 10.9 %collective-permute-start.1 = (bf16[96,3072]{1,0:T(8,128)(2,1)}, bf16[96,3072]{1,0:T(8,128)(2,1)}, u32[]{:S(2)}, u32[]{:S(2)}) collective-permute-start(bf16[96,3072]{1,0:T(8,128)(2,1)} %slice_bitcast_fusion.4), channel_id=1, source_target_pairs={{0,16},{8,24},{1,17},{9,25},{2,18},{10,26},{3,19},{11,27},{4,20},{... | collective-permute-start | bytes 1769480 | tf_op jit(solution)/shard_map/ppermute | solution.py:124
  57.8 19.4 %all_gather.40 = f32[2,3,384]{1,0,2:T(2,128)} all-gather(f32[2,3,96]{1,0,2:T(2,128)S(1)} %all_gather.39), channel_id=1, replica_groups=mesh['section'=4,'pair'=4,'core'=2] {'pair'}, dimensions={2}, use_global_device_ids=true | all-gather | bytes 11520 | tf_op jit(solution)/shard_map/all_gather | solution.py:261
  78.4 10.3 %all_gather.41 = f32[2,3,1536]{2,0,1:T(2,128)S(1)} all-gather(f32[2,3,384]{2,0,1:T(2,128)S(1)} %copy.148), channel_id=1, replica_groups=mesh['section'=4,'pair'=4,'core'=2] {'section'}, dimensions={2}, use_global_device_ids=true | all-gather | bytes 46080 | tf_op jit(solution)/shard_map/all_gather | solution.py:261
  94.9 5.4 reshape.739
  100.2 9.5 %slice_reduce_fusion = (bf16[192,8,192]{2,1,0:T(8,128)(2,1)}, bf16[192,8,192]{2,1,0:T(8,128)(2,1)}) fusion(bf16[192,8,2,192]{3,2,1,0:T(2,128)(2,1)} %reshape.739), kind=kLoop, calls=%fused_computation.102 | loop fusion | bytes 2359296 | tf_op jit(solution)/shard_map/slice | solution.py:245
  174.4 30.1 %all_gather.43 = bf16[256,1536]{1,0:T(8,128)(2,1)S(1)} all-gather(bf16[64,1536]{1,0:T(8,128)(2,1)S(1)} %reshape.731), channel_id=1, replica_groups=mesh['section'=4,'pair'=4,'core'=2] {'pair'}, dimensions={0}, use_global_device_ids=true | all-gather | bytes 983040 | tf_op jit(solution)/shard_map/all_gather | solution.py:189
  214.6 13.6 %multiply_convert_fusion.6 = (bf16[512,768]{1,0:T(8,128)(2,1)S(1)}, f32[512,768]{1,0:T(8,128)}, f32[512,768]{1,0:T(8,128)}) fusion(bf16[512,1536]{1,0:T(8,128)(2,1)S(1)} %constant_dynamic-update-slice_fusion, bf16[768,384]{1,0:T(8,128)(2,1)S(1)} %get-tuple-element.123, bf16[768,384]{1,0:T(8,128)(2,1)S(1)} %get-tuple-element.122, ...), kind=kOutput, calls=%fused_computation.134 | convolution fusion | flops 1242955776 | bytes 7864320 | tf_op jit(solution)/shard_map/dot_general | solution.py:35
  238.9 9.6 %collective-permute-done.16 = bf16[192,1536]{1,0:T(8,128)(2,1)} collective-permute-done((bf16[192,1536]{1,0:T(8,128)(2,1)}, bf16[192,1536]{1,0:T(8,128)(2,1)}, u32[]{:S(2)}, u32[]{:S(2)}) %collective-permute-start.16) | collective-permute-done | bytes 589856 | tf_op jit(solution)/shard_map/ppermute | solution.py:127
  263.9 12.0 %all_gather.45 = bf16[256,1536]{1,0:T(8,128)(2,1)S(1)} all-gather(bf16[64,1536]{1,0:T(8,128)(2,1)S(1)} %multiply_convert_fusion.8), channel_id=1, replica_groups=mesh['section'=4,'pair'=4,'core'=2] {'section'}, dimensions={0}, use_global_device_ids=true | all-gather | bytes 983040 | tf_op jit(solution)/shard_map/all_gather | solution.py:180
  291.9 12.6 %all_to_all.101 = bf16[4,64,1536]{2,1,0:T(8,128)(2,1)S(1)} all-to-all(bf16[4,64,1536]{2,1,0:T(8,128)(2,1)S(1)} %bitcast.350), channel_id=1, replica_groups=mesh['section'=4,'pair'=4,'core'=2] {'section'}, dimensions={0} | all-to-all | bytes 1572864 | tf_op jit(solution)/shard_map/all_to_all | solution.py:176
  305.1 12.1 %all_gather.46 = bf16[256,1536]{1,0:T(8,128)(2,1)} all-gather(bf16[64,1536]{1,0:T(8,128)(2,1)S(1)} %multiply_convert_fusion.7), channel_id=1, replica_groups=mesh['section'=4,'pair'=4,'core'=2] {'section'}, dimensions={0}, use_global_device_ids=true | all-gather | bytes 983040 | tf_op jit(solution)/shard_map/all_gather | solution.py:180
  317.2 8.2 %multiply_convert_fusion.5 = (bf16[256,1536]{1,0:T(8,128)(2,1)S(1)}, f32[256,1536]{1,0:T(8,128)}) fusion(bf16[256,1536]{1,0:T(8,128)(2,1)} %all_gather.46, bf16[1536,1536]{1,0:T(8,128)(2,1)} %all-gather.9.cloned.1.call-done), kind=kOutput, calls=%fused_computation.119 | convolution fusion | flops 1233518592 | bytes 7864320 | tf_op jit(solution)/shard_map/dot_general | solution.py:35
  330.2 7.7 %add_convert_fusion.1 = bf16[256,1536]{1,0:T(8,128)(2,1)S(1)} fusion(bf16[1536,1536]{1,0:T(8,128)(2,1)} %all-gather.11.cloned.1.call-done, bf16[256,1536]{1,0:T(8,128)(2,1)} %param.23, f32[256,1536]{1,0:T(8,128)} %get-tuple-element.175), kind=kOutput, calls=%fused_computation.118 | convolution fusion | flops 1236271104 | bytes 7864320 | tf_op jit(solution)/shard_map/dot_general | solution.py:39
  353.9 6.6 all-to-all-done.4
  364.0 11.4 %all_gather.49 = bf16[256,1536]{1,0:T(8,128)(2,1)S(1)} all-gather(bf16[64,1536]{1,0:T(8,128)(2,1)S(1)} %get-tuple-element.88), channel_id=1, replica_groups=mesh['section'=4,'pair'=4,'core'=2] {'section'}, dimensions={0}, use_global_device_ids=true | all-gather | bytes 983040 | tf_op jit(solution)/shard_map/all_gather | solution.py:180
  414.9 29.6 %all_gather.50 = bf16[256,1536]{1,0:T(8,128)(2,1)} all-gather(bf16[64,1536]{1,0:T(8,128)(2,1)S(1)} %get-tuple-element.86), channel_id=1, replica_groups=mesh['section'=4,'pair'=4,'core'=2] {'pair'}, dimensions={0}, use_global_device_ids=true | all-gather | bytes 983040 | tf_op jit(solution)/shard_map/all_gather | solution.py:189
  444.5 7.3 %convolution_convert_fusion.1 = bf16[1536,1152]{1,0:T(8,128)(2,1)} fusion(bf16[256,1536]{1,0:T(8,128)(2,1)S(1)} %copy-done.70, bf16[1024,1536]{1,0:T(8,128)(2,1)S(1)} %copy-done.41, bf16[256,384]{0,1:T(8,128)(2,1)S(1)} %bitcast.375, bf16[1280,384]{0,1:T(8,128)(2,1)S(1)} %bitcast.335, bf16[1280,384]{0,1:T(8,128)(2,1)S(1)} %bitcast.346), kind=kOutput, calls=%fused_computation.3 | convolution fusion | flops 4551278592 | bytes 9633792 | tf_op jit(solution)/shard_map/dot_general | solution.py:43
  520.4 12.2 %all_gather.51 = bf16[256,1536]{1,0:T(8,128)(2,1)S(1)} all-gather(bf16[64,1536]{1,0:T(8,128)(2,1)S(1)} %get-tuple-element.84), channel_id=1, replica_groups=mesh['section'=4,'pair'=4,'core'=2] {'section'}, dimensions={0}, use_global_device_ids=true | all-gather | bytes 983040 | tf_op jit(solution)/shard_map/all_gather | solution.py:180
  570.2 9.2 %convolution_convert_fusion = bf16[1536,1152]{1,0:T(8,128)(2,1)} fusion(bf16[256,1536]{1,0:T(8,128)(2,1)} %fusion.56, bf16[1024,1536]{1,0:T(8,128)(2,1)} %get-tuple-element.109, bf16[256,384]{0,1:T(8,128)(2,1)S(1)} %bitcast.377, bf16[1280,384]{0,1:T(8,128)(2,1)S(1)} %bitcast.333, bf16[1280,384]{0,1:T(8,128)(2,1)S(1)} %bitcast.343), kind=kOutput, calls=%fused_computation.2 | convolution fusion | flops 4551278592 | bytes 9633792 | tf_op jit(solution)/shard_map/dot_general | solution.py:43
  591.9 9.0 %multiply_reduce_fusion.1 = (f32[1536]{0:T(1024)S(1)}, f32[1536]{0:T(1024)S(1)}, f32[1024,1536]{1,0:T(8,128)}, f32[1024,1536]{1,0:T(8,128)}) fusion(bf16[1024,1536]{1,0:T(8,128)(2,1)S(1)} %copy-done.3, f32[1024]{0:T(1024)S(1)} %add_rsqrt_fusion, f32[1024]{0:T(1024)S(1)} %copy-done.98, f32[1024,1536]{1,0:T(8,128)} %convolution_add_fusion.1, ...), kind=kOutput, calls=%fused_computation.10 | convolution fusion | flops 1225257984 | bytes 30310400 | tf_op jit(solution)/shard_map/dot_general | solution.py:39
  601.6 6.1 all-to-all-start.11
  639.6 8.3 %all-to-all-done.9 = bf16[8,96,384]{2,1,0:T(8,128)(2,1)S(1)} async-done(((bf16[8,96,384]{2,1,0:T(8,128)(2,1)}), bf16[8,96,384]{2,1,0:T(8,128)(2,1)S(1)}, u32[]{:S(2)}, u32[]{:S(2)}) %all-to-all-start.9) | async-done | bytes 589856 | tf_op jit(solution)/shard_map/all_to_all | solution.py:471
  664.0 5.7 all-to-all-done.10
  (644 shorter events, 422.4 us)
Async XLA Ops:
  7.2 114.7 %all-gather.5.cloned.1.call-start = ((), (), s32[]{:S(2)}) async-start(), calls=%async_computation.19 | async-start | bytes 5308416 | tf_op jit(solution)/shard_map/all_gather | solution.py:265
  29.9 220.7 %all-gather.7.cloned.1.call-start = ((), (), s32[]{:S(2)}) async-start(), calls=%async_computation.20 | async-start | bytes 5308416 | tf_op jit(solution)/shard_map/all_gather | solution.py:265
  52.6 68.4 %collective-permute-start.5 = (bf16[192,1536]{1,0:T(8,128)(2,1)}, bf16[192,1536]{1,0:T(8,128)(2,1)}, u32[]{:S(2)}, u32[]{:S(2)}) collective-permute-start(bf16[192,1536]{1,0:T(8,128)(2,1)} %get-tuple-element.38), channel_id=1, source_target_pairs={{0,16},{8,24},{1,17},{9,25},{2,18},{10,26},{3,19},{11,27},{4,20},{... | collective-permute-start | bytes 1769480 | tf_op jit(solution)/shard_map/ppermute | solution.py:124
  114.6 44.7 %collective-permute-start.15 = (bf16[192,1536]{1,0:T(8,128)(2,1)}, bf16[192,1536]{1,0:T(8,128)(2,1)}, u32[]{:S(2)}, u32[]{:S(2)}) collective-permute-start(bf16[192,1536]{1,0:T(8,128)(2,1)} %reshape_squeeze.6), channel_id=1, source_target_pairs={{16,0},{24,8},{17,1},{25,9},{18,2},{26,10},{19,3},{27,11},{20,4},{... | collective-permute-start | bytes 1769480 | tf_op jit(solution)/shard_map/ppermute | solution.py:127
  159.3 157.9 %all-gather.9.cloned.1.call-start = ((), (), s32[]{:S(2)}) async-start(), calls=%async_computation.21 | async-start | bytes 5308416 | tf_op jit(solution)/shard_map/all_gather | solution.py:265
  163.0 44.6 %collective-permute-start.8 = (bf16[384,384]{1,0:T(8,128)(2,1)}, bf16[384,384]{1,0:T(8,128)(2,1)}, u32[]{:S(2)}, u32[]{:S(2)}) collective-permute-start(bf16[384,384]{1,0:T(8,128)(2,1)} %slice.538), channel_id=1, source_target_pairs={{0,16},{8,24},{16,0},{24,8},{1,17},{9,25},{17,1},{25,9},{2,18},{10... | collective-permute-start | bytes 884744 | tf_op jit(solution)/shard_map/ppermute | solution.py:118
  165.7 43.2 %collective-permute-start.9 = (bf16[384,384]{1,0:T(8,128)(2,1)}, bf16[384,384]{1,0:T(8,128)(2,1)}, u32[]{:S(2)}, u32[]{:S(2)}) collective-permute-start(bf16[384,384]{1,0:T(8,128)(2,1)} %slice.539), channel_id=1, source_target_pairs={{0,8},{8,0},{16,24},{24,16},{1,9},{9,1},{17,25},{25,17},{2,10},{10... | collective-permute-start | bytes 884744 | tf_op jit(solution)/shard_map/ppermute | solution.py:118
  168.8 42.2 %collective-permute-start.12 = (bf16[96,1536]{1,0:T(8,128)(2,1)}, bf16[96,1536]{1,0:T(8,128)(2,1)}, u32[]{:S(2)}, u32[]{:S(2)}) collective-permute-start(bf16[96,1536]{1,0:T(8,128)(2,1)} %slice.541), channel_id=1, source_target_pairs={{0,16},{8,24},{16,0},{24,8},{1,17},{9,25},{17,1},{25,9},{2,18},{10... | collective-permute-start | bytes 884744 | tf_op jit(solution)/shard_map/ppermute | solution.py:118
  172.2 40.1 %collective-permute-start.13 = (bf16[96,1536]{1,0:T(8,128)(2,1)}, bf16[96,1536]{1,0:T(8,128)(2,1)}, u32[]{:S(2)}, u32[]{:S(2)}) collective-permute-start(bf16[96,1536]{1,0:T(8,128)(2,1)} %slice.542), channel_id=1, source_target_pairs={{0,8},{8,0},{16,24},{24,16},{1,9},{9,1},{17,25},{25,17},{2,10},{10... | collective-permute-start | bytes 884744 | tf_op jit(solution)/shard_map/ppermute | solution.py:118
  238.9 91.2 %all-gather.11.cloned.1.call-start = ((), (), s32[]{:S(2)}) async-start(), calls=%async_computation.22 | async-start | bytes 5308416 | tf_op jit(solution)/shard_map/all_gather | solution.py:265
  250.5 207.2 %reduce-scatter.7.cloned.1.call-start = ((), (), s32[]{:S(2)}) async-start(), calls=%async_computation.23 | async-start | bytes 5308416 | tf_op jit(solution)/shard_map/reduce_scatter | solution.py:384
  329.9 127.8 %reduce-scatter.9.cloned.1.call-start = ((), (), s32[]{:S(2)}) async-start(), calls=%async_computation.24 | async-start | bytes 5308416 | tf_op jit(solution)/shard_map/reduce_scatter | solution.py:384
  352.4 298.2 %reduce-scatter.13.cloned.1.call-start = ((), (), s32[]{:S(2)}) async-start(), calls=%async_computation.26 | async-start | bytes 1327104 | tf_op jit(solution)/shard_map/reduce_scatter | solution.py:384
  408.0 46.2 %all-to-all-start.5 = ((bf16[4,256,384]{2,1,0:T(8,128)(2,1)}), bf16[4,256,384]{2,1,0:T(8,128)(2,1)}, u32[]{:S(2)}, u32[]{:S(2)}) async-start(bf16[4,256,384]{2,1,0:T(8,128)(2,1)} %pad_maximum_fusion.7), calls=%async_computation.5 | async-start | bytes 1572864 | tf_op jit(solution)/shard_map/all_to_all | solution.py:483
  412.3 238.3 %reduce-scatter.11.cloned.1.call-start = ((), (), s32[]{:S(2)}) async-start(), calls=%async_computation.25 | async-start | bytes 3981312 | tf_op jit(solution)/shard_map/reduce_scatter | solution.py:384
  470.4 75.7 %collective-permute-start.20 = (bf16[384,384]{1,0:T(8,128)(2,1)}, bf16[384,384]{1,0:T(8,128)(2,1)}, u32[]{:S(2)}, u32[]{:S(2)}) collective-permute-start(bf16[384,384]{1,0:T(8,128)(2,1)} %get-tuple-element.133), channel_id=1, source_target_pairs={{0,8},{8,0},{16,24},{24,16},{1,9},{9,1},{17,25},{25,17},{2,10},{10... | collective-permute-start | bytes 884744 | tf_op jit(solution)/shard_map/ppermute | solution.py:118
  472.3 73.7 %collective-permute-start.19 = (bf16[384,384]{1,0:T(8,128)(2,1)}, bf16[384,384]{1,0:T(8,128)(2,1)}, u32[]{:S(2)}, u32[]{:S(2)}) collective-permute-start(bf16[384,384]{1,0:T(8,128)(2,1)} %get-tuple-element.134), channel_id=1, source_target_pairs={{0,16},{8,24},{16,0},{24,8},{1,17},{9,25},{17,1},{25,9},{2,18},{10... | collective-permute-start | bytes 884744 | tf_op jit(solution)/shard_map/ppermute | solution.py:118
  474.7 74.6 %collective-permute-start.37 = (bf16[96,1536]{1,0:T(8,128)(2,1)}, bf16[96,1536]{1,0:T(8,128)(2,1)}, u32[]{:S(2)}, u32[]{:S(2)}) collective-permute-start(bf16[96,1536]{1,0:T(8,128)(2,1)} %get-tuple-element.131), channel_id=1, source_target_pairs={{0,8},{8,0},{16,24},{24,16},{1,9},{9,1},{17,25},{25,17},{2,10},{10... | collective-permute-start | bytes 884744 | tf_op jit(solution)/shard_map/ppermute | solution.py:118
  475.2 74.1 %collective-permute-start.36 = (bf16[96,1536]{1,0:T(8,128)(2,1)}, bf16[96,1536]{1,0:T(8,128)(2,1)}, u32[]{:S(2)}, u32[]{:S(2)}) collective-permute-start(bf16[96,1536]{1,0:T(8,128)(2,1)} %get-tuple-element.132), channel_id=1, source_target_pairs={{0,16},{8,24},{16,0},{24,8},{1,17},{9,25},{17,1},{25,9},{2,18},{10... | collective-permute-start | bytes 884744 | tf_op jit(solution)/shard_map/ppermute | solution.py:118
  478.5 37.7 %all-to-all-start.7 = ((bf16[4,64,1536]{2,1,0:T(8,128)(2,1)}), bf16[4,64,1536]{2,1,0:T(8,128)(2,1)}, u32[]{:S(2)}, u32[]{:S(2)}) async-start(bf16[4,64,1536]{2,1,0:T(8,128)(2,1)} %bitcast.59), calls=%async_computation.9 | async-start | bytes 1572864 | tf_op jit(solution)/shard_map/all_to_all | solution.py:197
  483.3 187.1 %reduce-scatter.17.cloned.1.call-start = ((), (), s32[]{:S(2)}) async-start(), calls=%async_computation.28 | async-start | bytes 1327104 | tf_op jit(solution)/shard_map/reduce_scatter | solution.py:384
  504.0 132.2 %collective-permute-start.41 = (bf16[192,1536]{1,0:T(8,128)(2,1)}, bf16[192,1536]{1,0:T(8,128)(2,1)}, u32[]{:S(2)}, u32[]{:S(2)}) collective-permute-start(bf16[192,1536]{1,0:T(8,128)(2,1)} %reduce-scatter.7.cloned.1.call-done), channel_id=1, source_target_pairs={{0,16},{8,24},{1,17},{9,25},{2,18},{10,26},{3,19},{11,27},{4,20},{... | collective-permute-start | bytes 1769480 | tf_op jit(solution)/shard_map/ppermute | solution.py:124
  569.9 126.7 %reduce-scatter.15.cloned.1.call-start = ((), (), s32[]{:S(2)}) async-start(), calls=%async_computation.27 | async-start | bytes 3981312 | tf_op jit(solution)/shard_map/reduce_scatter | solution.py:384
  582.5 53.7 %collective-permute-start.40 = (bf16[192,1536]{1,0:T(8,128)(2,1)}, bf16[192,1536]{1,0:T(8,128)(2,1)}, u32[]{:S(2)}, u32[]{:S(2)}) collective-permute-start(bf16[192,1536]{1,0:T(8,128)(2,1)} %fusion.83), channel_id=1, source_target_pairs={{16,0},{24,8},{17,1},{25,9},{18,2},{26,10},{19,3},{27,11},{20,4},{... | collective-permute-start | bytes 1769480 | tf_op jit(solution)/shard_map/ppermute | solution.py:127
  (163 other events, 1851.8 us)
Sparse Core Ops, SparseCore 0:
  30.0 65.5 all-gather.4
  97.3 54.1 all-gather.6
  162.3 65.8 all-gather.8
  250.6 52.7 all-gather.10
  330.0 55.6 reduce-scatter.6
  387.8 65.9 reduce-scatter.8
  456.1 31.3 reduce-scatter.12
  489.8 43.3 reduce-scatter.10
  546.1 33.0 reduce-scatter.16
  587.0 47.5 reduce-scatter.14

commit v11 on v10

--- a/solution.py
+++ b/solution.py
@@ -28,7 +28,12 @@
 
 
 def gelu_exact(values):
-    return jax.nn.gelu(values, approximate=False)
+    return 0.5 * values * (1.0 + lax.erf(values * math.sqrt(0.5)))
+
+
+def gelu_slope(values):
+    normal = 0.5 * (1.0 + lax.erf(values * math.sqrt(0.5)))
+    return normal + values * jnp.exp(-0.5 * values * values) * (1.0 / math.sqrt(2.0 * math.pi))
 
 
 def matmul(left, right):
@@ -197,10 +202,12 @@
         arrived = lax.all_to_all(blocks, "pair", split_axis=0, concat_axis=0)
         return jnp.sum(arrived.astype(full), axis=0)
 
-    def by_distance(rows):
+    def by_distance(rows, gate=None):
         half = rows.shape[0] // 2
         side = swapped(rows, 1)
         ahead = swapped(rows, 2)
+        if gate is not None:
+            side, ahead = after((side, ahead), gate)
         upper = swapped(side[:half], 2)
         lower = swapped(ahead[half:], 1)
         return rows, side, ahead, jnp.concatenate([upper, lower], axis=0)
@@ -229,8 +236,8 @@
             ]
         )
 
-    def gather_sections(rows):
-        by_mask = by_distance(rows)
+    def gather_sections(rows, gate):
+        by_mask = by_distance(rows, gate)
         ordered = []
         for target in range(section_count):
             chosen = by_mask[0]
@@ -296,14 +303,17 @@
             jnp.concatenate(pick(down[0], down[2]) + pick(down[1], down[3]), axis=0),
         )
 
-    up_late, down_late = after((w_up[0], w_down[0]), all_gains)
+    down_late = after(w_down[0], all_gains)
     down_second = gather(
         jnp.where(on_first, to_first(down_late[:half_hidden]), down_late[half_hidden:])
     )
-    up_even, up_odd = column_parts(up_late, half_hidden)
-    up_second = gather(jnp.where(on_first, to_first(up_even), up_odd))
-    up_w = [None, up_second]
-    down_w = [None, down_second]
+
+    def second_ffn(gate):
+        up_even, up_odd = column_parts(after(w_up[0], gate), half_hidden)
+        return gather(jnp.where(on_first, to_first(up_even), up_odd)), down_second
+
+    up_w = [None, None]
+    down_w = [None, None]
     query_w = [weight[:, :inner] for weight in qkv_w]
     key_w = [weight[:, inner : 2 * inner] for weight in qkv_w]
     value_w = [weight[:, 2 * inner :] for weight in qkv_w]
@@ -341,7 +351,8 @@
             latent_low = from_slots((unit_in * all_gains[layer, 1]).astype(low))
         projected = matmul(latent_low, qkv_w[layer]).astype(low)
         if layer == 0:
-            up_w[0], down_w[0] = first_ffn(projected)
+            up_w[0], down_w[0] = lax.optimization_barrier(first_ffn(projected))
+            up_w[1], down_w[1] = second_ffn(projected)
         query_low = projected[:, :inner]
         key_heads = split_heads(
             jnp.concatenate([media_key[layer], projected[:, inner : 2 * inner]], axis=0)
@@ -391,7 +402,7 @@
         grad_key, grad_value = after((grad_key[:seq_rows], grad_value[:seq_rows]), gate)
         part = matmul_nt(grad_key, key_w[layer]) + matmul_nt(grad_value, value_w[layer])
         media_gains.append(jnp.sum(part * media_unit, axis=0))
-        media_parts.append(part * all_gains[layer, 0])
+        media_parts.append((part * all_gains[layer, 0]).astype(low if layer else full))
 
     pieces = [None] * LAYERS
     for layer in (1, 0):
@@ -411,7 +422,7 @@
             active_low,
         ) = saved[layer]
         grad_active = matmul_nt(grad_low, down_w[layer])
-        grad_hidden = jax.vjp(gelu_exact, hidden_pre)[1](grad_active)[0].astype(low)
+        grad_hidden = (grad_active * gelu_slope(hidden_pre)).astype(low)
         if layer == 0:
             add_media(1, *media_grads, grad_hidden)
         down_grad = matmul_tn(active_low, grad_low)
@@ -466,9 +477,6 @@
             [jnp.pad(grad_query, ((seq_rows, 0), (0, 0))), grad_key, grad_value], axis=1
         )
         qkv_grad = matmul_tn(both_low, all_grads).astype(low)
-        if layer == 0:
-            up_half, qkv_grad = lax.optimization_barrier((up_half, qkv_grad))
-            up_half = lax.all_to_all(up_half, dp, split_axis=0, concat_axis=1, tiled=True)
         pieces[layer] = (scatter(qkv_grad), out_piece)
         if layer > 0:
             grad_low = from_sequences(grad_rows.astype(low))
@@ -489,34 +497,38 @@
         else:
             media_grads = (grad_key, grad_value)
         gain_rows[layer] = (gain_latent_grad, gain_ffn_grad)
-    latent_grad = to_columns(after(grad_rows, (pieces[1], up_half)))
     media_rows = seq_rows // section_count
-    media_sum = sum_over_sections(media_parts[0] + media_parts[1])
+    media_total = media_parts[0].astype(full) + media_parts[1]
+    up_half = lax.all_to_all(
+        after(up_half, media_total), dp, split_axis=0, concat_axis=1, tiled=True
+    )
+    media_sum = sum_over_sections(media_total)
     own_unit = lax.dynamic_slice_in_dim(media_unit, section * media_rows, media_rows, 0)
     own_inverse = lax.dynamic_slice_in_dim(media_inverse, section * media_rows, media_rows, 0)
-    media_grad = gather_sections(norm_back(own_unit, own_inverse, media_sum).astype(low)).astype(
-        full
-    )
-    gain_rows = [
-        jnp.stack([media_gains[1 - layer], *gain_rows[layer]]) for layer in range(LAYERS)
-    ]
-    gain_parts = jnp.stack(gain_rows).reshape(LAYERS, 3, section_count, -1)
-    gain_parts = jnp.sum(
-        lax.all_to_all(gain_parts, "section", split_axis=2, concat_axis=2), axis=2
-    )
-    gain_parts = gain_parts.reshape(LAYERS, 3, dp_count, -1)
-    gain_grad = jnp.sum(lax.all_to_all(gain_parts, dp, split_axis=2, concat_axis=2), axis=2)
+    media_grad = norm_back(own_unit, own_inverse, media_sum).astype(low)
 
     qkv_parts = [piece[0] for piece in pieces]
     own, other = pick(qkv_parts[0], qkv_parts[1])
     lower, upper = pick(own, swapped(other, 2))
+    out_grad = join_rows(*[piece[1] for piece in pieces])
+    media_grad = gather_sections(after(media_grad, out_grad), lower).astype(full)
     qkv_grads = [
         jnp.concatenate(
             [lower[:, i * inner : (i + 1) * inner], upper[:, i * inner : (i + 1) * inner]], axis=1
         ).astype(full)
         for i in range(3)
     ]
-    out_grad = join_rows(*[piece[1] for piece in pieces])
+    latent_grad = to_columns(after(grad_rows, media_sum))
+    gain_rows = [
+        jnp.stack([media_gains[1 - layer], *gain_rows[layer]]) for layer in range(LAYERS)
+    ]
+    gain_parts = after(jnp.stack(gain_rows), media_sum).reshape(LAYERS, 3, section_count, -1)
+    gain_parts = jnp.sum(
+        lax.all_to_all(gain_parts, "section", split_axis=2, concat_axis=2), axis=2
+    )
+    gain_parts = gain_parts.reshape(LAYERS, 3, dp_count, -1)
+    gain_grad = jnp.sum(lax.all_to_all(gain_parts, dp, split_axis=2, concat_axis=2), axis=2)
+
     down_piece, up_piece = ffn_pieces
     up_second_grad = interleave(to_second(up_piece), up_piece, half_hidden)
     down_second_grad = jnp.concatenate([to_second(down_piece), down_piece], axis=0)

time: 730 us -> 788 us (1.079)
  waiting for transfers between devices: 65.6 us -> 142 us
  matrix products: 157 us -> 146 us
  local copies, waits for them, and re-layouts: 99.1 us -> 90.3 us
    ppermute x26, waiting for transfers between devices: 24.6 us -> 49 us  [swapped(): return lax.ppermute(value, 'section', pairs)]
    all_to_all x2, waiting for transfers between devices: 0.01 us -> 24.3 us  [sum_to_sequence(): arrived = lax.all_to_all(blocks, 'pair', split_axis=0, concat_axis=0)]
    all_to_all x0 -> x1, blocking collectives: none -> 15.9 us  [per_device(): lax.all_to_all(jnp.stack(last), 'section', split_axis=0, concat_axis=0)]
    all_to_all x1, waiting for transfers between devices: 5.67 us -> 19.4 us  [to_columns(): lax.all_to_all(rows.astype(low), 'section', split_axis=1, concat_axis=0,...]
    dot_general x16, matrix products: 57.1 us -> 45.7 us  [matmul(): return jnp.dot(left, right, preferred_element_type=full)]
    reduce_scatter x6, starting transfers between devices: 0.59 us -> 11.8 us  [scatter(): return lax.psum_scatter(blocks, dp, scatter_dimension=0, tiled=True)]
    unnamed x250 -> x274, local copies, waits for them, and re-layouts: 20.8 us -> 16.5 us
  transfers between devices with their start and end apart: 64 -> 63, of which waited for: 14 -> 25; matrix products, arithmetic and copies ran while one was open for 46% -> 39% of each run, Pallas kernels for 0% -> 0%
where the time goes in v11:
time: 788 us; the launch traced here: 781 us
  blocking collectives  158 us (20%)
  matrix products  146 us (19%)
  waiting for transfers between devices  142 us (18%)
  starting transfers between devices  127 us (16%)
  other arithmetic  100 us (13%)
  local copies, waits for them, and re-layouts  90.3 us (11%)
  between operations  17.1 us (2%)
    all_gather x2, blocking collectives, from_sequences(): near = lax.all_gather(rows, 'pair', axis=0, tiled=True)  55.4 us
    ppermute x26, waiting for transfers between devices, swapped(): return lax.ppermute(value, 'section', pairs)  49 us
    dot_general x17, matrix products, matmul_nt(): lax.dot_general(left, right, (((1,), (1,)), ((), ())), preferred_element_...  48.9 us
    dot_general x16, matrix products, matmul(): return jnp.dot(left, right, preferred_element_type=full)  45.7 us
    all_gather x4, blocking collectives, from_slots(): return lax.all_gather(rows, 'section', axis=0, tiled=True)  44.8 us
    ppermute x26, starting transfers between devices, swapped(): return lax.ppermute(value, 'section', pairs)  33.6 us
    dot_general x8, matrix products, matmul_tn(): lax.dot_general(left, right, (((0,), (0,)), ((), ())), preferred_element_...  30.8 us
    all_gather x3, blocking collectives, per_device(): all_gains = lax.all_gather(all_gains, axis, axis=2, tiled=True)  30.1 us
  transfers between devices with their start and end apart: 63, of which 25 were waited for; matrix products, arithmetic and copies ran while one was open for 39% of the time, Pallas kernels for 0%

profile of v11, /device:TPU:0, one launch (start us, length us, event | category | flops | bytes accessed | tf_op | source)
XLA Modules:
  0.0 781.1 jit_solution(17149140664918175735)
XLA Ops:
  12.6 10.2 %collective-permute-done = bf16[192,1152]{1,0:T(8,128)(2,1)S(1)} collective-permute-done((bf16[192,1152]{1,0:T(8,128)(2,1)S(1)}, bf16[192,1152]{1,0:T(8,128)(2,1)S(1)}, u32[]{:S(2)}, u32[]{:S(2)}) %collective-permute-start) | collective-permute-done | bytes 442400 | tf_op jit(solution)/shard_map/ppermute | solution.py:123
  31.4 10.9 %collective-permute-start.1 = (bf16[96,3072]{1,0:T(8,128)(2,1)}, bf16[96,3072]{1,0:T(8,128)(2,1)}, u32[]{:S(2)}, u32[]{:S(2)}) collective-permute-start(bf16[96,3072]{1,0:T(8,128)(2,1)} %slice_bitcast_fusion.4), channel_id=1, source_target_pairs={{0,16},{8,24},{1,17},{9,25},{2,18},{10,26},{3,19},{11,27},{4,20},{... | collective-permute-start | bytes 1769480 | tf_op jit(solution)/shard_map/ppermute | solution.py:129
  57.8 18.5 %all_gather.40 = f32[2,3,384]{1,0,2:T(2,128)S(1)} all-gather(f32[2,3,96]{1,0,2:T(2,128)S(1)} %all_gather.39), channel_id=1, replica_groups=mesh['section'=4,'pair'=4,'core'=2] {'pair'}, dimensions={2}, use_global_device_ids=true | all-gather | bytes 11520 | tf_op jit(solution)/shard_map/all_gather | solution.py:268
  82.7 9.7 %all_gather.41 = f32[2,3,1536]{2,0,1:T(2,128)S(1)} all-gather(f32[2,3,384]{2,0,1:T(2,128)S(1)} %copy.149), channel_id=1, replica_groups=mesh['section'=4,'pair'=4,'core'=2] {'section'}, dimensions={2}, use_global_device_ids=true | all-gather | bytes 46080 | tf_op jit(solution)/shard_map/all_gather | solution.py:268
  162.8 26.7 %all_gather.43 = bf16[256,1536]{1,0:T(8,128)(2,1)S(1)} all-gather(bf16[64,1536]{1,0:T(8,128)(2,1)S(1)} %reshape.717), channel_id=1, replica_groups=mesh['section'=4,'pair'=4,'core'=2] {'pair'}, dimensions={0}, use_global_device_ids=true | all-gather | bytes 983040 | tf_op jit(solution)/shard_map/all_gather | solution.py:194
  196.1 6.6 collective-permute-done.13
  218.4 9.7 %collective-permute-done.16 = bf16[192,1536]{1,0:T(8,128)(2,1)} collective-permute-done((bf16[192,1536]{1,0:T(8,128)(2,1)}, bf16[192,1536]{1,0:T(8,128)(2,1)}, u32[]{:S(2)}, u32[]{:S(2)}) %collective-permute-start.16) | collective-permute-done | bytes 589856 | tf_op jit(solution)/shard_map/ppermute | solution.py:132
  230.1 11.1 %reduce-scatter.7.cloned.1.call-start = ((), (), s32[]{:S(2)}) async-start(), calls=%async_computation.23 | async-start | bytes 5308416 | tf_op jit(solution)/shard_map/reduce_scatter | solution.py:395
  253.8 10.3 %all_gather.45 = bf16[256,1536]{1,0:T(8,128)(2,1)S(1)} all-gather(bf16[64,1536]{1,0:T(8,128)(2,1)S(1)} %multiply_convert_fusion.9), channel_id=1, replica_groups=mesh['section'=4,'pair'=4,'core'=2] {'section'}, dimensions={0}, use_global_device_ids=true | all-gather | bytes 983040 | tf_op jit(solution)/shard_map/all_gather | solution.py:185
  282.3 12.1 %all_to_all.101 = bf16[4,64,1536]{2,1,0:T(8,128)(2,1)S(1)} all-to-all(bf16[4,64,1536]{2,1,0:T(8,128)(2,1)S(1)} %bitcast.361), channel_id=1, replica_groups=mesh['section'=4,'pair'=4,'core'=2] {'section'}, dimensions={0} | all-to-all | bytes 1572864 | tf_op jit(solution)/shard_map/all_to_all | solution.py:181
  295.4 12.0 %all_gather.46 = bf16[256,1536]{1,0:T(8,128)(2,1)} all-gather(bf16[64,1536]{1,0:T(8,128)(2,1)S(1)} %multiply_convert_fusion.8), channel_id=1, replica_groups=mesh['section'=4,'pair'=4,'core'=2] {'section'}, dimensions={0}, use_global_device_ids=true | all-gather | bytes 983040 | tf_op jit(solution)/shard_map/all_gather | solution.py:185
  344.3 11.5 %all_gather.49 = bf16[256,1536]{1,0:T(8,128)(2,1)S(1)} all-gather(bf16[64,1536]{1,0:T(8,128)(2,1)S(1)} %get-tuple-element.96), channel_id=1, replica_groups=mesh['section'=4,'pair'=4,'core'=2] {'section'}, dimensions={0}, use_global_device_ids=true | all-gather | bytes 983040 | tf_op jit(solution)/shard_map/all_gather | solution.py:185
  393.9 28.8 %all_gather.50 = bf16[256,1536]{1,0:T(8,128)(2,1)S(1)} all-gather(bf16[64,1536]{1,0:T(8,128)(2,1)S(1)} %get-tuple-element.94), channel_id=1, replica_groups=mesh['section'=4,'pair'=4,'core'=2] {'pair'}, dimensions={0}, use_global_device_ids=true | all-gather | bytes 983040 | tf_op jit(solution)/shard_map/all_gather | solution.py:194
  422.8 15.9 %all_to_all.102 = bf16[4,256,384]{2,1,0:T(8,128)(2,1)S(1)} all-to-all(bf16[4,256,384]{2,1,0:T(8,128)(2,1)S(1)} %pad_maximum_fusion.7), channel_id=1, replica_groups=mesh['section'=4,'pair'=4,'core'=2] {'section'}, dimensions={0} | all-to-all | bytes 1572864 | tf_op jit(solution)/shard_map/all_to_all | solution.py:491
  456.5 24.3 %all-to-all-done.7 = bf16[4,64,1536]{2,1,0:T(8,128)(2,1)S(1)} async-done(((bf16[4,64,1536]{2,1,0:T(8,128)(2,1)}), bf16[4,64,1536]{2,1,0:T(8,128)(2,1)S(1)}, u32[]{:S(2)}, u32[]{:S(2)}) %all-to-all-start.7) | async-done | bytes 786464 | tf_op jit(solution)/shard_map/all_to_all | solution.py:202
  484.8 11.0 %all_gather.51 = bf16[256,1536]{1,0:T(8,128)(2,1)S(1)} all-gather(bf16[64,1536]{1,0:T(8,128)(2,1)S(1)} %get-tuple-element.92), channel_id=1, replica_groups=mesh['section'=4,'pair'=4,'core'=2] {'section'}, dimensions={0}, use_global_device_ids=true | all-gather | bytes 983040 | tf_op jit(solution)/shard_map/all_gather | solution.py:185
  502.4 8.6 %convolution_convert_fusion = bf16[1536,1152]{1,0:T(8,128)(2,1)} fusion(bf16[256,1536]{1,0:T(8,128)(2,1)} %copy-done.75, bf16[1024,1536]{1,0:T(8,128)(2,1)S(1)} %copy-done.42, bf16[256,384]{0,1:T(8,128)(2,1)} %bitcast.387, bf16[1280,384]{0,1:T(8,128)(2,1)S(1)} %bitcast.345, bf16[1280,384]{0,1:T(8,128)(2,1)} %bitcast.355), kind=kOutput, calls=%fused_computation.2 | convolution fusion | flops 4551278592 | bytes 9633792 | tf_op jit(solution)/shard_map/dot_general | solution.py:48
  582.9 7.3 convolution_convert_fusion.1
  604.4 7.9 %multiply_reduce_fusion.1 = (f32[1536]{0:T(1024)S(1)}, f32[1536]{0:T(1024)S(1)}, f32[1024,1536]{1,0:T(8,128)S(1)}, f32[1024,1536]{1,0:T(8,128)}) fusion(bf16[1024,1536]{1,0:T(8,128)(2,1)S(1)} %copy-done.3, f32[1024]{0:T(1024)S(1)} %copy-done.97, f32[1024]{0:T(1024)S(1)} %copy-done.96, f32[1024,1536]{1,0:T(8,128)} %convolution_add_fusion.1, ...), kind=kOutput, calls=%fused_computation.10 | convolution fusion | flops 1228403712 | bytes 30310400 | tf_op jit(solution)/shard_map/dot_general | solution.py:44
  633.5 7.0 collective-permute-done.33
  645.7 10.6 %collective-permute-done.22 = bf16[256,1536]{1,0:T(8,128)(2,1)S(1)} collective-permute-done((bf16[256,1536]{1,0:T(8,128)(2,1)}, bf16[256,1536]{1,0:T(8,128)(2,1)S(1)}, u32[]{:S(2)}, u32[]{:S(2)}) %collective-permute-start.22) | collective-permute-done | bytes 786464 | tf_op jit(solution)/shard_map/ppermute | solution.py:123
  676.3 12.5 %all-to-all-done.12 = bf16[8,96,384]{2,1,0:T(8,128)(2,1)S(1)} async-done(((bf16[8,96,384]{2,1,0:T(8,128)(2,1)}), bf16[8,96,384]{2,1,0:T(8,128)(2,1)S(1)}, u32[]{:S(2)}, u32[]{:S(2)}) %all-to-all-start.12) | async-done | bytes 589856 | tf_op jit(solution)/shard_map/all_to_all | solution.py:502
  710.4 19.4 %all-to-all-done.9 = bf16[64,4,384]{2,0,1:T(8,128)(2,1)S(1)} async-done(((bf16[64,4,384]{2,0,1:T(8,128)(2,1)}), bf16[64,4,384]{2,0,1:T(8,128)(2,1)S(1)}, u32[]{:S(2)}, u32[]{:S(2)}) %all-to-all-start.9) | async-done | bytes 196640 | tf_op jit(solution)/shard_map/all_to_all | solution.py:188
  742.2 10.1 %collective-permute-done.29 = bf16[48,1536]{1,0:T(8,128)(2,1)S(1)} collective-permute-done((bf16[48,1536]{1,0:T(8,128)(2,1)S(1)}, bf16[48,1536]{1,0:T(8,128)(2,1)S(1)}, u32[]{:S(2)}, u32[]{:S(2)}) %collective-permute-start.29) | collective-permute-done | bytes 147488 | tf_op jit(solution)/shard_map/ppermute | solution.py:163
  (674 shorter events, 451.2 us)
Async XLA Ops:
  7.2 94.8 %all-gather.5.cloned.1.call-start = ((), (), s32[]{:S(2)}) async-start(), calls=%async_computation.19 | async-start | bytes 5308416 | tf_op jit(solution)/shard_map/all_gather | solution.py:272
  29.3 212.0 %all-gather.7.cloned.1.call-start = ((), (), s32[]{:S(2)}) async-start(), calls=%async_computation.20 | async-start | bytes 5308416 | tf_op jit(solution)/shard_map/all_gather | solution.py:272
  52.9 44.8 %collective-permute-start.5 = (bf16[192,1536]{1,0:T(8,128)(2,1)}, bf16[192,1536]{1,0:T(8,128)(2,1)}, u32[]{:S(2)}, u32[]{:S(2)}) collective-permute-start(bf16[192,1536]{1,0:T(8,128)(2,1)} %get-tuple-element.42), channel_id=1, source_target_pairs={{0,16},{8,24},{1,17},{9,25},{2,18},{10,26},{3,19},{11,27},{4,20},{... | collective-permute-start | bytes 1769480 | tf_op jit(solution)/shard_map/ppermute | solution.py:129
  82.6 224.8 %all-gather.9.cloned.1.call-start = ((), (), s32[]{:S(2)}) async-start(), calls=%async_computation.21 | async-start | bytes 5308416 | tf_op jit(solution)/shard_map/all_gather | solution.py:272
  106.1 44.8 %collective-permute-start.7 = (bf16[768,384]{1,0:T(8,128)(2,1)}, bf16[768,384]{1,0:T(8,128)(2,1)}, u32[]{:S(2)}, u32[]{:S(2)}) collective-permute-start(bf16[768,384]{1,0:T(8,128)(2,1)} %bitcast.25), channel_id=1, source_target_pairs={{0,8},{8,0},{16,24},{24,16},{1,9},{9,1},{17,25},{25,17},{2,10},{10... | collective-permute-start | bytes 1769480 | tf_op jit(solution)/shard_map/ppermute | solution.py:123
  107.6 45.1 %collective-permute-start.6 = (bf16[768,384]{1,0:T(8,128)(2,1)}, bf16[768,384]{1,0:T(8,128)(2,1)}, u32[]{:S(2)}, u32[]{:S(2)}) collective-permute-start(bf16[768,384]{1,0:T(8,128)(2,1)} %bitcast.25), channel_id=1, source_target_pairs={{0,16},{8,24},{16,0},{24,8},{1,17},{9,25},{17,1},{25,9},{2,18},{10... | collective-permute-start | bytes 1769480 | tf_op jit(solution)/shard_map/ppermute | solution.py:123
  111.8 44.7 %collective-permute-start.11 = (bf16[192,1536]{1,0:T(8,128)(2,1)}, bf16[192,1536]{1,0:T(8,128)(2,1)}, u32[]{:S(2)}, u32[]{:S(2)}) collective-permute-start(bf16[192,1536]{1,0:T(8,128)(2,1)} %broadcast_select_fusion.5), channel_id=1, source_target_pairs={{0,8},{8,0},{16,24},{24,16},{1,9},{9,1},{17,25},{25,17},{2,10},{10... | collective-permute-start | bytes 1769480 | tf_op jit(solution)/shard_map/ppermute | solution.py:123
  218.4 98.8 %all-gather.11.cloned.1.call-start = ((), (), s32[]{:S(2)}) async-start(), calls=%async_computation.22 | async-start | bytes 5308416 | tf_op jit(solution)/shard_map/all_gather | solution.py:272
  230.1 210.7 %reduce-scatter.7.cloned.1.call-start = ((), (), s32[]{:S(2)}) async-start(), calls=%async_computation.23 | async-start | bytes 5308416 | tf_op jit(solution)/shard_map/reduce_scatter | solution.py:395
  331.4 109.5 %reduce-scatter.9.cloned.1.call-start = ((), (), s32[]{:S(2)}) async-start(), calls=%async_computation.24 | async-start | bytes 5308416 | tf_op jit(solution)/shard_map/reduce_scatter | solution.py:395
  455.2 278.6 %reduce-scatter.17.cloned.1.call-start = ((), (), s32[]{:S(2)}) async-start(), calls=%async_computation.28 | async-start | bytes 1327104 | tf_op jit(solution)/shard_map/reduce_scatter | solution.py:395
  456.0 277.9 %reduce-scatter.15.cloned.1.call-start = ((), (), s32[]{:S(2)}) async-start(), calls=%async_computation.27 | async-start | bytes 1327104 | tf_op jit(solution)/shard_map/reduce_scatter | solution.py:395
  497.6 243.2 %reduce-scatter.13.cloned.1.call-start = ((), (), s32[]{:S(2)}) async-start(), calls=%async_computation.26 | async-start | bytes 3981312 | tf_op jit(solution)/shard_map/reduce_scatter | solution.py:395
  511.1 229.8 %reduce-scatter.11.cloned.1.call-start = ((), (), s32[]{:S(2)}) async-start(), calls=%async_computation.25 | async-start | bytes 3981312 | tf_op jit(solution)/shard_map/reduce_scatter | solution.py:395
  520.8 52.6 %collective-permute-start.31 = (bf16[384,384]{1,0:T(8,128)(2,1)}, bf16[384,384]{1,0:T(8,128)(2,1)}, u32[]{:S(2)}, u32[]{:S(2)}) collective-permute-start(bf16[384,384]{1,0:T(8,128)(2,1)} %get-tuple-element.139), channel_id=1, source_target_pairs={{0,8},{8,0},{16,24},{24,16},{1,9},{9,1},{17,25},{25,17},{2,10},{10... | collective-permute-start | bytes 884744 | tf_op jit(solution)/shard_map/ppermute | solution.py:123
  522.3 51.1 %collective-permute-start.30 = (bf16[384,384]{1,0:T(8,128)(2,1)}, bf16[384,384]{1,0:T(8,128)(2,1)}, u32[]{:S(2)}, u32[]{:S(2)}) collective-permute-start(bf16[384,384]{1,0:T(8,128)(2,1)} %get-tuple-element.140), channel_id=1, source_target_pairs={{0,16},{8,24},{16,0},{24,8},{1,17},{9,25},{17,1},{25,9},{2,18},{10... | collective-permute-start | bytes 884744 | tf_op jit(solution)/shard_map/ppermute | solution.py:123
  523.7 49.7 %collective-permute-start.37 = (bf16[96,1536]{1,0:T(8,128)(2,1)}, bf16[96,1536]{1,0:T(8,128)(2,1)}, u32[]{:S(2)}, u32[]{:S(2)}) collective-permute-start(bf16[96,1536]{1,0:T(8,128)(2,1)} %get-tuple-element.137), channel_id=1, source_target_pairs={{0,8},{8,0},{16,24},{24,16},{1,9},{9,1},{17,25},{25,17},{2,10},{10... | collective-permute-start | bytes 884744 | tf_op jit(solution)/shard_map/ppermute | solution.py:123
  525.2 48.2 %collective-permute-start.36 = (bf16[96,1536]{1,0:T(8,128)(2,1)}, bf16[96,1536]{1,0:T(8,128)(2,1)}, u32[]{:S(2)}, u32[]{:S(2)}) collective-permute-start(bf16[96,1536]{1,0:T(8,128)(2,1)} %get-tuple-element.138), channel_id=1, source_target_pairs={{0,16},{8,24},{16,0},{24,8},{1,17},{9,25},{17,1},{25,9},{2,18},{10... | collective-permute-start | bytes 884744 | tf_op jit(solution)/shard_map/ppermute | solution.py:123
  544.9 160.2 %collective-permute-start.41 = (bf16[192,1536]{1,0:T(8,128)(2,1)}, bf16[192,1536]{1,0:T(8,128)(2,1)}, u32[]{:S(2)}, u32[]{:S(2)}) collective-permute-start(bf16[192,1536]{1,0:T(8,128)(2,1)} %reduce-scatter.7.cloned.1.call-done), channel_id=1, source_target_pairs={{0,16},{8,24},{1,17},{9,25},{2,18},{10,26},{3,19},{11,27},{4,20},{... | collective-permute-start | bytes 1769480 | tf_op jit(solution)/shard_map/ppermute | solution.py:129
  576.0 53.7 %collective-permute-start.39 = (bf16[192,1536]{1,0:T(8,128)(2,1)}, bf16[192,1536]{1,0:T(8,128)(2,1)}, u32[]{:S(2)}, u32[]{:S(2)}) collective-permute-start(bf16[192,1536]{1,0:T(8,128)(2,1)} %pad_maximum_fusion.13), channel_id=1, source_target_pairs={{0,16},{8,24},{16,0},{24,8},{1,17},{9,25},{17,1},{25,9},{2,18},{10... | collective-permute-start | bytes 1769480 | tf_op jit(solution)/shard_map/ppermute | solution.py:123
  577.9 52.4 %collective-permute-start.38 = (bf16[192,1536]{1,0:T(8,128)(2,1)}, bf16[192,1536]{1,0:T(8,128)(2,1)}, u32[]{:S(2)}, u32[]{:S(2)}) collective-permute-start(bf16[192,1536]{1,0:T(8,128)(2,1)} %pad_maximum_fusion.12), channel_id=1, source_target_pairs={{0,8},{8,0},{16,24},{24,16},{1,9},{9,1},{17,25},{25,17},{2,10},{10... | collective-permute-start | bytes 1769480 | tf_op jit(solution)/shard_map/ppermute | solution.py:123
  640.6 64.6 %collective-permute-start.40 = (bf16[192,1536]{1,0:T(8,128)(2,1)}, bf16[192,1536]{1,0:T(8,128)(2,1)}, u32[]{:S(2)}, u32[]{:S(2)}) collective-permute-start(bf16[192,1536]{1,0:T(8,128)(2,1)} %fusion.81), channel_id=1, source_target_pairs={{16,0},{24,8},{17,1},{25,9},{18,2},{26,10},{19,3},{27,11},{20,4},{... | collective-permute-start | bytes 1769480 | tf_op jit(solution)/shard_map/ppermute | solution.py:132
  697.0 58.1 %collective-permute-start.24 = (bf16[256,1536]{1,0:T(8,128)(2,1)}, bf16[256,1536]{1,0:T(8,128)(2,1)}, u32[]{:S(2)}, u32[]{:S(2)}) collective-permute-start(bf16[256,1536]{1,0:T(8,128)(2,1)} %multiply_convert_fusion.5), channel_id=1, source_target_pairs={{0,16},{8,24},{16,0},{24,8},{1,17},{9,25},{17,1},{25,9},{2,18},{10... | collective-permute-start | bytes 2359304 | tf_op jit(solution)/shard_map/ppermute | solution.py:123
  700.4 54.7 %collective-permute-start.23 = (bf16[256,1536]{1,0:T(8,128)(2,1)}, bf16[256,1536]{1,0:T(8,128)(2,1)}, u32[]{:S(2)}, u32[]{:S(2)}) collective-permute-start(bf16[256,1536]{1,0:T(8,128)(2,1)} %multiply_convert_fusion.5), channel_id=1, source_target_pairs={{0,8},{8,0},{16,24},{24,16},{1,9},{9,1},{17,25},{25,17},{2,10},{10... | collective-permute-start | bytes 2359304 | tf_op jit(solution)/shard_map/ppermute | solution.py:123
  (174 other events, 1672.2 us)
Sparse Core Ops, SparseCore 0:
  29.4 72.5 all-gather.4
  103.6 52.1 all-gather.6
  158.0 59.0 all-gather.8
  230.2 50.8 all-gather.10
  317.4 55.3 reduce-scatter.6
  374.9 65.9 reduce-scatter.8
  458.4 34.2 reduce-scatter.16
  497.7 30.1 reduce-scatter.14
  530.2 42.0 reduce-scatter.12
  590.3 41.9 reduce-scatter.10

commit v12 on v10

--- a/solution.py
+++ b/solution.py
@@ -28,7 +28,12 @@
 
 
 def gelu_exact(values):
-    return jax.nn.gelu(values, approximate=False)
+    return 0.5 * values * (1.0 + lax.erf(values * math.sqrt(0.5)))
+
+
+def gelu_slope(values):
+    normal = 0.5 * (1.0 + lax.erf(values * math.sqrt(0.5)))
+    return normal + values * jnp.exp(-0.5 * values * values) * (1.0 / math.sqrt(2.0 * math.pi))
 
 
 def matmul(left, right):
@@ -254,9 +259,7 @@
     other_heads = swapped(jnp.concatenate([half[1] for half in halves], axis=1), 2)
     qkv_pieces = pick(own_heads, other_heads)
     half_hidden = w_down.shape[1] // 2
-    half_depth = w_up.shape[1] // 2
-    up_share = share_first(w_up[0, :half_depth], w_up[0, half_depth:])
-    all_gains = after(gains, (other_heads, up_share))
+    all_gains = after(gains, other_heads)
     for axis in ("core", "pair", "section"):
         all_gains = lax.all_gather(all_gains, axis, axis=2, tiled=True)
     out_pieces = exchange_rows(after(w_out[0], other_heads))
@@ -271,39 +274,34 @@
     qkv_w = [weight[:, : 3 * inner] for weight in stacked]
     out_w = [unfold(weight[:, 3 * inner :]) for weight in stacked]
 
-    up_turned = lax.all_to_all(up_share, dp, split_axis=1, concat_axis=0, tiled=True)
-    down_share = share_first(
-        *after((w_down[0, :half_hidden], w_down[0, half_hidden:]), other_heads)
-    )
-
-    def by_depth(rows):
-        return rows.reshape(-1, dp_count, 2, half_depth).swapaxes(1, 2).reshape(rows.shape)
-
-    def in_depth(rows):
-        return rows.reshape(-1, 2, dp_count, half_depth).swapaxes(1, 2).reshape(rows.shape)
+    def share_first(shard):
+        return jnp.where(on_first, shard, to_second(shard))
+
+    up_turned = lax.all_to_all(w_up[0], dp, split_axis=1, concat_axis=0, tiled=True)
+    up_own = share_first(up_turned)
+    down_own = share_first(after(w_down[0], other_heads))
+    down_other = swapped(after(down_own, all_gains), 1)
 
     def first_ffn(gate):
-        down, up = after((down_share, up_turned), gate)
-        down, up = by_distance(down), by_distance(up)
-        return (
-            jnp.concatenate(
-                [
-                    jnp.concatenate(pick(up[0], up[2]), axis=0),
-                    jnp.concatenate(pick(up[1], up[3]), axis=0),
-                ],
-                axis=1,
-            ),
-            jnp.concatenate(pick(down[0], down[2]) + pick(down[1], down[3]), axis=0),
-        )
-
-    up_late, down_late = after((w_up[0], w_down[0]), all_gains)
+        up_other = swapped(after(up_own, gate), 1)
+        return lax.optimization_barrier(
+            (
+                jnp.concatenate([up_own, up_other], axis=1),
+                jnp.concatenate([down_own, down_other], axis=0),
+            )
+        )
+
+    down_late = after(w_down[0], all_gains)
     down_second = gather(
         jnp.where(on_first, to_first(down_late[:half_hidden]), down_late[half_hidden:])
     )
-    up_even, up_odd = column_parts(up_late, half_hidden)
-    up_second = gather(jnp.where(on_first, to_first(up_even), up_odd))
-    up_w = [None, up_second]
-    down_w = [None, down_second]
+
+    def second_ffn(gate):
+        up_even, up_odd = column_parts(after(w_up[0], gate), half_hidden)
+        return gather(jnp.where(on_first, to_first(up_even), up_odd)), down_second
+
+    up_w = [None, None]
+    down_w = [None, None]
     query_w = [weight[:, :inner] for weight in qkv_w]
     key_w = [weight[:, inner : 2 * inner] for weight in qkv_w]
     value_w = [weight[:, 2 * inner :] for weight in qkv_w]
@@ -342,6 +340,7 @@
         projected = matmul(latent_low, qkv_w[layer]).astype(low)
         if layer == 0:
             up_w[0], down_w[0] = first_ffn(projected)
+            up_w[1], down_w[1] = second_ffn(projected)
         query_low = projected[:, :inner]
         key_heads = split_heads(
             jnp.concatenate([media_key[layer], projected[:, inner : 2 * inner]], axis=0)
@@ -357,7 +356,7 @@
         middle = current + sum_to_slots(matmul(attended_low, out_w[layer]))
         unit_mid, inverse_mid = unit_rows(middle)
         ffn_low = (unit_mid * all_gains[layer, 2]).astype(low)
-        ffn_low = from_slots(ffn_low) if layer else from_sequences(by_depth(ffn_low))
+        ffn_low = from_slots(ffn_low) if layer else from_sequences(ffn_low)
         hidden_pre = matmul(ffn_low, up_w[layer])
         active_low = gelu_exact(hidden_pre).astype(low)
         if layer == 0:
@@ -391,7 +390,7 @@
         grad_key, grad_value = after((grad_key[:seq_rows], grad_value[:seq_rows]), gate)
         part = matmul_nt(grad_key, key_w[layer]) + matmul_nt(grad_value, value_w[layer])
         media_gains.append(jnp.sum(part * media_unit, axis=0))
-        media_parts.append(part * all_gains[layer, 0])
+        media_parts.append((part * all_gains[layer, 0]).astype(low if layer else full))
 
     pieces = [None] * LAYERS
     for layer in (1, 0):
@@ -411,7 +410,7 @@
             active_low,
         ) = saved[layer]
         grad_active = matmul_nt(grad_low, down_w[layer])
-        grad_hidden = jax.vjp(gelu_exact, hidden_pre)[1](grad_active)[0].astype(low)
+        grad_hidden = (grad_active * gelu_slope(hidden_pre)).astype(low)
         if layer == 0:
             add_media(1, *media_grads, grad_hidden)
         down_grad = matmul_tn(active_low, grad_low)
@@ -423,24 +422,22 @@
             ffn_pieces = (scatter(down_grad), scatter(up_grad.astype(low)))
             ffn_grad = sum_to_slots(matmul_nt(grad_hidden, up_w[layer]))
         else:
-            ffn_grad = in_depth(sum_to_sequence(grad_hidden, up_w[layer], matmul_nt))
-            blocks = down_grad.reshape(2, 2, half_hidden, feature_width)
-            own, ahead = pick(blocks[0, 0], blocks[0, 1])
-            side, across = pick(blocks[1, 0], blocks[1, 1])
-            down_blocks = (own, side, ahead, across)
-            width = up_grad.shape[1] // 2
-            blocks = up_grad.reshape(2, -1, 2 * width)
-            own, ahead = pick(blocks[0][:, :width], blocks[1][:, :width])
-            side, across = pick(blocks[0][:, width:], blocks[1][:, width:])
-            up_blocks = (own, side, ahead, across)
+            ffn_grad = sum_to_sequence(grad_hidden, up_w[layer], matmul_nt)
+            down_far = down_grad[down_grad.shape[0] // 2 :].astype(low)
+            up_far = up_grad[:, up_grad.shape[1] // 2 :].astype(low)
+            ffn_grad = after(ffn_grad, (down_far, up_far, media_parts))
+            down_far, up_far = swapped(down_far, 1), swapped(up_far, 1)
         gain_ffn_grad = jnp.sum(ffn_grad * unit_mid, axis=0)
         grad_middle = grad_rows + norm_back(
             unit_mid, inverse_mid, ffn_grad * all_gains[layer, 2]
         )
         middle_low = from_slots(grad_middle.astype(low))
         if layer == 0:
-            up_half = sum_by_distance(*up_blocks, middle_low).astype(low)
-            down_half = sum_by_distance(*down_blocks, middle_low).astype(low)
+            down_far, up_far = after((down_far, up_far), middle_low)
+            down_half = down_grad[: down_far.shape[0]] + down_far.astype(full)
+            up_half = up_grad[:, : up_far.shape[1]] + up_far.astype(full)
+            down_half = down_half + to_first(down_half.astype(low)).astype(full)
+            up_half = (up_half + to_first(up_half.astype(low)).astype(full)).astype(low)
         grad_heads = split_heads(matmul_nt(middle_low, out_w[layer]).astype(low))
         out_grad = by_device(matmul_tn(attended_low, middle_low)).astype(low)
         out_piece = scatter(out_grad)
@@ -451,21 +448,23 @@
         grad_query = grad_query.reshape(-1, inner).astype(low)
         grad_key = grad_key.reshape(-1, inner).astype(low)
         grad_value = grad_value.reshape(-1, inner).astype(low)
+        both_low = jnp.concatenate([media_low[layer], latent_low], axis=0)
+        all_grads = jnp.concatenate(
+            [jnp.pad(grad_query, ((seq_rows, 0), (0, 0))), grad_key, grad_value], axis=1
+        )
+        qkv_grad = matmul_tn(both_low, all_grads).astype(low)
         latent_part = (
             matmul_nt(grad_query, query_w[layer])
             + matmul_nt(grad_key[seq_rows:], key_w[layer])
             + matmul_nt(grad_value[seq_rows:], value_w[layer])
         )
         latent_grad_rows = sum_to_slots(latent_part)
+        if layer:
+            latent_grad_rows = after(latent_grad_rows, qkv_grad)
         gain_latent_grad = jnp.sum(latent_grad_rows * unit_in, axis=0)
         grad_rows = grad_middle + norm_back(
             unit_in, inverse_in, latent_grad_rows * all_gains[layer, 1]
         )
-        both_low = jnp.concatenate([media_low[layer], latent_low], axis=0)
-        all_grads = jnp.concatenate(
-            [jnp.pad(grad_query, ((seq_rows, 0), (0, 0))), grad_key, grad_value], axis=1
-        )
-        qkv_grad = matmul_tn(both_low, all_grads).astype(low)
         if layer == 0:
             up_half, qkv_grad = lax.optimization_barrier((up_half, qkv_grad))
             up_half = lax.all_to_all(up_half, dp, split_axis=0, concat_axis=1, tiled=True)
@@ -491,7 +490,7 @@
         gain_rows[layer] = (gain_latent_grad, gain_ffn_grad)
     latent_grad = to_columns(after(grad_rows, (pieces[1], up_half)))
     media_rows = seq_rows // section_count
-    media_sum = sum_over_sections(media_parts[0] + media_parts[1])
+    media_sum = sum_over_sections(media_parts[0].astype(full) + media_parts[1])
     own_unit = lax.dynamic_slice_in_dim(media_unit, section * media_rows, media_rows, 0)
     own_inverse = lax.dynamic_slice_in_dim(media_inverse, section * media_rows, media_rows, 0)
     media_grad = gather_sections(norm_back(own_unit, own_inverse, media_sum).astype(low)).astype(
@@ -520,10 +519,8 @@
     down_piece, up_piece = ffn_pieces
     up_second_grad = interleave(to_second(up_piece), up_piece, half_hidden)
     down_second_grad = jnp.concatenate([to_second(down_piece), down_piece], axis=0)
-    up_first_grad = jnp.concatenate([up_half, to_first(up_half)], axis=0)
-    down_first_grad = jnp.concatenate([down_half, to_first(down_half)], axis=0)
-    up_grad = jnp.where(on_first, up_first_grad, up_second_grad).astype(full)
-    down_grad = jnp.where(on_first, down_first_grad, down_second_grad).astype(full)
+    up_grad = jnp.where(on_first, up_half, up_second_grad).astype(full)
+    down_grad = jnp.where(on_first, down_half, down_second_grad.astype(full))
     return (
         latents_out,
         latent_grad,

time: 730 us -> 816 us (1.12)
  waiting for transfers between devices: 65.6 us -> 137 us
  blocking collectives: 152 us -> 219 us
  local copies, waits for them, and re-layouts: 99.1 us -> 74.3 us
  starting transfers between devices: 125 us -> 104 us
    all_gather x3, blocking collectives: 31.7 us -> 90.6 us  [per_device(): all_gains = lax.all_gather(all_gains, axis, axis=2, tiled=True)]
    ppermute x26 -> x14, starting transfers between devices: 33.6 us -> 9.77 us  [swapped(): return lax.ppermute(value, 'section', pairs)]
    ppermute x1, waiting for transfers between devices: 4.23 us -> 26.1 us  [join_rows(): far = lax.ppermute(far, everywhere, turn_pairs(1, True))]
    all_to_all x4, waiting for transfers between devices: 6.62 us -> 27.8 us  [sum_to_slots(): arrived = lax.all_to_all(blocks, 'section', split_axis=0, concat_axis=0)]
    ppermute x26 -> x14, waiting for transfers between devices: 24.6 us -> 40.1 us  [swapped(): return lax.ppermute(value, 'section', pairs)]
    dot_general x16, matrix products: 57.1 us -> 44.4 us  [matmul(): return jnp.dot(left, right, preferred_element_type=full)]
    all_to_all x1, waiting for transfers between devices: 0.01 us -> 10.7 us  [per_device(): lax.all_to_all(jnp.stack(last), 'section', split_axis=0, concat_axis=0)]
    all_gather x4, blocking collectives: 47.7 us -> 58.2 us  [from_slots(): return lax.all_gather(rows, 'section', axis=0, tiled=True)]
  transfers between devices with their start and end apart: 64 -> 52, of which waited for: 14 -> 17; matrix products, arithmetic and copies ran while one was open for 46% -> 38% of each run, Pallas kernels for 0% -> 0%
where the time goes in v12:
time: 816 us; the launch traced here: 804 us
  blocking collectives  219 us (27%)
  matrix products  161 us (20%)
  waiting for transfers between devices  137 us (17%)
  starting transfers between devices  104 us (13%)
  other arithmetic  93.1 us (11%)
  local copies, waits for them, and re-layouts  74.3 us (9%)
  between operations  16.7 us (2%)
    all_gather x3, blocking collectives, per_device(): all_gains = lax.all_gather(all_gains, axis, axis=2, tiled=True)  90.6 us
    all_gather x2, blocking collectives, from_sequences(): near = lax.all_gather(rows, 'pair', axis=0, tiled=True)  58.4 us
    all_gather x4, blocking collectives, from_slots(): return lax.all_gather(rows, 'section', axis=0, tiled=True)  58.2 us
    dot_general x17, matrix products, matmul_nt(): lax.dot_general(left, right, (((1,), (1,)), ((), ())), preferred_element_...  53.5 us
    dot_general x16, matrix products, matmul(): return jnp.dot(left, right, preferred_element_type=full)  44.4 us
    ppermute x14, waiting for transfers between devices, swapped(): return lax.ppermute(value, 'section', pairs)  40.1 us
    dot_general x8, matrix products, matmul_tn(): lax.dot_general(left, right, (((0,), (0,)), ((), ())), preferred_element_...  33.2 us
    all_to_all x4, waiting for transfers between devices, sum_to_slots(): arrived = lax.all_to_all(blocks, 'section', split_axis=0, concat_axis=0)  27.8 us
  transfers between devices with their start and end apart: 52, of which 17 were waited for; matrix products, arithmetic and copies ran while one was open for 38% of the time, Pallas kernels for 0%

profile of v12, /device:TPU:0, one launch (start us, length us, event | category | flops | bytes accessed | tf_op | source)
XLA Modules:
  0.0 804.1 jit_solution(13177176516081556189)
XLA Ops:
  12.6 10.2 %collective-permute-done = bf16[192,1152]{1,0:T(8,128)(2,1)S(1)} collective-permute-done((bf16[192,1152]{1,0:T(8,128)(2,1)S(1)}, bf16[192,1152]{1,0:T(8,128)(2,1)S(1)}, u32[]{:S(2)}, u32[]{:S(2)}) %collective-permute-start) | collective-permute-done | bytes 442400 | tf_op jit(solution)/shard_map/ppermute | solution.py:123
  31.6 12.6 %all-to-all-start.1 = ((bf16[192,8,384]{2,0,1:T(8,128)(2,1)}), bf16[192,8,384]{2,0,1:T(8,128)(2,1)}, u32[]{:S(2)}, u32[]{:S(2)}) async-start(bf16[192,8,384]{2,0,1:T(8,128)(2,1)} %copy.154), calls=%async_computation.1 | async-start | bytes 2359296 | tf_op jit(solution)/shard_map/all_to_all | solution.py:280
  52.8 64.2 %all_gather.40 = f32[2,3,384]{1,0,2:T(2,128)} all-gather(f32[2,3,96]{1,0,2:T(2,128)S(1)} %all_gather.39), channel_id=1, replica_groups=mesh['section'=4,'pair'=4,'core'=2] {'pair'}, dimensions={2}, use_global_device_ids=true | all-gather | bytes 11520 | tf_op jit(solution)/shard_map/all_gather | solution.py:264
  122.2 24.5 %all_gather.41 = f32[2,3,1536]{2,0,1:T(2,128)S(1)} all-gather(f32[2,3,384]{2,0,1:T(2,128)S(1)} %copy.149), channel_id=1, replica_groups=mesh['section'=4,'pair'=4,'core'=2] {'section'}, dimensions={2}, use_global_device_ids=true | all-gather | bytes 46080 | tf_op jit(solution)/shard_map/all_gather | solution.py:264
  224.7 28.0 %all_gather.43 = bf16[256,1536]{1,0:T(8,128)(2,1)S(1)} all-gather(bf16[64,1536]{1,0:T(8,128)(2,1)S(1)} %multiply_convert_fusion.10), channel_id=1, replica_groups=mesh['section'=4,'pair'=4,'core'=2] {'pair'}, dimensions={0}, use_global_device_ids=true | all-gather | bytes 983040 | tf_op jit(solution)/shard_map/all_gather | solution.py:194
  254.6 12.9 %collective-permute-done.5 = bf16[1536,384]{1,0:T(8,128)(2,1)} collective-permute-done((bf16[1536,384]{1,0:T(8,128)(2,1)}, bf16[1536,384]{1,0:T(8,128)(2,1)}, u32[]{:S(2)}, u32[]{:S(2)}) %collective-permute-start.5) | collective-permute-done | bytes 1179680 | tf_op jit(solution)/shard_map/ppermute | solution.py:123
  276.8 7.1 all-to-all-start.2
  283.9 6.7 collective-permute-done.10
  305.9 12.0 %all_gather.45 = bf16[256,1536]{1,0:T(8,128)(2,1)S(1)} all-gather(bf16[64,1536]{1,0:T(8,128)(2,1)S(1)} %multiply_convert_fusion.9), channel_id=1, replica_groups=mesh['section'=4,'pair'=4,'core'=2] {'section'}, dimensions={0}, use_global_device_ids=true | all-gather | bytes 983040 | tf_op jit(solution)/shard_map/all_gather | solution.py:185
  334.7 11.3 %all_to_all.101 = bf16[4,64,1536]{2,1,0:T(8,128)(2,1)S(1)} all-to-all(bf16[4,64,1536]{2,1,0:T(8,128)(2,1)S(1)} %bitcast.305), channel_id=1, replica_groups=mesh['section'=4,'pair'=4,'core'=2] {'section'}, dimensions={0} | all-to-all | bytes 1572864 | tf_op jit(solution)/shard_map/all_to_all | solution.py:181
  346.6 10.5 %all_gather.46 = bf16[256,1536]{1,0:T(8,128)(2,1)S(1)} all-gather(bf16[64,1536]{1,0:T(8,128)(2,1)S(1)} %multiply_convert_fusion.8), channel_id=1, replica_groups=mesh['section'=4,'pair'=4,'core'=2] {'section'}, dimensions={0}, use_global_device_ids=true | all-gather | bytes 983040 | tf_op jit(solution)/shard_map/all_gather | solution.py:185
  386.6 7.0 all-to-all-done.4
  395.8 11.0 %all_gather.49 = bf16[256,1536]{1,0:T(8,128)(2,1)S(1)} all-gather(bf16[64,1536]{1,0:T(8,128)(2,1)S(1)} %get-tuple-element.91), channel_id=1, replica_groups=mesh['section'=4,'pair'=4,'core'=2] {'section'}, dimensions={0}, use_global_device_ids=true | all-gather | bytes 983040 | tf_op jit(solution)/shard_map/all_gather | solution.py:185
  431.7 9.7 %convolution_convert_fusion.2 = bf16[1536,1152]{1,0:T(8,128)(2,1)} fusion(bf16[256,1536]{1,0:T(8,128)(2,1)} %copy-done.65, bf16[1024,1536]{1,0:T(8,128)(2,1)} %get-tuple-element.105, bf16[256,384]{0,1:T(8,128)(2,1)} %bitcast.327, bf16[1280,384]{0,1:T(8,128)(2,1)S(1)} %bitcast.289, bf16[1280,384]{0,1:T(8,128)(2,1)} %bitcast.299), kind=kOutput, calls=%fused_computation.4 | convolution fusion | flops 4551278592 | bytes 9633792 | tf_op jit(solution)/shard_map/dot_general | solution.py:48
  454.3 30.4 %all_gather.50 = bf16[256,1536]{1,0:T(8,128)(2,1)} all-gather(bf16[64,1536]{1,0:T(8,128)(2,1)S(1)} %get-tuple-element.89), channel_id=1, replica_groups=mesh['section'=4,'pair'=4,'core'=2] {'pair'}, dimensions={0}, use_global_device_ids=true | all-gather | bytes 983040 | tf_op jit(solution)/shard_map/all_gather | solution.py:194
  490.6 10.7 %all-to-all-done.5 = bf16[4,256,384]{2,1,0:T(8,128)(2,1)S(1)} async-done(((bf16[4,256,384]{2,1,0:T(8,128)(2,1)}), bf16[4,256,384]{2,1,0:T(8,128)(2,1)S(1)}, u32[]{:S(2)}, u32[]{:S(2)}) %all-to-all-start.5) | async-done | bytes 786464 | tf_op jit(solution)/shard_map/all_to_all | solution.py:482
  553.6 10.9 %collective-permute-done.27 = bf16[192,1536]{1,0:T(8,128)(2,1)} collective-permute-done((bf16[192,1536]{1,0:T(8,128)(2,1)}, bf16[192,1536]{1,0:T(8,128)(2,1)}, u32[]{:S(2)}, u32[]{:S(2)}) %collective-permute-start.27) | collective-permute-done | bytes 589856 | tf_op jit(solution)/shard_map/ppermute | solution.py:129
  569.5 24.7 %all_gather.51 = bf16[256,1536]{1,0:T(8,128)(2,1)S(1)} all-gather(bf16[64,1536]{1,0:T(8,128)(2,1)S(1)} %get-tuple-element.87), channel_id=1, replica_groups=mesh['section'=4,'pair'=4,'core'=2] {'section'}, dimensions={0}, use_global_device_ids=true | all-gather | bytes 983040 | tf_op jit(solution)/shard_map/all_gather | solution.py:185
  615.9 7.3 convolution_convert_fusion
  639.8 14.3 %all-to-all-done.8 = bf16[4,64,1536]{2,1,0:T(8,128)(2,1)S(1)} async-done(((bf16[4,64,1536]{2,1,0:T(8,128)(2,1)}), bf16[4,64,1536]{2,1,0:T(8,128)(2,1)S(1)}, u32[]{:S(2)}, u32[]{:S(2)}) %all-to-all-start.8) | async-done | bytes 786464 | tf_op jit(solution)/shard_map/all_to_all | solution.py:181
  661.6 8.5 %multiply_reduce_fusion.1 = (f32[1536]{0:T(1024)S(1)}, f32[1536]{0:T(1024)S(1)}, f32[1024,1536]{1,0:T(8,128)S(1)}, f32[1024,1536]{1,0:T(8,128)}) fusion(bf16[1024,1536]{1,0:T(8,128)(2,1)S(1)} %copy-done.2, f32[1024]{0:T(1024)S(1)} %copy-done.87, f32[1024]{0:T(1024)S(1)} %copy-done.85, f32[1024,1536]{1,0:T(8,128)} %get-tuple-element.163, ...), kind=kOutput, calls=%fused_computation.10 | convolution fusion | flops 1225257984 | bytes 33449984 | tf_op jit(solution)/shard_map/dot_general | solution.py:44
  701.4 7.9 all-to-all-done.10
  740.1 26.1 %collective-permute-done.26 = bf16[48,1536]{1,0:T(8,128)(2,1)S(1)} collective-permute-done((bf16[48,1536]{1,0:T(8,128)(2,1)S(1)}, bf16[48,1536]{1,0:T(8,128)(2,1)S(1)}, u32[]{:S(2)}, u32[]{:S(2)}) %collective-permute-start.26) | collective-permute-done | bytes 147488 | tf_op jit(solution)/shard_map/ppermute | solution.py:163
  787.1 6.9 collective-permute-done.24
  (565 shorter events, 412.2 us)
Async XLA Ops:
  7.2 152.6 %all-gather.5.cloned.1.call-start = ((), (), s32[]{:S(2)}) async-start(), calls=%async_computation.19 | async-start | bytes 5308416 | tf_op jit(solution)/shard_map/all_gather | solution.py:268
  29.3 264.0 %all-gather.7.cloned.1.call-start = ((), (), s32[]{:S(2)}) async-start(), calls=%async_computation.20 | async-start | bytes 5308416 | tf_op jit(solution)/shard_map/all_gather | solution.py:268
  31.6 122.1 %all-to-all-start.1 = ((bf16[192,8,384]{2,0,1:T(8,128)(2,1)}), bf16[192,8,384]{2,0,1:T(8,128)(2,1)}, u32[]{:S(2)}, u32[]{:S(2)}) async-start(bf16[192,8,384]{2,0,1:T(8,128)(2,1)} %copy.154), calls=%async_computation.1 | async-start | bytes 2359296 | tf_op jit(solution)/shard_map/all_to_all | solution.py:280
  44.2 312.9 %all-gather.9.cloned.1.call-start = ((), (), s32[]{:S(2)}) async-start(), calls=%async_computation.21 | async-start | bytes 5308416 | tf_op jit(solution)/shard_map/all_gather | solution.py:268
  118.1 93.1 %collective-permute-start.6 = (bf16[384,1536]{1,0:T(8,128)(2,1)}, bf16[384,1536]{1,0:T(8,128)(2,1)}, u32[]{:S(2)}, u32[]{:S(2)}) collective-permute-start(bf16[384,1536]{1,0:T(8,128)(2,1)} %bitcast.282), channel_id=1, source_target_pairs={{0,16},{8,24},{1,17},{9,25},{2,18},{10,26},{3,19},{11,27},{4,20},{... | collective-permute-start | bytes 3538952 | tf_op jit(solution)/shard_map/ppermute | solution.py:129
  153.7 60.7 %collective-permute-start.4 = (bf16[1536,384]{1,0:T(8,128)(2,1)}, bf16[1536,384]{1,0:T(8,128)(2,1)}, u32[]{:S(2)}, u32[]{:S(2)}) collective-permute-start(bf16[1536,384]{1,0:T(8,128)(2,1)} %bitcast.20), channel_id=1, source_target_pairs={{0,16},{8,24},{1,17},{9,25},{2,18},{10,26},{3,19},{11,27},{4,20},{... | collective-permute-start | bytes 3538952 | tf_op jit(solution)/shard_map/ppermute | solution.py:129
  212.4 40.3 %collective-permute-start.7 = (bf16[384,1536]{1,0:T(8,128)(2,1)}, bf16[384,1536]{1,0:T(8,128)(2,1)}, u32[]{:S(2)}, u32[]{:S(2)}) collective-permute-start(bf16[384,1536]{1,0:T(8,128)(2,1)} %broadcast_select_fusion), channel_id=1, source_target_pairs={{0,8},{8,0},{16,24},{24,16},{1,9},{9,1},{17,25},{25,17},{2,10},{10... | collective-permute-start | bytes 3538952 | tf_op jit(solution)/shard_map/ppermute | solution.py:123
  216.8 50.7 %collective-permute-start.5 = (bf16[1536,384]{1,0:T(8,128)(2,1)}, bf16[1536,384]{1,0:T(8,128)(2,1)}, u32[]{:S(2)}, u32[]{:S(2)}) collective-permute-start(bf16[1536,384]{1,0:T(8,128)(2,1)} %broadcast_select_fusion.1), channel_id=1, source_target_pairs={{0,8},{8,0},{16,24},{24,16},{1,9},{9,1},{17,25},{25,17},{2,10},{10... | collective-permute-start | bytes 3538952 | tf_op jit(solution)/shard_map/ppermute | solution.py:123
  283.9 82.9 %all-gather.11.cloned.1.call-start = ((), (), s32[]{:S(2)}) async-start(), calls=%async_computation.22 | async-start | bytes 5308416 | tf_op jit(solution)/shard_map/all_gather | solution.py:268
  292.8 212.0 %reduce-scatter.7.cloned.1.call-start = ((), (), s32[]{:S(2)}) async-start(), calls=%async_computation.23 | async-start | bytes 5308416 | tf_op jit(solution)/shard_map/reduce_scatter | solution.py:383
  366.6 138.2 %reduce-scatter.9.cloned.1.call-start = ((), (), s32[]{:S(2)}) async-start(), calls=%async_computation.24 | async-start | bytes 5308416 | tf_op jit(solution)/shard_map/reduce_scatter | solution.py:383
  385.1 288.4 %reduce-scatter.13.cloned.1.call-start = ((), (), s32[]{:S(2)}) async-start(), calls=%async_computation.26 | async-start | bytes 1327104 | tf_op jit(solution)/shard_map/reduce_scatter | solution.py:383
  489.8 183.7 %reduce-scatter.11.cloned.1.call-start = ((), (), s32[]{:S(2)}) async-start(), calls=%async_computation.25 | async-start | bytes 3981312 | tf_op jit(solution)/shard_map/reduce_scatter | solution.py:383
  520.4 46.5 %all-to-all-start.7 = ((bf16[4,64,1536]{2,1,0:T(8,128)(2,1)}), bf16[4,64,1536]{2,1,0:T(8,128)(2,1)}, u32[]{:S(2)}, u32[]{:S(2)}) async-start(bf16[4,64,1536]{2,1,0:T(8,128)(2,1)} %bitcast.323), calls=%async_computation.9 | async-start | bytes 1572864 | tf_op jit(solution)/shard_map/all_to_all | solution.py:202
  525.2 203.6 %reduce-scatter.17.cloned.1.call-start = ((), (), s32[]{:S(2)}) async-start(), calls=%async_computation.28 | async-start | bytes 1327104 | tf_op jit(solution)/shard_map/reduce_scatter | solution.py:383
  532.5 71.4 %collective-permute-start.14 = (bf16[1536,384]{1,0:T(8,128)(2,1)}, bf16[1536,384]{1,0:T(8,128)(2,1)}, u32[]{:S(2)}, u32[]{:S(2)}) collective-permute-start(bf16[1536,384]{1,0:T(8,128)(2,1)} %slice.579), channel_id=1, source_target_pairs={{0,8},{8,0},{16,24},{24,16},{1,9},{9,1},{17,25},{25,17},{2,10},{10... | collective-permute-start | bytes 3538952 | tf_op jit(solution)/shard_map/ppermute | solution.py:123
  535.1 68.8 %collective-permute-start.13 = (bf16[384,1536]{1,0:T(8,128)(2,1)}, bf16[384,1536]{1,0:T(8,128)(2,1)}, u32[]{:S(2)}, u32[]{:S(2)}) collective-permute-start(bf16[384,1536]{1,0:T(8,128)(2,1)} %slice.580), channel_id=1, source_target_pairs={{0,8},{8,0},{16,24},{24,16},{1,9},{9,1},{17,25},{25,17},{2,10},{10... | collective-permute-start | bytes 3538952 | tf_op jit(solution)/shard_map/ppermute | solution.py:123
  535.7 178.6 %collective-permute-start.29 = (bf16[192,1536]{1,0:T(8,128)(2,1)}, bf16[192,1536]{1,0:T(8,128)(2,1)}, u32[]{:S(2)}, u32[]{:S(2)}) collective-permute-start(bf16[192,1536]{1,0:T(8,128)(2,1)} %reduce-scatter.7.cloned.1.call-done), channel_id=1, source_target_pairs={{0,16},{8,24},{1,17},{9,25},{2,18},{10,26},{3,19},{11,27},{4,20},{... | collective-permute-start | bytes 1769480 | tf_op jit(solution)/shard_map/ppermute | solution.py:129
  614.6 39.8 %collective-permute-start.15 = (bf16[1536,384]{1,0:T(8,128)(2,1)}, bf16[1536,384]{1,0:T(8,128)(2,1)}, u32[]{:S(2)}, u32[]{:S(2)}) collective-permute-start(bf16[1536,384]{1,0:T(8,128)(2,1)} %fusion.68), channel_id=1, source_target_pairs={{16,0},{24,8},{17,1},{25,9},{18,2},{26,10},{19,3},{27,11},{20,4},{... | collective-permute-start | bytes 3538952 | tf_op jit(solution)/shard_map/ppermute | solution.py:132
  634.8 147.6 %reduce-scatter.15.cloned.1.call-start = ((), (), s32[]{:S(2)}) async-start(), calls=%async_computation.27 | async-start | bytes 3981312 | tf_op jit(solution)/shard_map/reduce_scatter | solution.py:383
  638.5 75.8 %collective-permute-start.28 = (bf16[384,1536]{1,0:T(8,128)(2,1)}, bf16[384,1536]{1,0:T(8,128)(2,1)}, u32[]{:S(2)}, u32[]{:S(2)}) collective-permute-start(bf16[384,1536]{1,0:T(8,128)(2,1)} %fusion.69), channel_id=1, source_target_pairs={{16,0},{24,8},{17,1},{25,9},{18,2},{26,10},{19,3},{27,11},{20,4},{... | collective-permute-start | bytes 3538952 | tf_op jit(solution)/shard_map/ppermute | solution.py:132
  689.7 36.5 %collective-permute-start.19 = (bf16[256,1536]{1,0:T(8,128)(2,1)}, bf16[256,1536]{1,0:T(8,128)(2,1)S(1)}, u32[]{:S(2)}, u32[]{:S(2)}) collective-permute-start(bf16[256,1536]{1,0:T(8,128)(2,1)} %pad_maximum_fusion.10), channel_id=1, source_target_pairs={{0,16},{8,24},{16,0},{24,8},{1,17},{9,25},{17,1},{25,9},{2,18},{10... | collective-permute-start | bytes 2359304 | tf_op jit(solution)/shard_map/ppermute | solution.py:123
  720.0 49.6 %all-to-all-start.12 = ((bf16[8,192,384]{2,1,0:T(8,128)(2,1)}), bf16[8,192,384]{2,1,0:T(8,128)(2,1)}, u32[]{:S(2)}, u32[]{:S(2)}) async-start(bf16[8,192,384]{2,1,0:T(8,128)(2,1)} %bitcast.99), calls=%async_computation.18 | async-start | bytes 2359296 | tf_op jit(solution)/shard_map/all_to_all | solution.py:470
  730.5 35.7 %collective-permute-start.26 = (bf16[48,1536]{1,0:T(8,128)(2,1)S(1)}, bf16[48,1536]{1,0:T(8,128)(2,1)S(1)}, u32[]{:S(2)}, u32[]{:S(2)}) collective-permute-start(bf16[48,1536]{1,0:T(8,128)(2,1)S(1)} %get-tuple-element.133), channel_id=1, source_target_pairs={{4,0},{5,1},{6,2},{7,3},{20,4},{21,5},{22,6},{23,7},{12,8},{13,9},... | collective-permute-start | bytes 442376 | tf_op jit(solution)/shard_map/ppermute | solution.py:163
  (142 other events, 1805.4 us)
Sparse Core Ops, SparseCore 0:
  29.4 90.1 all-gather.4
  121.7 49.6 all-gather.6
  191.5 64.1 all-gather.8
  292.9 53.2 all-gather.10
  366.7 56.7 reduce-scatter.6
  425.6 65.9 reduce-scatter.8
  493.9 31.1 reduce-scatter.12
  527.5 48.8 reduce-scatter.10
  610.3 32.8 reduce-scatter.16
  658.4 42.8 reduce-scatter.14

commit v13 on v10

--- a/solution.py
+++ b/solution.py
@@ -28,7 +28,12 @@
 
 
 def gelu_exact(values):
-    return jax.nn.gelu(values, approximate=False)
+    return 0.5 * values * (1.0 + lax.erf(values * math.sqrt(0.5)))
+
+
+def gelu_slope(values):
+    normal = 0.5 * (1.0 + lax.erf(values * math.sqrt(0.5)))
+    return normal + values * jnp.exp(-0.5 * values * values) * (1.0 / math.sqrt(2.0 * math.pi))
 
 
 def matmul(left, right):
@@ -296,14 +301,17 @@
             jnp.concatenate(pick(down[0], down[2]) + pick(down[1], down[3]), axis=0),
         )
 
-    up_late, down_late = after((w_up[0], w_down[0]), all_gains)
+    down_late = after(w_down[0], all_gains)
     down_second = gather(
         jnp.where(on_first, to_first(down_late[:half_hidden]), down_late[half_hidden:])
     )
-    up_even, up_odd = column_parts(up_late, half_hidden)
-    up_second = gather(jnp.where(on_first, to_first(up_even), up_odd))
-    up_w = [None, up_second]
-    down_w = [None, down_second]
+
+    def second_ffn(gate):
+        up_even, up_odd = column_parts(after(w_up[0], gate), half_hidden)
+        return gather(jnp.where(on_first, to_first(up_even), up_odd)), down_second
+
+    up_w = [None, None]
+    down_w = [None, None]
     query_w = [weight[:, :inner] for weight in qkv_w]
     key_w = [weight[:, inner : 2 * inner] for weight in qkv_w]
     value_w = [weight[:, 2 * inner :] for weight in qkv_w]
@@ -341,7 +349,8 @@
             latent_low = from_slots((unit_in * all_gains[layer, 1]).astype(low))
         projected = matmul(latent_low, qkv_w[layer]).astype(low)
         if layer == 0:
-            up_w[0], down_w[0] = first_ffn(projected)
+            up_w[0], down_w[0] = lax.optimization_barrier(first_ffn(projected))
+            up_w[1], down_w[1] = second_ffn(media_value[0])
         query_low = projected[:, :inner]
         key_heads = split_heads(
             jnp.concatenate([media_key[layer], projected[:, inner : 2 * inner]], axis=0)
@@ -391,7 +400,7 @@
         grad_key, grad_value = after((grad_key[:seq_rows], grad_value[:seq_rows]), gate)
         part = matmul_nt(grad_key, key_w[layer]) + matmul_nt(grad_value, value_w[layer])
         media_gains.append(jnp.sum(part * media_unit, axis=0))
-        media_parts.append(part * all_gains[layer, 0])
+        media_parts.append((part * all_gains[layer, 0]).astype(low if layer else full))
 
     pieces = [None] * LAYERS
     for layer in (1, 0):
@@ -411,7 +420,7 @@
             active_low,
         ) = saved[layer]
         grad_active = matmul_nt(grad_low, down_w[layer])
-        grad_hidden = jax.vjp(gelu_exact, hidden_pre)[1](grad_active)[0].astype(low)
+        grad_hidden = (grad_active * gelu_slope(hidden_pre)).astype(low)
         if layer == 0:
             add_media(1, *media_grads, grad_hidden)
         down_grad = matmul_tn(active_low, grad_low)
@@ -475,12 +484,9 @@
             late = after(active_low, latent_part)
             here = (latent_slot == section)[:, None]
             kept = jnp.where(here, jnp.tile(middle, (section_count, 1)), 0.0)
-            width = feature_width // section_count
-            last = []
-            for i in range(section_count):
-                cut = slice(i * width, (i + 1) * width)
-                last.append((matmul(late, down_w[layer][:, cut]) + kept[:, cut]).astype(low))
-            last = lax.all_to_all(jnp.stack(last), "section", split_axis=0, concat_axis=0)
+            last = lax.optimization_barrier((matmul(late, down_w[layer]) + kept).astype(low))
+            last = last.reshape(latent_rows, section_count, -1).swapaxes(0, 1)
+            last = lax.all_to_all(last, "section", split_axis=0, concat_axis=0)
             latents_out = jnp.sum(last.astype(full), axis=0)
             grad_low = after(grad_low, latents_out)
             grad_low = after(grad_low, ffn_pieces)
@@ -491,7 +497,7 @@
         gain_rows[layer] = (gain_latent_grad, gain_ffn_grad)
     latent_grad = to_columns(after(grad_rows, (pieces[1], up_half)))
     media_rows = seq_rows // section_count
-    media_sum = sum_over_sections(media_parts[0] + media_parts[1])
+    media_sum = sum_over_sections(media_parts[0].astype(full) + media_parts[1])
     own_unit = lax.dynamic_slice_in_dim(media_unit, section * media_rows, media_rows, 0)
     own_inverse = lax.dynamic_slice_in_dim(media_inverse, section * media_rows, media_rows, 0)
     media_grad = gather_sections(norm_back(own_unit, own_inverse, media_sum).astype(low)).astype(

time: 730 us -> 729 us (level)
  waiting for transfers between devices: 65.6 us -> 86.4 us
  matrix products: 157 us -> 138 us
  local copies, waits for them, and re-layouts: 99.1 us -> 109 us
    dot_general x16 -> x13, matrix products: 57.1 us -> 39 us  [matmul(): return jnp.dot(left, right, preferred_element_type=full)]
    ppermute x4, waiting for transfers between devices: 9.61 us -> 20.9 us  [to_first(): return lax.ppermute(value, 'section', [(2, 0), (3, 1)])]
    unnamed x250 -> x272, local copies, waits for them, and re-layouts: 20.8 us -> 21.8 us
  transfers between devices with their start and end apart: 64 -> 64, of which waited for: 14 -> 22; matrix products, arithmetic and copies ran while one was open for 46% -> 46% of each run, Pallas kernels for 0% -> 0%
where the time goes in v13:
time: 729 us; the launch traced here: 720 us
  blocking collectives  145 us (20%)
  matrix products  138 us (19%)
  starting transfers between devices  118 us (16%)
  local copies, waits for them, and re-layouts  109 us (15%)
  other arithmetic  107 us (15%)
  waiting for transfers between devices  86.4 us (12%)
  between operations  17 us (2%)
    all_gather x2, blocking collectives, from_sequences(): near = lax.all_gather(rows, 'pair', axis=0, tiled=True)  57.2 us
    all_gather x4, blocking collectives, from_slots(): return lax.all_gather(rows, 'section', axis=0, tiled=True)  46.1 us
    dot_general x17, matrix products, matmul_nt(): lax.dot_general(left, right, (((1,), (1,)), ((), ())), preferred_element_...  44.8 us
    dot_general x13, matrix products, matmul(): return jnp.dot(left, right, preferred_element_type=full)  39 us
    ppermute x26, starting transfers between devices, swapped(): return lax.ppermute(value, 'section', pairs)  33.4 us
    dot_general x8, matrix products, matmul_tn(): lax.dot_general(left, right, (((0,), (0,)), ((), ())), preferred_element_...  31.7 us
    ppermute x26, waiting for transfers between devices, swapped(): return lax.ppermute(value, 'section', pairs)  31.4 us
    all_gather x3, blocking collectives, per_device(): all_gains = lax.all_gather(all_gains, axis, axis=2, tiled=True)  30.1 us
  transfers between devices with their start and end apart: 64, of which 22 were waited for; matrix products, arithmetic and copies ran while one was open for 46% of the time, Pallas kernels for 0%

profile of v13, /device:TPU:0, one launch (start us, length us, event | category | flops | bytes accessed | tf_op | source)
XLA Modules:
  0.0 720.1 jit_solution(16979451194719484262)
XLA Ops:
  12.6 10.2 %collective-permute-done = bf16[192,1152]{1,0:T(8,128)(2,1)S(1)} collective-permute-done((bf16[192,1152]{1,0:T(8,128)(2,1)S(1)}, bf16[192,1152]{1,0:T(8,128)(2,1)S(1)}, u32[]{:S(2)}, u32[]{:S(2)}) %collective-permute-start) | collective-permute-done | bytes 442400 | tf_op jit(solution)/shard_map/ppermute | solution.py:123
  31.4 10.9 %collective-permute-start.1 = (bf16[96,3072]{1,0:T(8,128)(2,1)}, bf16[96,3072]{1,0:T(8,128)(2,1)}, u32[]{:S(2)}, u32[]{:S(2)}) collective-permute-start(bf16[96,3072]{1,0:T(8,128)(2,1)} %slice_bitcast_fusion.4), channel_id=1, source_target_pairs={{0,16},{8,24},{1,17},{9,25},{2,18},{10,26},{3,19},{11,27},{4,20},{... | collective-permute-start | bytes 1769480 | tf_op jit(solution)/shard_map/ppermute | solution.py:129
  57.8 18.5 %all_gather.40 = f32[2,3,384]{1,0,2:T(2,128)S(1)} all-gather(f32[2,3,96]{1,0,2:T(2,128)S(1)} %all_gather.39), channel_id=1, replica_groups=mesh['section'=4,'pair'=4,'core'=2] {'pair'}, dimensions={2}, use_global_device_ids=true | all-gather | bytes 11520 | tf_op jit(solution)/shard_map/all_gather | solution.py:266
  82.7 9.8 %all_gather.41 = f32[2,3,1536]{2,0,1:T(2,128)S(1)} all-gather(f32[2,3,384]{2,0,1:T(2,128)S(1)} %copy.151), channel_id=1, replica_groups=mesh['section'=4,'pair'=4,'core'=2] {'section'}, dimensions={2}, use_global_device_ids=true | all-gather | bytes 46080 | tf_op jit(solution)/shard_map/all_gather | solution.py:266
  127.1 7.3 %slice_reduce_fusion = (bf16[192,8,192]{2,1,0:T(8,128)(2,1)}, bf16[192,8,192]{2,1,0:T(8,128)(2,1)S(1)}) fusion(bf16[192,8,2,192]{3,2,1,0:T(2,128)(2,1)S(1)} %reshape.742), kind=kLoop, calls=%fused_computation.111 | loop fusion | bytes 2359296 | tf_op jit(solution)/shard_map/slice | solution.py:250
  144.9 10.4 %collective-permute-done.15 = bf16[192,1536]{1,0:T(8,128)(2,1)S(1)} collective-permute-done((bf16[192,1536]{1,0:T(8,128)(2,1)}, bf16[192,1536]{1,0:T(8,128)(2,1)S(1)}, u32[]{:S(2)}, u32[]{:S(2)}) %collective-permute-start.15) | collective-permute-done | bytes 589856 | tf_op jit(solution)/shard_map/ppermute | solution.py:132
  175.2 29.1 %all_gather.43 = bf16[256,1536]{1,0:T(8,128)(2,1)S(1)} all-gather(bf16[64,1536]{1,0:T(8,128)(2,1)S(1)} %reshape.734), channel_id=1, replica_groups=mesh['section'=4,'pair'=4,'core'=2] {'pair'}, dimensions={0}, use_global_device_ids=true | all-gather | bytes 983040 | tf_op jit(solution)/shard_map/all_gather | solution.py:194
  211.2 6.4 collective-permute-done.13
  232.6 10.5 %collective-permute-done.16 = bf16[192,1536]{1,0:T(8,128)(2,1)} collective-permute-done((bf16[192,1536]{1,0:T(8,128)(2,1)}, bf16[192,1536]{1,0:T(8,128)(2,1)}, u32[]{:S(2)}, u32[]{:S(2)}) %collective-permute-start.16) | collective-permute-done | bytes 589856 | tf_op jit(solution)/shard_map/ppermute | solution.py:132
  245.1 5.0 convolution_convert_fusion.13
  257.7 11.3 %all_gather.45 = bf16[256,1536]{1,0:T(8,128)(2,1)S(1)} all-gather(bf16[64,1536]{1,0:T(8,128)(2,1)S(1)} %multiply_convert_fusion.9), channel_id=1, replica_groups=mesh['section'=4,'pair'=4,'core'=2] {'section'}, dimensions={0}, use_global_device_ids=true | all-gather | bytes 983040 | tf_op jit(solution)/shard_map/all_gather | solution.py:185
  287.3 11.2 %all_to_all.101 = bf16[4,64,1536]{2,1,0:T(8,128)(2,1)S(1)} all-to-all(bf16[4,64,1536]{2,1,0:T(8,128)(2,1)S(1)} %bitcast.357), channel_id=1, replica_groups=mesh['section'=4,'pair'=4,'core'=2] {'section'}, dimensions={0} | all-to-all | bytes 1572864 | tf_op jit(solution)/shard_map/all_to_all | solution.py:181
  299.6 11.4 %all_gather.46 = bf16[256,1536]{1,0:T(8,128)(2,1)} all-gather(bf16[64,1536]{1,0:T(8,128)(2,1)S(1)} %multiply_convert_fusion.8), channel_id=1, replica_groups=mesh['section'=4,'pair'=4,'core'=2] {'section'}, dimensions={0}, use_global_device_ids=true | all-gather | bytes 983040 | tf_op jit(solution)/shard_map/all_gather | solution.py:185
  311.0 5.2 multiply_convert_fusion.6
  330.0 4.9 convolution_convert_fusion.12
  352.1 11.0 %all_gather.49 = bf16[256,1536]{1,0:T(8,128)(2,1)S(1)} all-gather(bf16[64,1536]{1,0:T(8,128)(2,1)S(1)} %get-tuple-element.92), channel_id=1, replica_groups=mesh['section'=4,'pair'=4,'core'=2] {'section'}, dimensions={0}, use_global_device_ids=true | all-gather | bytes 983040 | tf_op jit(solution)/shard_map/all_gather | solution.py:185
  405.7 28.1 %all_gather.50 = bf16[256,1536]{1,0:T(8,128)(2,1)S(1)} all-gather(bf16[64,1536]{1,0:T(8,128)(2,1)S(1)} %get-tuple-element.90), channel_id=1, replica_groups=mesh['section'=4,'pair'=4,'core'=2] {'pair'}, dimensions={0}, use_global_device_ids=true | all-gather | bytes 983040 | tf_op jit(solution)/shard_map/all_gather | solution.py:194
  433.9 9.0 %convolution_convert_fusion.1 = bf16[1536,1152]{1,0:T(8,128)(2,1)} fusion(bf16[256,1536]{1,0:T(8,128)(2,1)S(1)} %copy-done.75, bf16[1024,1536]{1,0:T(8,128)(2,1)} %get-tuple-element.110, bf16[256,384]{0,1:T(8,128)(2,1)S(1)} %bitcast.384, bf16[1280,384]{0,1:T(8,128)(2,1)S(1)} %bitcast.342, bf16[1280,384]{0,1:T(8,128)(2,1)S(1)} %bitcast.353), kind=kOutput, calls=%fused_computation.3 | convolution fusion | flops 4551278592 | bytes 9633792 | tf_op jit(solution)/shard_map/dot_general | solution.py:48
  497.3 5.2 collective-permute-start.41
  521.9 12.3 %all_gather.51 = bf16[256,1536]{1,0:T(8,128)(2,1)S(1)} all-gather(bf16[64,1536]{1,0:T(8,128)(2,1)S(1)} %get-tuple-element.88), channel_id=1, replica_groups=mesh['section'=4,'pair'=4,'core'=2] {'section'}, dimensions={0}, use_global_device_ids=true | all-gather | bytes 983040 | tf_op jit(solution)/shard_map/all_gather | solution.py:185
  573.6 9.2 %convolution_convert_fusion = bf16[1536,1152]{1,0:T(8,128)(2,1)} fusion(bf16[256,1536]{1,0:T(8,128)(2,1)} %copy-done.73, bf16[1024,1536]{1,0:T(8,128)(2,1)} %get-tuple-element.111, bf16[256,384]{0,1:T(8,128)(2,1)} %bitcast.386, bf16[1280,384]{0,1:T(8,128)(2,1)S(1)} %bitcast.340, bf16[1280,384]{0,1:T(8,128)(2,1)S(1)} %bitcast.350), kind=kOutput, calls=%fused_computation.2 | convolution fusion | flops 4551278592 | bytes 9633792 | tf_op jit(solution)/shard_map/dot_general | solution.py:48
  598.2 9.2 %multiply_reduce_fusion.1 = (f32[1536]{0:T(1024)S(1)}, f32[1536]{0:T(1024)S(1)}, f32[1024,1536]{1,0:T(8,128)}, f32[1024,1536]{1,0:T(8,128)}) fusion(bf16[1024,1536]{1,0:T(8,128)(2,1)S(1)} %copy-done.3, f32[1024]{0:T(1024)S(1)} %copy-done.92, f32[1024]{0:T(1024)S(1)} %copy-done.91, f32[1024,1536]{1,0:T(8,128)} %convolution_add_fusion.1, ...), kind=kOutput, calls=%fused_computation.10 | convolution fusion | flops 1228403712 | bytes 30310400 | tf_op jit(solution)/shard_map/dot_general | solution.py:44
  642.5 8.9 %all-to-all-done.9 = bf16[8,96,384]{2,1,0:T(8,128)(2,1)S(1)} async-done(((bf16[8,96,384]{2,1,0:T(8,128)(2,1)}), bf16[8,96,384]{2,1,0:T(8,128)(2,1)S(1)}, u32[]{:S(2)}, u32[]{:S(2)}) %all-to-all-start.9) | async-done | bytes 589856 | tf_op jit(solution)/shard_map/all_to_all | solution.py:480
  667.8 5.4 all-to-all-done.10
  (666 shorter events, 442.8 us)
Async XLA Ops:
  7.2 94.8 %all-gather.5.cloned.1.call-start = ((), (), s32[]{:S(2)}) async-start(), calls=%async_computation.19 | async-start | bytes 5308416 | tf_op jit(solution)/shard_map/all_gather | solution.py:270
  29.3 215.8 %all-gather.7.cloned.1.call-start = ((), (), s32[]{:S(2)}) async-start(), calls=%async_computation.20 | async-start | bytes 5308416 | tf_op jit(solution)/shard_map/all_gather | solution.py:270
  52.8 44.8 %collective-permute-start.5 = (bf16[192,1536]{1,0:T(8,128)(2,1)}, bf16[192,1536]{1,0:T(8,128)(2,1)}, u32[]{:S(2)}, u32[]{:S(2)}) collective-permute-start(bf16[192,1536]{1,0:T(8,128)(2,1)} %get-tuple-element.40), channel_id=1, source_target_pairs={{0,16},{8,24},{1,17},{9,25},{2,18},{10,26},{3,19},{11,27},{4,20},{... | collective-permute-start | bytes 1769480 | tf_op jit(solution)/shard_map/ppermute | solution.py:129
  82.6 228.4 %all-gather.9.cloned.1.call-start = ((), (), s32[]{:S(2)}) async-start(), calls=%async_computation.21 | async-start | bytes 5308416 | tf_op jit(solution)/shard_map/all_gather | solution.py:270
  106.1 57.3 %collective-permute-start.7 = (bf16[768,384]{1,0:T(8,128)(2,1)}, bf16[768,384]{1,0:T(8,128)(2,1)}, u32[]{:S(2)}, u32[]{:S(2)}) collective-permute-start(bf16[768,384]{1,0:T(8,128)(2,1)} %bitcast.25), channel_id=1, source_target_pairs={{0,8},{8,0},{16,24},{24,16},{1,9},{9,1},{17,25},{25,17},{2,10},{10... | collective-permute-start | bytes 1769480 | tf_op jit(solution)/shard_map/ppermute | solution.py:123
  107.6 57.6 %collective-permute-start.6 = (bf16[768,384]{1,0:T(8,128)(2,1)}, bf16[768,384]{1,0:T(8,128)(2,1)}, u32[]{:S(2)}, u32[]{:S(2)}) collective-permute-start(bf16[768,384]{1,0:T(8,128)(2,1)} %bitcast.25), channel_id=1, source_target_pairs={{0,16},{8,24},{16,0},{24,8},{1,17},{9,25},{17,1},{25,9},{2,18},{10... | collective-permute-start | bytes 1769480 | tf_op jit(solution)/shard_map/ppermute | solution.py:123
  111.1 57.8 %collective-permute-start.11 = (bf16[192,1536]{1,0:T(8,128)(2,1)}, bf16[192,1536]{1,0:T(8,128)(2,1)}, u32[]{:S(2)}, u32[]{:S(2)}) collective-permute-start(bf16[192,1536]{1,0:T(8,128)(2,1)} %broadcast_select_fusion.5), channel_id=1, source_target_pairs={{0,8},{8,0},{16,24},{24,16},{1,9},{9,1},{17,25},{25,17},{2,10},{10... | collective-permute-start | bytes 1769480 | tf_op jit(solution)/shard_map/ppermute | solution.py:123
  161.4 43.0 %collective-permute-start.10 = (bf16[192,1536]{1,0:T(8,128)(2,1)}, bf16[192,1536]{1,0:T(8,128)(2,1)}, u32[]{:S(2)}, u32[]{:S(2)}) collective-permute-start(bf16[192,1536]{1,0:T(8,128)(2,1)} %broadcast_select_fusion.5), channel_id=1, source_target_pairs={{0,16},{8,24},{16,0},{24,8},{1,17},{9,25},{17,1},{25,9},{2,18},{10... | collective-permute-start | bytes 1769480 | tf_op jit(solution)/shard_map/ppermute | solution.py:123
  165.2 44.0 %collective-permute-start.8 = (bf16[384,384]{1,0:T(8,128)(2,1)}, bf16[384,384]{1,0:T(8,128)(2,1)S(1)}, u32[]{:S(2)}, u32[]{:S(2)}) collective-permute-start(bf16[384,384]{1,0:T(8,128)(2,1)} %slice.506), channel_id=1, source_target_pairs={{0,16},{8,24},{16,0},{24,8},{1,17},{9,25},{17,1},{25,9},{2,18},{10... | collective-permute-start | bytes 884744 | tf_op jit(solution)/shard_map/ppermute | solution.py:123
  166.9 42.3 %collective-permute-start.9 = (bf16[384,384]{1,0:T(8,128)(2,1)}, bf16[384,384]{1,0:T(8,128)(2,1)}, u32[]{:S(2)}, u32[]{:S(2)}) collective-permute-start(bf16[384,384]{1,0:T(8,128)(2,1)} %slice.507), channel_id=1, source_target_pairs={{0,8},{8,0},{16,24},{24,16},{1,9},{9,1},{17,25},{25,17},{2,10},{10... | collective-permute-start | bytes 884744 | tf_op jit(solution)/shard_map/ppermute | solution.py:123
  232.6 88.2 %all-gather.11.cloned.1.call-start = ((), (), s32[]{:S(2)}) async-start(), calls=%async_computation.22 | async-start | bytes 5308416 | tf_op jit(solution)/shard_map/all_gather | solution.py:270
  245.0 205.8 %reduce-scatter.7.cloned.1.call-start = ((), (), s32[]{:S(2)}) async-start(), calls=%async_computation.23 | async-start | bytes 5308416 | tf_op jit(solution)/shard_map/reduce_scatter | solution.py:393
  320.7 130.1 %reduce-scatter.9.cloned.1.call-start = ((), (), s32[]{:S(2)}) async-start(), calls=%async_computation.24 | async-start | bytes 5308416 | tf_op jit(solution)/shard_map/reduce_scatter | solution.py:393
  387.7 266.4 %reduce-scatter.13.cloned.1.call-start = ((), (), s32[]{:S(2)}) async-start(), calls=%async_computation.26 | async-start | bytes 1327104 | tf_op jit(solution)/shard_map/reduce_scatter | solution.py:393
  396.6 49.7 %all-to-all-start.5 = ((bf16[4,256,384]{2,1,0:T(8,128)(2,1)}), bf16[4,256,384]{2,1,0:T(8,128)(2,1)}, u32[]{:S(2)}, u32[]{:S(2)}) async-start(bf16[4,256,384]{2,1,0:T(8,128)(2,1)} %bitcast.294), calls=%async_computation.5 | async-start | bytes 1572864 | tf_op jit(solution)/shard_map/all_to_all | solution.py:489
  400.8 253.2 %reduce-scatter.11.cloned.1.call-start = ((), (), s32[]{:S(2)}) async-start(), calls=%async_computation.25 | async-start | bytes 3981312 | tf_op jit(solution)/shard_map/reduce_scatter | solution.py:393
  463.4 87.7 %collective-permute-start.20 = (bf16[384,384]{1,0:T(8,128)(2,1)}, bf16[384,384]{1,0:T(8,128)(2,1)}, u32[]{:S(2)}, u32[]{:S(2)}) collective-permute-start(bf16[384,384]{1,0:T(8,128)(2,1)} %get-tuple-element.135), channel_id=1, source_target_pairs={{0,8},{8,0},{16,24},{24,16},{1,9},{9,1},{17,25},{25,17},{2,10},{10... | collective-permute-start | bytes 884744 | tf_op jit(solution)/shard_map/ppermute | solution.py:123
  465.3 85.9 %collective-permute-start.19 = (bf16[384,384]{1,0:T(8,128)(2,1)}, bf16[384,384]{1,0:T(8,128)(2,1)}, u32[]{:S(2)}, u32[]{:S(2)}) collective-permute-start(bf16[384,384]{1,0:T(8,128)(2,1)} %get-tuple-element.136), channel_id=1, source_target_pairs={{0,16},{8,24},{16,0},{24,8},{1,17},{9,25},{17,1},{25,9},{2,18},{10... | collective-permute-start | bytes 884744 | tf_op jit(solution)/shard_map/ppermute | solution.py:123
  467.6 86.4 %collective-permute-start.37 = (bf16[96,1536]{1,0:T(8,128)(2,1)}, bf16[96,1536]{1,0:T(8,128)(2,1)}, u32[]{:S(2)}, u32[]{:S(2)}) collective-permute-start(bf16[96,1536]{1,0:T(8,128)(2,1)} %get-tuple-element.133), channel_id=1, source_target_pairs={{0,8},{8,0},{16,24},{24,16},{1,9},{9,1},{17,25},{25,17},{2,10},{10... | collective-permute-start | bytes 884744 | tf_op jit(solution)/shard_map/ppermute | solution.py:123
  468.2 85.8 %collective-permute-start.36 = (bf16[96,1536]{1,0:T(8,128)(2,1)}, bf16[96,1536]{1,0:T(8,128)(2,1)}, u32[]{:S(2)}, u32[]{:S(2)}) collective-permute-start(bf16[96,1536]{1,0:T(8,128)(2,1)} %get-tuple-element.134), channel_id=1, source_target_pairs={{0,16},{8,24},{16,0},{24,8},{1,17},{9,25},{17,1},{25,9},{2,18},{10... | collective-permute-start | bytes 884744 | tf_op jit(solution)/shard_map/ppermute | solution.py:123
  476.4 197.5 %reduce-scatter.17.cloned.1.call-start = ((), (), s32[]{:S(2)}) async-start(), calls=%async_computation.28 | async-start | bytes 1327104 | tf_op jit(solution)/shard_map/reduce_scatter | solution.py:393
  497.3 141.9 %collective-permute-start.41 = (bf16[192,1536]{1,0:T(8,128)(2,1)}, bf16[192,1536]{1,0:T(8,128)(2,1)}, u32[]{:S(2)}, u32[]{:S(2)}) collective-permute-start(bf16[192,1536]{1,0:T(8,128)(2,1)} %reduce-scatter.7.cloned.1.call-done), channel_id=1, source_target_pairs={{0,16},{8,24},{1,17},{9,25},{2,18},{10,26},{3,19},{11,27},{4,20},{... | collective-permute-start | bytes 1769480 | tf_op jit(solution)/shard_map/ppermute | solution.py:129
  573.5 126.6 %reduce-scatter.15.cloned.1.call-start = ((), (), s32[]{:S(2)}) async-start(), calls=%async_computation.27 | async-start | bytes 3981312 | tf_op jit(solution)/shard_map/reduce_scatter | solution.py:393
  585.2 54.1 %collective-permute-start.40 = (bf16[192,1536]{1,0:T(8,128)(2,1)S(1)}, bf16[192,1536]{1,0:T(8,128)(2,1)}, u32[]{:S(2)}, u32[]{:S(2)}) collective-permute-start(bf16[192,1536]{1,0:T(8,128)(2,1)S(1)} %fusion.78), channel_id=1, source_target_pairs={{16,0},{24,8},{17,1},{25,9},{18,2},{26,10},{19,3},{27,11},{20,4},{... | collective-permute-start | bytes 1769480 | tf_op jit(solution)/shard_map/ppermute | solution.py:132
  (174 other events, 1618.1 us)
Sparse Core Ops, SparseCore 0:
  29.4 72.5 all-gather.4
  103.6 52.1 all-gather.6
  158.0 62.8 all-gather.8
  245.1 50.6 all-gather.10
  320.8 54.3 reduce-scatter.6
  377.4 65.9 reduce-scatter.8
  445.7 31.0 reduce-scatter.12
  479.1 46.8 reduce-scatter.10
  551.2 33.0 reduce-scatter.16
  590.1 47.0 reduce-scatter.14

commit v14 on v13

--- a/solution.py
+++ b/solution.py
@@ -105,7 +105,6 @@
     dp_count = lax.axis_size("pair") * lax.axis_size("core")
     on_first = section // 2 == 0
     stride = dp_count // 2
-    row_first = dp_index // stride == 0
     seq_rows = segment_ids.shape[1]
     slot_count = slot_map.shape[1]
     feature_width = latents.shape[1]
@@ -134,34 +133,75 @@
     def after(value, earlier):
         return lax.optimization_barrier((value, earlier))[0]
 
-    def turn_pairs(flip, back):
+    def turn_pairs(span, flip, back):
         pairs = []
         for source in range(section_count):
             for index in range(dp_count):
                 layer, half = divmod(source, 2)
-                bit, lowest = divmod(index, stride)
-                moved = (layer ^ flip) * stride + lowest
+                high, bit, lowest = index // (2 * span), index // span % 2, index % span
+                moved = (2 * high + (layer ^ flip)) * span + lowest
                 target = (bit * 2 + half) * dp_count + moved
                 pair = (source * dp_count + index, target)
                 pairs.append(pair[::-1] if back else pair)
         return pairs
 
-    def exchange_rows(weight):
+    def first_bit(span):
+        return dp_index // span % 2 == 0
+
+    def exchange_rows(weight, span):
         half = weight.shape[0] // 2
         near, far = pick(weight[:half], weight[half:])
-        first = lax.ppermute(near, everywhere, turn_pairs(0, False))
-        second = lax.ppermute(far, everywhere, turn_pairs(1, False))
-        return (
-            jnp.where(row_first, first, second),
-            jnp.where(row_first, second, first),
-        )
-
-    def join_rows(first, second):
-        near = jnp.where(row_first, first, second)
-        far = jnp.where(row_first, second, first)
-        near = lax.ppermute(near, everywhere, turn_pairs(0, True))
-        far = lax.ppermute(far, everywhere, turn_pairs(1, True))
+        first = lax.ppermute(near, everywhere, turn_pairs(span, 0, False))
+        second = lax.ppermute(far, everywhere, turn_pairs(span, 1, False))
+        chosen = first_bit(span)
+        return jnp.where(chosen, first, second), jnp.where(chosen, second, first)
+
+    def join_rows(first, second, span):
+        chosen = first_bit(span)
+        near = jnp.where(chosen, first, second)
+        far = jnp.where(chosen, second, first)
+        near = lax.ppermute(near, everywhere, turn_pairs(span, 0, True))
+        far = lax.ppermute(far, everywhere, turn_pairs(span, 1, True))
         return jnp.concatenate(pick(near, far), axis=0).astype(full)
+
+    def exchange_second(weight, span):
+        half = weight.shape[0] // 2
+        parts = []
+        for bit in range(2):
+            pairs = [
+                pair
+                for flip in range(2)
+                for pair in turn_pairs(span, flip, False)
+                if pair[0] >= 2 * dp_count and pair[1] // span % 2 == bit
+            ]
+            parts.append(lax.ppermute(weight[bit * half : (bit + 1) * half], everywhere, pairs))
+        return jnp.where(first_bit(span), parts[0], parts[1])
+
+    def join_second(piece, span):
+        parts = []
+        for bit in range(2):
+            pairs = [
+                pair[::-1]
+                for flip in range(2)
+                for pair in turn_pairs(span, flip, False)
+                if pair[0] >= 2 * dp_count and pair[1] // span % 2 == bit
+            ]
+            parts.append(lax.ppermute(piece, everywhere, pairs))
+        return jnp.concatenate(parts, axis=0)
+
+    def in_rows(gathered, span):
+        if span > 1:
+            width = gathered.shape[1]
+            gathered = gathered.reshape(-1, 2, span, gathered.shape[0] // dp_count, width)
+            gathered = gathered.swapaxes(1, 2).reshape(-1, width)
+        return gathered
+
+    def in_shards(grad, span):
+        if span > 1:
+            width = grad.shape[1]
+            grad = grad.reshape(-1, span, 2, grad.shape[0] // dp_count, width)
+            grad = grad.swapaxes(1, 2).reshape(-1, width)
+        return grad
 
     def fold(piece):
         blocks = [piece[:, i * inner : (i + 1) * inner] for i in range(feature_width // inner)]
@@ -264,7 +304,7 @@
     all_gains = after(gains, (other_heads, up_share))
     for axis in ("core", "pair", "section"):
         all_gains = lax.all_gather(all_gains, axis, axis=2, tiled=True)
-    out_pieces = exchange_rows(after(w_out[0], other_heads))
+    out_pieces = exchange_rows(after(w_out[0], other_heads), stride)
 
     def gather(piece):
         return lax.all_gather(piece, dp, axis=0, tiled=True)
@@ -301,14 +341,13 @@
             jnp.concatenate(pick(down[0], down[2]) + pick(down[1], down[3]), axis=0),
         )
 
-    down_late = after(w_down[0], all_gains)
-    down_second = gather(
-        jnp.where(on_first, to_first(down_late[:half_hidden]), down_late[half_hidden:])
-    )
+    span = max(1, dp_count // 8)
+    hidden_block = w_up.shape[2] // 8
+    down_piece = exchange_second(after(w_down[0], all_gains), span)
 
     def second_ffn(gate):
-        up_even, up_odd = column_parts(after(w_up[0], gate), half_hidden)
-        return gather(jnp.where(on_first, to_first(up_even), up_odd)), down_second
+        up_even, up_odd = column_parts(after(w_up[0], gate), hidden_block)
+        return gather(jnp.where(on_first, to_first(up_even), up_odd))
 
     up_w = [None, None]
     down_w = [None, None]
@@ -333,9 +372,12 @@
     media_value = []
     for layer in range(LAYERS):
         media_low.append((media_unit * all_gains[layer, 0]).astype(low))
+        if layer == 0:
+            media_low[0], down_piece = lax.optimization_barrier((media_low[0], down_piece))
         media_key.append(matmul(media_low[layer], key_w[layer]).astype(low))
         media_value.append(matmul(media_low[layer], value_w[layer]).astype(low))
 
+    down_second = in_rows(gather(down_piece), span)
     saved = []
     current = lax.dynamic_slice_in_dim(latents, section * slot_rows, slot_rows, 0).astype(full)
     grad_rows = lax.dynamic_slice_in_dim(cotangent, section * slot_rows, slot_rows, 0).astype(full)
@@ -350,7 +392,6 @@
         projected = matmul(latent_low, qkv_w[layer]).astype(low)
         if layer == 0:
             up_w[0], down_w[0] = lax.optimization_barrier(first_ffn(projected))
-            up_w[1], down_w[1] = second_ffn(media_value[0])
         query_low = projected[:, :inner]
         key_heads = split_heads(
             jnp.concatenate([media_key[layer], projected[:, inner : 2 * inner]], axis=0)
@@ -367,6 +408,8 @@
         unit_mid, inverse_mid = unit_rows(middle)
         ffn_low = (unit_mid * all_gains[layer, 2]).astype(low)
         ffn_low = from_slots(ffn_low) if layer else from_sequences(by_depth(ffn_low))
+        if layer == 0:
+            up_w[1], down_w[1] = second_ffn(ffn_low), down_second
         hidden_pre = matmul(ffn_low, up_w[layer])
         active_low = gelu_exact(hidden_pre).astype(low)
         if layer == 0:
@@ -429,7 +472,7 @@
             grad_hidden = after(grad_hidden, down_grad)
         up_grad = matmul_tn(ffn_low, grad_hidden)
         if layer:
-            ffn_pieces = (scatter(down_grad), scatter(up_grad.astype(low)))
+            ffn_pieces = (scatter(in_shards(down_grad, span)), scatter(up_grad.astype(low)))
             ffn_grad = sum_to_slots(matmul_nt(grad_hidden, up_w[layer]))
         else:
             ffn_grad = in_depth(sum_to_sequence(grad_hidden, up_w[layer], matmul_nt))
@@ -495,7 +538,11 @@
         else:
             media_grads = (grad_key, grad_value)
         gain_rows[layer] = (gain_latent_grad, gain_ffn_grad)
-    latent_grad = to_columns(after(grad_rows, (pieces[1], up_half)))
+    qkv_parts = [piece[0] for piece in pieces]
+    own, other = pick(qkv_parts[0], qkv_parts[1])
+    lower, upper = pick(own, swapped(other, 2))
+    out_grad = join_rows(*[piece[1] for piece in pieces], stride)
+    latent_grad = to_columns(after(grad_rows, (lower, up_half)))
     media_rows = seq_rows // section_count
     media_sum = sum_over_sections(media_parts[0].astype(full) + media_parts[1])
     own_unit = lax.dynamic_slice_in_dim(media_unit, section * media_rows, media_rows, 0)
@@ -510,22 +557,18 @@
     gain_parts = jnp.sum(
         lax.all_to_all(gain_parts, "section", split_axis=2, concat_axis=2), axis=2
     )
-    gain_parts = gain_parts.reshape(LAYERS, 3, dp_count, -1)
+    gain_parts = after(gain_parts, out_grad).reshape(LAYERS, 3, dp_count, -1)
     gain_grad = jnp.sum(lax.all_to_all(gain_parts, dp, split_axis=2, concat_axis=2), axis=2)
 
-    qkv_parts = [piece[0] for piece in pieces]
-    own, other = pick(qkv_parts[0], qkv_parts[1])
-    lower, upper = pick(own, swapped(other, 2))
     qkv_grads = [
         jnp.concatenate(
             [lower[:, i * inner : (i + 1) * inner], upper[:, i * inner : (i + 1) * inner]], axis=1
         ).astype(full)
         for i in range(3)
     ]
-    out_grad = join_rows(*[piece[1] for piece in pieces])
     down_piece, up_piece = ffn_pieces
-    up_second_grad = interleave(to_second(up_piece), up_piece, half_hidden)
-    down_second_grad = jnp.concatenate([to_second(down_piece), down_piece], axis=0)
+    up_second_grad = interleave(to_second(up_piece), up_piece, hidden_block)
+    down_second_grad = join_second(down_piece, span)
     up_first_grad = jnp.concatenate([up_half, to_first(up_half)], axis=0)
     down_first_grad = jnp.concatenate([down_half, to_first(down_half)], axis=0)
     up_grad = jnp.where(on_first, up_first_grad, up_second_grad).astype(full)

time: 729 us -> 827 us (1.13)
  waiting for transfers between devices: 86.4 us -> 227 us
  local copies, waits for them, and re-layouts: 109 us -> 81.4 us
  other arithmetic: 107 us -> 92.4 us
  starting transfers between devices: 118 us -> 108 us
    all_to_all x2, waiting for transfers between devices: 0.01 us -> 45 us  [sum_to_sequence(): arrived = lax.all_to_all(blocks, 'pair', split_axis=0, concat_axis=0)]
    ppermute x26, waiting for transfers between devices: 31.4 us -> 69.7 us  [swapped(): return lax.ppermute(value, 'section', pairs)]
    all_to_all x1, waiting for transfers between devices: 0.98 us -> 25.5 us  [per_device(): lax.all_to_all(up_share, dp, split_axis=1, concat_axis=0, tiled=True)]
    ppermute x4 -> x3, waiting for transfers between devices: 0.7 us -> 18.3 us  [to_second(): return lax.ppermute(value, 'section', [(0, 2), (1, 3)])]
    all_to_all x0 -> x1, blocking collectives: none -> 14.7 us  [per_device(): last = lax.all_to_all(last, 'section', split_axis=0, concat_axis=0)]
    ppermute x4 -> x8, starting transfers between devices: 6.59 us -> 18.9 us  [the longest x2 6.35 us: join_second(): parts.append(lax.ppermute(piece, everywhere, pairs))]
    all_gather x2, blocking collectives: 57.2 us -> 45.1 us  [from_sequences(): near = lax.all_gather(rows, 'pair', axis=0, tiled=True)]
    all_to_all x4, waiting for transfers between devices: 6.67 us -> 15.8 us  [sum_to_slots(): arrived = lax.all_to_all(blocks, 'section', split_axis=0, concat_axis=0)]
  transfers between devices with their start and end apart: 64 -> 65, of which waited for: 22 -> 36; matrix products, arithmetic and copies ran while one was open for 46% -> 35% of each run, Pallas kernels for 0% -> 0%
where the time goes in v14:
time: 827 us; the launch traced here: 816 us
  waiting for transfers between devices  227 us (27%)
  blocking collectives  148 us (18%)
  matrix products  142 us (17%)
  starting transfers between devices  108 us (13%)
  other arithmetic  92.4 us (11%)
  local copies, waits for them, and re-layouts  81.4 us (10%)
  between operations  17 us (2%)
    ppermute x26, waiting for transfers between devices, swapped(): return lax.ppermute(value, 'section', pairs)  69.7 us
    dot_general x17, matrix products, matmul_nt(): lax.dot_general(left, right, (((1,), (1,)), ((), ())), preferred_element_...  47.4 us
    all_gather x2, blocking collectives, from_sequences(): near = lax.all_gather(rows, 'pair', axis=0, tiled=True)  45.1 us
    all_to_all x2, waiting for transfers between devices, sum_to_sequence(): arrived = lax.all_to_all(blocks, 'pair', split_axis=0, concat_axis=0)  45 us
    all_gather x4, blocking collectives, from_slots(): return lax.all_gather(rows, 'section', axis=0, tiled=True)  45 us
    dot_general x13, matrix products, matmul(): return jnp.dot(left, right, preferred_element_type=full)  38.8 us
    dot_general x8, matrix products, matmul_tn(): lax.dot_general(left, right, (((0,), (0,)), ((), ())), preferred_element_...  34.1 us
    all_gather x3, blocking collectives, per_device(): all_gains = lax.all_gather(all_gains, axis, axis=2, tiled=True)  30.9 us
  transfers between devices with their start and end apart: 65, of which 36 were waited for; matrix products, arithmetic and copies ran while one was open for 35% of the time, Pallas kernels for 0%

profile of v14, /device:TPU:0, one launch (start us, length us, event | category | flops | bytes accessed | tf_op | source)
XLA Modules:
  0.0 815.9 jit_solution(3543128671169123497)
XLA Ops:
  12.6 10.2 %collective-permute-done = bf16[192,1152]{1,0:T(8,128)(2,1)S(1)} collective-permute-done((bf16[192,1152]{1,0:T(8,128)(2,1)S(1)}, bf16[192,1152]{1,0:T(8,128)(2,1)S(1)}, u32[]{:S(2)}, u32[]{:S(2)}) %collective-permute-start) | collective-permute-done | bytes 442400 | tf_op jit(solution)/shard_map/ppermute | solution.py:122
  32.1 10.9 %collective-permute-start.1 = (bf16[96,3072]{1,0:T(8,128)(2,1)}, bf16[96,3072]{1,0:T(8,128)(2,1)}, u32[]{:S(2)}, u32[]{:S(2)}) collective-permute-start(bf16[96,3072]{1,0:T(8,128)(2,1)} %slice_bitcast_fusion.4), channel_id=1, source_target_pairs={{0,16},{8,24},{1,17},{9,25},{2,18},{10,26},{3,19},{11,27},{4,20},{... | collective-permute-start | bytes 1769480 | tf_op jit(solution)/shard_map/ppermute | solution.py:128
  58.1 19.5 %all_gather.40 = f32[2,3,384]{1,0,2:T(2,128)} all-gather(f32[2,3,96]{1,0,2:T(2,128)S(1)} %all_gather.39), channel_id=1, replica_groups=mesh['section'=4,'pair'=4,'core'=2] {'pair'}, dimensions={2}, use_global_device_ids=true | all-gather | bytes 11520 | tf_op jit(solution)/shard_map/all_gather | solution.py:306
  78.7 9.6 %all_gather.41 = f32[2,3,1536]{2,0,1:T(2,128)S(1)} all-gather(f32[2,3,384]{2,0,1:T(2,128)S(1)} %copy.151), channel_id=1, replica_groups=mesh['section'=4,'pair'=4,'core'=2] {'section'}, dimensions={2}, use_global_device_ids=true | all-gather | bytes 46080 | tf_op jit(solution)/shard_map/all_gather | solution.py:306
  100.0 7.9 collective-permute-done.2
  140.4 7.8 all-to-all-done
  150.3 17.5 %all_gather.43 = bf16[256,1536]{1,0:T(8,128)(2,1)S(1)} all-gather(bf16[64,1536]{1,0:T(8,128)(2,1)S(1)} %reshape.734), channel_id=1, replica_groups=mesh['section'=4,'pair'=4,'core'=2] {'pair'}, dimensions={0}, use_global_device_ids=true | all-gather | bytes 983040 | tf_op jit(solution)/shard_map/all_gather | solution.py:234
  180.1 15.9 %collective-permute-done.17 = bf16[192,1536]{1,0:T(8,128)(2,1)S(1)} collective-permute-done((bf16[192,1536]{1,0:T(8,128)(2,1)S(1)}, bf16[192,1536]{1,0:T(8,128)(2,1)S(1)}, u32[]{:S(2)}, u32[]{:S(2)}) %collective-permute-start.17) | collective-permute-done | bytes 589856 | tf_op jit(solution)/shard_map/ppermute | solution.py:131
  210.7 25.5 %all-to-all-done.1 = bf16[96,8,384]{2,0,1:T(8,128)(2,1)S(1)} async-done(((bf16[96,8,384]{2,0,1:T(8,128)(2,1)}), bf16[96,8,384]{2,0,1:T(8,128)(2,1)S(1)}, u32[]{:S(2)}, u32[]{:S(2)}) %all-to-all-start.1) | async-done | bytes 589856 | tf_op jit(solution)/shard_map/all_to_all | solution.py:319
  240.3 12.2 %collective-permute-done.9 = bf16[768,384]{1,0:T(8,128)(2,1)S(1)} collective-permute-done((bf16[768,384]{1,0:T(8,128)(2,1)S(1)}, bf16[768,384]{1,0:T(8,128)(2,1)S(1)}, u32[]{:S(2)}, u32[]{:S(2)}) %collective-permute-start.9) | collective-permute-done | bytes 589856 | tf_op jit(solution)/shard_map/ppermute | solution.py:122
  254.6 10.5 %collective-permute-done.13 = bf16[192,1536]{1,0:T(8,128)(2,1)S(1)} collective-permute-done((bf16[192,1536]{1,0:T(8,128)(2,1)S(1)}, bf16[192,1536]{1,0:T(8,128)(2,1)S(1)}, u32[]{:S(2)}, u32[]{:S(2)}) %collective-permute-start.13) | collective-permute-done | bytes 589856 | tf_op jit(solution)/shard_map/ppermute | solution.py:122
  303.4 20.7 %all-to-all-done.2 = bf16[4,64,1536]{2,1,0:T(8,128)(2,1)S(1)} async-done(((bf16[4,64,1536]{2,1,0:T(8,128)(2,1)}), bf16[4,64,1536]{2,1,0:T(8,128)(2,1)S(1)}, u32[]{:S(2)}, u32[]{:S(2)}) %all-to-all-start.2) | async-done | bytes 786464 | tf_op jit(solution)/shard_map/all_to_all | solution.py:242
  324.7 11.1 %all_gather.45 = bf16[256,1536]{1,0:T(8,128)(2,1)S(1)} all-gather(bf16[64,1536]{1,0:T(8,128)(2,1)S(1)} %multiply_convert_fusion.9), channel_id=1, replica_groups=mesh['section'=4,'pair'=4,'core'=2] {'section'}, dimensions={0}, use_global_device_ids=true | all-gather | bytes 983040 | tf_op jit(solution)/shard_map/all_gather | solution.py:225
  353.9 12.2 %all_to_all.101 = bf16[4,64,1536]{2,1,0:T(8,128)(2,1)S(1)} all-to-all(bf16[4,64,1536]{2,1,0:T(8,128)(2,1)S(1)} %bitcast.357), channel_id=1, replica_groups=mesh['section'=4,'pair'=4,'core'=2] {'section'}, dimensions={0} | all-to-all | bytes 1572864 | tf_op jit(solution)/shard_map/all_to_all | solution.py:221
  366.7 10.5 %all_gather.46 = bf16[256,1536]{1,0:T(8,128)(2,1)S(1)} all-gather(bf16[64,1536]{1,0:T(8,128)(2,1)S(1)} %multiply_convert_fusion.8), channel_id=1, replica_groups=mesh['section'=4,'pair'=4,'core'=2] {'section'}, dimensions={0}, use_global_device_ids=true | all-gather | bytes 983040 | tf_op jit(solution)/shard_map/all_gather | solution.py:225
  413.7 11.0 %all_gather.49 = bf16[256,1536]{1,0:T(8,128)(2,1)S(1)} all-gather(bf16[64,1536]{1,0:T(8,128)(2,1)S(1)} %get-tuple-element.96), channel_id=1, replica_groups=mesh['section'=4,'pair'=4,'core'=2] {'section'}, dimensions={0}, use_global_device_ids=true | all-gather | bytes 983040 | tf_op jit(solution)/shard_map/all_gather | solution.py:225
  458.6 27.6 %all_gather.50 = bf16[256,1536]{1,0:T(8,128)(2,1)S(1)} all-gather(bf16[64,1536]{1,0:T(8,128)(2,1)S(1)} %get-tuple-element.94), channel_id=1, replica_groups=mesh['section'=4,'pair'=4,'core'=2] {'pair'}, dimensions={0}, use_global_device_ids=true | all-gather | bytes 983040 | tf_op jit(solution)/shard_map/all_gather | solution.py:234
  490.0 14.7 %all_to_all.102 = bf16[4,256,384]{2,1,0:T(8,128)(2,1)S(1)} all-to-all(bf16[4,256,384]{2,1,0:T(8,128)(2,1)S(1)} %bitcast.356), channel_id=1, replica_groups=mesh['section'=4,'pair'=4,'core'=2] {'section'}, dimensions={0} | all-to-all | bytes 1572864 | tf_op jit(solution)/shard_map/all_to_all | solution.py:532
  523.9 24.3 %all-to-all-done.7 = bf16[4,64,1536]{2,1,0:T(8,128)(2,1)S(1)} async-done(((bf16[4,64,1536]{2,1,0:T(8,128)(2,1)}), bf16[4,64,1536]{2,1,0:T(8,128)(2,1)S(1)}, u32[]{:S(2)}, u32[]{:S(2)}) %all-to-all-start.7) | async-done | bytes 786464 | tf_op jit(solution)/shard_map/all_to_all | solution.py:242
  554.3 12.3 %all_gather.51 = bf16[256,1536]{1,0:T(8,128)(2,1)S(1)} all-gather(bf16[64,1536]{1,0:T(8,128)(2,1)S(1)} %get-tuple-element.92), channel_id=1, replica_groups=mesh['section'=4,'pair'=4,'core'=2] {'section'}, dimensions={0}, use_global_device_ids=true | all-gather | bytes 983040 | tf_op jit(solution)/shard_map/all_gather | solution.py:225
  573.4 9.6 %convolution_convert_fusion = bf16[1536,1152]{1,0:T(8,128)(2,1)} fusion(bf16[256,1536]{1,0:T(8,128)(2,1)} %copy-done.73, bf16[1024,1536]{1,0:T(8,128)(2,1)} %get-tuple-element.114, bf16[256,384]{0,1:T(8,128)(2,1)S(1)} %bitcast.388, bf16[1280,384]{0,1:T(8,128)(2,1)S(1)} %bitcast.341, bf16[1280,384]{0,1:T(8,128)(2,1)} %bitcast.351), kind=kOutput, calls=%fused_computation.2 | convolution fusion | flops 4551278592 | bytes 9633792 | tf_op jit(solution)/shard_map/dot_general | solution.py:48
  662.9 9.6 %convolution_convert_fusion.1 = bf16[1536,1152]{1,0:T(8,128)(2,1)} fusion(bf16[256,1536]{1,0:T(8,128)(2,1)S(1)} %copy-done.72, bf16[1024,1536]{1,0:T(8,128)(2,1)} %get-tuple-element.41, bf16[256,384]{0,1:T(8,128)(2,1)} %bitcast.390, bf16[1280,384]{0,1:T(8,128)(2,1)} %bitcast.344, bf16[1280,384]{0,1:T(8,128)(2,1)} %bitcast.354), kind=kOutput, calls=%fused_computation.3 | convolution fusion | flops 4551278592 | bytes 9633792 | tf_op jit(solution)/shard_map/dot_general | solution.py:48
  689.6 9.2 %multiply_reduce_fusion.1 = (f32[1536]{0:T(1024)S(1)}, f32[1536]{0:T(1024)S(1)}, f32[1024,1536]{1,0:T(8,128)}, f32[1024,1536]{1,0:T(8,128)}) fusion(bf16[1024,1536]{1,0:T(8,128)(2,1)S(1)} %copy-done.3, f32[1024]{0:T(1024)S(1)} %copy-done.96, f32[1024]{0:T(1024)S(1)} %copy-done.95, f32[1024,1536]{1,0:T(8,128)} %convolution_add_fusion.1, ...), kind=kOutput, calls=%fused_computation.10 | convolution fusion | flops 1228403712 | bytes 30310400 | tf_op jit(solution)/shard_map/dot_general | solution.py:44
  764.2 8.2 %collective-permute-done.29 = bf16[256,1536]{1,0:T(8,128)(2,1)} collective-permute-done((bf16[256,1536]{1,0:T(8,128)(2,1)S(1)}, bf16[256,1536]{1,0:T(8,128)(2,1)}, u32[]{:S(2)}, u32[]{:S(2)}) %collective-permute-start.29) | collective-permute-done | bytes 786464 | tf_op jit(solution)/shard_map/ppermute | solution.py:122
  (682 shorter events, 470.5 us)
Async XLA Ops:
  7.2 102.7 %all-gather.5.cloned.1.call-start = ((), (), s32[]{:S(2)}) async-start(), calls=%async_computation.19 | async-start | bytes 5308416 | tf_op jit(solution)/shard_map/all_gather | solution.py:310
  29.9 261.8 %all-gather.7.cloned.1.call-start = ((), (), s32[]{:S(2)}) async-start(), calls=%async_computation.20 | async-start | bytes 5308416 | tf_op jit(solution)/shard_map/all_gather | solution.py:310
  140.1 237.1 %all-gather.9.cloned.1.call-start = ((), (), s32[]{:S(2)}) async-start(), calls=%async_computation.21 | async-start | bytes 5308416 | tf_op jit(solution)/shard_map/all_gather | solution.py:310
  199.4 36.9 %all-to-all-start.1 = ((bf16[96,8,384]{2,0,1:T(8,128)(2,1)}), bf16[96,8,384]{2,0,1:T(8,128)(2,1)S(1)}, u32[]{:S(2)}, u32[]{:S(2)}) async-start(bf16[96,8,384]{2,0,1:T(8,128)(2,1)} %bitcast.297), calls=%async_computation.1 | async-start | bytes 1179648 | tf_op jit(solution)/shard_map/all_to_all | solution.py:319
  287.6 36.5 %all-to-all-start.2 = ((bf16[4,64,1536]{2,1,0:T(8,128)(2,1)}), bf16[4,64,1536]{2,1,0:T(8,128)(2,1)S(1)}, u32[]{:S(2)}, u32[]{:S(2)}) async-start(bf16[4,64,1536]{2,1,0:T(8,128)(2,1)} %bitcast.27), calls=%async_computation.2 | async-start | bytes 1572864 | tf_op jit(solution)/shard_map/all_to_all | solution.py:242
  291.1 95.7 %all-gather.11.cloned.1.call-start = ((), (), s32[]{:S(2)}) async-start(), calls=%async_computation.22 | async-start | bytes 5308416 | tf_op jit(solution)/shard_map/all_gather | solution.py:310
  291.7 214.1 %reduce-scatter.7.cloned.1.call-start = ((), (), s32[]{:S(2)}) async-start(), calls=%async_computation.23 | async-start | bytes 5308416 | tf_op jit(solution)/shard_map/reduce_scatter | solution.py:436
  400.9 109.8 %reduce-scatter.9.cloned.1.call-start = ((), (), s32[]{:S(2)}) async-start(), calls=%async_computation.24 | async-start | bytes 5308416 | tf_op jit(solution)/shard_map/reduce_scatter | solution.py:436
  519.5 28.7 %all-to-all-start.7 = ((bf16[4,64,1536]{2,1,0:T(8,128)(2,1)}), bf16[4,64,1536]{2,1,0:T(8,128)(2,1)S(1)}, u32[]{:S(2)}, u32[]{:S(2)}) async-start(bf16[4,64,1536]{2,1,0:T(8,128)(2,1)} %bitcast.384), calls=%async_computation.9 | async-start | bytes 1572864 | tf_op jit(solution)/shard_map/all_to_all | solution.py:242
  523.0 231.9 %reduce-scatter.17.cloned.1.call-start = ((), (), s32[]{:S(2)}) async-start(), calls=%async_computation.28 | async-start | bytes 1327104 | tf_op jit(solution)/shard_map/reduce_scatter | solution.py:436
  523.8 231.1 %reduce-scatter.15.cloned.1.call-start = ((), (), s32[]{:S(2)}) async-start(), calls=%async_computation.27 | async-start | bytes 1327104 | tf_op jit(solution)/shard_map/reduce_scatter | solution.py:436
  569.1 219.8 %reduce-scatter.13.cloned.1.call-start = ((), (), s32[]{:S(2)}) async-start(), calls=%async_computation.26 | async-start | bytes 3981312 | tf_op jit(solution)/shard_map/reduce_scatter | solution.py:436
  592.0 47.4 %collective-permute-start.21 = (bf16[384,384]{1,0:T(8,128)(2,1)}, bf16[384,384]{1,0:T(8,128)(2,1)}, u32[]{:S(2)}, u32[]{:S(2)}) collective-permute-start(bf16[384,384]{1,0:T(8,128)(2,1)} %get-tuple-element.141), channel_id=1, source_target_pairs={{0,8},{8,0},{16,24},{24,16},{1,9},{9,1},{17,25},{25,17},{2,10},{10... | collective-permute-start | bytes 884744 | tf_op jit(solution)/shard_map/ppermute | solution.py:122
  592.0 47.5 %collective-permute-start.20 = (bf16[384,384]{1,0:T(8,128)(2,1)}, bf16[384,384]{1,0:T(8,128)(2,1)}, u32[]{:S(2)}, u32[]{:S(2)}) collective-permute-start(bf16[384,384]{1,0:T(8,128)(2,1)} %get-tuple-element.142), channel_id=1, source_target_pairs={{0,16},{8,24},{16,0},{24,8},{1,17},{9,25},{17,1},{25,9},{2,18},{10... | collective-permute-start | bytes 884744 | tf_op jit(solution)/shard_map/ppermute | solution.py:122
  594.9 44.6 %collective-permute-start.38 = (bf16[96,1536]{1,0:T(8,128)(2,1)}, bf16[96,1536]{1,0:T(8,128)(2,1)}, u32[]{:S(2)}, u32[]{:S(2)}) collective-permute-start(bf16[96,1536]{1,0:T(8,128)(2,1)} %get-tuple-element.139), channel_id=1, source_target_pairs={{0,8},{8,0},{16,24},{24,16},{1,9},{9,1},{17,25},{25,17},{2,10},{10... | collective-permute-start | bytes 884744 | tf_op jit(solution)/shard_map/ppermute | solution.py:122
  594.9 44.6 %collective-permute-start.37 = (bf16[96,1536]{1,0:T(8,128)(2,1)}, bf16[96,1536]{1,0:T(8,128)(2,1)}, u32[]{:S(2)}, u32[]{:S(2)}) collective-permute-start(bf16[96,1536]{1,0:T(8,128)(2,1)} %get-tuple-element.140), channel_id=1, source_target_pairs={{0,16},{8,24},{16,0},{24,8},{1,17},{9,25},{17,1},{25,9},{2,18},{10... | collective-permute-start | bytes 884744 | tf_op jit(solution)/shard_map/ppermute | solution.py:122
  615.8 115.9 %collective-permute-start.43 = (bf16[192,1536]{1,0:T(8,128)(2,1)}, bf16[192,1536]{1,0:T(8,128)(2,1)}, u32[]{:S(2)}, u32[]{:S(2)}) collective-permute-start(bf16[192,1536]{1,0:T(8,128)(2,1)} %reduce-scatter.7.cloned.1.call-done), channel_id=1, source_target_pairs={{1,16},{17,17},{3,18},{19,19},{5,20},{21,21},{7,22},{23,23},{9,24}... | collective-permute-start | bytes 1769480 | tf_op jit(solution)/shard_map/ppermute | solution.py:189
  641.8 30.7 %collective-permute-start.40 = (bf16[192,1536]{1,0:T(8,128)(2,1)}, bf16[192,1536]{1,0:T(8,128)(2,1)}, u32[]{:S(2)}, u32[]{:S(2)}) collective-permute-start(bf16[192,1536]{1,0:T(8,128)(2,1)} %pad_maximum_fusion.12), channel_id=1, source_target_pairs={{0,16},{8,24},{16,0},{24,8},{1,17},{9,25},{17,1},{25,9},{2,18},{10... | collective-permute-start | bytes 1769480 | tf_op jit(solution)/shard_map/ppermute | solution.py:122
  646.9 30.2 %collective-permute-start.39 = (bf16[192,1536]{1,0:T(8,128)(2,1)}, bf16[192,1536]{1,0:T(8,128)(2,1)}, u32[]{:S(2)}, u32[]{:S(2)}) collective-permute-start(bf16[192,1536]{1,0:T(8,128)(2,1)} %pad_maximum_fusion.11), channel_id=1, source_target_pairs={{0,8},{8,0},{16,24},{24,16},{1,9},{9,1},{17,25},{25,17},{2,10},{10... | collective-permute-start | bytes 1769480 | tf_op jit(solution)/shard_map/ppermute | solution.py:122
  650.6 30.9 %collective-permute-start.23 = (bf16[768,384]{1,0:T(8,128)(2,1)}, bf16[768,384]{1,0:T(8,128)(2,1)}, u32[]{:S(2)}, u32[]{:S(2)}) collective-permute-start(bf16[768,384]{1,0:T(8,128)(2,1)} %pad_maximum_fusion.10), channel_id=1, source_target_pairs={{0,16},{8,24},{16,0},{24,8},{1,17},{9,25},{17,1},{25,9},{2,18},{10... | collective-permute-start | bytes 1769480 | tf_op jit(solution)/shard_map/ppermute | solution.py:122
  652.7 28.8 %collective-permute-start.22 = (bf16[768,384]{1,0:T(8,128)(2,1)}, bf16[768,384]{1,0:T(8,128)(2,1)}, u32[]{:S(2)}, u32[]{:S(2)}) collective-permute-start(bf16[768,384]{1,0:T(8,128)(2,1)} %pad_maximum_fusion.9), channel_id=1, source_target_pairs={{0,8},{8,0},{16,24},{24,16},{1,9},{9,1},{17,25},{25,17},{2,10},{10... | collective-permute-start | bytes 1769480 | tf_op jit(solution)/shard_map/ppermute | solution.py:122
  662.4 126.6 %reduce-scatter.11.cloned.1.call-start = ((), (), s32[]{:S(2)}) async-start(), calls=%async_computation.25 | async-start | bytes 3981312 | tf_op jit(solution)/shard_map/reduce_scatter | solution.py:436
  672.4 59.3 %collective-permute-start.42 = (bf16[192,1536]{1,0:T(8,128)(2,1)}, bf16[192,1536]{1,0:T(8,128)(2,1)}, u32[]{:S(2)}, u32[]{:S(2)}) collective-permute-start(bf16[192,1536]{1,0:T(8,128)(2,1)} %reduce-scatter.7.cloned.1.call-done), channel_id=1, source_target_pairs={{0,16},{16,17},{2,18},{18,19},{4,20},{20,21},{6,22},{22,23},{8,24}... | collective-permute-start | bytes 1769480 | tf_op jit(solution)/shard_map/ppermute | solution.py:189
  680.2 51.5 %collective-permute-start.41 = (bf16[192,1536]{1,0:T(8,128)(2,1)}, bf16[192,1536]{1,0:T(8,128)(2,1)}, u32[]{:S(2)}, u32[]{:S(2)}) collective-permute-start(bf16[192,1536]{1,0:T(8,128)(2,1)} %fusion.78), channel_id=1, source_target_pairs={{16,0},{24,8},{17,1},{25,9},{18,2},{26,10},{19,3},{27,11},{20,4},{... | collective-permute-start | bytes 1769480 | tf_op jit(solution)/shard_map/ppermute | solution.py:131
  (181 other events, 1647.9 us)
Sparse Core Ops, SparseCore 0:
  30.0 65.5 all-gather.4
  97.9 50.5 all-gather.6
  197.0 62.9 all-gather.8
  293.3 58.2 all-gather.10
  386.9 55.4 reduce-scatter.6
  444.5 66.1 reduce-scatter.8
  526.1 35.2 reduce-scatter.16
  569.3 30.2 reduce-scatter.14
  601.8 41.8 reduce-scatter.12
  684.7 44.5 reduce-scatter.10

commit v15 on v14

--- a/solution.py
+++ b/solution.py
@@ -327,18 +327,21 @@
     def in_depth(rows):
         return rows.reshape(-1, 2, dp_count, half_depth).swapaxes(1, 2).reshape(rows.shape)
 
-    def first_ffn(gate):
+    def first_hops(gate):
         down, up = after((down_share, up_turned), gate)
-        down, up = by_distance(down), by_distance(up)
-        return (
-            jnp.concatenate(
-                [
-                    jnp.concatenate(pick(up[0], up[2]), axis=0),
-                    jnp.concatenate(pick(up[1], up[3]), axis=0),
-                ],
-                axis=1,
-            ),
-            jnp.concatenate(pick(down[0], down[2]) + pick(down[1], down[3]), axis=0),
+        return [(rows, swapped(rows, 1), swapped(rows, 2)) for rows in (down, up)]
+
+    def second_hops(hops):
+        out = []
+        for rows, side, ahead in hops:
+            half = rows.shape[0] // 2
+            upper, lower = swapped(side[:half], 2), swapped(ahead[half:], 1)
+            across = jnp.concatenate([upper, lower], axis=0)
+            near, far = pick(rows, ahead), pick(side, across)
+            out.append([jnp.concatenate(pair, axis=0) for pair in (near, far)])
+        down, up = out
+        return lax.optimization_barrier(
+            (jnp.concatenate(up, axis=1), jnp.concatenate(down, axis=0))
         )
 
     span = max(1, dp_count // 8)
@@ -391,7 +394,8 @@
             latent_low = from_slots((unit_in * all_gains[layer, 1]).astype(low))
         projected = matmul(latent_low, qkv_w[layer]).astype(low)
         if layer == 0:
-            up_w[0], down_w[0] = lax.optimization_barrier(first_ffn(projected))
+            media_key[0], up_turned = lax.optimization_barrier((media_key[0], up_turned))
+            hops = first_hops(projected)
         query_low = projected[:, :inner]
         key_heads = split_heads(
             jnp.concatenate([media_key[layer], projected[:, inner : 2 * inner]], axis=0)
@@ -407,7 +411,12 @@
         middle = current + sum_to_slots(matmul(attended_low, out_w[layer]))
         unit_mid, inverse_mid = unit_rows(middle)
         ffn_low = (unit_mid * all_gains[layer, 2]).astype(low)
-        ffn_low = from_slots(ffn_low) if layer else from_sequences(by_depth(ffn_low))
+        if layer:
+            ffn_low = from_slots(ffn_low)
+        else:
+            ffn_low, hops = lax.optimization_barrier((by_depth(ffn_low), hops))
+            up_w[0], down_w[0] = second_hops(hops)
+            ffn_low = from_sequences(ffn_low)
         if layer == 0:
             up_w[1], down_w[1] = second_ffn(ffn_low), down_second
         hidden_pre = matmul(ffn_low, up_w[layer])
@@ -489,7 +498,10 @@
         grad_middle = grad_rows + norm_back(
             unit_mid, inverse_mid, ffn_grad * all_gains[layer, 2]
         )
-        middle_low = from_slots(grad_middle.astype(low))
+        middle_low = grad_middle.astype(low)
+        if layer == 0:
+            middle_low = after(middle_low, (up_grad, down_grad, media_parts[0], latents_out))
+        middle_low = from_slots(middle_low)
         if layer == 0:
             up_half = sum_by_distance(*up_blocks, middle_low).astype(low)
             down_half = sum_by_distance(*down_blocks, middle_low).astype(low)
@@ -503,21 +515,23 @@
         grad_query = grad_query.reshape(-1, inner).astype(low)
         grad_key = grad_key.reshape(-1, inner).astype(low)
         grad_value = grad_value.reshape(-1, inner).astype(low)
+        both_low = jnp.concatenate([media_low[layer], latent_low], axis=0)
+        all_grads = jnp.concatenate(
+            [jnp.pad(grad_query, ((seq_rows, 0), (0, 0))), grad_key, grad_value], axis=1
+        )
+        qkv_grad = matmul_tn(both_low, all_grads).astype(low)
         latent_part = (
             matmul_nt(grad_query, query_w[layer])
             + matmul_nt(grad_key[seq_rows:], key_w[layer])
             + matmul_nt(grad_value[seq_rows:], value_w[layer])
         )
         latent_grad_rows = sum_to_slots(latent_part)
+        if layer:
+            latent_grad_rows = after(latent_grad_rows, qkv_grad)
         gain_latent_grad = jnp.sum(latent_grad_rows * unit_in, axis=0)
         grad_rows = grad_middle + norm_back(
             unit_in, inverse_in, latent_grad_rows * all_gains[layer, 1]
         )
-        both_low = jnp.concatenate([media_low[layer], latent_low], axis=0)
-        all_grads = jnp.concatenate(
-            [jnp.pad(grad_query, ((seq_rows, 0), (0, 0))), grad_key, grad_value], axis=1
-        )
-        qkv_grad = matmul_tn(both_low, all_grads).astype(low)
         if layer == 0:
             up_half, qkv_grad = lax.optimization_barrier((up_half, qkv_grad))
             up_half = lax.all_to_all(up_half, dp, split_axis=0, concat_axis=1, tiled=True)
@@ -531,7 +545,6 @@
             last = last.reshape(latent_rows, section_count, -1).swapaxes(0, 1)
             last = lax.all_to_all(last, "section", split_axis=0, concat_axis=0)
             latents_out = jnp.sum(last.astype(full), axis=0)
-            grad_low = after(grad_low, latents_out)
             grad_low = after(grad_low, ffn_pieces)
         if layer == 0:
             add_media(0, grad_key, grad_value, qkv_grad)
@@ -542,7 +555,7 @@
     own, other = pick(qkv_parts[0], qkv_parts[1])
     lower, upper = pick(own, swapped(other, 2))
     out_grad = join_rows(*[piece[1] for piece in pieces], stride)
-    latent_grad = to_columns(after(grad_rows, (lower, up_half)))
+    latent_grad = to_columns(after(grad_rows, (pieces[1], up_half)))
     media_rows = seq_rows // section_count
     media_sum = sum_over_sections(media_parts[0].astype(full) + media_parts[1])
     own_unit = lax.dynamic_slice_in_dim(media_unit, section * media_rows, media_rows, 0)
@@ -557,7 +570,7 @@
     gain_parts = jnp.sum(
         lax.all_to_all(gain_parts, "section", split_axis=2, concat_axis=2), axis=2
     )
-    gain_parts = after(gain_parts, out_grad).reshape(LAYERS, 3, dp_count, -1)
+    gain_parts = gain_parts.reshape(LAYERS, 3, dp_count, -1)
     gain_grad = jnp.sum(lax.all_to_all(gain_parts, dp, split_axis=2, concat_axis=2), axis=2)
 
     qkv_grads = [

time: 827 us -> 772 us (0.933)
  waiting for transfers between devices: 227 us -> 159 us
  starting transfers between devices: 108 us -> 122 us
  other arithmetic: 92.4 us -> 103 us
  blocking collectives: 148 us -> 138 us
    all_to_all x1, waiting for transfers between devices: 25.5 us -> 0.01 us  [per_device(): lax.all_to_all(up_share, dp, split_axis=1, concat_axis=0, tiled=True)]
    ppermute x3, waiting for transfers between devices: 18.3 us -> 0.01 us  [to_second(): return lax.ppermute(value, 'section', [(0, 2), (1, 3)])]
    ppermute x26, waiting for transfers between devices: 69.7 us -> 51.5 us  [swapped(): return lax.ppermute(value, 'section', pairs)]
    all_to_all x1 -> x0, blocking collectives: 14.7 us -> none  [per_device(): last = lax.all_to_all(last, 'section', split_axis=0, concat_axis=0)]
    all_to_all x2, waiting for transfers between devices: 45 us -> 35.3 us  [sum_to_sequence(): arrived = lax.all_to_all(blocks, 'pair', split_axis=0, concat_axis=0)]
    all_to_all x0 -> x1, waiting for transfers between devices: none -> 9.3 us  [per_device(): last = lax.all_to_all(last, 'section', split_axis=0, concat_axis=0)]
    unnamed x287 -> x208, local copies, waits for them, and re-layouts: 20.7 us -> 19.1 us
  transfers between devices with their start and end apart: 65 -> 66, of which waited for: 36 -> 24; matrix products, arithmetic and copies ran while one was open for 35% -> 39% of each run, Pallas kernels for 0% -> 0%
where the time goes in v15:
time: 772 us; the launch traced here: 761 us
  waiting for transfers between devices  159 us (21%)
  matrix products  140 us (18%)
  blocking collectives  138 us (18%)
  starting transfers between devices  122 us (16%)
  other arithmetic  103 us (13%)
  local copies, waits for them, and re-layouts  83.9 us (11%)
  between operations  16.6 us (2%)
    ppermute x26, waiting for transfers between devices, swapped(): return lax.ppermute(value, 'section', pairs)  51.5 us
    dot_general x17, matrix products, matmul_nt(): lax.dot_general(left, right, (((1,), (1,)), ((), ())), preferred_element_...  51.3 us
    all_gather x2, blocking collectives, from_sequences(): near = lax.all_gather(rows, 'pair', axis=0, tiled=True)  48.2 us
    all_gather x4, blocking collectives, from_slots(): return lax.all_gather(rows, 'section', axis=0, tiled=True)  44.7 us
    dot_general x13, matrix products, matmul(): return jnp.dot(left, right, preferred_element_type=full)  39.2 us
    all_to_all x2, waiting for transfers between devices, sum_to_sequence(): arrived = lax.all_to_all(blocks, 'pair', split_axis=0, concat_axis=0)  35.3 us
    ppermute x26, starting transfers between devices, swapped(): return lax.ppermute(value, 'section', pairs)  33.3 us
    all_gather x3, blocking collectives, per_device(): all_gains = lax.all_gather(all_gains, axis, axis=2, tiled=True)  31.2 us
  transfers between devices with their start and end apart: 66, of which 24 were waited for; matrix products, arithmetic and copies ran while one was open for 39% of the time, Pallas kernels for 0%

profile of v15, /device:TPU:0, one launch (start us, length us, event | category | flops | bytes accessed | tf_op | source)
XLA Modules:
  0.0 761.3 jit_solution(7719994465089616441)
XLA Ops:
  12.6 10.2 %collective-permute-done = bf16[192,1152]{1,0:T(8,128)(2,1)S(1)} collective-permute-done((bf16[192,1152]{1,0:T(8,128)(2,1)S(1)}, bf16[192,1152]{1,0:T(8,128)(2,1)S(1)}, u32[]{:S(2)}, u32[]{:S(2)}) %collective-permute-start) | collective-permute-done | bytes 442400 | tf_op jit(solution)/shard_map/ppermute | solution.py:122
  32.1 10.9 %collective-permute-start.1 = (bf16[96,3072]{1,0:T(8,128)(2,1)}, bf16[96,3072]{1,0:T(8,128)(2,1)}, u32[]{:S(2)}, u32[]{:S(2)}) collective-permute-start(bf16[96,3072]{1,0:T(8,128)(2,1)} %slice_bitcast_fusion.4), channel_id=1, source_target_pairs={{0,16},{8,24},{1,17},{9,25},{2,18},{10,26},{3,19},{11,27},{4,20},{... | collective-permute-start | bytes 1769480 | tf_op jit(solution)/shard_map/ppermute | solution.py:128
  58.0 19.0 %all_gather.40 = f32[2,3,384]{1,0,2:T(2,128)} all-gather(f32[2,3,96]{1,0,2:T(2,128)S(1)} %all_gather.39), channel_id=1, replica_groups=mesh['section'=4,'pair'=4,'core'=2] {'pair'}, dimensions={2}, use_global_device_ids=true | all-gather | bytes 11520 | tf_op jit(solution)/shard_map/all_gather | solution.py:306
  78.2 10.3 %all_gather.41 = f32[2,3,1536]{2,0,1:T(2,128)S(1)} all-gather(f32[2,3,384]{2,0,1:T(2,128)S(1)} %copy.152), channel_id=1, replica_groups=mesh['section'=4,'pair'=4,'core'=2] {'section'}, dimensions={2}, use_global_device_ids=true | all-gather | bytes 46080 | tf_op jit(solution)/shard_map/all_gather | solution.py:306
  107.4 8.0 %collective-permute-done.2 = bf16[192,1536]{1,0:T(8,128)(2,1)} collective-permute-done((bf16[192,1536]{1,0:T(8,128)(2,1)}, bf16[192,1536]{1,0:T(8,128)(2,1)}, u32[]{:S(2)}, u32[]{:S(2)}) %collective-permute-start.2) | collective-permute-done | bytes 589856 | tf_op jit(solution)/shard_map/ppermute | solution.py:177
  153.2 6.9 all-to-all-done.1
  162.3 8.4 %collective-permute-done.8 = bf16[192,1536]{1,0:T(8,128)(2,1)} collective-permute-done((bf16[192,1536]{1,0:T(8,128)(2,1)S(1)}, bf16[192,1536]{1,0:T(8,128)(2,1)}, u32[]{:S(2)}, u32[]{:S(2)}) %collective-permute-start.8) | collective-permute-done | bytes 589856 | tf_op jit(solution)/shard_map/ppermute | solution.py:122
  172.9 9.2 %collective-permute-done.10 = bf16[768,384]{1,0:T(8,128)(2,1)} collective-permute-done((bf16[768,384]{1,0:T(8,128)(2,1)}, bf16[768,384]{1,0:T(8,128)(2,1)}, u32[]{:S(2)}, u32[]{:S(2)}) %collective-permute-start.10) | collective-permute-done | bytes 589856 | tf_op jit(solution)/shard_map/ppermute | solution.py:122
  182.1 19.9 %all_gather.43 = bf16[256,1536]{1,0:T(8,128)(2,1)S(1)} all-gather(bf16[64,1536]{1,0:T(8,128)(2,1)S(1)} %reshape.734), channel_id=1, replica_groups=mesh['section'=4,'pair'=4,'core'=2] {'pair'}, dimensions={0}, use_global_device_ids=true | all-gather | bytes 983040 | tf_op jit(solution)/shard_map/all_gather | solution.py:234
  214.2 15.9 %collective-permute-done.17 = bf16[192,1536]{1,0:T(8,128)(2,1)S(1)} collective-permute-done((bf16[192,1536]{1,0:T(8,128)(2,1)S(1)}, bf16[192,1536]{1,0:T(8,128)(2,1)S(1)}, u32[]{:S(2)}, u32[]{:S(2)}) %collective-permute-start.17) | collective-permute-done | bytes 589856 | tf_op jit(solution)/shard_map/ppermute | solution.py:131
  241.6 6.9 collective-permute-done.12
  278.3 17.2 %all-to-all-done.2 = bf16[4,64,1536]{2,1,0:T(8,128)(2,1)S(1)} async-done(((bf16[4,64,1536]{2,1,0:T(8,128)(2,1)}), bf16[4,64,1536]{2,1,0:T(8,128)(2,1)S(1)}, u32[]{:S(2)}, u32[]{:S(2)}) %all-to-all-start.2) | async-done | bytes 786464 | tf_op jit(solution)/shard_map/all_to_all | solution.py:242
  296.1 11.2 %all_gather.45 = bf16[256,1536]{1,0:T(8,128)(2,1)S(1)} all-gather(bf16[64,1536]{1,0:T(8,128)(2,1)S(1)} %multiply_convert_fusion.9), channel_id=1, replica_groups=mesh['section'=4,'pair'=4,'core'=2] {'section'}, dimensions={0}, use_global_device_ids=true | all-gather | bytes 983040 | tf_op jit(solution)/shard_map/all_gather | solution.py:225
  322.9 13.4 %all_to_all.101 = bf16[4,64,1536]{2,1,0:T(8,128)(2,1)S(1)} all-to-all(bf16[4,64,1536]{2,1,0:T(8,128)(2,1)S(1)} %bitcast.355), channel_id=1, replica_groups=mesh['section'=4,'pair'=4,'core'=2] {'section'}, dimensions={0} | all-to-all | bytes 1572864 | tf_op jit(solution)/shard_map/all_to_all | solution.py:221
  337.0 12.2 %all_gather.46 = bf16[256,1536]{1,0:T(8,128)(2,1)} all-gather(bf16[64,1536]{1,0:T(8,128)(2,1)S(1)} %multiply_convert_fusion.8), channel_id=1, replica_groups=mesh['section'=4,'pair'=4,'core'=2] {'section'}, dimensions={0}, use_global_device_ids=true | all-gather | bytes 983040 | tf_op jit(solution)/shard_map/all_gather | solution.py:225
  389.7 11.0 %all_gather.49 = bf16[256,1536]{1,0:T(8,128)(2,1)S(1)} all-gather(bf16[64,1536]{1,0:T(8,128)(2,1)S(1)} %get-tuple-element.116), channel_id=1, replica_groups=mesh['section'=4,'pair'=4,'core'=2] {'section'}, dimensions={0}, use_global_device_ids=true | all-gather | bytes 983040 | tf_op jit(solution)/shard_map/all_gather | solution.py:225
  424.4 9.3 %convolution_convert_fusion.2 = bf16[1536,1152]{1,0:T(8,128)(2,1)} fusion(bf16[256,1536]{1,0:T(8,128)(2,1)} %copy-done.68, bf16[1024,1536]{1,0:T(8,128)(2,1)} %get-tuple-element.134, bf16[256,384]{0,1:T(8,128)(2,1)S(1)} %bitcast.385, bf16[1280,384]{0,1:T(8,128)(2,1)S(1)} %bitcast.338, bf16[1280,384]{0,1:T(8,128)(2,1)S(1)} %bitcast.349), kind=kOutput, calls=%fused_computation.4 | convolution fusion | flops 4551278592 | bytes 9633792 | tf_op jit(solution)/shard_map/dot_general | solution.py:48
  436.3 28.3 %all_gather.50 = bf16[256,1536]{1,0:T(8,128)(2,1)} all-gather(bf16[64,1536]{1,0:T(8,128)(2,1)S(1)} %get-tuple-element.114), channel_id=1, replica_groups=mesh['section'=4,'pair'=4,'core'=2] {'pair'}, dimensions={0}, use_global_device_ids=true | all-gather | bytes 983040 | tf_op jit(solution)/shard_map/all_gather | solution.py:234
  476.3 9.3 %all-to-all-done.5 = bf16[4,256,384]{2,1,0:T(8,128)(2,1)} async-done(((bf16[4,256,384]{2,1,0:T(8,128)(2,1)}), bf16[4,256,384]{2,1,0:T(8,128)(2,1)}, u32[]{:S(2)}, u32[]{:S(2)}) %all-to-all-start.5) | async-done | bytes 786464 | tf_op jit(solution)/shard_map/all_to_all | solution.py:546
  539.0 18.2 %all-to-all-done.7 = bf16[4,64,1536]{2,1,0:T(8,128)(2,1)} async-done(((bf16[4,64,1536]{2,1,0:T(8,128)(2,1)}), bf16[4,64,1536]{2,1,0:T(8,128)(2,1)}, u32[]{:S(2)}, u32[]{:S(2)}) %all-to-all-start.7) | async-done | bytes 786464 | tf_op jit(solution)/shard_map/all_to_all | solution.py:242
  561.4 10.3 %all_gather.51 = bf16[256,1536]{1,0:T(8,128)(2,1)S(1)} all-gather(bf16[64,1536]{1,0:T(8,128)(2,1)S(1)} %get-tuple-element.77), channel_id=1, replica_groups=mesh['section'=4,'pair'=4,'core'=2] {'section'}, dimensions={0}, use_global_device_ids=true | all-gather | bytes 983040 | tf_op jit(solution)/shard_map/all_gather | solution.py:225
  610.7 9.6 %convolution_convert_fusion = bf16[1536,1152]{1,0:T(8,128)(2,1)} fusion(bf16[256,1536]{1,0:T(8,128)(2,1)S(1)} %copy-done.67, bf16[1024,1536]{1,0:T(8,128)(2,1)} %get-tuple-element.51, bf16[256,384]{0,1:T(8,128)(2,1)S(1)} %bitcast.387, bf16[1280,384]{0,1:T(8,128)(2,1)} %bitcast.342, bf16[1280,384]{0,1:T(8,128)(2,1)} %bitcast.352), kind=kOutput, calls=%fused_computation.2 | convolution fusion | flops 4551278592 | bytes 9633792 | tf_op jit(solution)/shard_map/dot_general | solution.py:48
  637.7 8.8 %multiply_reduce_fusion.1 = (f32[1536]{0:T(1024)S(1)}, f32[1536]{0:T(1024)S(1)}, f32[1024,1536]{1,0:T(8,128)}, f32[1024,1536]{1,0:T(8,128)}) fusion(bf16[1024,1536]{1,0:T(8,128)(2,1)S(1)} %copy-done.3, f32[1024]{0:T(1024)S(1)} %copy-done.83, f32[1024]{0:T(1024)S(1)} %copy-done.82, f32[1024,1536]{1,0:T(8,128)} %get-tuple-element.208, ...), kind=kOutput, calls=%fused_computation.10 | convolution fusion | flops 1225257984 | bytes 33449984 | tf_op jit(solution)/shard_map/dot_general | solution.py:44
  684.0 7.7 %all-to-all-done.9 = bf16[8,96,384]{2,1,0:T(8,128)(2,1)S(1)} async-done(((bf16[8,96,384]{2,1,0:T(8,128)(2,1)}), bf16[8,96,384]{2,1,0:T(8,128)(2,1)S(1)}, u32[]{:S(2)}, u32[]{:S(2)}) %all-to-all-start.9) | async-done | bytes 589856 | tf_op jit(solution)/shard_map/all_to_all | solution.py:537
  (602 shorter events, 452.6 us)
Async XLA Ops:
  7.2 110.4 %all-gather.5.cloned.1.call-start = ((), (), s32[]{:S(2)}) async-start(), calls=%async_computation.19 | async-start | bytes 5308416 | tf_op jit(solution)/shard_map/all_gather | solution.py:310
  53.0 95.0 %collective-permute-start.6 = (bf16[192,1536]{1,0:T(8,128)(2,1)}, bf16[192,1536]{1,0:T(8,128)(2,1)}, u32[]{:S(2)}, u32[]{:S(2)}) collective-permute-start(bf16[192,1536]{1,0:T(8,128)(2,1)} %get-tuple-element.55), channel_id=1, source_target_pairs={{0,16},{8,24},{1,17},{9,25},{2,18},{10,26},{3,19},{11,27},{4,20},{... | collective-permute-start | bytes 1769480 | tf_op jit(solution)/shard_map/ppermute | solution.py:128
  90.4 37.2 %all-to-all-start = ((bf16[96,8,384]{2,0,1:T(8,128)(2,1)}), bf16[96,8,384]{2,0,1:T(8,128)(2,1)}, u32[]{:S(2)}, u32[]{:S(2)}) async-start(bf16[96,8,384]{2,0,1:T(8,128)(2,1)} %bitcast.360), calls=%async_computation | async-start | bytes 1179648 | tf_op jit(solution)/shard_map/all_to_all | solution.py:319
  94.6 171.8 %all-gather.7.cloned.1.call-start = ((), (), s32[]{:S(2)}) async-start(), calls=%async_computation.20 | async-start | bytes 5308416 | tf_op jit(solution)/shard_map/all_gather | solution.py:310
  147.9 201.3 %all-gather.9.cloned.1.call-start = ((), (), s32[]{:S(2)}) async-start(), calls=%async_computation.21 | async-start | bytes 5308416 | tf_op jit(solution)/shard_map/all_gather | solution.py:310
  262.1 33.4 %all-to-all-start.2 = ((bf16[4,64,1536]{2,1,0:T(8,128)(2,1)}), bf16[4,64,1536]{2,1,0:T(8,128)(2,1)S(1)}, u32[]{:S(2)}, u32[]{:S(2)}) async-start(bf16[4,64,1536]{2,1,0:T(8,128)(2,1)} %bitcast.380), calls=%async_computation.2 | async-start | bytes 1572864 | tf_op jit(solution)/shard_map/all_to_all | solution.py:242
  265.6 93.8 %all-gather.11.cloned.1.call-start = ((), (), s32[]{:S(2)}) async-start(), calls=%async_computation.22 | async-start | bytes 5308416 | tf_op jit(solution)/shard_map/all_gather | solution.py:310
  266.2 223.0 %reduce-scatter.7.cloned.1.call-start = ((), (), s32[]{:S(2)}) async-start(), calls=%async_computation.23 | async-start | bytes 5308416 | tf_op jit(solution)/shard_map/reduce_scatter | solution.py:445
  358.9 130.3 %reduce-scatter.9.cloned.1.call-start = ((), (), s32[]{:S(2)}) async-start(), calls=%async_computation.24 | async-start | bytes 5308416 | tf_op jit(solution)/shard_map/reduce_scatter | solution.py:445
  378.1 317.2 %reduce-scatter.13.cloned.1.call-start = ((), (), s32[]{:S(2)}) async-start(), calls=%async_computation.26 | async-start | bytes 1327104 | tf_op jit(solution)/shard_map/reduce_scatter | solution.py:445
  473.6 221.6 %reduce-scatter.11.cloned.1.call-start = ((), (), s32[]{:S(2)}) async-start(), calls=%async_computation.25 | async-start | bytes 3981312 | tf_op jit(solution)/shard_map/reduce_scatter | solution.py:445
  501.5 84.5 %collective-permute-start.21 = (bf16[384,384]{1,0:T(8,128)(2,1)}, bf16[384,384]{1,0:T(8,128)(2,1)}, u32[]{:S(2)}, u32[]{:S(2)}) collective-permute-start(bf16[384,384]{1,0:T(8,128)(2,1)} %get-tuple-element.161), channel_id=1, source_target_pairs={{0,8},{8,0},{16,24},{24,16},{1,9},{9,1},{17,25},{25,17},{2,10},{10... | collective-permute-start | bytes 884744 | tf_op jit(solution)/shard_map/ppermute | solution.py:122
  502.9 83.1 %collective-permute-start.20 = (bf16[384,384]{1,0:T(8,128)(2,1)}, bf16[384,384]{1,0:T(8,128)(2,1)}, u32[]{:S(2)}, u32[]{:S(2)}) collective-permute-start(bf16[384,384]{1,0:T(8,128)(2,1)} %get-tuple-element.162), channel_id=1, source_target_pairs={{0,16},{8,24},{16,0},{24,8},{1,17},{9,25},{17,1},{25,9},{2,18},{10... | collective-permute-start | bytes 884744 | tf_op jit(solution)/shard_map/ppermute | solution.py:122
  504.3 81.7 %collective-permute-start.38 = (bf16[96,1536]{1,0:T(8,128)(2,1)}, bf16[96,1536]{1,0:T(8,128)(2,1)}, u32[]{:S(2)}, u32[]{:S(2)}) collective-permute-start(bf16[96,1536]{1,0:T(8,128)(2,1)} %get-tuple-element.159), channel_id=1, source_target_pairs={{0,8},{8,0},{16,24},{24,16},{1,9},{9,1},{17,25},{25,17},{2,10},{10... | collective-permute-start | bytes 884744 | tf_op jit(solution)/shard_map/ppermute | solution.py:122
  505.9 80.1 %collective-permute-start.37 = (bf16[96,1536]{1,0:T(8,128)(2,1)}, bf16[96,1536]{1,0:T(8,128)(2,1)}, u32[]{:S(2)}, u32[]{:S(2)}) collective-permute-start(bf16[96,1536]{1,0:T(8,128)(2,1)} %get-tuple-element.160), channel_id=1, source_target_pairs={{0,16},{8,24},{16,0},{24,8},{1,17},{9,25},{17,1},{25,9},{2,18},{10... | collective-permute-start | bytes 884744 | tf_op jit(solution)/shard_map/ppermute | solution.py:122
  519.8 37.4 %all-to-all-start.7 = ((bf16[4,64,1536]{2,1,0:T(8,128)(2,1)}), bf16[4,64,1536]{2,1,0:T(8,128)(2,1)}, u32[]{:S(2)}, u32[]{:S(2)}) async-start(bf16[4,64,1536]{2,1,0:T(8,128)(2,1)} %bitcast.59), calls=%async_computation.9 | async-start | bytes 1572864 | tf_op jit(solution)/shard_map/all_to_all | solution.py:242
  524.0 191.1 %reduce-scatter.17.cloned.1.call-start = ((), (), s32[]{:S(2)}) async-start(), calls=%async_computation.28 | async-start | bytes 1327104 | tf_op jit(solution)/shard_map/reduce_scatter | solution.py:445
  531.9 148.7 %collective-permute-start.43 = (bf16[192,1536]{1,0:T(8,128)(2,1)}, bf16[192,1536]{1,0:T(8,128)(2,1)}, u32[]{:S(2)}, u32[]{:S(2)}) collective-permute-start(bf16[192,1536]{1,0:T(8,128)(2,1)} %reduce-scatter.7.cloned.1.call-done), channel_id=1, source_target_pairs={{1,16},{17,17},{3,18},{19,19},{5,20},{21,21},{7,22},{23,23},{9,24}... | collective-permute-start | bytes 1769480 | tf_op jit(solution)/shard_map/ppermute | solution.py:189
  588.2 41.4 %collective-permute-start.23 = (bf16[768,384]{1,0:T(8,128)(2,1)}, bf16[768,384]{1,0:T(8,128)(2,1)}, u32[]{:S(2)}, u32[]{:S(2)}) collective-permute-start(bf16[768,384]{1,0:T(8,128)(2,1)} %pad_maximum_fusion.10), channel_id=1, source_target_pairs={{0,16},{8,24},{16,0},{24,8},{1,17},{9,25},{17,1},{25,9},{2,18},{10... | collective-permute-start | bytes 1769480 | tf_op jit(solution)/shard_map/ppermute | solution.py:122
  592.8 36.9 %collective-permute-start.22 = (bf16[768,384]{1,0:T(8,128)(2,1)}, bf16[768,384]{1,0:T(8,128)(2,1)}, u32[]{:S(2)}, u32[]{:S(2)}) collective-permute-start(bf16[768,384]{1,0:T(8,128)(2,1)} %pad_maximum_fusion.9), channel_id=1, source_target_pairs={{0,8},{8,0},{16,24},{24,16},{1,9},{9,1},{17,25},{25,17},{2,10},{10... | collective-permute-start | bytes 1769480 | tf_op jit(solution)/shard_map/ppermute | solution.py:122
  610.7 131.5 %reduce-scatter.15.cloned.1.call-start = ((), (), s32[]{:S(2)}) async-start(), calls=%async_computation.27 | async-start | bytes 3981312 | tf_op jit(solution)/shard_map/reduce_scatter | solution.py:445
  620.3 60.3 %collective-permute-start.42 = (bf16[192,1536]{1,0:T(8,128)(2,1)}, bf16[192,1536]{1,0:T(8,128)(2,1)}, u32[]{:S(2)}, u32[]{:S(2)}) collective-permute-start(bf16[192,1536]{1,0:T(8,128)(2,1)} %reduce-scatter.7.cloned.1.call-done), channel_id=1, source_target_pairs={{0,16},{16,17},{2,18},{18,19},{4,20},{20,21},{6,22},{22,23},{8,24}... | collective-permute-start | bytes 1769480 | tf_op jit(solution)/shard_map/ppermute | solution.py:189
  628.3 52.3 %collective-permute-start.41 = (bf16[192,1536]{1,0:T(8,128)(2,1)}, bf16[192,1536]{1,0:T(8,128)(2,1)}, u32[]{:S(2)}, u32[]{:S(2)}) collective-permute-start(bf16[192,1536]{1,0:T(8,128)(2,1)} %fusion.78), channel_id=1, source_target_pairs={{16,0},{24,8},{17,1},{25,9},{18,2},{26,10},{19,3},{27,11},{20,4},{... | collective-permute-start | bytes 1769480 | tf_op jit(solution)/shard_map/ppermute | solution.py:131
  669.2 31.4 %collective-permute-start.27 = (bf16[256,1536]{1,0:T(8,128)(2,1)}, bf16[256,1536]{1,0:T(8,128)(2,1)}, u32[]{:S(2)}, u32[]{:S(2)}) collective-permute-start(bf16[256,1536]{1,0:T(8,128)(2,1)} %pad_maximum_fusion.8), channel_id=1, source_target_pairs={{0,16},{8,24},{16,0},{24,8},{1,17},{9,25},{17,1},{25,9},{2,18},{10... | collective-permute-start | bytes 2359304 | tf_op jit(solution)/shard_map/ppermute | solution.py:122
  (143 other events, 1432.6 us)
Sparse Core Ops, SparseCore 0:
  30.0 65.5 all-gather.4
  102.0 57.1 all-gather.6
  231.0 58.1 all-gather.8
  290.7 55.6 all-gather.10
  359.0 52.1 reduce-scatter.6
  413.4 65.9 reduce-scatter.8
  481.7 30.9 reduce-scatter.12
  515.0 54.5 reduce-scatter.10
  599.9 31.6 reduce-scatter.16
  633.8 44.5 reduce-scatter.14

commit v16 on v14

--- a/solution.py
+++ b/solution.py
@@ -372,8 +372,6 @@
     media_value = []
     for layer in range(LAYERS):
         media_low.append((media_unit * all_gains[layer, 0]).astype(low))
-        if layer == 0:
-            media_low[0], down_piece = lax.optimization_barrier((media_low[0], down_piece))
         media_key.append(matmul(media_low[layer], key_w[layer]).astype(low))
         media_value.append(matmul(media_low[layer], value_w[layer]).astype(low))
 
@@ -392,6 +390,7 @@
         projected = matmul(latent_low, qkv_w[layer]).astype(low)
         if layer == 0:
             up_w[0], down_w[0] = lax.optimization_barrier(first_ffn(projected))
+            up_w[1], down_w[1] = second_ffn(projected), down_second
         query_low = projected[:, :inner]
         key_heads = split_heads(
             jnp.concatenate([media_key[layer], projected[:, inner : 2 * inner]], axis=0)
@@ -408,8 +407,6 @@
         unit_mid, inverse_mid = unit_rows(middle)
         ffn_low = (unit_mid * all_gains[layer, 2]).astype(low)
         ffn_low = from_slots(ffn_low) if layer else from_sequences(by_depth(ffn_low))
-        if layer == 0:
-            up_w[1], down_w[1] = second_ffn(ffn_low), down_second
         hidden_pre = matmul(ffn_low, up_w[layer])
         active_low = gelu_exact(hidden_pre).astype(low)
         if layer == 0:
@@ -503,21 +500,23 @@
         grad_query = grad_query.reshape(-1, inner).astype(low)
         grad_key = grad_key.reshape(-1, inner).astype(low)
         grad_value = grad_value.reshape(-1, inner).astype(low)
+        both_low = jnp.concatenate([media_low[layer], latent_low], axis=0)
+        all_grads = jnp.concatenate(
+            [jnp.pad(grad_query, ((seq_rows, 0), (0, 0))), grad_key, grad_value], axis=1
+        )
+        qkv_grad = matmul_tn(both_low, all_grads).astype(low)
         latent_part = (
             matmul_nt(grad_query, query_w[layer])
             + matmul_nt(grad_key[seq_rows:], key_w[layer])
             + matmul_nt(grad_value[seq_rows:], value_w[layer])
         )
         latent_grad_rows = sum_to_slots(latent_part)
+        if layer:
+            latent_grad_rows = after(latent_grad_rows, qkv_grad)
         gain_latent_grad = jnp.sum(latent_grad_rows * unit_in, axis=0)
         grad_rows = grad_middle + norm_back(
             unit_in, inverse_in, latent_grad_rows * all_gains[layer, 1]
         )
-        both_low = jnp.concatenate([media_low[layer], latent_low], axis=0)
-        all_grads = jnp.concatenate(
-            [jnp.pad(grad_query, ((seq_rows, 0), (0, 0))), grad_key, grad_value], axis=1
-        )
-        qkv_grad = matmul_tn(both_low, all_grads).astype(low)
         if layer == 0:
             up_half, qkv_grad = lax.optimization_barrier((up_half, qkv_grad))
             up_half = lax.all_to_all(up_half, dp, split_axis=0, concat_axis=1, tiled=True)
@@ -538,11 +537,8 @@
         else:
             media_grads = (grad_key, grad_value)
         gain_rows[layer] = (gain_latent_grad, gain_ffn_grad)
-    qkv_parts = [piece[0] for piece in pieces]
-    own, other = pick(qkv_parts[0], qkv_parts[1])
-    lower, upper = pick(own, swapped(other, 2))
     out_grad = join_rows(*[piece[1] for piece in pieces], stride)
-    latent_grad = to_columns(after(grad_rows, (lower, up_half)))
+    latent_grad = to_columns(after(grad_rows, (pieces[1], up_half)))
     media_rows = seq_rows // section_count
     media_sum = sum_over_sections(media_parts[0].astype(full) + media_parts[1])
     own_unit = lax.dynamic_slice_in_dim(media_unit, section * media_rows, media_rows, 0)
@@ -557,9 +553,12 @@
     gain_parts = jnp.sum(
         lax.all_to_all(gain_parts, "section", split_axis=2, concat_axis=2), axis=2
     )
-    gain_parts = after(gain_parts, out_grad).reshape(LAYERS, 3, dp_count, -1)
+    gain_parts = gain_parts.reshape(LAYERS, 3, dp_count, -1)
     gain_grad = jnp.sum(lax.all_to_all(gain_parts, dp, split_axis=2, concat_axis=2), axis=2)
 
+    qkv_parts = [piece[0] for piece in pieces]
+    own, other = pick(qkv_parts[0], qkv_parts[1])
+    lower, upper = pick(own, swapped(other, 2))
     qkv_grads = [
         jnp.concatenate(
             [lower[:, i * inner : (i + 1) * inner], upper[:, i * inner : (i + 1) * inner]], axis=1

time: 827 us -> 718 us (0.87)
  waiting for transfers between devices: 227 us -> 84.7 us
  starting transfers between devices: 108 us -> 124 us
  blocking collectives: 148 us -> 159 us
    all_to_all x2, waiting for transfers between devices: 45 us -> 0.35 us  [sum_to_sequence(): arrived = lax.all_to_all(blocks, 'pair', split_axis=0, concat_axis=0)]
    ppermute x26, waiting for transfers between devices: 69.7 us -> 28.4 us  [swapped(): return lax.ppermute(value, 'section', pairs)]
    all_to_all x1, waiting for transfers between devices: 25.5 us -> 2.63 us  [per_device(): lax.all_to_all(up_share, dp, split_axis=1, concat_axis=0, tiled=True)]
    ppermute x3, waiting for transfers between devices: 16.4 us -> 0.01 us  [to_first(): return lax.ppermute(value, 'section', [(2, 0), (3, 1)])]
    all_to_all x1 -> x0, blocking collectives: 14.7 us -> none  [per_device(): last = lax.all_to_all(last, 'section', split_axis=0, concat_axis=0)]
    all_gather x2, blocking collectives: 45.1 us -> 57.4 us  [from_sequences(): near = lax.all_gather(rows, 'pair', axis=0, tiled=True)]
    all_gather x4, blocking collectives: 45 us -> 56.9 us  [from_slots(): return lax.all_gather(rows, 'section', axis=0, tiled=True)]
    ppermute x3, waiting for transfers between devices: 18.3 us -> 6.87 us  [to_second(): return lax.ppermute(value, 'section', [(0, 2), (1, 3)])]
  transfers between devices with their start and end apart: 65 -> 66, of which waited for: 36 -> 20; matrix products, arithmetic and copies ran while one was open for 35% -> 42% of each run, Pallas kernels for 0% -> 0%
where the time goes in v16:
time: 718 us; the launch traced here: 708 us
  blocking collectives  159 us (22%)
  matrix products  140 us (19%)
  starting transfers between devices  124 us (17%)
  other arithmetic  98.3 us (14%)
  local copies, waits for them, and re-layouts  85 us (12%)
  waiting for transfers between devices  84.7 us (12%)
  between operations  16.6 us (2%)
    all_gather x2, blocking collectives, from_sequences(): near = lax.all_gather(rows, 'pair', axis=0, tiled=True)  57.4 us
    all_gather x4, blocking collectives, from_slots(): return lax.all_gather(rows, 'section', axis=0, tiled=True)  56.9 us
    dot_general x17, matrix products, matmul_nt(): lax.dot_general(left, right, (((1,), (1,)), ((), ())), preferred_element_...  47.1 us
    dot_general x13, matrix products, matmul(): return jnp.dot(left, right, preferred_element_type=full)  40.5 us
    ppermute x26, starting transfers between devices, swapped(): return lax.ppermute(value, 'section', pairs)  33.9 us
    all_gather x3, blocking collectives, per_device(): all_gains = lax.all_gather(all_gains, axis, axis=2, tiled=True)  31.6 us
    dot_general x8, matrix products, matmul_tn(): lax.dot_general(left, right, (((0,), (0,)), ((), ())), preferred_element_...  29.7 us
    ppermute x26, waiting for transfers between devices, swapped(): return lax.ppermute(value, 'section', pairs)  28.4 us
  transfers between devices with their start and end apart: 66, of which 20 were waited for; matrix products, arithmetic and copies ran while one was open for 42% of the time, Pallas kernels for 0%

profile of v16, /device:TPU:0, one launch (start us, length us, event | category | flops | bytes accessed | tf_op | source)
XLA Modules:
  0.0 707.7 jit_solution(2838467736299598851)
XLA Ops:
  12.6 10.2 %collective-permute-done = bf16[192,1152]{1,0:T(8,128)(2,1)S(1)} collective-permute-done((bf16[192,1152]{1,0:T(8,128)(2,1)S(1)}, bf16[192,1152]{1,0:T(8,128)(2,1)S(1)}, u32[]{:S(2)}, u32[]{:S(2)}) %collective-permute-start) | collective-permute-done | bytes 442400 | tf_op jit(solution)/shard_map/ppermute | solution.py:122
  31.9 10.9 %collective-permute-start.1 = (bf16[96,3072]{1,0:T(8,128)(2,1)}, bf16[96,3072]{1,0:T(8,128)(2,1)}, u32[]{:S(2)}, u32[]{:S(2)}) collective-permute-start(bf16[96,3072]{1,0:T(8,128)(2,1)} %slice_bitcast_fusion.4), channel_id=1, source_target_pairs={{0,16},{8,24},{1,17},{9,25},{2,18},{10,26},{3,19},{11,27},{4,20},{... | collective-permute-start | bytes 1769480 | tf_op jit(solution)/shard_map/ppermute | solution.py:128
  58.9 19.0 %all_gather.40 = f32[2,3,384]{1,0,2:T(2,128)} all-gather(f32[2,3,96]{1,0,2:T(2,128)S(1)} %all_gather.39), channel_id=1, replica_groups=mesh['section'=4,'pair'=4,'core'=2] {'pair'}, dimensions={2}, use_global_device_ids=true | all-gather | bytes 11520 | tf_op jit(solution)/shard_map/all_gather | solution.py:306
  85.2 10.7 %all_gather.41 = f32[2,3,1536]{2,0,1:T(2,128)S(1)} all-gather(f32[2,3,384]{2,0,1:T(2,128)S(1)} %copy.152), channel_id=1, replica_groups=mesh['section'=4,'pair'=4,'core'=2] {'section'}, dimensions={2}, use_global_device_ids=true | all-gather | bytes 46080 | tf_op jit(solution)/shard_map/all_gather | solution.py:306
  112.2 6.3 slice_reduce_fusion
  161.7 28.0 %all_gather.43 = bf16[256,1536]{1,0:T(8,128)(2,1)S(1)} all-gather(bf16[64,1536]{1,0:T(8,128)(2,1)S(1)} %reshape.734), channel_id=1, replica_groups=mesh['section'=4,'pair'=4,'core'=2] {'pair'}, dimensions={0}, use_global_device_ids=true | all-gather | bytes 983040 | tf_op jit(solution)/shard_map/all_gather | solution.py:234
  196.9 6.0 collective-permute-done.13
  221.8 8.2 %collective-permute-done.16 = bf16[192,1536]{1,0:T(8,128)(2,1)} collective-permute-done((bf16[192,1536]{1,0:T(8,128)(2,1)}, bf16[192,1536]{1,0:T(8,128)(2,1)}, u32[]{:S(2)}, u32[]{:S(2)}) %collective-permute-start.16) | collective-permute-done | bytes 589856 | tf_op jit(solution)/shard_map/ppermute | solution.py:177
  232.1 5.0 convolution_convert_fusion.13
  245.0 21.4 %all_gather.45 = bf16[256,1536]{1,0:T(8,128)(2,1)S(1)} all-gather(bf16[64,1536]{1,0:T(8,128)(2,1)S(1)} %multiply_convert_fusion.9), channel_id=1, replica_groups=mesh['section'=4,'pair'=4,'core'=2] {'section'}, dimensions={0}, use_global_device_ids=true | all-gather | bytes 983040 | tf_op jit(solution)/shard_map/all_gather | solution.py:225
  281.8 13.5 %all_to_all.101 = bf16[4,64,1536]{2,1,0:T(8,128)(2,1)S(1)} all-to-all(bf16[4,64,1536]{2,1,0:T(8,128)(2,1)S(1)} %bitcast.358), channel_id=1, replica_groups=mesh['section'=4,'pair'=4,'core'=2] {'section'}, dimensions={0} | all-to-all | bytes 1572864 | tf_op jit(solution)/shard_map/all_to_all | solution.py:221
  296.0 12.0 %all_gather.46 = bf16[256,1536]{1,0:T(8,128)(2,1)} all-gather(bf16[64,1536]{1,0:T(8,128)(2,1)S(1)} %multiply_convert_fusion.8), channel_id=1, replica_groups=mesh['section'=4,'pair'=4,'core'=2] {'section'}, dimensions={0}, use_global_device_ids=true | all-gather | bytes 983040 | tf_op jit(solution)/shard_map/all_gather | solution.py:225
  308.0 5.2 multiply_convert_fusion.6
  338.0 6.6 all-to-all-done.4
  348.1 11.0 %all_gather.49 = bf16[256,1536]{1,0:T(8,128)(2,1)S(1)} all-gather(bf16[64,1536]{1,0:T(8,128)(2,1)S(1)} %get-tuple-element.94), channel_id=1, replica_groups=mesh['section'=4,'pair'=4,'core'=2] {'section'}, dimensions={0}, use_global_device_ids=true | all-gather | bytes 983040 | tf_op jit(solution)/shard_map/all_gather | solution.py:225
  382.7 9.3 %convolution_convert_fusion.2 = bf16[1536,1152]{1,0:T(8,128)(2,1)} fusion(bf16[256,1536]{1,0:T(8,128)(2,1)} %copy-done.68, bf16[1024,1536]{1,0:T(8,128)(2,1)} %get-tuple-element.112, bf16[256,384]{0,1:T(8,128)(2,1)S(1)} %bitcast.390, bf16[1280,384]{0,1:T(8,128)(2,1)S(1)} %bitcast.340, bf16[1280,384]{0,1:T(8,128)(2,1)S(1)} %bitcast.351), kind=kOutput, calls=%fused_computation.4 | convolution fusion | flops 4551278592 | bytes 9633792 | tf_op jit(solution)/shard_map/dot_general | solution.py:48
  394.6 29.4 %all_gather.50 = bf16[256,1536]{1,0:T(8,128)(2,1)} all-gather(bf16[64,1536]{1,0:T(8,128)(2,1)S(1)} %get-tuple-element.92), channel_id=1, replica_groups=mesh['section'=4,'pair'=4,'core'=2] {'pair'}, dimensions={0}, use_global_device_ids=true | all-gather | bytes 983040 | tf_op jit(solution)/shard_map/all_gather | solution.py:234
  435.8 9.3 %all-to-all-done.5 = bf16[4,256,384]{2,1,0:T(8,128)(2,1)} async-done(((bf16[4,256,384]{2,1,0:T(8,128)(2,1)}), bf16[4,256,384]{2,1,0:T(8,128)(2,1)}, u32[]{:S(2)}, u32[]{:S(2)}) %all-to-all-start.5) | async-done | bytes 786464 | tf_op jit(solution)/shard_map/all_to_all | solution.py:531
  506.1 12.5 %all_gather.51 = bf16[256,1536]{1,0:T(8,128)(2,1)S(1)} all-gather(bf16[64,1536]{1,0:T(8,128)(2,1)S(1)} %get-tuple-element.90), channel_id=1, replica_groups=mesh['section'=4,'pair'=4,'core'=2] {'section'}, dimensions={0}, use_global_device_ids=true | all-gather | bytes 983040 | tf_op jit(solution)/shard_map/all_gather | solution.py:225
  556.0 9.5 %convolution_convert_fusion = bf16[1536,1152]{1,0:T(8,128)(2,1)} fusion(bf16[256,1536]{1,0:T(8,128)(2,1)} %copy-done.67, bf16[1024,1536]{1,0:T(8,128)(2,1)} %get-tuple-element.113, bf16[256,384]{0,1:T(8,128)(2,1)S(1)} %bitcast.388, bf16[1280,384]{0,1:T(8,128)(2,1)S(1)} %bitcast.344, bf16[1280,384]{0,1:T(8,128)(2,1)} %bitcast.354), kind=kOutput, calls=%fused_computation.2 | convolution fusion | flops 4551278592 | bytes 9633792 | tf_op jit(solution)/shard_map/dot_general | solution.py:48
  583.7 8.9 %multiply_reduce_fusion.1 = (f32[1536]{0:T(1024)S(1)}, f32[1536]{0:T(1024)S(1)}, f32[1024,1536]{1,0:T(8,128)}, f32[1024,1536]{1,0:T(8,128)}) fusion(bf16[1024,1536]{1,0:T(8,128)(2,1)S(1)} %copy-done.3, f32[1024]{0:T(1024)S(1)} %add_rsqrt_fusion, f32[1024]{0:T(1024)S(1)} %copy-done.87, f32[1024,1536]{1,0:T(8,128)} %convolution_add_fusion.1, ...), kind=kOutput, calls=%fused_computation.10 | convolution fusion | flops 1228403712 | bytes 30310400 | tf_op jit(solution)/shard_map/dot_general | solution.py:44
  607.2 5.1 all-to-all-start.12
  631.1 7.3 %all-to-all-done.9 = bf16[8,96,384]{2,1,0:T(8,128)(2,1)S(1)} async-done(((bf16[8,96,384]{2,1,0:T(8,128)(2,1)}), bf16[8,96,384]{2,1,0:T(8,128)(2,1)S(1)}, u32[]{:S(2)}, u32[]{:S(2)}) %all-to-all-start.9) | async-done | bytes 589856 | tf_op jit(solution)/shard_map/all_to_all | solution.py:522
  642.6 5.2 all-to-all-start.10
  (607 shorter events, 420.7 us)
Async XLA Ops:
  7.2 93.8 %all-gather.5.cloned.1.call-start = ((), (), s32[]{:S(2)}) async-start(), calls=%async_computation.19 | async-start | bytes 5308416 | tf_op jit(solution)/shard_map/all_gather | solution.py:310
  29.9 202.2 %all-gather.7.cloned.1.call-start = ((), (), s32[]{:S(2)}) async-start(), calls=%async_computation.20 | async-start | bytes 5308416 | tf_op jit(solution)/shard_map/all_gather | solution.py:310
  50.9 49.0 %collective-permute-start.5 = (bf16[192,1536]{1,0:T(8,128)(2,1)}, bf16[192,1536]{1,0:T(8,128)(2,1)}, u32[]{:S(2)}, u32[]{:S(2)}) collective-permute-start(bf16[192,1536]{1,0:T(8,128)(2,1)} %get-tuple-element.41), channel_id=1, source_target_pairs={{0,16},{8,24},{1,17},{9,25},{2,18},{10,26},{3,19},{11,27},{4,20},{... | collective-permute-start | bytes 1769480 | tf_op jit(solution)/shard_map/ppermute | solution.py:128
  85.1 222.8 %all-gather.9.cloned.1.call-start = ((), (), s32[]{:S(2)}) async-start(), calls=%async_computation.21 | async-start | bytes 5308416 | tf_op jit(solution)/shard_map/all_gather | solution.py:310
  106.8 43.8 %collective-permute-start.7 = (bf16[768,384]{1,0:T(8,128)(2,1)}, bf16[768,384]{1,0:T(8,128)(2,1)}, u32[]{:S(2)}, u32[]{:S(2)}) collective-permute-start(bf16[768,384]{1,0:T(8,128)(2,1)} %bitcast.25), channel_id=1, source_target_pairs={{0,8},{8,0},{16,24},{24,16},{1,9},{9,1},{17,25},{25,17},{2,10},{10... | collective-permute-start | bytes 1769480 | tf_op jit(solution)/shard_map/ppermute | solution.py:122
  108.3 44.1 %collective-permute-start.6 = (bf16[768,384]{1,0:T(8,128)(2,1)}, bf16[768,384]{1,0:T(8,128)(2,1)}, u32[]{:S(2)}, u32[]{:S(2)}) collective-permute-start(bf16[768,384]{1,0:T(8,128)(2,1)} %bitcast.25), channel_id=1, source_target_pairs={{0,16},{8,24},{16,0},{24,8},{1,17},{9,25},{17,1},{25,9},{2,18},{10... | collective-permute-start | bytes 1769480 | tf_op jit(solution)/shard_map/ppermute | solution.py:122
  148.3 41.3 %collective-permute-start.10 = (bf16[192,1536]{1,0:T(8,128)(2,1)}, bf16[192,1536]{1,0:T(8,128)(2,1)}, u32[]{:S(2)}, u32[]{:S(2)}) collective-permute-start(bf16[192,1536]{1,0:T(8,128)(2,1)} %broadcast_select_fusion.6), channel_id=1, source_target_pairs={{0,16},{8,24},{16,0},{24,8},{1,17},{9,25},{17,1},{25,9},{2,18},{10... | collective-permute-start | bytes 1769480 | tf_op jit(solution)/shard_map/ppermute | solution.py:122
  152.4 41.5 %collective-permute-start.8 = (bf16[384,384]{1,0:T(8,128)(2,1)}, bf16[384,384]{1,0:T(8,128)(2,1)}, u32[]{:S(2)}, u32[]{:S(2)}) collective-permute-start(bf16[384,384]{1,0:T(8,128)(2,1)} %slice.506), channel_id=1, source_target_pairs={{0,16},{8,24},{16,0},{24,8},{1,17},{9,25},{17,1},{25,9},{2,18},{10... | collective-permute-start | bytes 884744 | tf_op jit(solution)/shard_map/ppermute | solution.py:122
  154.1 40.8 %collective-permute-start.9 = (bf16[384,384]{1,0:T(8,128)(2,1)}, bf16[384,384]{1,0:T(8,128)(2,1)}, u32[]{:S(2)}, u32[]{:S(2)}) collective-permute-start(bf16[384,384]{1,0:T(8,128)(2,1)} %slice.507), channel_id=1, source_target_pairs={{0,8},{8,0},{16,24},{24,16},{1,9},{9,1},{17,25},{25,17},{2,10},{10... | collective-permute-start | bytes 884744 | tf_op jit(solution)/shard_map/ppermute | solution.py:122
  157.6 38.3 %collective-permute-start.12 = (bf16[96,1536]{1,0:T(8,128)(2,1)}, bf16[96,1536]{1,0:T(8,128)(2,1)}, u32[]{:S(2)}, u32[]{:S(2)}) collective-permute-start(bf16[96,1536]{1,0:T(8,128)(2,1)} %slice.508), channel_id=1, source_target_pairs={{0,16},{8,24},{16,0},{24,8},{1,17},{9,25},{17,1},{25,9},{2,18},{10... | collective-permute-start | bytes 884744 | tf_op jit(solution)/shard_map/ppermute | solution.py:122
  221.8 96.4 %all-gather.11.cloned.1.call-start = ((), (), s32[]{:S(2)}) async-start(), calls=%async_computation.22 | async-start | bytes 5308416 | tf_op jit(solution)/shard_map/all_gather | solution.py:310
  232.0 216.7 %reduce-scatter.7.cloned.1.call-start = ((), (), s32[]{:S(2)}) async-start(), calls=%async_computation.23 | async-start | bytes 5308416 | tf_op jit(solution)/shard_map/reduce_scatter | solution.py:433
  317.7 130.9 %reduce-scatter.9.cloned.1.call-start = ((), (), s32[]{:S(2)}) async-start(), calls=%async_computation.24 | async-start | bytes 5308416 | tf_op jit(solution)/shard_map/reduce_scatter | solution.py:433
  336.5 305.4 %reduce-scatter.13.cloned.1.call-start = ((), (), s32[]{:S(2)}) async-start(), calls=%async_computation.26 | async-start | bytes 1327104 | tf_op jit(solution)/shard_map/reduce_scatter | solution.py:433
  433.0 208.9 %reduce-scatter.11.cloned.1.call-start = ((), (), s32[]{:S(2)}) async-start(), calls=%async_computation.25 | async-start | bytes 3981312 | tf_op jit(solution)/shard_map/reduce_scatter | solution.py:433
  460.4 73.5 %collective-permute-start.21 = (bf16[384,384]{1,0:T(8,128)(2,1)}, bf16[384,384]{1,0:T(8,128)(2,1)}, u32[]{:S(2)}, u32[]{:S(2)}) collective-permute-start(bf16[384,384]{1,0:T(8,128)(2,1)} %get-tuple-element.139), channel_id=1, source_target_pairs={{0,8},{8,0},{16,24},{24,16},{1,9},{9,1},{17,25},{25,17},{2,10},{10... | collective-permute-start | bytes 884744 | tf_op jit(solution)/shard_map/ppermute | solution.py:122
  461.8 72.0 %collective-permute-start.20 = (bf16[384,384]{1,0:T(8,128)(2,1)}, bf16[384,384]{1,0:T(8,128)(2,1)}, u32[]{:S(2)}, u32[]{:S(2)}) collective-permute-start(bf16[384,384]{1,0:T(8,128)(2,1)} %get-tuple-element.140), channel_id=1, source_target_pairs={{0,16},{8,24},{16,0},{24,8},{1,17},{9,25},{17,1},{25,9},{2,18},{10... | collective-permute-start | bytes 884744 | tf_op jit(solution)/shard_map/ppermute | solution.py:122
  463.2 73.5 %collective-permute-start.38 = (bf16[96,1536]{1,0:T(8,128)(2,1)}, bf16[96,1536]{1,0:T(8,128)(2,1)}, u32[]{:S(2)}, u32[]{:S(2)}) collective-permute-start(bf16[96,1536]{1,0:T(8,128)(2,1)} %get-tuple-element.137), channel_id=1, source_target_pairs={{0,8},{8,0},{16,24},{24,16},{1,9},{9,1},{17,25},{25,17},{2,10},{10... | collective-permute-start | bytes 884744 | tf_op jit(solution)/shard_map/ppermute | solution.py:122
  464.7 72.0 %collective-permute-start.37 = (bf16[96,1536]{1,0:T(8,128)(2,1)}, bf16[96,1536]{1,0:T(8,128)(2,1)}, u32[]{:S(2)}, u32[]{:S(2)}) collective-permute-start(bf16[96,1536]{1,0:T(8,128)(2,1)} %get-tuple-element.138), channel_id=1, source_target_pairs={{0,16},{8,24},{16,0},{24,8},{1,17},{9,25},{17,1},{25,9},{2,18},{10... | collective-permute-start | bytes 884744 | tf_op jit(solution)/shard_map/ppermute | solution.py:122
  473.3 188.5 %reduce-scatter.17.cloned.1.call-start = ((), (), s32[]{:S(2)}) async-start(), calls=%async_computation.28 | async-start | bytes 1327104 | tf_op jit(solution)/shard_map/reduce_scatter | solution.py:433
  494.5 133.3 %collective-permute-start.43 = (bf16[192,1536]{1,0:T(8,128)(2,1)}, bf16[192,1536]{1,0:T(8,128)(2,1)}, u32[]{:S(2)}, u32[]{:S(2)}) collective-permute-start(bf16[192,1536]{1,0:T(8,128)(2,1)} %reduce-scatter.7.cloned.1.call-done), channel_id=1, source_target_pairs={{1,16},{17,17},{3,18},{19,19},{5,20},{21,21},{7,22},{23,23},{9,24}... | collective-permute-start | bytes 1769480 | tf_op jit(solution)/shard_map/ppermute | solution.py:189
  556.0 132.9 %reduce-scatter.15.cloned.1.call-start = ((), (), s32[]{:S(2)}) async-start(), calls=%async_computation.27 | async-start | bytes 3981312 | tf_op jit(solution)/shard_map/reduce_scatter | solution.py:433
  565.5 62.2 %collective-permute-start.42 = (bf16[192,1536]{1,0:T(8,128)(2,1)}, bf16[192,1536]{1,0:T(8,128)(2,1)}, u32[]{:S(2)}, u32[]{:S(2)}) collective-permute-start(bf16[192,1536]{1,0:T(8,128)(2,1)} %reduce-scatter.7.cloned.1.call-done), channel_id=1, source_target_pairs={{0,16},{16,17},{2,18},{18,19},{4,20},{20,21},{6,22},{22,23},{8,24}... | collective-permute-start | bytes 1769480 | tf_op jit(solution)/shard_map/ppermute | solution.py:189
  573.5 54.3 %collective-permute-start.41 = (bf16[192,1536]{1,0:T(8,128)(2,1)}, bf16[192,1536]{1,0:T(8,128)(2,1)}, u32[]{:S(2)}, u32[]{:S(2)}) collective-permute-start(bf16[192,1536]{1,0:T(8,128)(2,1)} %fusion.78), channel_id=1, source_target_pairs={{16,0},{24,8},{17,1},{25,9},{18,2},{26,10},{19,3},{27,11},{20,4},{... | collective-permute-start | bytes 1769480 | tf_op jit(solution)/shard_map/ppermute | solution.py:131
  (145 other events, 1429.0 us)
Sparse Core Ops, SparseCore 0:
  30.0 70.6 all-gather.4
  102.3 51.7 all-gather.6
  156.3 60.8 all-gather.8
  232.1 51.2 all-gather.10
  317.8 54.9 reduce-scatter.6
  375.0 65.9 reduce-scatter.8
  443.3 30.9 reduce-scatter.12
  476.7 46.4 reduce-scatter.10
  533.9 34.1 reduce-scatter.16
  578.0 47.3 reduce-scatter.14

commit v17 on v16

--- a/solution.py
+++ b/solution.py
@@ -486,7 +486,10 @@
         grad_middle = grad_rows + norm_back(
             unit_mid, inverse_mid, ffn_grad * all_gains[layer, 2]
         )
-        middle_low = from_slots(grad_middle.astype(low))
+        middle_low = grad_middle.astype(low)
+        if layer == 0:
+            middle_low = after(middle_low, latents_out)
+        middle_low = from_slots(middle_low)
         if layer == 0:
             up_half = sum_by_distance(*up_blocks, middle_low).astype(low)
             down_half = sum_by_distance(*down_blocks, middle_low).astype(low)
@@ -523,14 +526,13 @@
         pieces[layer] = (scatter(qkv_grad), out_piece)
         if layer > 0:
             grad_low = from_sequences(grad_rows.astype(low))
-            late = after(active_low, latent_part)
+            late = after(active_low, grad_low)
             here = (latent_slot == section)[:, None]
             kept = jnp.where(here, jnp.tile(middle, (section_count, 1)), 0.0)
             last = lax.optimization_barrier((matmul(late, down_w[layer]) + kept).astype(low))
             last = last.reshape(latent_rows, section_count, -1).swapaxes(0, 1)
             last = lax.all_to_all(last, "section", split_axis=0, concat_axis=0)
             latents_out = jnp.sum(last.astype(full), axis=0)
-            grad_low = after(grad_low, latents_out)
             grad_low = after(grad_low, ffn_pieces)
         if layer == 0:
             add_media(0, grad_key, grad_value, qkv_grad)

time: 718 us -> 729 us (1.015)
  waiting for transfers between devices: 84.7 us -> 99.8 us
    unnamed x212 -> x213, local copies, waits for them, and re-layouts: 20.3 us -> 19.6 us
  transfers between devices with their start and end apart: 66 -> 66, of which waited for: 20 -> 23; matrix products, arithmetic and copies ran while one was open for 42% -> 42% of each run, Pallas kernels for 0% -> 0%
where the time goes in v17:
time: 729 us; the launch traced here: 720 us
  blocking collectives  158 us (22%)
  matrix products  143 us (20%)
  starting transfers between devices  120 us (16%)
  waiting for transfers between devices  99.8 us (14%)
  other arithmetic  95.9 us (13%)
  local copies, waits for them, and re-layouts  86.8 us (12%)
  between operations  16.6 us (2%)
    all_gather x2, blocking collectives, from_sequences(): near = lax.all_gather(rows, 'pair', axis=0, tiled=True)  56.6 us
    all_gather x4, blocking collectives, from_slots(): return lax.all_gather(rows, 'section', axis=0, tiled=True)  56.4 us
    dot_general x17, matrix products, matmul_nt(): lax.dot_general(left, right, (((1,), (1,)), ((), ())), preferred_element_...  48.9 us
    dot_general x13, matrix products, matmul(): return jnp.dot(left, right, preferred_element_type=full)  40.4 us
    ppermute x26, waiting for transfers between devices, swapped(): return lax.ppermute(value, 'section', pairs)  34.2 us
    dot_general x8, matrix products, matmul_tn(): lax.dot_general(left, right, (((0,), (0,)), ((), ())), preferred_element_...  32.8 us
    ppermute x26, starting transfers between devices, swapped(): return lax.ppermute(value, 'section', pairs)  31.9 us
    all_gather x3, blocking collectives, per_device(): all_gains = lax.all_gather(all_gains, axis, axis=2, tiled=True)  31.4 us
  transfers between devices with their start and end apart: 66, of which 23 were waited for; matrix products, arithmetic and copies ran while one was open for 42% of the time, Pallas kernels for 0%

profile of v17, /device:TPU:0, one launch (start us, length us, event | category | flops | bytes accessed | tf_op | source)
XLA Modules:
  0.0 720.0 jit_solution(16048953254532498324)
XLA Ops:
  12.6 10.2 %collective-permute-done = bf16[192,1152]{1,0:T(8,128)(2,1)S(1)} collective-permute-done((bf16[192,1152]{1,0:T(8,128)(2,1)S(1)}, bf16[192,1152]{1,0:T(8,128)(2,1)S(1)}, u32[]{:S(2)}, u32[]{:S(2)}) %collective-permute-start) | collective-permute-done | bytes 442400 | tf_op jit(solution)/shard_map/ppermute | solution.py:122
  31.9 10.9 %collective-permute-start.1 = (bf16[96,3072]{1,0:T(8,128)(2,1)}, bf16[96,3072]{1,0:T(8,128)(2,1)}, u32[]{:S(2)}, u32[]{:S(2)}) collective-permute-start(bf16[96,3072]{1,0:T(8,128)(2,1)} %slice_bitcast_fusion.4), channel_id=1, source_target_pairs={{0,16},{8,24},{1,17},{9,25},{2,18},{10,26},{3,19},{11,27},{4,20},{... | collective-permute-start | bytes 1769480 | tf_op jit(solution)/shard_map/ppermute | solution.py:128
  58.9 19.0 %all_gather.40 = f32[2,3,384]{1,0,2:T(2,128)} all-gather(f32[2,3,96]{1,0,2:T(2,128)S(1)} %all_gather.39), channel_id=1, replica_groups=mesh['section'=4,'pair'=4,'core'=2] {'pair'}, dimensions={2}, use_global_device_ids=true | all-gather | bytes 11520 | tf_op jit(solution)/shard_map/all_gather | solution.py:306
  85.2 10.6 %all_gather.41 = f32[2,3,1536]{2,0,1:T(2,128)S(1)} all-gather(f32[2,3,384]{2,0,1:T(2,128)S(1)} %copy.152), channel_id=1, replica_groups=mesh['section'=4,'pair'=4,'core'=2] {'section'}, dimensions={2}, use_global_device_ids=true | all-gather | bytes 46080 | tf_op jit(solution)/shard_map/all_gather | solution.py:306
  112.2 6.3 slice_reduce_fusion
  162.2 27.8 %all_gather.43 = bf16[256,1536]{1,0:T(8,128)(2,1)S(1)} all-gather(bf16[64,1536]{1,0:T(8,128)(2,1)S(1)} %reshape.734), channel_id=1, replica_groups=mesh['section'=4,'pair'=4,'core'=2] {'pair'}, dimensions={0}, use_global_device_ids=true | all-gather | bytes 983040 | tf_op jit(solution)/shard_map/all_gather | solution.py:234
  195.2 6.9 collective-permute-done.13
  220.4 7.6 %collective-permute-done.16 = bf16[192,1536]{1,0:T(8,128)(2,1)} collective-permute-done((bf16[192,1536]{1,0:T(8,128)(2,1)S(1)}, bf16[192,1536]{1,0:T(8,128)(2,1)}, u32[]{:S(2)}, u32[]{:S(2)}) %collective-permute-start.16) | collective-permute-done | bytes 589856 | tf_op jit(solution)/shard_map/ppermute | solution.py:177
  243.0 21.8 %all_gather.45 = bf16[256,1536]{1,0:T(8,128)(2,1)S(1)} all-gather(bf16[64,1536]{1,0:T(8,128)(2,1)S(1)} %multiply_convert_fusion.9), channel_id=1, replica_groups=mesh['section'=4,'pair'=4,'core'=2] {'section'}, dimensions={0}, use_global_device_ids=true | all-gather | bytes 983040 | tf_op jit(solution)/shard_map/all_gather | solution.py:225
  280.4 13.5 %all_to_all.101 = bf16[4,64,1536]{2,1,0:T(8,128)(2,1)S(1)} all-to-all(bf16[4,64,1536]{2,1,0:T(8,128)(2,1)S(1)} %bitcast.357), channel_id=1, replica_groups=mesh['section'=4,'pair'=4,'core'=2] {'section'}, dimensions={0} | all-to-all | bytes 1572864 | tf_op jit(solution)/shard_map/all_to_all | solution.py:221
  294.5 11.6 %all_gather.46 = bf16[256,1536]{1,0:T(8,128)(2,1)S(1)} all-gather(bf16[64,1536]{1,0:T(8,128)(2,1)S(1)} %multiply_convert_fusion.8), channel_id=1, replica_groups=mesh['section'=4,'pair'=4,'core'=2] {'section'}, dimensions={0}, use_global_device_ids=true | all-gather | bytes 983040 | tf_op jit(solution)/shard_map/all_gather | solution.py:225
  334.3 7.9 %all-to-all-done.4 = bf16[4,64,1536]{2,1,0:T(8,128)(2,1)S(1)} async-done(((bf16[4,64,1536]{2,1,0:T(8,128)(2,1)}), bf16[4,64,1536]{2,1,0:T(8,128)(2,1)S(1)}, u32[]{:S(2)}, u32[]{:S(2)}) %all-to-all-start.4) | async-done | bytes 786464 | tf_op jit(solution)/shard_map/all_to_all | solution.py:221
  344.5 11.0 %all_gather.49 = bf16[256,1536]{1,0:T(8,128)(2,1)S(1)} all-gather(bf16[64,1536]{1,0:T(8,128)(2,1)S(1)} %get-tuple-element.94), channel_id=1, replica_groups=mesh['section'=4,'pair'=4,'core'=2] {'section'}, dimensions={0}, use_global_device_ids=true | all-gather | bytes 983040 | tf_op jit(solution)/shard_map/all_gather | solution.py:225
  383.8 9.3 %convolution_convert_fusion.2 = bf16[1536,1152]{1,0:T(8,128)(2,1)} fusion(bf16[256,1536]{1,0:T(8,128)(2,1)} %copy-done.68, bf16[1024,1536]{1,0:T(8,128)(2,1)} %get-tuple-element.112, bf16[256,384]{0,1:T(8,128)(2,1)S(1)} %bitcast.389, bf16[1280,384]{0,1:T(8,128)(2,1)S(1)} %bitcast.340, bf16[1280,384]{0,1:T(8,128)(2,1)S(1)} %bitcast.351), kind=kOutput, calls=%fused_computation.4 | convolution fusion | flops 4551278592 | bytes 9633792 | tf_op jit(solution)/shard_map/dot_general | solution.py:48
  396.6 28.8 %all_gather.50 = bf16[256,1536]{1,0:T(8,128)(2,1)S(1)} all-gather(bf16[64,1536]{1,0:T(8,128)(2,1)S(1)} %get-tuple-element.92), channel_id=1, replica_groups=mesh['section'=4,'pair'=4,'core'=2] {'pair'}, dimensions={0}, use_global_device_ids=true | all-gather | bytes 983040 | tf_op jit(solution)/shard_map/all_gather | solution.py:234
  440.8 8.2 %all-to-all-done.6 = bf16[4,256,384]{2,1,0:T(8,128)(2,1)} async-done(((bf16[4,256,384]{2,1,0:T(8,128)(2,1)}), bf16[4,256,384]{2,1,0:T(8,128)(2,1)}, u32[]{:S(2)}, u32[]{:S(2)}) %all-to-all-start.6) | async-done | bytes 786464 | tf_op jit(solution)/shard_map/all_to_all | solution.py:534
  473.8 5.3 all-to-all-start.7
  504.8 7.1 all-to-all-done.7
  520.9 12.0 %all_gather.51 = bf16[256,1536]{1,0:T(8,128)(2,1)S(1)} all-gather(bf16[64,1536]{1,0:T(8,128)(2,1)S(1)} %get-tuple-element.53), channel_id=1, replica_groups=mesh['section'=4,'pair'=4,'core'=2] {'section'}, dimensions={0}, use_global_device_ids=true | all-gather | bytes 983040 | tf_op jit(solution)/shard_map/all_gather | solution.py:225
  569.2 9.5 %convolution_convert_fusion = bf16[1536,1152]{1,0:T(8,128)(2,1)} fusion(bf16[256,1536]{1,0:T(8,128)(2,1)S(1)} %copy-done.67, bf16[1024,1536]{1,0:T(8,128)(2,1)} %get-tuple-element.113, bf16[256,384]{0,1:T(8,128)(2,1)S(1)} %bitcast.387, bf16[1280,384]{0,1:T(8,128)(2,1)} %bitcast.344, bf16[1280,384]{0,1:T(8,128)(2,1)} %bitcast.354), kind=kOutput, calls=%fused_computation.2 | convolution fusion | flops 4551278592 | bytes 9633792 | tf_op jit(solution)/shard_map/dot_general | solution.py:48
  596.3 9.1 %multiply_reduce_fusion.1 = (f32[1536]{0:T(1024)S(1)}, f32[1536]{0:T(1024)S(1)}, f32[1024,1536]{1,0:T(8,128)}, f32[1024,1536]{1,0:T(8,128)}) fusion(bf16[1024,1536]{1,0:T(8,128)(2,1)S(1)} %copy-done.3, f32[1024]{0:T(1024)S(1)} %add_rsqrt_fusion, f32[1024]{0:T(1024)S(1)} %copy-done.86, f32[1024,1536]{1,0:T(8,128)} %convolution_add_fusion.1, ...), kind=kOutput, calls=%fused_computation.10 | convolution fusion | flops 1228403712 | bytes 30310400 | tf_op jit(solution)/shard_map/dot_general | solution.py:44
  606.0 5.4 all-to-all-start.11
  642.4 8.1 %all-to-all-done.9 = bf16[8,96,384]{2,1,0:T(8,128)(2,1)S(1)} async-done(((bf16[8,96,384]{2,1,0:T(8,128)(2,1)}), bf16[8,96,384]{2,1,0:T(8,128)(2,1)S(1)}, u32[]{:S(2)}, u32[]{:S(2)}) %all-to-all-start.9) | async-done | bytes 589856 | tf_op jit(solution)/shard_map/all_to_all | solution.py:525
  666.2 6.2 all-to-all-done.10
  (608 shorter events, 429.7 us)
Async XLA Ops:
  7.2 93.6 %all-gather.5.cloned.1.call-start = ((), (), s32[]{:S(2)}) async-start(), calls=%async_computation.19 | async-start | bytes 5308416 | tf_op jit(solution)/shard_map/all_gather | solution.py:310
  29.9 200.1 %all-gather.7.cloned.1.call-start = ((), (), s32[]{:S(2)}) async-start(), calls=%async_computation.20 | async-start | bytes 5308416 | tf_op jit(solution)/shard_map/all_gather | solution.py:310
  50.8 49.0 %collective-permute-start.5 = (bf16[192,1536]{1,0:T(8,128)(2,1)}, bf16[192,1536]{1,0:T(8,128)(2,1)}, u32[]{:S(2)}, u32[]{:S(2)}) collective-permute-start(bf16[192,1536]{1,0:T(8,128)(2,1)} %get-tuple-element.41), channel_id=1, source_target_pairs={{0,16},{8,24},{1,17},{9,25},{2,18},{10,26},{3,19},{11,27},{4,20},{... | collective-permute-start | bytes 1769480 | tf_op jit(solution)/shard_map/ppermute | solution.py:128
  85.1 220.9 %all-gather.9.cloned.1.call-start = ((), (), s32[]{:S(2)}) async-start(), calls=%async_computation.21 | async-start | bytes 5308416 | tf_op jit(solution)/shard_map/all_gather | solution.py:310
  106.8 44.3 %collective-permute-start.7 = (bf16[768,384]{1,0:T(8,128)(2,1)}, bf16[768,384]{1,0:T(8,128)(2,1)}, u32[]{:S(2)}, u32[]{:S(2)}) collective-permute-start(bf16[768,384]{1,0:T(8,128)(2,1)} %bitcast.25), channel_id=1, source_target_pairs={{0,8},{8,0},{16,24},{24,16},{1,9},{9,1},{17,25},{25,17},{2,10},{10... | collective-permute-start | bytes 1769480 | tf_op jit(solution)/shard_map/ppermute | solution.py:122
  108.3 43.9 %collective-permute-start.6 = (bf16[768,384]{1,0:T(8,128)(2,1)}, bf16[768,384]{1,0:T(8,128)(2,1)}, u32[]{:S(2)}, u32[]{:S(2)}) collective-permute-start(bf16[768,384]{1,0:T(8,128)(2,1)} %bitcast.25), channel_id=1, source_target_pairs={{0,16},{8,24},{16,0},{24,8},{1,17},{9,25},{17,1},{25,9},{2,18},{10... | collective-permute-start | bytes 1769480 | tf_op jit(solution)/shard_map/ppermute | solution.py:122
  148.8 41.2 %collective-permute-start.10 = (bf16[192,1536]{1,0:T(8,128)(2,1)}, bf16[192,1536]{1,0:T(8,128)(2,1)S(1)}, u32[]{:S(2)}, u32[]{:S(2)}) collective-permute-start(bf16[192,1536]{1,0:T(8,128)(2,1)} %broadcast_select_fusion.6), channel_id=1, source_target_pairs={{0,16},{8,24},{16,0},{24,8},{1,17},{9,25},{17,1},{25,9},{2,18},{10... | collective-permute-start | bytes 1769480 | tf_op jit(solution)/shard_map/ppermute | solution.py:122
  152.1 41.0 %collective-permute-start.8 = (bf16[384,384]{1,0:T(8,128)(2,1)S(1)}, bf16[384,384]{1,0:T(8,128)(2,1)S(1)}, u32[]{:S(2)}, u32[]{:S(2)}) collective-permute-start(bf16[384,384]{1,0:T(8,128)(2,1)S(1)} %slice.506), channel_id=1, source_target_pairs={{0,16},{8,24},{16,0},{24,8},{1,17},{9,25},{17,1},{25,9},{2,18},{10... | collective-permute-start | bytes 884744 | tf_op jit(solution)/shard_map/ppermute | solution.py:122
  153.9 39.3 %collective-permute-start.9 = (bf16[384,384]{1,0:T(8,128)(2,1)}, bf16[384,384]{1,0:T(8,128)(2,1)}, u32[]{:S(2)}, u32[]{:S(2)}) collective-permute-start(bf16[384,384]{1,0:T(8,128)(2,1)} %slice.507), channel_id=1, source_target_pairs={{0,8},{8,0},{16,24},{24,16},{1,9},{9,1},{17,25},{25,17},{2,10},{10... | collective-permute-start | bytes 884744 | tf_op jit(solution)/shard_map/ppermute | solution.py:122
  220.4 95.5 %all-gather.11.cloned.1.call-start = ((), (), s32[]{:S(2)}) async-start(), calls=%async_computation.22 | async-start | bytes 5308416 | tf_op jit(solution)/shard_map/all_gather | solution.py:310
  230.0 221.0 %reduce-scatter.7.cloned.1.call-start = ((), (), s32[]{:S(2)}) async-start(), calls=%async_computation.23 | async-start | bytes 5308416 | tf_op jit(solution)/shard_map/reduce_scatter | solution.py:433
  315.6 135.4 %reduce-scatter.9.cloned.1.call-start = ((), (), s32[]{:S(2)}) async-start(), calls=%async_computation.24 | async-start | bytes 5308416 | tf_op jit(solution)/shard_map/reduce_scatter | solution.py:433
  334.2 319.1 %reduce-scatter.13.cloned.1.call-start = ((), (), s32[]{:S(2)}) async-start(), calls=%async_computation.26 | async-start | bytes 1327104 | tf_op jit(solution)/shard_map/reduce_scatter | solution.py:433
  437.5 215.7 %reduce-scatter.11.cloned.1.call-start = ((), (), s32[]{:S(2)}) async-start(), calls=%async_computation.25 | async-start | bytes 3981312 | tf_op jit(solution)/shard_map/reduce_scatter | solution.py:433
  465.1 83.1 %collective-permute-start.21 = (bf16[384,384]{1,0:T(8,128)(2,1)}, bf16[384,384]{1,0:T(8,128)(2,1)}, u32[]{:S(2)}, u32[]{:S(2)}) collective-permute-start(bf16[384,384]{1,0:T(8,128)(2,1)} %get-tuple-element.139), channel_id=1, source_target_pairs={{0,8},{8,0},{16,24},{24,16},{1,9},{9,1},{17,25},{25,17},{2,10},{10... | collective-permute-start | bytes 884744 | tf_op jit(solution)/shard_map/ppermute | solution.py:122
  466.6 81.6 %collective-permute-start.20 = (bf16[384,384]{1,0:T(8,128)(2,1)}, bf16[384,384]{1,0:T(8,128)(2,1)}, u32[]{:S(2)}, u32[]{:S(2)}) collective-permute-start(bf16[384,384]{1,0:T(8,128)(2,1)} %get-tuple-element.140), channel_id=1, source_target_pairs={{0,16},{8,24},{16,0},{24,8},{1,17},{9,25},{17,1},{25,9},{2,18},{10... | collective-permute-start | bytes 884744 | tf_op jit(solution)/shard_map/ppermute | solution.py:122
  468.9 86.7 %collective-permute-start.38 = (bf16[96,1536]{1,0:T(8,128)(2,1)}, bf16[96,1536]{1,0:T(8,128)(2,1)}, u32[]{:S(2)}, u32[]{:S(2)}) collective-permute-start(bf16[96,1536]{1,0:T(8,128)(2,1)} %get-tuple-element.137), channel_id=1, source_target_pairs={{0,8},{8,0},{16,24},{24,16},{1,9},{9,1},{17,25},{25,17},{2,10},{10... | collective-permute-start | bytes 884744 | tf_op jit(solution)/shard_map/ppermute | solution.py:122
  470.4 85.2 %collective-permute-start.37 = (bf16[96,1536]{1,0:T(8,128)(2,1)}, bf16[96,1536]{1,0:T(8,128)(2,1)}, u32[]{:S(2)}, u32[]{:S(2)}) collective-permute-start(bf16[96,1536]{1,0:T(8,128)(2,1)} %get-tuple-element.138), channel_id=1, source_target_pairs={{0,16},{8,24},{16,0},{24,8},{1,17},{9,25},{17,1},{25,9},{2,18},{10... | collective-permute-start | bytes 884744 | tf_op jit(solution)/shard_map/ppermute | solution.py:122
  473.8 38.0 %all-to-all-start.7 = ((bf16[4,64,1536]{2,1,0:T(8,128)(2,1)}), bf16[4,64,1536]{2,1,0:T(8,128)(2,1)}, u32[]{:S(2)}, u32[]{:S(2)}) async-start(bf16[4,64,1536]{2,1,0:T(8,128)(2,1)} %bitcast.382), calls=%async_computation.9 | async-start | bytes 1572864 | tf_op jit(solution)/shard_map/all_to_all | solution.py:242
  479.1 194.1 %reduce-scatter.17.cloned.1.call-start = ((), (), s32[]{:S(2)}) async-start(), calls=%async_computation.28 | async-start | bytes 1327104 | tf_op jit(solution)/shard_map/reduce_scatter | solution.py:433
  499.4 139.7 %collective-permute-start.43 = (bf16[192,1536]{1,0:T(8,128)(2,1)}, bf16[192,1536]{1,0:T(8,128)(2,1)}, u32[]{:S(2)}, u32[]{:S(2)}) collective-permute-start(bf16[192,1536]{1,0:T(8,128)(2,1)} %reduce-scatter.7.cloned.1.call-done), channel_id=1, source_target_pairs={{1,16},{17,17},{3,18},{19,19},{5,20},{21,21},{7,22},{23,23},{9,24}... | collective-permute-start | bytes 1769480 | tf_op jit(solution)/shard_map/ppermute | solution.py:189
  568.8 131.4 %reduce-scatter.15.cloned.1.call-start = ((), (), s32[]{:S(2)}) async-start(), calls=%async_computation.27 | async-start | bytes 3981312 | tf_op jit(solution)/shard_map/reduce_scatter | solution.py:433
  579.9 59.2 %collective-permute-start.42 = (bf16[192,1536]{1,0:T(8,128)(2,1)}, bf16[192,1536]{1,0:T(8,128)(2,1)}, u32[]{:S(2)}, u32[]{:S(2)}) collective-permute-start(bf16[192,1536]{1,0:T(8,128)(2,1)} %reduce-scatter.7.cloned.1.call-done), channel_id=1, source_target_pairs={{0,16},{16,17},{2,18},{18,19},{4,20},{20,21},{6,22},{22,23},{8,24}... | collective-permute-start | bytes 1769480 | tf_op jit(solution)/shard_map/ppermute | solution.py:189
  586.9 52.2 %collective-permute-start.41 = (bf16[192,1536]{1,0:T(8,128)(2,1)}, bf16[192,1536]{1,0:T(8,128)(2,1)}, u32[]{:S(2)}, u32[]{:S(2)}) collective-permute-start(bf16[192,1536]{1,0:T(8,128)(2,1)} %fusion.79), channel_id=1, source_target_pairs={{16,0},{24,8},{17,1},{25,9},{18,2},{26,10},{19,3},{27,11},{20,4},{... | collective-permute-start | bytes 1769480 | tf_op jit(solution)/shard_map/ppermute | solution.py:131
  (145 other events, 1411.6 us)
Sparse Core Ops, SparseCore 0:
  30.0 70.6 all-gather.4
  102.3 51.7 all-gather.6
  156.4 61.0 all-gather.8
  230.1 51.5 all-gather.10
  315.7 54.9 reduce-scatter.6
  372.9 65.9 reduce-scatter.8
  441.1 31.1 reduce-scatter.12
  474.7 54.4 reduce-scatter.10
  548.3 30.9 reduce-scatter.16
  591.4 45.0 reduce-scatter.14

commit v18 on v16

--- a/solution.py
+++ b/solution.py
@@ -549,7 +549,7 @@
     gain_rows = [
         jnp.stack([media_gains[1 - layer], *gain_rows[layer]]) for layer in range(LAYERS)
     ]
-    gain_parts = jnp.stack(gain_rows).reshape(LAYERS, 3, section_count, -1)
+    gain_parts = after(jnp.stack(gain_rows), media_sum).reshape(LAYERS, 3, section_count, -1)
     gain_parts = jnp.sum(
         lax.all_to_all(gain_parts, "section", split_axis=2, concat_axis=2), axis=2
     )

time: 718 us -> 726 us (1.011)
  waiting for transfers between devices: 84.7 us -> 106 us
    ppermute x26, waiting for transfers between devices: 28.4 us -> 55.6 us  [swapped(): return lax.ppermute(value, 'section', pairs)]
    all_to_all x1, waiting for transfers between devices: 7.28 us -> 0.01 us  [per_device(): lax.all_to_all(up_half, dp, split_axis=0, concat_axis=1, tiled=True)]
    unnamed x212 -> x208, local copies, waits for them, and re-layouts: 20.3 us -> 19.1 us
  transfers between devices with their start and end apart: 66 -> 66, of which waited for: 20 -> 23; matrix products, arithmetic and copies ran while one was open for 42% -> 40% of each run, Pallas kernels for 0% -> 0%
where the time goes in v18:
time: 726 us; the launch traced here: 718 us
  blocking collectives  159 us (22%)
  matrix products  139 us (19%)
  starting transfers between devices  125 us (17%)
  waiting for transfers between devices  106 us (15%)
  other arithmetic  94.8 us (13%)
  local copies, waits for them, and re-layouts  77.9 us (11%)
  between operations  16.7 us (2%)
    all_gather x2, blocking collectives, from_sequences(): near = lax.all_gather(rows, 'pair', axis=0, tiled=True)  57.4 us
    all_gather x4, blocking collectives, from_slots(): return lax.all_gather(rows, 'section', axis=0, tiled=True)  56.7 us
    ppermute x26, waiting for transfers between devices, swapped(): return lax.ppermute(value, 'section', pairs)  55.6 us
    dot_general x17, matrix products, matmul_nt(): lax.dot_general(left, right, (((1,), (1,)), ((), ())), preferred_element_...  46.3 us
    dot_general x13, matrix products, matmul(): return jnp.dot(left, right, preferred_element_type=full)  40.6 us
    ppermute x26, starting transfers between devices, swapped(): return lax.ppermute(value, 'section', pairs)  34.3 us
    all_gather x3, blocking collectives, per_device(): all_gains = lax.all_gather(all_gains, axis, axis=2, tiled=True)  31.6 us
    dot_general x8, matrix products, matmul_tn(): lax.dot_general(left, right, (((0,), (0,)), ((), ())), preferred_element_...  29.9 us
  transfers between devices with their start and end apart: 66, of which 23 were waited for; matrix products, arithmetic and copies ran while one was open for 40% of the time, Pallas kernels for 0%

profile of v18, /device:TPU:0, one launch (start us, length us, event | category | flops | bytes accessed | tf_op | source)
XLA Modules:
  0.0 718.3 jit_solution(15076719233380555167)
XLA Ops:
  12.6 10.2 %collective-permute-done = bf16[192,1152]{1,0:T(8,128)(2,1)S(1)} collective-permute-done((bf16[192,1152]{1,0:T(8,128)(2,1)S(1)}, bf16[192,1152]{1,0:T(8,128)(2,1)S(1)}, u32[]{:S(2)}, u32[]{:S(2)}) %collective-permute-start) | collective-permute-done | bytes 442400 | tf_op jit(solution)/shard_map/ppermute | solution.py:122
  31.9 10.9 %collective-permute-start.1 = (bf16[96,3072]{1,0:T(8,128)(2,1)}, bf16[96,3072]{1,0:T(8,128)(2,1)}, u32[]{:S(2)}, u32[]{:S(2)}) collective-permute-start(bf16[96,3072]{1,0:T(8,128)(2,1)} %slice_bitcast_fusion.4), channel_id=1, source_target_pairs={{0,16},{8,24},{1,17},{9,25},{2,18},{10,26},{3,19},{11,27},{4,20},{... | collective-permute-start | bytes 1769480 | tf_op jit(solution)/shard_map/ppermute | solution.py:128
  58.9 19.0 %all_gather.40 = f32[2,3,384]{1,0,2:T(2,128)} all-gather(f32[2,3,96]{1,0,2:T(2,128)S(1)} %all_gather.39), channel_id=1, replica_groups=mesh['section'=4,'pair'=4,'core'=2] {'pair'}, dimensions={2}, use_global_device_ids=true | all-gather | bytes 11520 | tf_op jit(solution)/shard_map/all_gather | solution.py:306
  85.2 10.8 %all_gather.41 = f32[2,3,1536]{2,0,1:T(2,128)S(1)} all-gather(f32[2,3,384]{2,0,1:T(2,128)S(1)} %copy.153), channel_id=1, replica_groups=mesh['section'=4,'pair'=4,'core'=2] {'section'}, dimensions={2}, use_global_device_ids=true | all-gather | bytes 46080 | tf_op jit(solution)/shard_map/all_gather | solution.py:306
  112.2 6.3 slice_reduce_fusion
  161.7 27.9 %all_gather.43 = bf16[256,1536]{1,0:T(8,128)(2,1)S(1)} all-gather(bf16[64,1536]{1,0:T(8,128)(2,1)S(1)} %reshape.720), channel_id=1, replica_groups=mesh['section'=4,'pair'=4,'core'=2] {'pair'}, dimensions={0}, use_global_device_ids=true | all-gather | bytes 983040 | tf_op jit(solution)/shard_map/all_gather | solution.py:234
  196.8 6.0 collective-permute-done.13
  221.8 8.1 %collective-permute-done.16 = bf16[192,1536]{1,0:T(8,128)(2,1)} collective-permute-done((bf16[192,1536]{1,0:T(8,128)(2,1)}, bf16[192,1536]{1,0:T(8,128)(2,1)}, u32[]{:S(2)}, u32[]{:S(2)}) %collective-permute-start.16) | collective-permute-done | bytes 589856 | tf_op jit(solution)/shard_map/ppermute | solution.py:177
  244.9 21.1 %all_gather.45 = bf16[256,1536]{1,0:T(8,128)(2,1)S(1)} all-gather(bf16[64,1536]{1,0:T(8,128)(2,1)S(1)} %multiply_convert_fusion.9), channel_id=1, replica_groups=mesh['section'=4,'pair'=4,'core'=2] {'section'}, dimensions={0}, use_global_device_ids=true | all-gather | bytes 983040 | tf_op jit(solution)/shard_map/all_gather | solution.py:225
  281.6 13.3 %all_to_all.101 = bf16[4,64,1536]{2,1,0:T(8,128)(2,1)S(1)} all-to-all(bf16[4,64,1536]{2,1,0:T(8,128)(2,1)S(1)} %bitcast.362), channel_id=1, replica_groups=mesh['section'=4,'pair'=4,'core'=2] {'section'}, dimensions={0} | all-to-all | bytes 1572864 | tf_op jit(solution)/shard_map/all_to_all | solution.py:221
  295.5 12.0 %all_gather.46 = bf16[256,1536]{1,0:T(8,128)(2,1)} all-gather(bf16[64,1536]{1,0:T(8,128)(2,1)S(1)} %multiply_convert_fusion.8), channel_id=1, replica_groups=mesh['section'=4,'pair'=4,'core'=2] {'section'}, dimensions={0}, use_global_device_ids=true | all-gather | bytes 983040 | tf_op jit(solution)/shard_map/all_gather | solution.py:225
  307.6 5.2 multiply_convert_fusion.6
  337.5 6.7 all-to-all-done.4
  347.7 11.0 %all_gather.49 = bf16[256,1536]{1,0:T(8,128)(2,1)S(1)} all-gather(bf16[64,1536]{1,0:T(8,128)(2,1)S(1)} %get-tuple-element.96), channel_id=1, replica_groups=mesh['section'=4,'pair'=4,'core'=2] {'section'}, dimensions={0}, use_global_device_ids=true | all-gather | bytes 983040 | tf_op jit(solution)/shard_map/all_gather | solution.py:225
  382.2 9.4 %convolution_convert_fusion.2 = bf16[1536,1152]{1,0:T(8,128)(2,1)} fusion(bf16[256,1536]{1,0:T(8,128)(2,1)} %copy-done.67, bf16[1024,1536]{1,0:T(8,128)(2,1)} %get-tuple-element.114, bf16[256,384]{0,1:T(8,128)(2,1)S(1)} %bitcast.394, bf16[1280,384]{0,1:T(8,128)(2,1)S(1)} %bitcast.344, bf16[1280,384]{0,1:T(8,128)(2,1)S(1)} %bitcast.355), kind=kOutput, calls=%fused_computation.4 | convolution fusion | flops 4551278592 | bytes 9633792 | tf_op jit(solution)/shard_map/dot_general | solution.py:48
  394.2 29.5 %all_gather.50 = bf16[256,1536]{1,0:T(8,128)(2,1)} all-gather(bf16[64,1536]{1,0:T(8,128)(2,1)S(1)} %get-tuple-element.94), channel_id=1, replica_groups=mesh['section'=4,'pair'=4,'core'=2] {'pair'}, dimensions={0}, use_global_device_ids=true | all-gather | bytes 983040 | tf_op jit(solution)/shard_map/all_gather | solution.py:234
  435.4 9.3 %all-to-all-done.5 = bf16[4,256,384]{2,1,0:T(8,128)(2,1)} async-done(((bf16[4,256,384]{2,1,0:T(8,128)(2,1)}), bf16[4,256,384]{2,1,0:T(8,128)(2,1)}, u32[]{:S(2)}, u32[]{:S(2)}) %all-to-all-start.5) | async-done | bytes 786464 | tf_op jit(solution)/shard_map/all_to_all | solution.py:531
  505.6 12.5 %all_gather.51 = bf16[256,1536]{1,0:T(8,128)(2,1)S(1)} all-gather(bf16[64,1536]{1,0:T(8,128)(2,1)S(1)} %get-tuple-element.92), channel_id=1, replica_groups=mesh['section'=4,'pair'=4,'core'=2] {'section'}, dimensions={0}, use_global_device_ids=true | all-gather | bytes 983040 | tf_op jit(solution)/shard_map/all_gather | solution.py:225
  555.3 9.6 %convolution_convert_fusion = bf16[1536,1152]{1,0:T(8,128)(2,1)} fusion(bf16[256,1536]{1,0:T(8,128)(2,1)} %copy-done.66, bf16[1024,1536]{1,0:T(8,128)(2,1)} %get-tuple-element.115, bf16[256,384]{0,1:T(8,128)(2,1)S(1)} %bitcast.392, bf16[1280,384]{0,1:T(8,128)(2,1)S(1)} %bitcast.348, bf16[1280,384]{0,1:T(8,128)(2,1)} %bitcast.358), kind=kOutput, calls=%fused_computation.2 | convolution fusion | flops 4551278592 | bytes 9633792 | tf_op jit(solution)/shard_map/dot_general | solution.py:48
  587.8 7.9 %multiply_reduce_fusion.1 = (f32[1536]{0:T(1024)S(1)}, f32[1536]{0:T(1024)S(1)}, f32[1024,1536]{1,0:T(8,128)S(1)}, f32[1024,1536]{1,0:T(8,128)}) fusion(bf16[1024,1536]{1,0:T(8,128)(2,1)S(1)} %copy-done.3, f32[1024]{0:T(1024)S(1)} %add_rsqrt_fusion, f32[1024]{0:T(1024)S(1)} %copy-done.85, f32[1024,1536]{1,0:T(8,128)} %convolution_add_fusion.1, ...), kind=kOutput, calls=%fused_computation.10 | convolution fusion | flops 1228403712 | bytes 30310400 | tf_op jit(solution)/shard_map/dot_general | solution.py:44
  601.2 8.0 %collective-permute-done.24 = bf16[128,1536]{1,0:T(8,128)(2,1)S(1)} collective-permute-done((bf16[128,1536]{1,0:T(8,128)(2,1)S(1)}, bf16[128,1536]{1,0:T(8,128)(2,1)S(1)}, u32[]{:S(2)}, u32[]{:S(2)}) %collective-permute-start.24) | collective-permute-done | bytes 393248 | tf_op jit(solution)/shard_map/ppermute | solution.py:122
  622.4 10.2 %collective-permute-done.27 = bf16[256,1536]{1,0:T(8,128)(2,1)} collective-permute-done((bf16[256,1536]{1,0:T(8,128)(2,1)}, bf16[256,1536]{1,0:T(8,128)(2,1)}, u32[]{:S(2)}, u32[]{:S(2)}) %collective-permute-start.27) | collective-permute-done | bytes 786464 | tf_op jit(solution)/shard_map/ppermute | solution.py:122
  674.6 6.4 collective-permute-done.28
  687.1 6.5 collective-permute-done.29
  (608 shorter events, 423.9 us)
Async XLA Ops:
  7.2 93.7 %all-gather.5.cloned.1.call-start = ((), (), s32[]{:S(2)}) async-start(), calls=%async_computation.19 | async-start | bytes 5308416 | tf_op jit(solution)/shard_map/all_gather | solution.py:310
  29.9 202.1 %all-gather.7.cloned.1.call-start = ((), (), s32[]{:S(2)}) async-start(), calls=%async_computation.20 | async-start | bytes 5308416 | tf_op jit(solution)/shard_map/all_gather | solution.py:310
  50.9 49.1 %collective-permute-start.5 = (bf16[192,1536]{1,0:T(8,128)(2,1)}, bf16[192,1536]{1,0:T(8,128)(2,1)}, u32[]{:S(2)}, u32[]{:S(2)}) collective-permute-start(bf16[192,1536]{1,0:T(8,128)(2,1)} %get-tuple-element.42), channel_id=1, source_target_pairs={{0,16},{8,24},{1,17},{9,25},{2,18},{10,26},{3,19},{11,27},{4,20},{... | collective-permute-start | bytes 1769480 | tf_op jit(solution)/shard_map/ppermute | solution.py:128
  85.1 222.4 %all-gather.9.cloned.1.call-start = ((), (), s32[]{:S(2)}) async-start(), calls=%async_computation.21 | async-start | bytes 5308416 | tf_op jit(solution)/shard_map/all_gather | solution.py:310
  106.8 43.8 %collective-permute-start.7 = (bf16[768,384]{1,0:T(8,128)(2,1)}, bf16[768,384]{1,0:T(8,128)(2,1)}, u32[]{:S(2)}, u32[]{:S(2)}) collective-permute-start(bf16[768,384]{1,0:T(8,128)(2,1)} %bitcast.25), channel_id=1, source_target_pairs={{0,8},{8,0},{16,24},{24,16},{1,9},{9,1},{17,25},{25,17},{2,10},{10... | collective-permute-start | bytes 1769480 | tf_op jit(solution)/shard_map/ppermute | solution.py:122
  108.3 44.1 %collective-permute-start.6 = (bf16[768,384]{1,0:T(8,128)(2,1)}, bf16[768,384]{1,0:T(8,128)(2,1)}, u32[]{:S(2)}, u32[]{:S(2)}) collective-permute-start(bf16[768,384]{1,0:T(8,128)(2,1)} %bitcast.25), channel_id=1, source_target_pairs={{0,16},{8,24},{16,0},{24,8},{1,17},{9,25},{17,1},{25,9},{2,18},{10... | collective-permute-start | bytes 1769480 | tf_op jit(solution)/shard_map/ppermute | solution.py:122
  148.3 41.3 %collective-permute-start.10 = (bf16[192,1536]{1,0:T(8,128)(2,1)}, bf16[192,1536]{1,0:T(8,128)(2,1)}, u32[]{:S(2)}, u32[]{:S(2)}) collective-permute-start(bf16[192,1536]{1,0:T(8,128)(2,1)} %broadcast_select_fusion.6), channel_id=1, source_target_pairs={{0,16},{8,24},{16,0},{24,8},{1,17},{9,25},{17,1},{25,9},{2,18},{10... | collective-permute-start | bytes 1769480 | tf_op jit(solution)/shard_map/ppermute | solution.py:122
  152.3 41.4 %collective-permute-start.8 = (bf16[384,384]{1,0:T(8,128)(2,1)}, bf16[384,384]{1,0:T(8,128)(2,1)}, u32[]{:S(2)}, u32[]{:S(2)}) collective-permute-start(bf16[384,384]{1,0:T(8,128)(2,1)} %slice.506), channel_id=1, source_target_pairs={{0,16},{8,24},{16,0},{24,8},{1,17},{9,25},{17,1},{25,9},{2,18},{10... | collective-permute-start | bytes 884744 | tf_op jit(solution)/shard_map/ppermute | solution.py:122
  154.1 40.7 %collective-permute-start.9 = (bf16[384,384]{1,0:T(8,128)(2,1)}, bf16[384,384]{1,0:T(8,128)(2,1)}, u32[]{:S(2)}, u32[]{:S(2)}) collective-permute-start(bf16[384,384]{1,0:T(8,128)(2,1)} %slice.507), channel_id=1, source_target_pairs={{0,8},{8,0},{16,24},{24,16},{1,9},{9,1},{17,25},{25,17},{2,10},{10... | collective-permute-start | bytes 884744 | tf_op jit(solution)/shard_map/ppermute | solution.py:122
  221.8 96.0 %all-gather.11.cloned.1.call-start = ((), (), s32[]{:S(2)}) async-start(), calls=%async_computation.22 | async-start | bytes 5308416 | tf_op jit(solution)/shard_map/all_gather | solution.py:310
  231.9 216.4 %reduce-scatter.7.cloned.1.call-start = ((), (), s32[]{:S(2)}) async-start(), calls=%async_computation.23 | async-start | bytes 5308416 | tf_op jit(solution)/shard_map/reduce_scatter | solution.py:433
  317.4 131.0 %reduce-scatter.9.cloned.1.call-start = ((), (), s32[]{:S(2)}) async-start(), calls=%async_computation.24 | async-start | bytes 5308416 | tf_op jit(solution)/shard_map/reduce_scatter | solution.py:433
  336.1 285.7 %reduce-scatter.13.cloned.1.call-start = ((), (), s32[]{:S(2)}) async-start(), calls=%async_computation.26 | async-start | bytes 1327104 | tf_op jit(solution)/shard_map/reduce_scatter | solution.py:433
  432.7 189.1 %reduce-scatter.11.cloned.1.call-start = ((), (), s32[]{:S(2)}) async-start(), calls=%async_computation.25 | async-start | bytes 3981312 | tf_op jit(solution)/shard_map/reduce_scatter | solution.py:433
  459.9 72.8 %collective-permute-start.21 = (bf16[384,384]{1,0:T(8,128)(2,1)}, bf16[384,384]{1,0:T(8,128)(2,1)}, u32[]{:S(2)}, u32[]{:S(2)}) collective-permute-start(bf16[384,384]{1,0:T(8,128)(2,1)} %get-tuple-element.141), channel_id=1, source_target_pairs={{0,8},{8,0},{16,24},{24,16},{1,9},{9,1},{17,25},{25,17},{2,10},{10... | collective-permute-start | bytes 884744 | tf_op jit(solution)/shard_map/ppermute | solution.py:122
  461.4 71.3 %collective-permute-start.20 = (bf16[384,384]{1,0:T(8,128)(2,1)}, bf16[384,384]{1,0:T(8,128)(2,1)}, u32[]{:S(2)}, u32[]{:S(2)}) collective-permute-start(bf16[384,384]{1,0:T(8,128)(2,1)} %get-tuple-element.142), channel_id=1, source_target_pairs={{0,16},{8,24},{16,0},{24,8},{1,17},{9,25},{17,1},{25,9},{2,18},{10... | collective-permute-start | bytes 884744 | tf_op jit(solution)/shard_map/ppermute | solution.py:122
  462.8 73.2 %collective-permute-start.38 = (bf16[96,1536]{1,0:T(8,128)(2,1)}, bf16[96,1536]{1,0:T(8,128)(2,1)}, u32[]{:S(2)}, u32[]{:S(2)}) collective-permute-start(bf16[96,1536]{1,0:T(8,128)(2,1)} %get-tuple-element.139), channel_id=1, source_target_pairs={{0,8},{8,0},{16,24},{24,16},{1,9},{9,1},{17,25},{25,17},{2,10},{10... | collective-permute-start | bytes 884744 | tf_op jit(solution)/shard_map/ppermute | solution.py:122
  464.3 71.7 %collective-permute-start.37 = (bf16[96,1536]{1,0:T(8,128)(2,1)}, bf16[96,1536]{1,0:T(8,128)(2,1)}, u32[]{:S(2)}, u32[]{:S(2)}) collective-permute-start(bf16[96,1536]{1,0:T(8,128)(2,1)} %get-tuple-element.140), channel_id=1, source_target_pairs={{0,16},{8,24},{16,0},{24,8},{1,17},{9,25},{17,1},{25,9},{2,18},{10... | collective-permute-start | bytes 884744 | tf_op jit(solution)/shard_map/ppermute | solution.py:122
  472.9 192.0 %reduce-scatter.17.cloned.1.call-start = ((), (), s32[]{:S(2)}) async-start(), calls=%async_computation.28 | async-start | bytes 1327104 | tf_op jit(solution)/shard_map/reduce_scatter | solution.py:433
  494.1 120.7 %collective-permute-start.43 = (bf16[192,1536]{1,0:T(8,128)(2,1)}, bf16[192,1536]{1,0:T(8,128)(2,1)}, u32[]{:S(2)}, u32[]{:S(2)}) collective-permute-start(bf16[192,1536]{1,0:T(8,128)(2,1)} %reduce-scatter.7.cloned.1.call-done), channel_id=1, source_target_pairs={{1,16},{17,17},{3,18},{19,19},{5,20},{21,21},{7,22},{23,23},{9,24}... | collective-permute-start | bytes 1769480 | tf_op jit(solution)/shard_map/ppermute | solution.py:189
  555.2 140.9 %reduce-scatter.15.cloned.1.call-start = ((), (), s32[]{:S(2)}) async-start(), calls=%async_computation.27 | async-start | bytes 3981312 | tf_op jit(solution)/shard_map/reduce_scatter | solution.py:433
  564.8 50.0 %collective-permute-start.42 = (bf16[192,1536]{1,0:T(8,128)(2,1)}, bf16[192,1536]{1,0:T(8,128)(2,1)}, u32[]{:S(2)}, u32[]{:S(2)}) collective-permute-start(bf16[192,1536]{1,0:T(8,128)(2,1)} %reduce-scatter.7.cloned.1.call-done), channel_id=1, source_target_pairs={{0,16},{16,17},{2,18},{18,19},{4,20},{20,21},{6,22},{22,23},{8,24}... | collective-permute-start | bytes 1769480 | tf_op jit(solution)/shard_map/ppermute | solution.py:189
  572.8 42.1 %collective-permute-start.41 = (bf16[192,1536]{1,0:T(8,128)(2,1)}, bf16[192,1536]{1,0:T(8,128)(2,1)}, u32[]{:S(2)}, u32[]{:S(2)}) collective-permute-start(bf16[192,1536]{1,0:T(8,128)(2,1)} %fusion.78), channel_id=1, source_target_pairs={{16,0},{24,8},{17,1},{25,9},{18,2},{26,10},{19,3},{27,11},{20,4},{... | collective-permute-start | bytes 1769480 | tf_op jit(solution)/shard_map/ppermute | solution.py:131
  620.4 51.2 %collective-permute-start.35 = (bf16[96,3072]{1,0:T(8,128)(2,1)}, bf16[96,3072]{1,0:T(8,128)(2,1)}, u32[]{:S(2)}, u32[]{:S(2)}) collective-permute-start(bf16[96,3072]{1,0:T(8,128)(2,1)} %bitcast.137), channel_id=1, source_target_pairs={{16,0},{24,8},{17,1},{25,9},{18,2},{26,10},{19,3},{27,11},{20,4},{... | collective-permute-start | bytes 1769480 | tf_op jit(solution)/shard_map/ppermute | solution.py:131
  (143 other events, 1470.5 us)
Sparse Core Ops, SparseCore 0:
  30.0 70.6 all-gather.4
  102.3 51.7 all-gather.6
  156.3 60.8 all-gather.8
  232.0 51.3 all-gather.10
  317.5 55.0 reduce-scatter.6
  374.8 65.9 reduce-scatter.8
  443.0 30.9 reduce-scatter.12
  476.4 46.1 reduce-scatter.10
  532.8 34.3 reduce-scatter.16
  577.3 54.0 reduce-scatter.14

commit v19 on v18

--- a/solution.py
+++ b/solution.py
@@ -282,7 +282,7 @@
             for mask in range(1, section_count):
                 chosen = jnp.where(section ^ mask == target, by_mask[mask], chosen)
             ordered.append(chosen)
-        return jnp.concatenate(ordered, axis=0)
+        return jnp.concatenate(ordered, axis=0), by_mask[1]
 
     def column_parts(weight, block):
         rows, width = weight.shape
@@ -538,18 +538,17 @@
             media_grads = (grad_key, grad_value)
         gain_rows[layer] = (gain_latent_grad, gain_ffn_grad)
     out_grad = join_rows(*[piece[1] for piece in pieces], stride)
-    latent_grad = to_columns(after(grad_rows, (pieces[1], up_half)))
     media_rows = seq_rows // section_count
     media_sum = sum_over_sections(media_parts[0].astype(full) + media_parts[1])
     own_unit = lax.dynamic_slice_in_dim(media_unit, section * media_rows, media_rows, 0)
     own_inverse = lax.dynamic_slice_in_dim(media_inverse, section * media_rows, media_rows, 0)
-    media_grad = gather_sections(norm_back(own_unit, own_inverse, media_sum).astype(low)).astype(
-        full
-    )
+    media_grad, media_hop = gather_sections(norm_back(own_unit, own_inverse, media_sum).astype(low))
+    media_grad = media_grad.astype(full)
+    latent_grad = to_columns(after(grad_rows, (pieces[1], up_half, media_hop)))
     gain_rows = [
         jnp.stack([media_gains[1 - layer], *gain_rows[layer]]) for layer in range(LAYERS)
     ]
-    gain_parts = after(jnp.stack(gain_rows), media_sum).reshape(LAYERS, 3, section_count, -1)
+    gain_parts = after(jnp.stack(gain_rows), media_hop).reshape(LAYERS, 3, section_count, -1)
     gain_parts = jnp.sum(
         lax.all_to_all(gain_parts, "section", split_axis=2, concat_axis=2), axis=2
     )

time: 726 us -> 774 us (1.066)
  local copies, waits for them, and re-layouts: 77.9 us -> 97.3 us
  blocking collectives: 159 us -> 171 us
  waiting for transfers between devices: 106 us -> 116 us
    all_to_all x2, waiting for transfers between devices: 0.21 us -> 28.8 us  [sum_to_sequence(): arrived = lax.all_to_all(blocks, 'pair', split_axis=0, concat_axis=0)]
    all_to_all x0 -> x1, blocking collectives: none -> 16 us  [per_device(): last = lax.all_to_all(last, 'section', split_axis=0, concat_axis=0)]
    all_to_all x1 -> x0, waiting for transfers between devices: 9.32 us -> none  [per_device(): last = lax.all_to_all(last, 'section', split_axis=0, concat_axis=0)]
    ppermute x26, waiting for transfers between devices: 55.6 us -> 47.5 us  [swapped(): return lax.ppermute(value, 'section', pairs)]
    unnamed x208 -> x280, local copies, waits for them, and re-layouts: 19.1 us -> 20.6 us
  transfers between devices with their start and end apart: 66 -> 65, of which waited for: 23 -> 19; matrix products, arithmetic and copies ran while one was open for 40% -> 40% of each run, Pallas kernels for 0% -> 0%
where the time goes in v19:
time: 774 us; the launch traced here: 766 us
  blocking collectives  171 us (22%)
  matrix products  138 us (18%)
  starting transfers between devices  126 us (16%)
  waiting for transfers between devices  116 us (15%)
  other arithmetic  102 us (13%)
  local copies, waits for them, and re-layouts  97.3 us (13%)
  between operations  16.9 us (2%)
    all_gather x2, blocking collectives, from_sequences(): near = lax.all_gather(rows, 'pair', axis=0, tiled=True)  57.7 us
    all_gather x4, blocking collectives, from_slots(): return lax.all_gather(rows, 'section', axis=0, tiled=True)  55.1 us
    ppermute x26, waiting for transfers between devices, swapped(): return lax.ppermute(value, 'section', pairs)  47.5 us
    dot_general x17, matrix products, matmul_nt(): lax.dot_general(left, right, (((1,), (1,)), ((), ())), preferred_element_...  44.8 us
    dot_general x13, matrix products, matmul(): return jnp.dot(left, right, preferred_element_type=full)  40.4 us
    ppermute x26, starting transfers between devices, swapped(): return lax.ppermute(value, 'section', pairs)  36.2 us
    dot_general x8, matrix products, matmul_tn(): lax.dot_general(left, right, (((0,), (0,)), ((), ())), preferred_element_...  32.3 us
    all_gather x3, blocking collectives, per_device(): all_gains = lax.all_gather(all_gains, axis, axis=2, tiled=True)  31.2 us
  transfers between devices with their start and end apart: 65, of which 19 were waited for; matrix products, arithmetic and copies ran while one was open for 40% of the time, Pallas kernels for 0%

profile of v19, /device:TPU:0, one launch (start us, length us, event | category | flops | bytes accessed | tf_op | source)
XLA Modules:
  0.0 766.5 jit_solution(6121052359739276798)
XLA Ops:
  12.6 10.2 %collective-permute-done = bf16[192,1152]{1,0:T(8,128)(2,1)S(1)} collective-permute-done((bf16[192,1152]{1,0:T(8,128)(2,1)S(1)}, bf16[192,1152]{1,0:T(8,128)(2,1)S(1)}, u32[]{:S(2)}, u32[]{:S(2)}) %collective-permute-start) | collective-permute-done | bytes 442400 | tf_op jit(solution)/shard_map/ppermute | solution.py:122
  31.2 10.9 %collective-permute-start.1 = (bf16[96,3072]{1,0:T(8,128)(2,1)}, bf16[96,3072]{1,0:T(8,128)(2,1)}, u32[]{:S(2)}, u32[]{:S(2)}) collective-permute-start(bf16[96,3072]{1,0:T(8,128)(2,1)} %slice_bitcast_fusion.4), channel_id=1, source_target_pairs={{0,16},{8,24},{1,17},{9,25},{2,18},{10,26},{3,19},{11,27},{4,20},{... | collective-permute-start | bytes 1769480 | tf_op jit(solution)/shard_map/ppermute | solution.py:128
  57.1 18.6 %all_gather.40 = f32[2,3,384]{1,0,2:T(2,128)S(1)} all-gather(f32[2,3,96]{1,0,2:T(2,128)S(1)} %all_gather.39), channel_id=1, replica_groups=mesh['section'=4,'pair'=4,'core'=2] {'pair'}, dimensions={2}, use_global_device_ids=true | all-gather | bytes 11520 | tf_op jit(solution)/shard_map/all_gather | solution.py:306
  82.1 10.7 %all_gather.41 = f32[2,3,1536]{2,0,1:T(2,128)S(1)} all-gather(f32[2,3,384]{2,0,1:T(2,128)S(1)} %copy.153), channel_id=1, replica_groups=mesh['section'=4,'pair'=4,'core'=2] {'section'}, dimensions={2}, use_global_device_ids=true | all-gather | bytes 46080 | tf_op jit(solution)/shard_map/all_gather | solution.py:306
  99.0 6.4 all-gather.5.cloned.1.call-done
  111.9 6.3 slice_reduce_fusion
  163.3 29.1 %all_gather.43 = bf16[256,1536]{1,0:T(8,128)(2,1)S(1)} all-gather(bf16[64,1536]{1,0:T(8,128)(2,1)S(1)} %reshape.720), channel_id=1, replica_groups=mesh['section'=4,'pair'=4,'core'=2] {'pair'}, dimensions={0}, use_global_device_ids=true | all-gather | bytes 983040 | tf_op jit(solution)/shard_map/all_gather | solution.py:234
  198.6 7.1 collective-permute-done.13
  223.6 9.1 %collective-permute-done.16 = bf16[192,1536]{1,0:T(8,128)(2,1)S(1)} collective-permute-done((bf16[192,1536]{1,0:T(8,128)(2,1)}, bf16[192,1536]{1,0:T(8,128)(2,1)S(1)}, u32[]{:S(2)}, u32[]{:S(2)}) %collective-permute-start.16) | collective-permute-done | bytes 589856 | tf_op jit(solution)/shard_map/ppermute | solution.py:177
  250.3 21.0 %all_gather.45 = bf16[256,1536]{1,0:T(8,128)(2,1)S(1)} all-gather(bf16[64,1536]{1,0:T(8,128)(2,1)S(1)} %multiply_convert_fusion.9), channel_id=1, replica_groups=mesh['section'=4,'pair'=4,'core'=2] {'section'}, dimensions={0}, use_global_device_ids=true | all-gather | bytes 983040 | tf_op jit(solution)/shard_map/all_gather | solution.py:225
  289.5 11.1 %all_to_all.101 = bf16[4,64,1536]{2,1,0:T(8,128)(2,1)S(1)} all-to-all(bf16[4,64,1536]{2,1,0:T(8,128)(2,1)S(1)} %bitcast.368), channel_id=1, replica_groups=mesh['section'=4,'pair'=4,'core'=2] {'section'}, dimensions={0} | all-to-all | bytes 1572864 | tf_op jit(solution)/shard_map/all_to_all | solution.py:221
  301.6 11.1 %all_gather.46 = bf16[256,1536]{1,0:T(8,128)(2,1)} all-gather(bf16[64,1536]{1,0:T(8,128)(2,1)S(1)} %multiply_convert_fusion.8), channel_id=1, replica_groups=mesh['section'=4,'pair'=4,'core'=2] {'section'}, dimensions={0}, use_global_device_ids=true | all-gather | bytes 983040 | tf_op jit(solution)/shard_map/all_gather | solution.py:225
  350.1 11.6 %all_gather.49 = bf16[256,1536]{1,0:T(8,128)(2,1)S(1)} all-gather(bf16[64,1536]{1,0:T(8,128)(2,1)S(1)} %get-tuple-element.96), channel_id=1, replica_groups=mesh['section'=4,'pair'=4,'core'=2] {'section'}, dimensions={0}, use_global_device_ids=true | all-gather | bytes 983040 | tf_op jit(solution)/shard_map/all_gather | solution.py:225
  386.1 9.5 %convolution_convert_fusion.2 = bf16[1536,1152]{1,0:T(8,128)(2,1)} fusion(bf16[256,1536]{1,0:T(8,128)(2,1)} %copy-done.74, bf16[1024,1536]{1,0:T(8,128)(2,1)} %get-tuple-element.114, bf16[256,384]{0,1:T(8,128)(2,1)S(1)} %bitcast.400, bf16[1280,384]{0,1:T(8,128)(2,1)S(1)} %bitcast.348, bf16[1280,384]{0,1:T(8,128)(2,1)} %bitcast.358), kind=kOutput, calls=%fused_computation.4 | convolution fusion | flops 4551278592 | bytes 9633792 | tf_op jit(solution)/shard_map/dot_general | solution.py:48
  400.4 28.6 %all_gather.50 = bf16[256,1536]{1,0:T(8,128)(2,1)S(1)} all-gather(bf16[64,1536]{1,0:T(8,128)(2,1)S(1)} %get-tuple-element.94), channel_id=1, replica_groups=mesh['section'=4,'pair'=4,'core'=2] {'pair'}, dimensions={0}, use_global_device_ids=true | all-gather | bytes 983040 | tf_op jit(solution)/shard_map/all_gather | solution.py:234
  432.8 16.0 %all_to_all.102 = bf16[4,256,384]{2,1,0:T(8,128)(2,1)S(1)} all-to-all(bf16[4,256,384]{2,1,0:T(8,128)(2,1)S(1)} %bitcast.367), channel_id=1, replica_groups=mesh['section'=4,'pair'=4,'core'=2] {'section'}, dimensions={0} | all-to-all | bytes 1572864 | tf_op jit(solution)/shard_map/all_to_all | solution.py:531
  466.2 24.7 %all-to-all-done.7 = bf16[4,64,1536]{2,1,0:T(8,128)(2,1)S(1)} async-done(((bf16[4,64,1536]{2,1,0:T(8,128)(2,1)}), bf16[4,64,1536]{2,1,0:T(8,128)(2,1)S(1)}, u32[]{:S(2)}, u32[]{:S(2)}) %all-to-all-start.7) | async-done | bytes 786464 | tf_op jit(solution)/shard_map/all_to_all | solution.py:242
  500.9 11.3 %all_gather.51 = bf16[256,1536]{1,0:T(8,128)(2,1)S(1)} all-gather(bf16[64,1536]{1,0:T(8,128)(2,1)S(1)} %get-tuple-element.92), channel_id=1, replica_groups=mesh['section'=4,'pair'=4,'core'=2] {'section'}, dimensions={0}, use_global_device_ids=true | all-gather | bytes 983040 | tf_op jit(solution)/shard_map/all_gather | solution.py:225
  596.0 9.3 %convolution_convert_fusion = bf16[1536,1152]{1,0:T(8,128)(2,1)} fusion(bf16[256,1536]{1,0:T(8,128)(2,1)} %copy-done.73, bf16[1024,1536]{1,0:T(8,128)(2,1)} %get-tuple-element.115, bf16[256,384]{0,1:T(8,128)(2,1)S(1)} %bitcast.398, bf16[1280,384]{0,1:T(8,128)(2,1)S(1)} %bitcast.352, bf16[1280,384]{0,1:T(8,128)(2,1)S(1)} %bitcast.362), kind=kOutput, calls=%fused_computation.2 | convolution fusion | flops 4551278592 | bytes 9633792 | tf_op jit(solution)/shard_map/dot_general | solution.py:48
  620.8 7.9 %multiply_reduce_fusion.1 = (f32[1536]{0:T(1024)S(1)}, f32[1536]{0:T(1024)S(1)}, f32[1024,1536]{1,0:T(8,128)S(1)}, f32[1024,1536]{1,0:T(8,128)}) fusion(bf16[1024,1536]{1,0:T(8,128)(2,1)S(1)} %copy-done.3, f32[1024]{0:T(1024)S(1)} %copy-done.93, f32[1024]{0:T(1024)S(1)} %copy-done.92, f32[1024,1536]{1,0:T(8,128)} %convolution_add_fusion.1, ...), kind=kOutput, calls=%fused_computation.10 | convolution fusion | flops 1228403712 | bytes 30310400 | tf_op jit(solution)/shard_map/dot_general | solution.py:44
  644.7 6.9 collective-permute-done.24
  657.7 16.0 %collective-permute-done.27 = bf16[256,1536]{1,0:T(8,128)(2,1)S(1)} collective-permute-done((bf16[256,1536]{1,0:T(8,128)(2,1)S(1)}, bf16[256,1536]{1,0:T(8,128)(2,1)S(1)}, u32[]{:S(2)}, u32[]{:S(2)}) %collective-permute-start.27) | collective-permute-done | bytes 786464 | tf_op jit(solution)/shard_map/ppermute | solution.py:122
  706.8 7.9 %all-to-all-done.11 = f32[2,3,4,384]{3,0,1,2:T(2,128)S(1)} async-done(((f32[2,3,4,384]{3,0,1,2:T(2,128)}), f32[2,3,4,384]{3,0,1,2:T(2,128)S(1)}, u32[]{:S(2)}, u32[]{:S(2)}) %all-to-all-start.11) | async-done | bytes 36896 | tf_op jit(solution)/shard_map/all_to_all | solution.py:553
  715.5 10.8 %all-to-all-start.12 = ((f32[8,1,288]{2,1,0:T(1,128)}), f32[8,1,288]{2,1,0:T(1,128)S(1)}, u32[]{:S(2)}, u32[]{:S(2)}) async-start(f32[8,1,288]{2,1,0:T(1,128)} %reshape.758), calls=%async_computation.16 | async-start | bytes 24576 | tf_op jit(solution)/shard_map/all_to_all | solution.py:556
  (681 shorter events, 437.6 us)
Async XLA Ops:
  7.2 98.2 %all-gather.5.cloned.1.call-start = ((), (), s32[]{:S(2)}) async-start(), calls=%async_computation.19 | async-start | bytes 5308416 | tf_op jit(solution)/shard_map/all_gather | solution.py:310
  29.3 204.4 %all-gather.7.cloned.1.call-start = ((), (), s32[]{:S(2)}) async-start(), calls=%async_computation.20 | async-start | bytes 5308416 | tf_op jit(solution)/shard_map/all_gather | solution.py:310
  52.1 45.9 %collective-permute-start.5 = (bf16[192,1536]{1,0:T(8,128)(2,1)}, bf16[192,1536]{1,0:T(8,128)(2,1)}, u32[]{:S(2)}, u32[]{:S(2)}) collective-permute-start(bf16[192,1536]{1,0:T(8,128)(2,1)} %get-tuple-element.42), channel_id=1, source_target_pairs={{0,16},{8,24},{1,17},{9,25},{2,18},{10,26},{3,19},{11,27},{4,20},{... | collective-permute-start | bytes 1769480 | tf_op jit(solution)/shard_map/ppermute | solution.py:128
  82.0 230.8 %all-gather.9.cloned.1.call-start = ((), (), s32[]{:S(2)}) async-start(), calls=%async_computation.21 | async-start | bytes 5308416 | tf_op jit(solution)/shard_map/all_gather | solution.py:310
  108.6 43.2 %collective-permute-start.7 = (bf16[768,384]{1,0:T(8,128)(2,1)}, bf16[768,384]{1,0:T(8,128)(2,1)}, u32[]{:S(2)}, u32[]{:S(2)}) collective-permute-start(bf16[768,384]{1,0:T(8,128)(2,1)} %bitcast.25), channel_id=1, source_target_pairs={{0,8},{8,0},{16,24},{24,16},{1,9},{9,1},{17,25},{25,17},{2,10},{10... | collective-permute-start | bytes 1769480 | tf_op jit(solution)/shard_map/ppermute | solution.py:122
  110.1 43.4 %collective-permute-start.6 = (bf16[768,384]{1,0:T(8,128)(2,1)}, bf16[768,384]{1,0:T(8,128)(2,1)}, u32[]{:S(2)}, u32[]{:S(2)}) collective-permute-start(bf16[768,384]{1,0:T(8,128)(2,1)} %bitcast.25), channel_id=1, source_target_pairs={{0,16},{8,24},{16,0},{24,8},{1,17},{9,25},{17,1},{25,9},{2,18},{10... | collective-permute-start | bytes 1769480 | tf_op jit(solution)/shard_map/ppermute | solution.py:122
  149.4 43.0 %collective-permute-start.10 = (bf16[192,1536]{1,0:T(8,128)(2,1)}, bf16[192,1536]{1,0:T(8,128)(2,1)}, u32[]{:S(2)}, u32[]{:S(2)}) collective-permute-start(bf16[192,1536]{1,0:T(8,128)(2,1)} %broadcast_select_fusion.6), channel_id=1, source_target_pairs={{0,16},{8,24},{16,0},{24,8},{1,17},{9,25},{17,1},{25,9},{2,18},{10... | collective-permute-start | bytes 1769480 | tf_op jit(solution)/shard_map/ppermute | solution.py:122
  153.4 43.1 %collective-permute-start.8 = (bf16[384,384]{1,0:T(8,128)(2,1)}, bf16[384,384]{1,0:T(8,128)(2,1)S(1)}, u32[]{:S(2)}, u32[]{:S(2)}) collective-permute-start(bf16[384,384]{1,0:T(8,128)(2,1)} %slice.506), channel_id=1, source_target_pairs={{0,16},{8,24},{16,0},{24,8},{1,17},{9,25},{17,1},{25,9},{2,18},{10... | collective-permute-start | bytes 884744 | tf_op jit(solution)/shard_map/ppermute | solution.py:122
  155.2 41.4 %collective-permute-start.9 = (bf16[384,384]{1,0:T(8,128)(2,1)}, bf16[384,384]{1,0:T(8,128)(2,1)}, u32[]{:S(2)}, u32[]{:S(2)}) collective-permute-start(bf16[384,384]{1,0:T(8,128)(2,1)} %slice.507), channel_id=1, source_target_pairs={{0,8},{8,0},{16,24},{24,16},{1,9},{9,1},{17,25},{25,17},{2,10},{10... | collective-permute-start | bytes 884744 | tf_op jit(solution)/shard_map/ppermute | solution.py:122
  223.6 99.5 %all-gather.11.cloned.1.call-start = ((), (), s32[]{:S(2)}) async-start(), calls=%async_computation.22 | async-start | bytes 5308416 | tf_op jit(solution)/shard_map/all_gather | solution.py:310
  233.6 217.4 %reduce-scatter.7.cloned.1.call-start = ((), (), s32[]{:S(2)}) async-start(), calls=%async_computation.23 | async-start | bytes 5308416 | tf_op jit(solution)/shard_map/reduce_scatter | solution.py:433
  337.2 113.7 %reduce-scatter.9.cloned.1.call-start = ((), (), s32[]{:S(2)}) async-start(), calls=%async_computation.24 | async-start | bytes 5308416 | tf_op jit(solution)/shard_map/reduce_scatter | solution.py:433
  465.3 224.3 %reduce-scatter.13.cloned.1.call-start = ((), (), s32[]{:S(2)}) async-start(), calls=%async_computation.26 | async-start | bytes 1327104 | tf_op jit(solution)/shard_map/reduce_scatter | solution.py:433
  466.1 223.5 %reduce-scatter.17.cloned.1.call-start = ((), (), s32[]{:S(2)}) async-start(), calls=%async_computation.28 | async-start | bytes 1327104 | tf_op jit(solution)/shard_map/reduce_scatter | solution.py:433
  514.8 214.8 %reduce-scatter.11.cloned.1.call-start = ((), (), s32[]{:S(2)}) async-start(), calls=%async_computation.25 | async-start | bytes 3981312 | tf_op jit(solution)/shard_map/reduce_scatter | solution.py:433
  527.4 47.9 %collective-permute-start.21 = (bf16[384,384]{1,0:T(8,128)(2,1)}, bf16[384,384]{1,0:T(8,128)(2,1)}, u32[]{:S(2)}, u32[]{:S(2)}) collective-permute-start(bf16[384,384]{1,0:T(8,128)(2,1)} %get-tuple-element.141), channel_id=1, source_target_pairs={{0,8},{8,0},{16,24},{24,16},{1,9},{9,1},{17,25},{25,17},{2,10},{10... | collective-permute-start | bytes 884744 | tf_op jit(solution)/shard_map/ppermute | solution.py:122
  528.7 46.7 %collective-permute-start.20 = (bf16[384,384]{1,0:T(8,128)(2,1)}, bf16[384,384]{1,0:T(8,128)(2,1)}, u32[]{:S(2)}, u32[]{:S(2)}) collective-permute-start(bf16[384,384]{1,0:T(8,128)(2,1)} %get-tuple-element.142), channel_id=1, source_target_pairs={{0,16},{8,24},{16,0},{24,8},{1,17},{9,25},{17,1},{25,9},{2,18},{10... | collective-permute-start | bytes 884744 | tf_op jit(solution)/shard_map/ppermute | solution.py:122
  530.3 45.1 %collective-permute-start.38 = (bf16[96,1536]{1,0:T(8,128)(2,1)}, bf16[96,1536]{1,0:T(8,128)(2,1)}, u32[]{:S(2)}, u32[]{:S(2)}) collective-permute-start(bf16[96,1536]{1,0:T(8,128)(2,1)} %get-tuple-element.139), channel_id=1, source_target_pairs={{0,8},{8,0},{16,24},{24,16},{1,9},{9,1},{17,25},{25,17},{2,10},{10... | collective-permute-start | bytes 884744 | tf_op jit(solution)/shard_map/ppermute | solution.py:122
  531.6 43.8 %collective-permute-start.37 = (bf16[96,1536]{1,0:T(8,128)(2,1)}, bf16[96,1536]{1,0:T(8,128)(2,1)}, u32[]{:S(2)}, u32[]{:S(2)}) collective-permute-start(bf16[96,1536]{1,0:T(8,128)(2,1)} %get-tuple-element.140), channel_id=1, source_target_pairs={{0,16},{8,24},{16,0},{24,8},{1,17},{9,25},{17,1},{25,9},{2,18},{10... | collective-permute-start | bytes 884744 | tf_op jit(solution)/shard_map/ppermute | solution.py:122
  551.4 128.9 %collective-permute-start.43 = (bf16[192,1536]{1,0:T(8,128)(2,1)}, bf16[192,1536]{1,0:T(8,128)(2,1)}, u32[]{:S(2)}, u32[]{:S(2)}) collective-permute-start(bf16[192,1536]{1,0:T(8,128)(2,1)} %reduce-scatter.7.cloned.1.call-done), channel_id=1, source_target_pairs={{1,16},{17,17},{3,18},{19,19},{5,20},{21,21},{7,22},{23,23},{9,24}... | collective-permute-start | bytes 1769480 | tf_op jit(solution)/shard_map/ppermute | solution.py:189
  595.5 149.2 %reduce-scatter.15.cloned.1.call-start = ((), (), s32[]{:S(2)}) async-start(), calls=%async_computation.27 | async-start | bytes 3981312 | tf_op jit(solution)/shard_map/reduce_scatter | solution.py:433
  605.3 75.0 %collective-permute-start.42 = (bf16[192,1536]{1,0:T(8,128)(2,1)}, bf16[192,1536]{1,0:T(8,128)(2,1)}, u32[]{:S(2)}, u32[]{:S(2)}) collective-permute-start(bf16[192,1536]{1,0:T(8,128)(2,1)} %reduce-scatter.7.cloned.1.call-done), channel_id=1, source_target_pairs={{0,16},{16,17},{2,18},{18,19},{4,20},{20,21},{6,22},{22,23},{8,24}... | collective-permute-start | bytes 1769480 | tf_op jit(solution)/shard_map/ppermute | solution.py:189
  613.1 67.2 %collective-permute-start.41 = (bf16[192,1536]{1,0:T(8,128)(2,1)}, bf16[192,1536]{1,0:T(8,128)(2,1)}, u32[]{:S(2)}, u32[]{:S(2)}) collective-permute-start(bf16[192,1536]{1,0:T(8,128)(2,1)} %fusion.78), channel_id=1, source_target_pairs={{16,0},{24,8},{17,1},{25,9},{18,2},{26,10},{19,3},{27,11},{20,4},{... | collective-permute-start | bytes 1769480 | tf_op jit(solution)/shard_map/ppermute | solution.py:131
  632.4 45.7 %all-to-all-start.9 = ((bf16[8,96,384]{2,1,0:T(8,128)(2,1)}), bf16[8,96,384]{2,1,0:T(8,128)(2,1)S(1)}, u32[]{:S(2)}, u32[]{:S(2)}) async-start(bf16[8,96,384]{2,1,0:T(8,128)(2,1)} %bitcast.370), calls=%async_computation.13 | async-start | bytes 1179648 | tf_op jit(solution)/shard_map/all_to_all | solution.py:522
  (178 other events, 1834.8 us)
Sparse Core Ops, SparseCore 0:
  29.4 75.9 all-gather.4
  107.0 49.1 all-gather.6
  158.4 59.9 all-gather.8
  233.7 50.8 all-gather.10
  322.7 56.0 reduce-scatter.6
  380.9 65.9 reduce-scatter.8
  468.4 34.3 reduce-scatter.12
  514.9 29.8 reduce-scatter.16
  547.1 42.1 reduce-scatter.10
  617.6 53.7 reduce-scatter.14
